TPU v7x, 32 devices: a whole 2x2x4 slice. The times are simulated.
32 devices in a mesh: dp: 8 (over z, x), patch: 4 (over y, core).
Axes of the slice: x: 2, y: 2, z: 4, core: 2. Of those that a mesh axis runs over, the one named last changes fastest.
Arguments:
- text_in: bfloat16 [2, 16384, 768], P(None, ('dp', 'patch')), may hold values from -6 to 6
- image_grid: bfloat16 [2, 128, 144, 1024], P(None, 'dp', 'patch'), may hold values from -6 to 6
- image_cls: bfloat16 [2, 128, 1024], P(None, ('dp', 'patch')), may hold values from -6 to 6
- text_lengths: int32 [2, 128], P(None, ('dp', 'patch')), may hold values from 8 to 128, as said below
- phrase_counts: int32 [2, 128], P(None, ('dp', 'patch')), may hold values from 0 to 6, as said below
- phrase_boxes: int32 [2, 128, 6, 144], P(None, ('dp', 'patch')), may hold values from 0 to 1, as said below
- cotangent: bfloat16 [2, 16384, 768], P(None, ('dp', 'patch')), may hold values from -6 to 6
- self_qkv: bfloat16 [768, 2304], P('dp', 'patch'), may hold values from -0.21875 to 0.21875
- self_out: bfloat16 [768, 768], P('dp', 'patch'), may hold values from -1.75 to 1.75
- cross_q: bfloat16 [768, 768], P('dp', 'patch'), may hold values from -0.21875 to 0.21875
- cross_kv: bfloat16 [1024, 1536], P('dp', 'patch'), may hold values from -0.1875 to 0.1875
- cross_out: bfloat16 [768, 768], P('dp', 'patch'), may hold values from -0.875 to 0.875
- ffn_in: bfloat16 [768, 3072], P('dp', 'patch'), may hold values from -0.21875 to 0.21875
- ffn_out: bfloat16 [3072, 768], P('dp', 'patch'), may hold values from -0.109375 to 0.109375
- vectors: bfloat16 [13, 768], P(None, 'dp'), as said below
- ffn_bias_in: bfloat16 [3072], P('dp'), may hold values from -3 to 3
Outputs:
- layer_out: float32 [2, 16384, 768], P(None, ('dp', 'patch'))
- text_grad: float32 [2, 16384, 768], P(None, ('dp', 'patch'))
- grid_grad: float32 [2, 128, 144, 1024], P(None, 'dp', 'patch')
- cls_grad: float32 [2, 128, 1024], P(None, ('dp', 'patch'))
- self_qkv_grad: float32 [768, 2304], P('dp', 'patch')
- self_out_grad: float32 [768, 768], P('dp', 'patch')
- cross_q_grad: float32 [768, 768], P('dp', 'patch')
- cross_kv_grad: float32 [1024, 1536], P('dp', 'patch')
- cross_out_grad: float32 [768, 768], P('dp', 'patch')
- ffn_in_grad: float32 [768, 3072], P('dp', 'patch')
- ffn_out_grad: float32 [3072, 768], P('dp', 'patch')
- vectors_grad: float32 [13, 768], P(None, 'dp')
- ffn_bias_in_grad: float32 [3072], P('dp')
Inputs may be any that keep to these rules, and one draw needn't show every extreme that they name: `text_lengths`: the first item of every micro-batch has 128 positions. `phrase_counts`: the second item of every micro-batch has 6 phrases. `phrase_boxes`: cells are row-major over a 12 by 12 grid; each phrase's box is a rectangle of one or more whole cells. `vectors`: rows 3, 8 and 11 are gains near one; the other rows are biases.
All inputs are finite; a program needn't handle non-finite values.
Results may differ from a plain program's by a relative error of at most 0.02.
Values may be sent and summed in bfloat16 or wider, within the bound.
No kernel may reach another device: no remote copies, remote signals or barrier semaphores. Data moves between devices by JAX's collectives and lax.ppermute only.
A program may use at most 256 MiB of HBM per device.

v0:
```python
import jax
import jax.numpy as jnp
from jax import lax
from jax.sharding import PartitionSpec as P

HEAD = 64


EPS = 1e-06
NEG = -1e30


def norm_forward(total_in, gain_row, shift_row):
    center = total_in - jnp.mean(total_in, -1, keepdims=True)
    spread = lax.rsqrt(jnp.mean(center * center, -1, keepdims=True) + EPS)
    return center * spread * gain_row + shift_row


def exact_gelu(pre_act):
    return jax.nn.gelu(pre_act, approximate=False)


def self_allowed(lengths, length_max):
    positions = jnp.arange(length_max, dtype=jnp.int32)
    key_ok = positions[None, :] < lengths[:, None]
    return jnp.broadcast_to(key_ok[:, None, :], (lengths.shape[0], length_max, length_max))


def cross_allowed(lengths, counts, boxes, length_max):
    positions = jnp.arange(length_max, dtype=jnp.int32)[None, :]
    uses_box = (counts[:, None] > 0) & (positions < lengths[:, None])
    phrase_of = jnp.where(uses_box, positions * counts[:, None] // lengths[:, None], 0)
    phrase_ids = jnp.arange(boxes.shape[1], dtype=jnp.int32)
    chosen = phrase_of[:, :, None] == phrase_ids[None, None, :]
    in_box = jnp.any(chosen[:, :, :, None] & (boxes[:, None] > 0), axis=2)
    grid_ok = jnp.where(uses_box[:, :, None], in_box, True)
    cls_column = jnp.ones(grid_ok.shape[:2] + (1,), dtype=jnp.bool_)
    return jnp.concatenate([cls_column, grid_ok], -1)


def attend_forward(queries, key_in, values, allowed, score_scale):
    scores = (
        jnp.einsum("iqhd,ikhd->ihqk", queries, key_in, preferred_element_type=jnp.float32)
        * score_scale
    )
    scores = jnp.where(allowed[:, None], scores, NEG)
    top_score = jnp.max(scores, -1, keepdims=True)
    exponent = jnp.exp(scores - top_score)
    soft_probs = exponent / jnp.sum(exponent, -1, keepdims=True)
    probs_low = soft_probs.astype(jnp.bfloat16)
    result = jnp.einsum("ihqk,ikhd->iqhd", probs_low, values, preferred_element_type=jnp.float32)
    return (result, soft_probs, probs_low)


def attend_backward(grad_low, queries, key_in, values, soft_probs, probs_low, score_scale):
    grad_probs = jnp.einsum("iqhd,ikhd->ihqk", grad_low, values, preferred_element_type=jnp.float32)
    grad_scores = soft_probs * (grad_probs - jnp.sum(soft_probs * grad_probs, -1, keepdims=True))
    scores_low = grad_scores.astype(jnp.bfloat16)
    grad_query = (
        jnp.einsum("ihqk,ikhd->iqhd", scores_low, key_in, preferred_element_type=jnp.float32)
        * score_scale
    )
    grad_key = (
        jnp.einsum("ihqk,iqhd->ikhd", scores_low, queries, preferred_element_type=jnp.float32)
        * score_scale
    )
    grad_value = jnp.einsum(
        "ihqk,iqhd->ikhd", probs_low, grad_low, preferred_element_type=jnp.float32
    )
    return (grad_query, grad_key, grad_value)


def fetch_weights(
    self_qkv, self_out, cross_q, cross_kv, cross_out, ffn_in, ffn_out, vectors, ffn_bias_in
):
    by_rows = (
        lax.all_gather(self_qkv, "dp", axis=0, tiled=True),
        lax.all_gather(self_out, "dp", axis=0, tiled=True),
        lax.all_gather(cross_q, "dp", axis=0, tiled=True),
        lax.all_gather(cross_kv, "dp", axis=0, tiled=True),
        lax.all_gather(cross_out, "dp", axis=0, tiled=True),
        lax.all_gather(ffn_in, "dp", axis=0, tiled=True),
        lax.all_gather(ffn_out, "dp", axis=0, tiled=True),
        lax.all_gather(vectors, "dp", axis=1, tiled=True),
        lax.all_gather(ffn_bias_in, "dp", axis=0, tiled=True),
    )
    by_cols = (
        lax.all_gather(by_rows[0], "patch", axis=1, tiled=True),
        lax.all_gather(by_rows[1], "patch", axis=1, tiled=True),
        lax.all_gather(by_rows[2], "patch", axis=1, tiled=True),
        lax.all_gather(by_rows[3], "patch", axis=1, tiled=True),
        lax.all_gather(by_rows[4], "patch", axis=1, tiled=True),
        lax.all_gather(by_rows[5], "patch", axis=1, tiled=True),
        lax.all_gather(by_rows[6], "patch", axis=1, tiled=True),
    )
    return (
        by_cols[0],
        by_cols[1],
        by_cols[2],
        by_cols[3],
        by_cols[4],
        by_cols[5],
        by_cols[6],
        by_rows[7].astype(jnp.float32),
        by_rows[8].astype(jnp.float32),
    )


def forward_pass(weights, text_local, grid_local, cls_local, lengths, counts, boxes):
    w_qkv, w_out, w_cq, w_ckv, w_cout, w_fin, w_fout, vec_rows, bias_in = weights
    model_width = w_out.shape[0]
    head_count = model_width // HEAD
    item_count = lengths.shape[0]
    seq_len = text_local.shape[0] // item_count
    score_scale = HEAD ** (-0.5)
    zero_row = jnp.zeros((model_width,), jnp.float32)
    qkv_full = jnp.dot(text_local, w_qkv, preferred_element_type=jnp.float32) + jnp.concatenate(
        [vec_rows[0], zero_row, vec_rows[1]]
    )
    qkv_low = qkv_full.astype(jnp.bfloat16).reshape(item_count, seq_len, 3, head_count, HEAD)
    self_q = qkv_low[:, :, 0]
    self_k = qkv_low[:, :, 1]
    self_v = qkv_low[:, :, 2]
    self_res, self_probs, self_plow = attend_forward(
        self_q, self_k, self_v, self_allowed(lengths, seq_len), score_scale
    )
    attn_low = self_res.reshape(-1, model_width).astype(jnp.bfloat16)
    total_one = (
        text_local.astype(jnp.float32)
        + jnp.dot(attn_low, w_out, preferred_element_type=jnp.float32)
        + vec_rows[2]
    )
    hidden_one = norm_forward(total_one, vec_rows[3], vec_rows[4])
    hidden_one_low = hidden_one.astype(jnp.bfloat16)
    cross_query = (
        jnp.dot(hidden_one_low, w_cq, preferred_element_type=jnp.float32) + vec_rows[5]
    ).astype(jnp.bfloat16)
    cross_query = cross_query.reshape(item_count, seq_len, head_count, HEAD)
    kv_bias = jnp.concatenate([zero_row, vec_rows[6]])
    local_kv = (
        jnp.einsum("ipv,ve->ipe", grid_local, w_ckv, preferred_element_type=jnp.float32) + kv_bias
    ).astype(jnp.bfloat16)
    grid_kv = lax.all_to_all(local_kv, "patch", split_axis=0, concat_axis=1, tiled=True)
    cls_kv = (jnp.dot(cls_local, w_ckv, preferred_element_type=jnp.float32) + kv_bias).astype(
        jnp.bfloat16
    )
    patch_kv = jnp.concatenate([cls_kv[:, None], grid_kv], 1)
    patch_count = patch_kv.shape[1]
    cross_key = patch_kv[:, :, :model_width].reshape(item_count, patch_count, head_count, HEAD)
    cross_value = patch_kv[:, :, model_width:].reshape(item_count, patch_count, head_count, HEAD)
    cross_res, cross_probs, cross_plow = attend_forward(
        cross_query,
        cross_key,
        cross_value,
        cross_allowed(lengths, counts, boxes, seq_len),
        score_scale,
    )
    cross_low = cross_res.reshape(-1, model_width).astype(jnp.bfloat16)
    total_two = (
        hidden_one + jnp.dot(cross_low, w_cout, preferred_element_type=jnp.float32) + vec_rows[7]
    )
    hidden_two = norm_forward(total_two, vec_rows[8], vec_rows[9])
    hidden_two_low = hidden_two.astype(jnp.bfloat16)
    pre_act = jnp.dot(hidden_two_low, w_fin, preferred_element_type=jnp.float32) + bias_in
    act_low = exact_gelu(pre_act).astype(jnp.bfloat16)
    total_three = (
        hidden_two + jnp.dot(act_low, w_fout, preferred_element_type=jnp.float32) + vec_rows[10]
    )
    return {
        "text_local": text_local,
        "self_q": self_q,
        "self_k": self_k,
        "self_v": self_v,
        "self_probs": self_probs,
        "self_plow": self_plow,
        "attn_low": attn_low,
        "total_one": total_one,
        "hidden_one_low": hidden_one_low,
        "cross_query": cross_query,
        "cross_key": cross_key,
        "cross_value": cross_value,
        "cross_probs": cross_probs,
        "cross_plow": cross_plow,
        "cross_low": cross_low,
        "total_two": total_two,
        "hidden_two_low": hidden_two_low,
        "pre_act": pre_act,
        "act_low": act_low,
        "total_three": total_three,
        "grid_mine": grid_local,
        "cls_local": cls_local,
    }


def backward_pass(weights, saved, cot_local):
    w_qkv, w_out, w_cq, w_ckv, w_cout, w_fin, w_fout, vec_rows, bias_in = weights
    model_width = w_out.shape[0]
    score_scale = HEAD ** (-0.5)
    item_count = saved["cross_query"].shape[0]
    patch_count = saved["cross_key"].shape[1]
    layer_out, norm_three = jax.vjp(norm_forward, saved["total_three"], vec_rows[11], vec_rows[12])
    grad_three, gain_three, shift_three = norm_three(cot_local.astype(jnp.float32))
    grad_three_low = grad_three.astype(jnp.bfloat16)
    grad_fout = jnp.einsum(
        "rf,rd->fd", saved["act_low"], grad_three_low, preferred_element_type=jnp.float32
    )
    bias_fout = jnp.sum(grad_three_low, 0, dtype=jnp.float32)
    grad_act = jnp.einsum("rd,fd->rf", grad_three_low, w_fout, preferred_element_type=jnp.float32)
    gelu_out, gelu_pull = jax.vjp(exact_gelu, saved["pre_act"])
    grad_pre_low = gelu_pull(grad_act)[0].astype(jnp.bfloat16)
    grad_fin = jnp.einsum(
        "rd,rf->df", saved["hidden_two_low"], grad_pre_low, preferred_element_type=jnp.float32
    )
    bias_fin = jnp.sum(grad_pre_low, 0, dtype=jnp.float32)
    grad_hidden_two = grad_three + jnp.einsum(
        "rf,df->rd", grad_pre_low, w_fin, preferred_element_type=jnp.float32
    )
    hidden_two, norm_two = jax.vjp(norm_forward, saved["total_two"], vec_rows[8], vec_rows[9])
    grad_two, gain_two, shift_two = norm_two(grad_hidden_two)
    grad_two_low = grad_two.astype(jnp.bfloat16)
    grad_cout = jnp.einsum(
        "rd,re->de", saved["cross_low"], grad_two_low, preferred_element_type=jnp.float32
    )
    bias_cout = jnp.sum(grad_two_low, 0, dtype=jnp.float32)
    grad_cross_ctx = jnp.einsum(
        "re,de->rd", grad_two_low, w_cout, preferred_element_type=jnp.float32
    ).astype(jnp.bfloat16)
    grad_cross_ctx = grad_cross_ctx.reshape(saved["cross_query"].shape)
    grad_cq4, grad_ck4, grad_cv4 = attend_backward(
        grad_cross_ctx,
        saved["cross_query"],
        saved["cross_key"],
        saved["cross_value"],
        saved["cross_probs"],
        saved["cross_plow"],
        score_scale,
    )
    grad_cq_low = grad_cq4.reshape(-1, model_width).astype(jnp.bfloat16)
    grad_cq = jnp.einsum(
        "rd,re->de", saved["hidden_one_low"], grad_cq_low, preferred_element_type=jnp.float32
    )
    bias_cq = jnp.sum(grad_cq_low, 0, dtype=jnp.float32)
    grad_hidden_one = grad_two + jnp.einsum(
        "re,de->rd", grad_cq_low, w_cq, preferred_element_type=jnp.float32
    )
    patch_grad = jnp.concatenate(
        [
            grad_ck4.reshape(item_count, patch_count, model_width),
            grad_cv4.reshape(item_count, patch_count, model_width),
        ],
        -1,
    ).astype(jnp.bfloat16)
    bias_cv = jnp.sum(patch_grad[:, :, model_width:], (0, 1), dtype=jnp.float32)
    cls_part = patch_grad[:, 0]
    grid_part = patch_grad[:, 1:]
    cls_term = jnp.einsum(
        "iv,ie->ve", saved["cls_local"], cls_part, preferred_element_type=jnp.float32
    )
    cls_grad = jnp.einsum("ie,ve->iv", cls_part, w_ckv, preferred_element_type=jnp.float32)
    grid_back = lax.all_to_all(grid_part, "patch", split_axis=1, concat_axis=0, tiled=True)
    grad_ckv = (
        jnp.einsum("ipv,ipe->ve", saved["grid_mine"], grid_back, preferred_element_type=jnp.float32)
        + cls_term
    )
    grid_grad = jnp.einsum("ipe,ve->ipv", grid_back, w_ckv, preferred_element_type=jnp.float32)
    hidden_one, norm_one = jax.vjp(norm_forward, saved["total_one"], vec_rows[3], vec_rows[4])
    grad_one, gain_one, shift_one = norm_one(grad_hidden_one)
    grad_one_low = grad_one.astype(jnp.bfloat16)
    grad_out = jnp.einsum(
        "rd,re->de", saved["attn_low"], grad_one_low, preferred_element_type=jnp.float32
    )
    bias_out = jnp.sum(grad_one_low, 0, dtype=jnp.float32)
    grad_self_ctx = jnp.einsum(
        "re,de->rd", grad_one_low, w_out, preferred_element_type=jnp.float32
    ).astype(jnp.bfloat16)
    grad_self_ctx = grad_self_ctx.reshape(saved["self_q"].shape)
    grad_sq, grad_sk, grad_sv = attend_backward(
        grad_self_ctx,
        saved["self_q"],
        saved["self_k"],
        saved["self_v"],
        saved["self_probs"],
        saved["self_plow"],
        score_scale,
    )
    grad_qkv_low = (
        jnp.stack([grad_sq, grad_sk, grad_sv], 2).reshape(-1, 3 * model_width).astype(jnp.bfloat16)
    )
    grad_qkv = jnp.einsum(
        "rd,re->de", saved["text_local"], grad_qkv_low, preferred_element_type=jnp.float32
    )
    bias_q = jnp.sum(grad_qkv_low[:, :model_width], 0, dtype=jnp.float32)
    bias_v = jnp.sum(grad_qkv_low[:, 2 * model_width :], 0, dtype=jnp.float32)
    text_grad = grad_one + jnp.einsum(
        "re,de->rd", grad_qkv_low, w_qkv, preferred_element_type=jnp.float32
    )
    grad_vec = jnp.stack(
        [
            bias_q,
            bias_v,
            bias_out,
            gain_one,
            shift_one,
            bias_cq,
            bias_cv,
            bias_cout,
            gain_two,
            shift_two,
            bias_fout,
            gain_three,
            shift_three,
        ]
    )
    local_grads = (
        grad_qkv,
        grad_out,
        grad_cq,
        grad_ckv,
        grad_cout,
        grad_fin,
        grad_fout,
        grad_vec,
        bias_fin,
    )
    return (layer_out, text_grad, grid_grad, cls_grad, local_grads)


def reduce_grads(local_grads):
    grad_qkv, grad_out, grad_cq, grad_ckv, grad_cout, grad_fin, grad_fout, grad_vec, grad_bias = (
        local_grads
    )
    spread = lax.axis_size("patch")
    section_one = (
        lax.psum_scatter(grad_qkv, "dp", scatter_dimension=0, tiled=True),
        lax.psum_scatter(grad_out, "dp", scatter_dimension=0, tiled=True),
        lax.psum_scatter(grad_cq, "dp", scatter_dimension=0, tiled=True),
        lax.psum_scatter(grad_ckv, "dp", scatter_dimension=0, tiled=True),
        lax.psum_scatter(grad_cout, "dp", scatter_dimension=0, tiled=True),
        lax.psum_scatter(grad_fin, "dp", scatter_dimension=0, tiled=True),
        lax.psum_scatter(grad_fout, "dp", scatter_dimension=0, tiled=True),
        lax.psum_scatter(grad_vec, "dp", scatter_dimension=1, tiled=True),
        lax.psum_scatter(grad_bias, "dp", scatter_dimension=0, tiled=True),
    )
    section_two = (
        lax.psum_scatter(
            section_one[0].astype(jnp.bfloat16), "patch", scatter_dimension=1, tiled=True
        ).astype(jnp.float32),
        lax.psum_scatter(
            section_one[1].astype(jnp.bfloat16), "patch", scatter_dimension=1, tiled=True
        ).astype(jnp.float32),
        lax.psum_scatter(
            section_one[2].astype(jnp.bfloat16), "patch", scatter_dimension=1, tiled=True
        ).astype(jnp.float32),
        lax.psum_scatter(
            section_one[3].astype(jnp.bfloat16), "patch", scatter_dimension=1, tiled=True
        ).astype(jnp.float32),
        lax.psum_scatter(
            section_one[4].astype(jnp.bfloat16), "patch", scatter_dimension=1, tiled=True
        ).astype(jnp.float32),
        lax.psum_scatter(
            section_one[5].astype(jnp.bfloat16), "patch", scatter_dimension=1, tiled=True
        ).astype(jnp.float32),
        lax.psum_scatter(
            section_one[6].astype(jnp.bfloat16), "patch", scatter_dimension=1, tiled=True
        ).astype(jnp.float32),
        lax.psum_scatter(
            jnp.broadcast_to(section_one[7], (spread,) + section_one[7].shape).astype(jnp.bfloat16),
            "patch",
            scatter_dimension=0,
            tiled=True,
        ).astype(jnp.float32),
        lax.psum_scatter(
            jnp.broadcast_to(section_one[8], (spread,) + section_one[8].shape).astype(jnp.bfloat16),
            "patch",
            scatter_dimension=0,
            tiled=True,
        ).astype(jnp.float32),
    )
    return (
        section_two[0],
        section_two[1],
        section_two[2],
        section_two[3],
        section_two[4],
        section_two[5],
        section_two[6],
        section_two[7][0],
        section_two[8][0],
    )


def on_device(
    text_in,
    image_grid,
    image_cls,
    text_lengths,
    phrase_counts,
    phrase_boxes,
    cotangent,
    self_qkv,
    self_out,
    cross_q,
    cross_kv,
    cross_out,
    ffn_in,
    ffn_out,
    vectors,
    ffn_bias_in,
):
    micro_count = text_in.shape[0]
    out_list = []
    text_list = []
    grid_list = []
    cls_list = []
    running = None
    for micro_index in range(micro_count):
        forward_weights = fetch_weights(
            self_qkv, self_out, cross_q, cross_kv, cross_out, ffn_in, ffn_out, vectors, ffn_bias_in
        )
        saved = forward_pass(
            forward_weights,
            text_in[micro_index],
            image_grid[micro_index],
            image_cls[micro_index],
            text_lengths[micro_index],
            phrase_counts[micro_index],
            phrase_boxes[micro_index],
        )
        backward_weights = fetch_weights(
            self_qkv, self_out, cross_q, cross_kv, cross_out, ffn_in, ffn_out, vectors, ffn_bias_in
        )
        layer_out, text_grad, grid_grad, cls_grad, local_grads = backward_pass(
            backward_weights, saved, cotangent[micro_index]
        )
        reduced = reduce_grads(local_grads)
        running = reduced if running is None else jax.tree.map(jnp.add, running, reduced)
        out_list.append(layer_out)
        text_list.append(text_grad)
        grid_list.append(grid_grad)
        cls_list.append(cls_grad)
    return (
        jnp.stack(out_list),
        jnp.stack(text_list),
        jnp.stack(grid_list),
        jnp.stack(cls_list),
        running[0],
        running[1],
        running[2],
        running[3],
        running[4],
        running[5],
        running[6],
        running[7],
        running[8],
    )


def solution(mesh):
    return jax.shard_map(
        on_device,
        mesh=mesh,
        in_specs=(
            P(None, ("dp", "patch"), None),
            P(None, "dp", "patch", None),
            P(None, ("dp", "patch"), None),
            P(None, ("dp", "patch")),
            P(None, ("dp", "patch")),
            P(None, ("dp", "patch"), None, None),
            P(None, ("dp", "patch"), None),
            P("dp", "patch"),
            P("dp", "patch"),
            P("dp", "patch"),
            P("dp", "patch"),
            P("dp", "patch"),
            P("dp", "patch"),
            P("dp", "patch"),
            P(None, "dp"),
            P("dp"),
        ),
        out_specs=(
            P(None, ("dp", "patch"), None),
            P(None, ("dp", "patch"), None),
            P(None, "dp", "patch", None),
            P(None, ("dp", "patch"), None),
            P("dp", "patch"),
            P("dp", "patch"),
            P("dp", "patch"),
            P("dp", "patch"),
            P("dp", "patch"),
            P("dp", "patch"),
            P("dp", "patch"),
            P(None, "dp"),
            P("dp"),
        ),
        check_vma=False,
    )
```

profile of v0, /device:TPU:0, one launch (start us, length us, event | category | flops | bytes accessed | tf_op | source)
XLA Modules:
  0.0 2651.8 jit_solution(6619114772764363383)
XLA Ops:
  8.7 36.8 %all_gather.37 = bf16[1024,384]{1,0:T(8,128)(2,1)} all-gather(bf16[128,384]{1,0:T(8,128)(2,1)} %param.28), channel_id=1, replica_groups=mesh['dp'=8,'patch'=4] {'dp'}, dimensions={0}, use_global_device_ids=true | all-gather | bytes 884736 | tf_op jit(solution)/shard_map/all_gather | solution.py:80
  45.6 34.2 %all_gather.32 = bf16[768,576]{1,0:T(8,128)(2,1)S(1)} all-gather(bf16[96,576]{1,0:T(8,128)(2,1)S(1)} %copy-done.100), channel_id=1, replica_groups=mesh['dp'=8,'patch'=4] {'dp'}, dimensions={0}, use_global_device_ids=true | all-gather | bytes 995328 | tf_op jit(solution)/shard_map/all_gather | solution.py:77
  81.2 31.9 %all_gather.35 = bf16[768,192]{1,0:T(8,128)(2,1)S(1)} all-gather(bf16[96,192]{1,0:T(8,128)(2,1)S(1)} %copy-done.109), channel_id=1, replica_groups=mesh['dp'=8,'patch'=4] {'dp'}, dimensions={0}, use_global_device_ids=true | all-gather | bytes 331776 | tf_op jit(solution)/shard_map/all_gather | solution.py:78
  114.1 31.1 %all_gather.39 = bf16[768,192]{1,0:T(8,128)(2,1)S(1)} all-gather(bf16[96,192]{1,0:T(8,128)(2,1)S(1)} %copy-done.110), channel_id=1, replica_groups=mesh['dp'=8,'patch'=4] {'dp'}, dimensions={0}, use_global_device_ids=true | all-gather | bytes 331776 | tf_op jit(solution)/shard_map/all_gather | solution.py:79
  146.2 31.0 %all_gather.41 = bf16[768,192]{1,0:T(8,128)(2,1)S(1)} all-gather(bf16[96,192]{1,0:T(8,128)(2,1)S(1)} %copy-done.111), channel_id=1, replica_groups=mesh['dp'=8,'patch'=4] {'dp'}, dimensions={0}, use_global_device_ids=true | all-gather | bytes 331776 | tf_op jit(solution)/shard_map/all_gather | solution.py:81
  180.3 25.9 all-gather.1
  206.9 30.4 %all-gather = bf16[8,96,13]{1,2,0:T(8,128)(2,1)S(1)} all-gather(bf16[1,96,13]{1,2,0:T(8,128)(2,1)S(1)} %bitcast.510), channel_id=1, replica_groups=mesh['dp'=8,'patch'=4] {'dp'}, dimensions={0}, use_global_device_ids=true | all-gather | bytes 22464 | tf_op jit(solution)/shard_map/all_gather | solution.py:84
  377.5 34.8 %multiply_convert_fusion.1 = (bf16[512,3072]{1,0:T(8,128)(2,1)}, f32[512,3072]{1,0:T(8,128)}, bf16[512,3072]{1,0:T(8,128)(2,1)}, f32[512,3072]{1,0:T(8,128)}, f32[512,3072]{1,0:T(8,128)}) fusion(f32[3072]{0:T(1024)S(1)} %bitcast.508, f32[512,3072]{1,0:T(8,128)S(1)} %fusion.180, bf16[768,3072]{1,0:T(8,128)(2,1)S(1)} %copy-done.180, ...), kind=kOutput, calls=%fused_computation.29 | convolution fusion | flops 2625503232 | bytes 37771264 | tf_op jit(solution)/shard_map/dot_general | solution.py:164
  431.8 17.3 convert_reduce_fusion.1
  593.0 21.3 all-to-all-done.2
  637.1 22.2 all-to-all-done.3
  675.5 8.1 copy.406
  691.3 8.1 copy.408
  700.5 8.2 fusion.213
  709.9 8.2 fusion.212
  721.5 7.2 fusion.178
  728.8 13.3 reduce-scatter.67.cloned.1.call-done
  744.0 69.7 %reduce-scatter.65.cloned.1.call-done = f32[96,768]{1,0:T(8,128)} async-done(((f32[768,768]{1,0:T(8,128)}), f32[96,768]{1,0:T(8,128)}) %reduce-scatter.65.cloned.1.call-update) | async-done | bytes 294928 | tf_op jit(solution)/shard_map/reduce_scatter | solution.py:336
  815.7 7.2 fusion.184
  823.0 62.1 %reduce-scatter.79.cloned.1.call-done = f32[96,768]{1,0:T(8,128)} async-done(((f32[768,768]{1,0:T(8,128)}), f32[96,768]{1,0:T(8,128)}) %reduce-scatter.79.cloned.1.call-update) | async-done | bytes 294928 | tf_op jit(solution)/shard_map/reduce_scatter | solution.py:338
  886.9 69.6 %reduce-scatter.63.cloned.1.call-done = f32[96,768]{1,0:T(8,128)} async-done(((f32[768,768]{1,0:T(8,128)}), f32[96,768]{1,0:T(8,128)}) %reduce-scatter.63.cloned.1.call-update) | async-done | bytes 294928 | tf_op jit(solution)/shard_map/reduce_scatter | solution.py:335
  958.4 69.6 %reduce-scatter.61.cloned.1.call-done = f32[96,768]{1,0:T(8,128)} async-done(((f32[768,768]{1,0:T(8,128)}), f32[96,768]{1,0:T(8,128)}) %reduce-scatter.61.cloned.1.call-update) | async-done | bytes 294928 | tf_op jit(solution)/shard_map/reduce_scatter | solution.py:335
  1029.8 69.6 %reduce-scatter.77.cloned.1.call-done = f32[96,768]{1,0:T(8,128)} async-done(((f32[768,768]{1,0:T(8,128)}), f32[96,768]{1,0:T(8,128)}) %reduce-scatter.77.cloned.1.call-update) | async-done | bytes 294928 | tf_op jit(solution)/shard_map/reduce_scatter | solution.py:338
  1101.3 119.0 %reduce-scatter.69.cloned.1.call-done = f32[128,1536]{0,1:T(8,128)} async-done(((f32[1024,1536]{0,1:T(8,128)}), f32[128,1536]{0,1:T(8,128)}) %reduce-scatter.69.cloned.1.call-update) | async-done | bytes 786448 | tf_op jit(solution)/shard_map/reduce_scatter | solution.py:337
  1222.3 119.1 %reduce-scatter.73.cloned.1.call-done = f32[128,1536]{0,1:T(8,128)} async-done(((f32[1024,1536]{0,1:T(8,128)}), f32[128,1536]{0,1:T(8,128)}) %reduce-scatter.73.cloned.1.call-update) | async-done | bytes 786448 | tf_op jit(solution)/shard_map/reduce_scatter | solution.py:337
  1343.6 129.6 %reduce-scatter.97.cloned.1.call-done = f32[96,2304]{1,0:T(8,128)} async-done(((f32[768,2304]{1,0:T(8,128)}), f32[96,2304]{1,0:T(8,128)}) %reduce-scatter.97.cloned.1.call-update) | async-done | bytes 884752
  1475.5 129.9 %reduce-scatter.99.cloned.1.call-done = f32[96,2304]{1,0:T(8,128)} async-done(((f32[768,2304]{1,0:T(8,128)}), f32[96,2304]{1,0:T(8,128)}) %reduce-scatter.99.cloned.1.call-update) | async-done | bytes 884752
  1609.7 37.0 %all-reduce.7 = (bf16[3072]{0:T(1024)(128)(2,1)S(1)}, bf16[3072]{0:T(1024)(128)(2,1)S(1)}) all-reduce(f32[3072]{0:T(1024)S(1)} %copy-done.143, f32[3072]{0:T(1024)S(1)} %copy-done.142), channel_id=36, replica_groups=mesh['dp'=8,'patch'=4] {'dp'}, use_global_device_ids=true, to_apply=%region_100.102.clone | all-reduce | flops 6144 | bytes 36864
  1656.1 115.5 %reduce-scatter.91.cloned.1.call-done = f32[384,768]{1,0:T(8,128)} async-done(((f32[3072,768]{1,0:T(8,128)}), f32[384,768]{1,0:T(8,128)}) %reduce-scatter.91.cloned.1.call-update) | async-done | bytes 1179664 | tf_op jit(solution)/shard_map/reduce_scatter | solution.py:340
  1784.0 153.8 %reduce-scatter.89.cloned.1.call-done = f32[384,768]{1,0:T(8,128)} async-done(((f32[3072,768]{1,0:T(8,128)}), f32[384,768]{1,0:T(8,128)}) %reduce-scatter.89.cloned.1.call-update) | async-done | bytes 1179664 | tf_op jit(solution)/shard_map/reduce_scatter | solution.py:340
  1950.1 9.1 reduce-scatter.95.cloned.1.call-done
  1959.2 22.4 reduce-scatter.93.cloned.1.call-done
  1982.9 165.7 %reduce-scatter.85.cloned.1.call-done = f32[96,3072]{1,0:T(8,128)} async-done(((f32[768,3072]{1,0:T(8,128)}), f32[96,3072]{1,0:T(8,128)}) %reduce-scatter.85.cloned.1.call-update) | async-done | bytes 1179664 | tf_op jit(solution)/shard_map/reduce_scatter | solution.py:339
  2163.3 7.1 reduce-scatter.107.cloned.1.call-done
  2171.2 21.9 reduce-scatter.105.cloned.1.call-done
  2194.0 166.2 %reduce-scatter.81.cloned.1.call-done = f32[96,3072]{1,0:T(8,128)} async-done(((f32[768,3072]{1,0:T(8,128)}), f32[96,3072]{1,0:T(8,128)}) %reduce-scatter.81.cloned.1.call-update) | async-done | bytes 1179664 | tf_op jit(solution)/shard_map/reduce_scatter | solution.py:339
  2363.1 18.3 reduce-scatter.111.cloned.1.call-done
  2382.3 21.9 reduce-scatter.103.cloned.1.call-done
  2405.1 21.9 reduce-scatter.101.cloned.1.call-done
  2427.9 21.2 reduce-scatter.109.cloned.1.call-done
  2451.3 21.2 reduce-scatter.71.cloned.1.call-done
  2472.5 23.4 reduce-scatter.75.cloned.1.call-done
  2497.6 22.7 reduce-scatter.57.cloned.1.call-done
  2520.3 24.5 reduce-scatter.59.cloned.1.call-done
  2546.6 22.7 reduce-scatter.115.cloned.1.call-done
  2570.4 23.4 reduce-scatter.113.cloned.1.call-done
  2595.8 22.7 reduce-scatter.87.cloned.1.call-done
  2618.4 24.6 reduce-scatter.83.cloned.1.call-done
  (770 shorter events, 450.9 us)
Async XLA Ops:
  7.2 170.9 %all-gather.22.cloned.1.call-start = ((), (), s32[]{:S(2)}) async-start(), calls=%async_computation.41 | async-start | bytes 1327104 | tf_op jit(solution)/shard_map/all_gather | solution.py:82
  7.9 236.3 %all-gather.26.cloned.1.call-start = ((), (), s32[]{:S(2)}) async-start(), calls=%async_computation.43 | async-start | bytes 1327104 | tf_op jit(solution)/shard_map/all_gather | solution.py:83
  8.7 235.6 %all-gather.16.cloned.1.call-start = ((), (), s32[]{:S(2)}) async-start(), calls=%async_computation.38 | async-start | bytes 3932160 | tf_op jit(solution)/shard_map/all_gather | solution.py:91
  45.6 216.4 %all-gather.12.cloned.1.call-start = ((), (), s32[]{:S(2)}) async-start(), calls=%async_computation.36 | async-start | bytes 4423680 | tf_op jit(solution)/shard_map/all_gather | solution.py:88
  81.1 215.0 %all-gather.14.cloned.1.call-start = ((), (), s32[]{:S(2)}) async-start(), calls=%async_computation.37 | async-start | bytes 1474560 | tf_op jit(solution)/shard_map/all_gather | solution.py:89
  114.0 186.3 %all-gather.18.cloned.1.call-start = ((), (), s32[]{:S(2)}) async-start(), calls=%async_computation.39 | async-start | bytes 1474560 | tf_op jit(solution)/shard_map/all_gather | solution.py:90
  146.1 211.5 %all-gather.20.cloned.1.call-start = ((), (), s32[]{:S(2)}) async-start(), calls=%async_computation.40 | async-start | bytes 1474560 | tf_op jit(solution)/shard_map/all_gather | solution.py:92
  178.1 191.5 %all-gather.24.cloned.1.call-start = ((), (), s32[]{:S(2)}) async-start(), calls=%async_computation.42 | async-start | bytes 5898240 | tf_op jit(solution)/shard_map/all_gather | solution.py:93
  178.8 233.5 %all-gather.28.cloned.1.call-start = ((), (), s32[]{:S(2)}) async-start(), calls=%async_computation.44 | async-start | bytes 5898240 | tf_op jit(solution)/shard_map/all_gather | solution.py:94
  251.3 62.5 %all-to-all-start = ((bf16[16,36,1536]{2,1,0:T(8,128)(2,1)}), bf16[16,36,1536]{2,1,0:T(8,128)(2,1)}, u32[]{:S(2)}, u32[]{:S(2)}) async-start(bf16[16,36,1536]{2,1,0:T(8,128)(2,1)} %add_convert_fusion.3), calls=%async_computation | async-start | bytes 3932160 | tf_op jit(solution)/shard_map/all_to_all | solution.py:143
  313.8 27.9 %all-to-all-start.1 = ((bf16[16,36,1536]{2,1,0:T(8,128)(2,1)}), bf16[16,36,1536]{2,1,0:T(8,128)(2,1)S(1)}, u32[]{:S(2)}, u32[]{:S(2)}) async-start(bf16[16,36,1536]{2,1,0:T(8,128)(2,1)} %add_convert_fusion.2), calls=%async_computation.1 | async-start | bytes 3932160 | tf_op jit(solution)/shard_map/all_to_all | solution.py:143
  317.4 400.7 %reduce-scatter.119.cloned.1.call-start = ((), (), s32[]{:S(2)}) async-start(), calls=%async_computation.76 | async-start | bytes 442368
  547.6 172.3 %reduce-scatter.117.cloned.1.call-start = ((), (), s32[]{:S(2)}) async-start(), calls=%async_computation.75 | async-start | bytes 442368
  551.3 190.8 %reduce-scatter.67.cloned.1.call-start = ((), (), s32[]{:S(2)}) async-start(), calls=%async_computation.50 | async-start | bytes 2654208 | tf_op jit(solution)/shard_map/reduce_scatter | solution.py:336
  555.2 258.4 %reduce-scatter.65.cloned.1.call-start = ((), (), s32[]{:S(2)}) async-start(), calls=%async_computation.49 | async-start | bytes 2654208 | tf_op jit(solution)/shard_map/reduce_scatter | solution.py:336
  560.2 324.8 %reduce-scatter.79.cloned.1.call-start = ((), (), s32[]{:S(2)}) async-start(), calls=%async_computation.56 | async-start | bytes 2654208 | tf_op jit(solution)/shard_map/reduce_scatter | solution.py:338
  563.8 392.7 %reduce-scatter.63.cloned.1.call-start = ((), (), s32[]{:S(2)}) async-start(), calls=%async_computation.48 | async-start | bytes 2654208 | tf_op jit(solution)/shard_map/reduce_scatter | solution.py:335
  567.4 460.5 %reduce-scatter.61.cloned.1.call-start = ((), (), s32[]{:S(2)}) async-start(), calls=%async_computation.47 | async-start | bytes 2654208 | tf_op jit(solution)/shard_map/reduce_scatter | solution.py:335
  571.0 528.4 %reduce-scatter.77.cloned.1.call-start = ((), (), s32[]{:S(2)}) async-start(), calls=%async_computation.55 | async-start | bytes 2654208 | tf_op jit(solution)/shard_map/reduce_scatter | solution.py:338
  587.7 26.6 %all-to-all-start.2 = ((bf16[4,144,1536]{2,0,1:T(4,128)(2,1)}), bf16[4,144,1536]{2,0,1:T(4,128)(2,1)}, u32[]{:S(2)}, u32[]{:S(2)}) async-start(bf16[4,144,1536]{2,0,1:T(4,128)(2,1)} %fusion.49), calls=%async_computation.2 | async-start | bytes 3538944 | tf_op jit(solution)/shard_map/all_to_all | solution.py:260
  592.1 628.3 %reduce-scatter.69.cloned.1.call-start = ((), (), s32[]{:S(2)}) async-start(), calls=%async_computation.51 | async-start | bytes 7077888 | tf_op jit(solution)/shard_map/reduce_scatter | solution.py:337
  632.6 26.7 %all-to-all-start.3 = ((bf16[4,144,1536]{2,0,1:T(4,128)(2,1)}), bf16[4,144,1536]{2,0,1:T(4,128)(2,1)}, u32[]{:S(2)}, u32[]{:S(2)}) async-start(bf16[4,144,1536]{2,0,1:T(4,128)(2,1)} %fusion.48), calls=%async_computation.3 | async-start | bytes 3538944 | tf_op jit(solution)/shard_map/all_to_all | solution.py:260
  637.0 704.5 %reduce-scatter.73.cloned.1.call-start = ((), (), s32[]{:S(2)}) async-start(), calls=%async_computation.53 | async-start | bytes 7077888 | tf_op jit(solution)/shard_map/reduce_scatter | solution.py:337
  667.9 805.3 %reduce-scatter.97.cloned.1.call-start = ((), (), s32[]{:S(2)}) async-start(), calls=%async_computation.65 | async-start | bytes 7962624
  683.6 921.8 %reduce-scatter.99.cloned.1.call-start = ((), (), s32[]{:S(2)}) async-start(), calls=%async_computation.66 | async-start | bytes 7962624
  699.4 1072.3 %reduce-scatter.91.cloned.1.call-start = ((), (), s32[]{:S(2)}) async-start(), calls=%async_computation.62 | async-start | bytes 10616832 | tf_op jit(solution)/shard_map/reduce_scatter | solution.py:340
  708.7 1229.1 %reduce-scatter.89.cloned.1.call-start = ((), (), s32[]{:S(2)}) async-start(), calls=%async_computation.61 | async-start | bytes 10616832 | tf_op jit(solution)/shard_map/reduce_scatter | solution.py:340
  718.1 1241.1 %reduce-scatter.95.cloned.1.call-start = ((), (), s32[]{:S(2)}) async-start(), calls=%async_computation.64 | async-start | bytes 20480 | tf_op jit(solution)/shard_map/reduce_scatter | solution.py:366
  719.8 1261.8 %reduce-scatter.93.cloned.1.call-start = ((), (), s32[]{:S(2)}) async-start(), calls=%async_computation.63 | async-start | bytes 20480 | tf_op jit(solution)/shard_map/reduce_scatter | solution.py:366
  721.4 1427.2 %reduce-scatter.85.cloned.1.call-start = ((), (), s32[]{:S(2)}) async-start(), calls=%async_computation.59 | async-start | bytes 10616832 | tf_op jit(solution)/shard_map/reduce_scatter | solution.py:339
  728.7 1441.6 %reduce-scatter.107.cloned.1.call-start = ((), (), s32[]{:S(2)}) async-start(), calls=%async_computation.70 | async-start | bytes 245760
  743.9 1449.2 %reduce-scatter.105.cloned.1.call-start = ((), (), s32[]{:S(2)}) async-start(), calls=%async_computation.69 | async-start | bytes 245760
  815.5 1544.8 %reduce-scatter.81.cloned.1.call-start = ((), (), s32[]{:S(2)}) async-start(), calls=%async_computation.57 | async-start | bytes 10616832 | tf_op jit(solution)/shard_map/reduce_scatter | solution.py:339
  823.0 1558.5 %reduce-scatter.111.cloned.1.call-start = ((), (), s32[]{:S(2)}) async-start(), calls=%async_computation.72 | async-start | bytes 245760
  886.9 1517.3 %reduce-scatter.103.cloned.1.call-start = ((), (), s32[]{:S(2)}) async-start(), calls=%async_computation.68 | async-start | bytes 245760
  958.3 1468.7 %reduce-scatter.101.cloned.1.call-start = ((), (), s32[]{:S(2)}) async-start(), calls=%async_computation.67 | async-start | bytes 245760
  1029.8 1419.3 %reduce-scatter.109.cloned.1.call-start = ((), (), s32[]{:S(2)}) async-start(), calls=%async_computation.71 | async-start | bytes 245760
  1101.3 1371.2 %reduce-scatter.71.cloned.1.call-start = ((), (), s32[]{:S(2)}) async-start(), calls=%async_computation.52 | async-start | bytes 491520 | tf_op jit(solution)/shard_map/reduce_scatter | solution.py:354
  1222.3 1273.5 %reduce-scatter.75.cloned.1.call-start = ((), (), s32[]{:S(2)}) async-start(), calls=%async_computation.54 | async-start | bytes 491520 | tf_op jit(solution)/shard_map/reduce_scatter | solution.py:354
  1343.5 266.2 %copy-start.142 = (f32[3072]{0:T(1024)S(1)}, f32[3072]{0:T(1024)}, u32[]{:S(2)}) copy-start(f32[3072]{0:T(1024)} %get-tuple-element.133) | copy-start | bytes 36868
  1343.5 310.8 %copy-start.24 = (f32[1,512,768]{2,1,0:T(8,128)S(1)}, f32[1,512,768]{2,1,0:T(8,128)}, u32[]{:S(2)}) copy-start(f32[1,512,768]{2,1,0:T(8,128)} %get-tuple-element.178) | copy-start | bytes 4718596
  1343.5 310.8 %copy-start.25 = (f32[1,512,768]{2,1,0:T(8,128)S(1)}, f32[1,512,768]{2,1,0:T(8,128)}, u32[]{:S(2)}) copy-start(f32[1,512,768]{2,1,0:T(8,128)} %get-tuple-element.179) | copy-start | bytes 4718596
  1343.5 1176.8 %reduce-scatter.57.cloned.1.call-start = ((), (), s32[]{:S(2)}) async-start(), calls=%async_computation.45 | async-start | bytes 737280 | tf_op jit(solution)/shard_map/reduce_scatter | solution.py:345
  1475.5 1069.3 %reduce-scatter.59.cloned.1.call-start = ((), (), s32[]{:S(2)}) async-start(), calls=%async_computation.46 | async-start | bytes 737280 | tf_op jit(solution)/shard_map/reduce_scatter | solution.py:345
  1607.7 961.6 %reduce-scatter.115.cloned.1.call-start = ((), (), s32[]{:S(2)}) async-start(), calls=%async_computation.74 | async-start | bytes 737280
  1776.0 817.8 %reduce-scatter.113.cloned.1.call-start = ((), (), s32[]{:S(2)}) async-start(), calls=%async_computation.73 | async-start | bytes 737280
  1942.2 676.3 %reduce-scatter.87.cloned.1.call-start = ((), (), s32[]{:S(2)}) async-start(), calls=%async_computation.60 | async-start | bytes 737280 | tf_op jit(solution)/shard_map/reduce_scatter | solution.py:360
  2150.8 492.3 %reduce-scatter.83.cloned.1.call-start = ((), (), s32[]{:S(2)}) async-start(), calls=%async_computation.58 | async-start | bytes 737280 | tf_op jit(solution)/shard_map/reduce_scatter | solution.py:360
  (190 other events, 3213.0 us)
Sparse Core Ops, SparseCore 0:
  10.2 49.4 all-gather.21
  61.8 44.6 all-gather.25
  108.0 27.6 all-gather.15
  137.7 30.7 all-gather.11
  169.9 17.4 all-gather.13
  189.4 17.4 all-gather.17
  209.0 17.4 all-gather.19
  228.1 42.1 all-gather.23
  271.8 40.5 all-gather.27
  547.7 59.2 reduce-scatter.118
  610.3 60.3 reduce-scatter.116
  674.0 68.0 reduce-scatter.66
  745.6 68.0 reduce-scatter.64
  817.0 68.0 reduce-scatter.78
  888.4 68.0 reduce-scatter.62
  959.9 68.0 reduce-scatter.60
  1031.3 68.0 reduce-scatter.76
  1102.9 117.3 reduce-scatter.68
  1223.9 117.4 reduce-scatter.72
  1345.0 128.1 reduce-scatter.96
  1477.3 128.0 reduce-scatter.98
  1609.0 162.5 reduce-scatter.90
  1775.3 162.5 reduce-scatter.88
  1940.7 18.4 reduce-scatter.94
  1962.3 19.2 reduce-scatter.92
  1985.0 163.4 reduce-scatter.84
  2151.4 18.8 reduce-scatter.106
  2173.3 19.7 reduce-scatter.104
  2196.7 163.4 reduce-scatter.80
  2362.5 18.8 reduce-scatter.110
  2384.4 19.7 reduce-scatter.102
  2407.2 19.7 reduce-scatter.100
  2429.3 19.7 reduce-scatter.108
  2451.6 20.8 reduce-scatter.70
  2475.0 20.8 reduce-scatter.74
  2498.2 22.0 reduce-scatter.56
  2522.6 22.0 reduce-scatter.58
  2547.2 22.0 reduce-scatter.114
  2571.7 22.0 reduce-scatter.112
  2596.3 22.0 reduce-scatter.86
  2620.9 22.0 reduce-scatter.82
where the time goes:
time: 2660 us; the launch traced here: 2650 us
  waiting for transfers between devices  1830 us (69%)
  blocking collectives  265 us (10%)
  matrix products  262 us (10%)
  local copies, waits for them, and re-layouts  184 us (7%)
  other arithmetic  68.5 us (3%)
    unnamed x53, waiting for transfers between devices  421 us
    reduce_scatter x2, waiting for transfers between devices, reduce_grads(): lax.psum_scatter(grad_fin, 'dp', scatter_dimension=0, tiled=True)  332 us
    reduce_scatter x2, waiting for transfers between devices, reduce_grads(): lax.psum_scatter(grad_fout, 'dp', scatter_dimension=0, tiled=True)  269 us
    reduce_scatter x2, waiting for transfers between devices, reduce_grads(): lax.psum_scatter(grad_ckv, 'dp', scatter_dimension=0, tiled=True)  238 us
    reduce_scatter x2, waiting for transfers between devices, reduce_grads(): lax.psum_scatter(grad_out, 'dp', scatter_dimension=0, tiled=True)  139 us
    reduce_scatter x2, waiting for transfers between devices, reduce_grads(): lax.psum_scatter(grad_cout, 'dp', scatter_dimension=0, tiled=True)  132 us
    unnamed x421, local copies, waits for them, and re-layouts  94.4 us
    reduce_scatter x2, waiting for transfers between devices, reduce_grads(): lax.psum_scatter(grad_cq, 'dp', scatter_dimension=0, tiled=True)  83 us
  transfers between devices with their start and end apart: 45, of which 33 were waited for; matrix products, arithmetic and copies ran while one was open for 13% of the time, Pallas kernels for 0%

commit v1 on v0

--- a/solution.py
+++ b/solution.py
@@ -1,13 +1,371 @@
+import functools
+
 import jax
 import jax.numpy as jnp
 from jax import lax
+from jax.experimental import pallas as pl
+from jax.experimental.pallas import tpu as pltpu
 from jax.sharding import PartitionSpec as P
 
 HEAD = 64
-
-
 EPS = 1e-06
 NEG = -1e30
+BF16 = jnp.bfloat16
+F32 = jnp.float32
+AXES = ("dp", "patch")
+VMEM_SPEC = pl.BlockSpec(memory_space=pltpu.VMEM)
+SMEM_SPEC = pl.BlockSpec(memory_space=pltpu.SMEM)
+PARAMS = pltpu.CompilerParams(vmem_limit_bytes=62 * 2**20)
+
+QKV, OUT, CQ, CKV, COUT, FIN, FOUT = range(7)
+GROUPS = ((QKV, OUT), (CQ, CKV, COUT), (FIN,), (FOUT,))
+
+
+class Plan:
+    def __init__(self, dp, patch, shards):
+        self.dp, self.patch = dp, patch
+        self.zs = dp // 2
+        self.devices = dp * patch
+        self.chunk = shards[OUT][1] * 2
+        self.half = [s[0] // 2 for s in shards]
+        self.cols = [s[1] for s in shards]
+        self.chunks = [s[1] * 2 // self.chunk for s in shards]
+        self.full = [(s[0] * dp, s[1] * patch) for s in shards]
+        self.rows = [sum(self.half[w] * self.chunks[w] for w in g) for g in GROUPS]
+        self.fast = (
+            dp % 2 == 0
+            and patch == 4
+            and all(h % 16 == 0 for h in self.half)
+            and all(s[1] * 2 % self.chunk == 0 for s in shards)
+            and self.chunk % 128 == 0
+        )
+
+    def flip(self, pick):
+        return [(i, i ^ pick(i)) for i in range(self.devices)]
+
+    def core(self):
+        return self.flip(lambda i: 1)
+
+    def first(self):
+        return self.flip(lambda i: 4 if i % 2 == 0 else 2)
+
+    def second(self):
+        return self.flip(lambda i: 2 if i % 2 == 0 else 4)
+
+    def z_up(self, k):
+        return [(i, (i + 8 * k) % self.devices) for i in range(self.devices)]
+
+
+def send(value, perm):
+    return lax.ppermute(value, AXES, perm)
+
+
+def coords():
+    dp, patch = lax.axis_index("dp"), lax.axis_index("patch")
+    return jnp.stack([dp // 2, dp % 2, patch // 2, patch % 2]).astype(jnp.int32)
+
+
+def piece_rows(group, plan):
+    at, found = 0, []
+    for w in group:
+        for j in range(plan.chunks[w]):
+            found.append((w, j, at))
+            at += plan.half[w]
+    return found
+
+
+def group_starts(plan):
+    starts, at = [], 0
+    for rows in plan.rows:
+        starts.append(at)
+        at += rows
+    return starts, at
+
+
+def pack_split(plan, where, shards):
+    _, total = group_starts(plan)
+    wide = plan.chunk // 2
+
+    def body(where_ref, *refs):
+        shard_refs, (own_ref, send_ref) = refs[:7], refs[7:]
+        core = where_ref[3]
+        at = 0
+        for group in GROUPS:
+            for w in group:
+                high = plan.half[w]
+                for b in range(plan.chunks[w]):
+                    cut = slice(b * wide, (b + 1) * wide)
+                    own_ref[at : at + high, :] = shard_refs[w][pl.ds(core * high, high), cut]
+                    send_ref[at : at + high, :] = shard_refs[w][
+                        pl.ds((1 - core) * high, high), cut
+                    ]
+                    at += high
+
+    shape = jax.ShapeDtypeStruct((total, wide), BF16)
+    return pl.pallas_call(
+        body,
+        out_shape=(shape, shape),
+        in_specs=[SMEM_SPEC] + [VMEM_SPEC] * 7,
+        out_specs=(VMEM_SPEC, VMEM_SPEC),
+        compiler_params=PARAMS,
+        name="pack_split",
+    )(where, *shards)
+
+
+def pack_join(plan, where, own, got):
+    starts, total = group_starts(plan)
+    wide = plan.chunk // 2
+
+    def body(where_ref, own_ref, got_ref, *unit_refs):
+        core = where_ref[3]
+
+        def fill(low_ref, high_ref):
+            for g, group in enumerate(GROUPS):
+                at = starts[g]
+                for w in group:
+                    high, count = plan.half[w], plan.chunks[w]
+                    for j in range(count):
+                        pair = []
+                        for b in (2 * j, 2 * j + 1):
+                            src = low_ref if b < count else high_ref
+                            row = at + (b % count) * high
+                            pair.append(src[row : row + high, :])
+                        to = at - starts[g] + j * high
+                        unit_refs[g][to : to + high, :] = jnp.concatenate(pair, axis=1)
+                    at += count * high
+
+        @pl.when(core == 0)
+        def _():
+            fill(own_ref, got_ref)
+
+        @pl.when(core == 1)
+        def _():
+            fill(got_ref, own_ref)
+
+    return pl.pallas_call(
+        body,
+        out_shape=tuple(jax.ShapeDtypeStruct((r, plan.chunk), BF16) for r in plan.rows),
+        in_specs=[SMEM_SPEC, VMEM_SPEC, VMEM_SPEC],
+        out_specs=(VMEM_SPEC,) * len(GROUPS),
+        compiler_params=PARAMS,
+        name="pack_join",
+    )(where, own, got)
+
+
+def gather_group(plan, unit):
+    stack = jnp.stack([unit] + [send(unit, plan.z_up(k)) for k in range(1, plan.zs)])
+    near = send(stack, plan.first())
+    side, far = send(stack, plan.second()), send(near, plan.second())
+    mine = [stack, near, side, far]
+    return mine + [send(part, plan.core()) for part in mine]
+
+
+def each_piece(plan, group, where_ref, visit):
+    z, x, y, core = (where_ref[i] for i in range(4))
+    for other in range(2):
+        half = core ^ other
+        for second in range(2):
+            for first in range(2):
+                x_at = x ^ jnp.where(half == 0, first, second)
+                y_at = y ^ jnp.where(half == 0, second, first)
+                for k in range(plan.zs):
+                    z_at = lax.rem(z + plan.zs - k, plan.zs)
+                    place = (z_at * 2 + x_at) * 2 + half
+                    for w, j, row in piece_rows(group, plan):
+                        high = plan.half[w]
+                        to_row = pl.multiple_of(place * high, 16)
+                        to_col = pl.multiple_of(
+                            y_at * (plan.full[w][1] // 2) + j * plan.chunk, 128
+                        )
+                        stack = other * 4 + second * 2 + first
+                        visit(stack, k, row, w, to_row, to_col, high)
+
+
+def assemble(plan, g, where, stacks):
+    group = GROUPS[g]
+
+    def body(where_ref, *refs):
+        stack_refs, full_refs = refs[:8], dict(zip(group, refs[8:]))
+
+        def visit(stack, k, row, w, to_row, to_col, high):
+            full_refs[w][pl.ds(to_row, high), pl.ds(to_col, plan.chunk)] = stack_refs[stack][
+                k, row : row + high, :
+            ]
+
+        each_piece(plan, group, where_ref, visit)
+
+    return pl.pallas_call(
+        body,
+        out_shape=tuple(jax.ShapeDtypeStruct(plan.full[w], BF16) for w in group),
+        in_specs=[SMEM_SPEC] + [VMEM_SPEC] * 8,
+        out_specs=(VMEM_SPEC,) * len(group),
+        compiler_params=PARAMS,
+        name="assemble",
+    )(where, *stacks)
+
+
+def disassemble(plan, g, where, grads):
+    group = GROUPS[g]
+
+    def body(where_ref, *refs):
+        full_refs, stack_refs = dict(zip(group, refs[: len(group)])), refs[len(group) :]
+
+        def visit(stack, k, row, w, to_row, to_col, high):
+            stack_refs[stack][k, row : row + high, :] = full_refs[w][
+                pl.ds(to_row, high), pl.ds(to_col, plan.chunk)
+            ]
+
+        each_piece(plan, group, where_ref, visit)
+
+    shape = jax.ShapeDtypeStruct((plan.zs, plan.rows[g], plan.chunk), BF16)
+    return pl.pallas_call(
+        body,
+        out_shape=(shape,) * 8,
+        in_specs=[SMEM_SPEC] + [VMEM_SPEC] * len(group),
+        out_specs=(VMEM_SPEC,) * 8,
+        compiler_params=PARAMS,
+        name="disassemble",
+    )(where, *grads)
+
+
+def add_low(one, two):
+    return (one.astype(F32) + two.astype(F32)).astype(BF16)
+
+
+def reduce_group(plan, g, where, stacks):
+    got = [send(part, plan.core()) for part in stacks[4:]]
+    mine = [add_low(a, b) for a, b in zip(stacks[:4], got)]
+    side, far = send(mine[2], plan.second()), send(mine[3], plan.second())
+    mine = [add_low(mine[0], side), add_low(mine[1], far)]
+    near = send(mine[1], plan.first())
+    total = add_low(mine[0], near)
+    parts = [total[0]]
+    for k in range(1, plan.zs):
+        parts.append(send(total[k], plan.z_up(plan.zs - k)))
+    own, give = unpack_split(plan, g, where, parts)
+    return unpack_join(plan, g, where, own, send(give, plan.core()))
+
+
+def unpack_split(plan, g, where, parts):
+    group, rows, wide = GROUPS[g], plan.rows[g], plan.chunk // 2
+
+    def body(where_ref, *refs):
+        part_refs, (own_ref, give_ref) = refs[:-2], refs[-2:]
+        core = where_ref[3]
+
+        def fill(low_ref, high_ref):
+            at = 0
+            for w in group:
+                high, count = plan.half[w], plan.chunks[w]
+                for j in range(count):
+                    row = at + j * high
+                    value = sum(p[row : row + high, :].astype(F32) for p in part_refs)
+                    for b in (2 * j, 2 * j + 1):
+                        dst = low_ref if b < count else high_ref
+                        to = at + (b % count) * high
+                        cut = (b - 2 * j) * wide
+                        dst[to : to + high, :] = value[:, cut : cut + wide]
+                at += count * high
+
+        @pl.when(core == 0)
+        def _():
+            fill(own_ref, give_ref)
+
+        @pl.when(core == 1)
+        def _():
+            fill(give_ref, own_ref)
+
+    shape = jax.ShapeDtypeStruct((rows, wide), F32)
+    return pl.pallas_call(
+        body,
+        out_shape=(shape, shape),
+        in_specs=[SMEM_SPEC] + [VMEM_SPEC] * len(parts),
+        out_specs=(VMEM_SPEC, VMEM_SPEC),
+        compiler_params=PARAMS,
+        name="unpack_split",
+    )(where, *parts)
+
+
+def unpack_join(plan, g, where, own, got):
+    group, wide = GROUPS[g], plan.chunk // 2
+
+    def body(where_ref, own_ref, got_ref, *out_refs):
+        core = where_ref[3]
+        at = 0
+        for w, out_ref in zip(group, out_refs):
+            high, count = plan.half[w], plan.chunks[w]
+            own_rows = pl.ds(pl.multiple_of(core * high, 16), high)
+            got_rows = pl.ds(pl.multiple_of((1 - core) * high, 16), high)
+            for b in range(count):
+                row, cut = at + b * high, slice(b * wide, (b + 1) * wide)
+                out_ref[own_rows, cut] = own_ref[row : row + high, :]
+                out_ref[got_rows, cut] = got_ref[row : row + high, :]
+            at += count * high
+
+    return pl.pallas_call(
+        body,
+        out_shape=tuple(
+            jax.ShapeDtypeStruct((2 * plan.half[w], plan.cols[w]), F32) for w in group
+        ),
+        in_specs=[SMEM_SPEC, VMEM_SPEC, VMEM_SPEC],
+        out_specs=(VMEM_SPEC,) * len(group),
+        compiler_params=PARAMS,
+        name="unpack_join",
+    )(where, own, got)
+
+
+def gather_small(plan, where, vectors, bias):
+    count, part = vectors.shape
+    flat = jnp.concatenate([vectors.reshape(-1), bias])
+    size = flat.shape[0]
+    flat = jnp.pad(flat, (0, -size % 2048)).reshape(-1, 128)
+    pair = jnp.stack([flat, send(flat, plan.flip(lambda i: 4))])
+    every = jnp.stack([pair] + [send(pair, plan.z_up(k)) for k in range(1, plan.zs)])
+    every = every.reshape((plan.dp,) + flat.shape)
+    at = jnp.arange(plan.dp, dtype=jnp.int32)
+    slot = lax.rem(where[0] - at // 2 + plan.zs, plan.zs) * 2 + ((at % 2) ^ where[1])
+    every = jnp.take(every, slot, axis=0).reshape(plan.dp, -1)[:, :size].astype(F32)
+    rows = every[:, : count * part].reshape(plan.dp, count, part)
+    rows = rows.transpose(1, 0, 2).reshape(count, plan.dp * part)
+    return rows, every[:, count * part :].reshape(-1)
+
+
+def reduce_small(plan, where, rows, bias):
+    count, width = rows.shape
+    flat = jnp.concatenate([rows.reshape(-1), bias]).astype(F32)
+    size = flat.shape[0]
+    flat = jnp.pad(flat, (0, -size % 1024)).reshape(-1, 128)
+    for bit in (1, 2, 4):
+        flat = flat + send(flat, plan.flip(lambda i: bit))
+    flat = flat + sum(send(flat, plan.z_up(k)) for k in range(1, plan.zs))
+    flat = flat.reshape(-1)
+    dp = where[0] * 2 + where[1]
+    whole = flat[: count * width].reshape(count, width)
+    own = lax.dynamic_slice_in_dim(whole, dp * (width // plan.dp), width // plan.dp, axis=1)
+    tail = flat[count * width : size]
+    step = bias.shape[0] // plan.dp
+    return own, lax.dynamic_slice_in_dim(tail, dp * step, step, axis=0)
+
+
+def fetch_plain(weights, vectors, bias):
+    whole = [
+        lax.all_gather(lax.all_gather(w, "dp", axis=0, tiled=True), "patch", axis=1, tiled=True)
+        for w in weights
+    ]
+    rows = lax.all_gather(vectors, "dp", axis=1, tiled=True)
+    return whole, rows.astype(F32), lax.all_gather(bias, "dp", axis=0, tiled=True).astype(F32)
+
+
+def reduce_plain(grads, rows, bias):
+    whole = []
+    for grad in grads:
+        part = lax.psum_scatter(grad, "dp", scatter_dimension=0, tiled=True)
+        whole.append(
+            lax.psum_scatter(part, "patch", scatter_dimension=1, tiled=True).astype(F32)
+        )
+    rows = lax.psum(lax.psum_scatter(rows, "dp", scatter_dimension=1, tiled=True), "patch")
+    bias = lax.psum(lax.psum_scatter(bias, "dp", scatter_dimension=0, tiled=True), "patch")
+    return whole, rows, bias
 
 
 def norm_forward(total_in, gain_row, shift_row):
@@ -70,43 +428,7 @@
     return (grad_query, grad_key, grad_value)
 
 
-def fetch_weights(
-    self_qkv, self_out, cross_q, cross_kv, cross_out, ffn_in, ffn_out, vectors, ffn_bias_in
-):
-    by_rows = (
-        lax.all_gather(self_qkv, "dp", axis=0, tiled=True),
-        lax.all_gather(self_out, "dp", axis=0, tiled=True),
-        lax.all_gather(cross_q, "dp", axis=0, tiled=True),
-        lax.all_gather(cross_kv, "dp", axis=0, tiled=True),
-        lax.all_gather(cross_out, "dp", axis=0, tiled=True),
-        lax.all_gather(ffn_in, "dp", axis=0, tiled=True),
-        lax.all_gather(ffn_out, "dp", axis=0, tiled=True),
-        lax.all_gather(vectors, "dp", axis=1, tiled=True),
-        lax.all_gather(ffn_bias_in, "dp", axis=0, tiled=True),
-    )
-    by_cols = (
-        lax.all_gather(by_rows[0], "patch", axis=1, tiled=True),
-        lax.all_gather(by_rows[1], "patch", axis=1, tiled=True),
-        lax.all_gather(by_rows[2], "patch", axis=1, tiled=True),
-        lax.all_gather(by_rows[3], "patch", axis=1, tiled=True),
-        lax.all_gather(by_rows[4], "patch", axis=1, tiled=True),
-        lax.all_gather(by_rows[5], "patch", axis=1, tiled=True),
-        lax.all_gather(by_rows[6], "patch", axis=1, tiled=True),
-    )
-    return (
-        by_cols[0],
-        by_cols[1],
-        by_cols[2],
-        by_cols[3],
-        by_cols[4],
-        by_cols[5],
-        by_cols[6],
-        by_rows[7].astype(jnp.float32),
-        by_rows[8].astype(jnp.float32),
-    )
-
-
-def forward_pass(weights, text_local, grid_local, cls_local, lengths, counts, boxes):
+def forward_pass(weights, text_local, patches, lengths, counts, boxes):
     w_qkv, w_out, w_cq, w_ckv, w_cout, w_fin, w_fout, vec_rows, bias_in = weights
     model_width = w_out.shape[0]
     head_count = model_width // HEAD
@@ -137,14 +459,9 @@
     ).astype(jnp.bfloat16)
     cross_query = cross_query.reshape(item_count, seq_len, head_count, HEAD)
     kv_bias = jnp.concatenate([zero_row, vec_rows[6]])
-    local_kv = (
-        jnp.einsum("ipv,ve->ipe", grid_local, w_ckv, preferred_element_type=jnp.float32) + kv_bias
+    patch_kv = (
+        jnp.einsum("ipv,ve->ipe", patches, w_ckv, preferred_element_type=jnp.float32) + kv_bias
     ).astype(jnp.bfloat16)
-    grid_kv = lax.all_to_all(local_kv, "patch", split_axis=0, concat_axis=1, tiled=True)
-    cls_kv = (jnp.dot(cls_local, w_ckv, preferred_element_type=jnp.float32) + kv_bias).astype(
-        jnp.bfloat16
-    )
-    patch_kv = jnp.concatenate([cls_kv[:, None], grid_kv], 1)
     patch_count = patch_kv.shape[1]
     cross_key = patch_kv[:, :, :model_width].reshape(item_count, patch_count, head_count, HEAD)
     cross_value = patch_kv[:, :, model_width:].reshape(item_count, patch_count, head_count, HEAD)
@@ -187,8 +504,7 @@
         "pre_act": pre_act,
         "act_low": act_low,
         "total_three": total_three,
-        "grid_mine": grid_local,
-        "cls_local": cls_local,
+        "patches": patches,
     }
 
 
@@ -251,18 +567,10 @@
         -1,
     ).astype(jnp.bfloat16)
     bias_cv = jnp.sum(patch_grad[:, :, model_width:], (0, 1), dtype=jnp.float32)
-    cls_part = patch_grad[:, 0]
-    grid_part = patch_grad[:, 1:]
-    cls_term = jnp.einsum(
-        "iv,ie->ve", saved["cls_local"], cls_part, preferred_element_type=jnp.float32
-    )
-    cls_grad = jnp.einsum("ie,ve->iv", cls_part, w_ckv, preferred_element_type=jnp.float32)
-    grid_back = lax.all_to_all(grid_part, "patch", split_axis=1, concat_axis=0, tiled=True)
-    grad_ckv = (
-        jnp.einsum("ipv,ipe->ve", saved["grid_mine"], grid_back, preferred_element_type=jnp.float32)
-        + cls_term
-    )
-    grid_grad = jnp.einsum("ipe,ve->ipv", grid_back, w_ckv, preferred_element_type=jnp.float32)
+    grad_ckv = jnp.einsum(
+        "ipv,ipe->ve", saved["patches"], patch_grad, preferred_element_type=jnp.float32
+    )
+    patches_grad = jnp.einsum("ipe,ve->ipv", patch_grad, w_ckv, preferred_element_type=jnp.float32)
     hidden_one, norm_one = jax.vjp(norm_forward, saved["total_one"], vec_rows[3], vec_rows[4])
     grad_one, gain_one, shift_one = norm_one(grad_hidden_one)
     grad_one_low = grad_one.astype(jnp.bfloat16)
@@ -322,74 +630,28 @@
         grad_vec,
         bias_fin,
     )
-    return (layer_out, text_grad, grid_grad, cls_grad, local_grads)
-
-
-def reduce_grads(local_grads):
-    grad_qkv, grad_out, grad_cq, grad_ckv, grad_cout, grad_fin, grad_fout, grad_vec, grad_bias = (
-        local_grads
-    )
-    spread = lax.axis_size("patch")
-    section_one = (
-        lax.psum_scatter(grad_qkv, "dp", scatter_dimension=0, tiled=True),
-        lax.psum_scatter(grad_out, "dp", scatter_dimension=0, tiled=True),
-        lax.psum_scatter(grad_cq, "dp", scatter_dimension=0, tiled=True),
-        lax.psum_scatter(grad_ckv, "dp", scatter_dimension=0, tiled=True),
-        lax.psum_scatter(grad_cout, "dp", scatter_dimension=0, tiled=True),
-        lax.psum_scatter(grad_fin, "dp", scatter_dimension=0, tiled=True),
-        lax.psum_scatter(grad_fout, "dp", scatter_dimension=0, tiled=True),
-        lax.psum_scatter(grad_vec, "dp", scatter_dimension=1, tiled=True),
-        lax.psum_scatter(grad_bias, "dp", scatter_dimension=0, tiled=True),
-    )
-    section_two = (
-        lax.psum_scatter(
-            section_one[0].astype(jnp.bfloat16), "patch", scatter_dimension=1, tiled=True
-        ).astype(jnp.float32),
-        lax.psum_scatter(
-            section_one[1].astype(jnp.bfloat16), "patch", scatter_dimension=1, tiled=True
-        ).astype(jnp.float32),
-        lax.psum_scatter(
-            section_one[2].astype(jnp.bfloat16), "patch", scatter_dimension=1, tiled=True
-        ).astype(jnp.float32),
-        lax.psum_scatter(
-            section_one[3].astype(jnp.bfloat16), "patch", scatter_dimension=1, tiled=True
-        ).astype(jnp.float32),
-        lax.psum_scatter(
-            section_one[4].astype(jnp.bfloat16), "patch", scatter_dimension=1, tiled=True
-        ).astype(jnp.float32),
-        lax.psum_scatter(
-            section_one[5].astype(jnp.bfloat16), "patch", scatter_dimension=1, tiled=True
-        ).astype(jnp.float32),
-        lax.psum_scatter(
-            section_one[6].astype(jnp.bfloat16), "patch", scatter_dimension=1, tiled=True
-        ).astype(jnp.float32),
-        lax.psum_scatter(
-            jnp.broadcast_to(section_one[7], (spread,) + section_one[7].shape).astype(jnp.bfloat16),
-            "patch",
-            scatter_dimension=0,
-            tiled=True,
-        ).astype(jnp.float32),
-        lax.psum_scatter(
-            jnp.broadcast_to(section_one[8], (spread,) + section_one[8].shape).astype(jnp.bfloat16),
-            "patch",
-            scatter_dimension=0,
-            tiled=True,
-        ).astype(jnp.float32),
-    )
-    return (
-        section_two[0],
-        section_two[1],
-        section_two[2],
-        section_two[3],
-        section_two[4],
-        section_two[5],
-        section_two[6],
-        section_two[7][0],
-        section_two[8][0],
-    )
+    return (layer_out, text_grad, patches_grad, local_grads)
+
+
+def trade_in(image_grid, count):
+    micro, items, own, width = image_grid.shape
+    cut = image_grid.reshape(micro, count, items // count, own, width).transpose(1, 0, 2, 3, 4)
+    got = lax.all_to_all(cut, "patch", split_axis=0, concat_axis=0, tiled=True)
+    return got.transpose(1, 2, 0, 3, 4).reshape(micro * items // count, count * own, width)
+
+
+def trade_back(grads, micro, count):
+    items, patches, width = grads.shape
+    cut = grads.reshape(micro, items // micro, count, patches // count, width)
+    got = lax.all_to_all(
+        cut.transpose(2, 0, 1, 3, 4), "patch", split_axis=0, concat_axis=0, tiled=True
+    )
+    got = got.transpose(1, 0, 2, 3, 4)
+    return got.reshape(micro, items // micro * count, patches // count, width)
 
 
 def on_device(
+    plan,
     text_in,
     image_grid,
     image_cls,
@@ -397,100 +659,86 @@
     phrase_counts,
     phrase_boxes,
     cotangent,
-    self_qkv,
-    self_out,
-    cross_q,
-    cross_kv,
-    cross_out,
-    ffn_in,
-    ffn_out,
-    vectors,
-    ffn_bias_in,
+    *params,
 ):
-    micro_count = text_in.shape[0]
-    out_list = []
-    text_list = []
-    grid_list = []
-    cls_list = []
-    running = None
-    for micro_index in range(micro_count):
-        forward_weights = fetch_weights(
-            self_qkv, self_out, cross_q, cross_kv, cross_out, ffn_in, ffn_out, vectors, ffn_bias_in
-        )
-        saved = forward_pass(
-            forward_weights,
-            text_in[micro_index],
-            image_grid[micro_index],
-            image_cls[micro_index],
-            text_lengths[micro_index],
-            phrase_counts[micro_index],
-            phrase_boxes[micro_index],
-        )
-        backward_weights = fetch_weights(
-            self_qkv, self_out, cross_q, cross_kv, cross_out, ffn_in, ffn_out, vectors, ffn_bias_in
-        )
-        layer_out, text_grad, grid_grad, cls_grad, local_grads = backward_pass(
-            backward_weights, saved, cotangent[micro_index]
-        )
-        reduced = reduce_grads(local_grads)
-        running = reduced if running is None else jax.tree.map(jnp.add, running, reduced)
-        out_list.append(layer_out)
-        text_list.append(text_grad)
-        grid_list.append(grid_grad)
-        cls_list.append(cls_grad)
+    micro, width = text_in.shape[0], text_in.shape[2]
+    shards, vectors, ffn_bias = params[:7], params[7], params[8]
+    where = coords()
+    items = text_lengths.size
+    grid = trade_in(image_grid, plan.patch)
+    patches = jnp.concatenate([image_cls.reshape(items, 1, -1), grid], axis=1)
+    if plan.fast:
+        own, give = pack_split(plan, where, shards)
+        units = pack_join(plan, where, own, send(give, plan.core()))
+        weights = [None] * 7
+        for g, group in enumerate(GROUPS):
+            full = assemble(plan, g, where, gather_group(plan, units[g]))
+            for w, value in zip(group, full):
+                weights[w] = value
+        rows, bias = gather_small(plan, where, vectors, ffn_bias)
+    else:
+        weights, rows, bias = fetch_plain(shards, vectors, ffn_bias)
+    pack = (*weights, rows, bias)
+    saved = forward_pass(
+        pack,
+        text_in.reshape(-1, width),
+        patches,
+        text_lengths.reshape(-1),
+        phrase_counts.reshape(-1),
+        phrase_boxes.reshape((items,) + phrase_boxes.shape[2:]),
+    )
+    layer_out, text_grad, patches_grad, local = backward_pass(
+        pack, saved, cotangent.reshape(-1, width)
+    )
+    low = [grad.astype(BF16) for grad in local[:7]]
+    if plan.fast:
+        grads = [None] * 7
+        for g in (3, 2, 1, 0):
+            stacks = disassemble(plan, g, where, [low[w] for w in GROUPS[g]])
+            for w, value in zip(GROUPS[g], reduce_group(plan, g, where, stacks)):
+                grads[w] = value
+        rows_grad, bias_grad = reduce_small(plan, where, local[7], local[8])
+    else:
+        grads, rows_grad, bias_grad = reduce_plain(low, local[7], local[8])
+    cls_grad = patches_grad[:, 0].reshape(image_cls.shape)
+    grid_grad = trade_back(patches_grad[:, 1:].astype(BF16), micro, plan.patch).astype(F32)
     return (
-        jnp.stack(out_list),
-        jnp.stack(text_list),
-        jnp.stack(grid_list),
-        jnp.stack(cls_list),
-        running[0],
-        running[1],
-        running[2],
-        running[3],
-        running[4],
-        running[5],
-        running[6],
-        running[7],
-        running[8],
+        layer_out.reshape(text_in.shape),
+        text_grad.reshape(text_in.shape),
+        grid_grad,
+        cls_grad,
+        *grads,
+        rows_grad,
+        bias_grad,
     )
 
 
 def solution(mesh):
-    return jax.shard_map(
-        on_device,
-        mesh=mesh,
-        in_specs=(
-            P(None, ("dp", "patch"), None),
-            P(None, "dp", "patch", None),
-            P(None, ("dp", "patch"), None),
-            P(None, ("dp", "patch")),
-            P(None, ("dp", "patch")),
-            P(None, ("dp", "patch"), None, None),
-            P(None, ("dp", "patch"), None),
-            P("dp", "patch"),
-            P("dp", "patch"),
-            P("dp", "patch"),
-            P("dp", "patch"),
-            P("dp", "patch"),
-            P("dp", "patch"),
-            P("dp", "patch"),
-            P(None, "dp"),
-            P("dp"),
-        ),
-        out_specs=(
-            P(None, ("dp", "patch"), None),
-            P(None, ("dp", "patch"), None),
-            P(None, "dp", "patch", None),
-            P(None, ("dp", "patch"), None),
-            P("dp", "patch"),
-            P("dp", "patch"),
-            P("dp", "patch"),
-            P("dp", "patch"),
-            P("dp", "patch"),
-            P("dp", "patch"),
-            P("dp", "patch"),
-            P(None, "dp"),
-            P("dp"),
-        ),
-        check_vma=False,
-    )
+    dp, patch = mesh.shape["dp"], mesh.shape["patch"]
+    both = P(None, ("dp", "patch"), None)
+    weight = P("dp", "patch")
+
+    def run(*args):
+        shards = [(w.shape[0] // dp, w.shape[1] // patch) for w in args[7:14]]
+        plan = Plan(dp, patch, shards)
+        return jax.shard_map(
+            functools.partial(on_device, plan),
+            mesh=mesh,
+            in_specs=(
+                both,
+                P(None, "dp", "patch", None),
+                both,
+                P(None, ("dp", "patch")),
+                P(None, ("dp", "patch")),
+                P(None, ("dp", "patch"), None, None),
+                both,
+            )
+            + (weight,) * 7
+            + (P(None, "dp"), P("dp")),
+            out_specs=(both, both, P(None, "dp", "patch", None), both)
+            + (weight,) * 7
+            + (P(None, "dp"), P("dp")),
+            check_vma=False,
+        )(*args)
+
+    return run

time: 2660 us -> 649 us (0.24)
  waiting for transfers between devices: 1830 us -> 119 us
  blocking collectives: 265 us -> 0 us
  starting transfers between devices: 20.2 us -> 106 us
  local copies, waits for them, and re-layouts: 184 us -> 105 us
  matrix products: 262 us -> 197 us
  Pallas kernels: 0 us -> 61.2 us
    reduce_scatter x20 -> x0, waiting for transfers between devices: 1360 us -> none  [the longest x2 332 us: reduce_grads(): lax.psum_scatter(grad_fin, 'dp', scatter_dimension=0, tiled=True)]
    unnamed x53 -> x0, waiting for transfers between devices: 421 us -> none
    all_gather x7 -> x0, blocking collectives: 221 us -> none  [the longest x1 36.8 us: fetch_weights(): lax.all_gather(cross_kv, 'dp', axis=0, tiled=True)]
    ppermute x0 -> x95, waiting for transfers between devices: none -> 119 us  [send(): return lax.ppermute(value, AXES, perm)]
    ppermute x0 -> x95, starting transfers between devices: none -> 96.5 us  [send(): return lax.ppermute(value, AXES, perm)]
    unnamed x421 -> x285, local copies, waits for them, and re-layouts: 94.4 us -> 30.3 us
    pallas_call x0 -> x18, Pallas kernels: none -> 61.2 us  [the longest x4 20.8 us: disassemble(): pl.pallas_call(body, out_shape=(shape,) * 8, in_specs=[SMEM_SPEC] + [VMEM...]
    all_to_all x4 -> x2, waiting for transfers between devices: 50.3 us -> 0.01 us  [the longest x1 0.01 us: trade_in(): got = lax.all_to_all(cut, 'patch', split_axis=0, concat_axis=0, tiled=True)]
  transfers between devices with their start and end apart: 45 -> 97, of which waited for: 33 -> 25; matrix products, arithmetic and copies ran while one was open for 13% -> 15% of each run, Pallas kernels for 0% -> 8%
where the time goes in v1:
time: 649 us; the launch traced here: 643 us
  matrix products  197 us (30%)
  waiting for transfers between devices  119 us (18%)
  starting transfers between devices  106 us (16%)
  local copies, waits for them, and re-layouts  105 us (16%)
  Pallas kernels  61.2 us (9%)
  other arithmetic  51.8 us (8%)
    ppermute x95, waiting for transfers between devices, send(): return lax.ppermute(value, AXES, perm)  119 us
    ppermute x95, starting transfers between devices, send(): return lax.ppermute(value, AXES, perm)  96.5 us
    dot_general x1, matrix products, forward_pass(): jnp.dot(hidden_two_low, w_fin, preferred_element_type=jnp.float32) + bias_in  35.1 us
    unnamed x285, local copies, waits for them, and re-layouts  30.3 us
    pallas_call x4, Pallas kernels, disassemble(): pl.pallas_call(body, out_shape=(shape,) * 8, in_specs=[SMEM_SPEC] + [VMEM...  20.8 us
    pallas_call x4, Pallas kernels, assemble(): pl.pallas_call(body, out_shape=tuple((jax.ShapeDtypeStruct(plan.full[w],...  20.3 us
    dot_general x1, matrix products, backward_pass(): jnp.einsum('rd,fd->rf', grad_three_low, w_fout, preferred_element_type=jn...  18.3 us
    dot_general x2, matrix products, attend_backward(): jnp.einsum('iqhd,ikhd->ihqk', grad_low, values, preferred_element_type=jn...  15.6 us
  transfers between devices with their start and end apart: 97, of which 25 were waited for; matrix products, arithmetic and copies ran while one was open for 15% of the time, Pallas kernels for 8%

profile of v1, /device:TPU:0, one launch (start us, length us, event | category | flops | bytes accessed | tf_op | source)
XLA Modules:
  0.0 642.9 jit_solution(13090418506841815723)
XLA Ops:
  17.1 4.6 all-to-all-start
  34.0 8.8 %collective-permute-done.2 = bf16[192,384]{1,0:T(8,128)(2,1)S(1)} collective-permute-done((bf16[192,384]{1,0:T(8,128)(2,1)}, bf16[192,384]{1,0:T(8,128)(2,1)S(1)}, u32[]{:S(2)}, u32[]{:S(2)}) %collective-permute-start.2) | collective-permute-done | bytes 147488 | tf_op jit(solution)/shard_map/ppermute | solution.py:60
  59.0 5.4 collective-permute-start.5
  66.0 5.7 collective-permute-start.35
  71.9 7.0 %collective-permute-done.36 = bf16[192,384]{1,0:T(8,128)(2,1)S(1)} collective-permute-done((bf16[192,384]{1,0:T(8,128)(2,1)S(1)}, bf16[192,384]{1,0:T(8,128)(2,1)S(1)}, u32[]{:S(2)}, u32[]{:S(2)}) %collective-permute-start.36) | collective-permute-done | bytes 147488 | tf_op jit(solution)/shard_map/ppermute | solution.py:60
  106.9 4.9 assemble.4
  111.8 7.1 %fusion.26 = bf16[288,8,8,128]{3,1,2,0:T(8,128)(2,1)S(1)} fusion(f32[2304]{0:T(1024)S(1)} %pad_maximum_fusion.11, bf16[768,2304]{1,0:T(8,128)(2,1)} %get-tuple-element.72, bf16[1024,768]{1,0:T(8,128)(2,1)} %bitcast.326), kind=kOutput, calls=%fused_computation.101 | convolution fusion | flops 3628597248 | bytes 9839616 | tf_op jit(solution)/shard_map/dot_general | solution.py:439
  129.6 10.3 %collective-permute-done.30.refs_3_ = bf16[4,192,384]{2,1,0:T(8,128)(2,1)S(1)} collective-permute-done((bf16[4,192,384]{2,1,0:T(8,128)(2,1)}, bf16[4,192,384]{2,1,0:T(8,128)(2,1)S(1)}, u32[]{:S(2)}, u32[]{:S(2)}) %collective-permute-start.30) | collective-permute-done | bytes 589856 | tf_op jit(solution)/shard_map/ppermute | solution.py:60
  151.1 5.0 assemble.6
  156.1 5.5 fusion.121
  162.7 4.8 assemble.7
  170.0 5.5 assemble.5
  175.5 6.7 %add_convert_fusion.2 = bf16[8,145,1536]{2,1,0:T(8,128)(2,1)S(1)} fusion(f32[1536]{0:T(1024)S(1)} %concatenate.25, bf16[1024,1536]{1,0:T(8,128)(2,1)} %get-tuple-element.75, bf16[8,144,1024]{2,1,0:T(8,128)(2,1)} %copy.129, bf16[8,1,1024]{2,1,0:T(2,128)(2,1)S(1)} %reshape.579), kind=kOutput, calls=%fused_computation.27 | convolution fusion | flops 3657359360 | bytes 9091072 | tf_op jit(solution)/shard_map/ipv,ve->ipe/dot_general | solution.py:463
  189.7 6.1 add_convert_fusion.3
  213.5 35.1 %multiply_convert_fusion = (bf16[1024,3072]{1,0:T(8,128)(2,1)S(1)}, f32[1024,3072]{1,0:T(8,128)}, f32[1024,3072]{1,0:T(8,128)}) fusion(f32[3072]{0:T(1024)S(1)} %add.381, bf16[768,3072]{1,0:T(8,128)(2,1)S(1)} %bitcast.286, f32[1024,768]{1,0:T(8,128)S(1)} %get-tuple-element.249, f32[768]{0:T(1024)S(1)} %add.378, f32[768]{0:T(1024)S(1)} %mul.311, ...), kind=kOutput, calls=%fused_computation.7 | convolution fusion | flops 5043388416 | bytes 39348224 | tf_op jit(solution)/shard_map/dot_general | solution.py:481
  248.7 5.4 fusion.124
  262.2 18.3 %convert_reduce_fusion = (f32[3072]{0:T(1024)S(1)}, bf16[1024,3072]{1,0:T(8,128)(2,1)}) fusion(f32[1024,3072]{1,0:T(8,128)} %get-tuple-element.213, bf16[1024,768]{1,0:T(8,128)(2,1)} %get-tuple-element.201, bf16[3072,768]{1,0:T(8,128)(2,1)} %assemble.7, f32[1024,3072]{1,0:T(8,128)} %get-tuple-element.250, f32[3072]{0:T(1024)S(1)} %add.381), kind=kOutput, calls=%fused_computation.5 | convolution fusion | flops 4885312512 | bytes 37773312 | tf_op jit(solution)/shard_map/rd,fd->rf/dot_general | solution.py:524
  280.6 9.6 %multiply_reduce_fusion.2 = (f32[768]{0:T(1024)S(1)}, f32[1024]{0:T(1024)S(1)}, f32[768]{0:T(1024)S(1)}, f32[1024,768]{1,0:T(8,128)S(1)}) fusion(f32[1024,768]{1,0:T(8,128)S(1)} %get-tuple-element.249, f32[1024]{0:T(1024)S(1)} %fusion.83, f32[1024]{0:T(1024)S(1)} %broadcast_multiply_fusion.1, f32[768]{0:T(1024)S(1)} %mul.311, ...), kind=kOutput, calls=%fused_computation.64 | convolution fusion | flops 4839699456 | bytes 20472832 | tf_op jit(solution)/shard_map/rf,df->rd/dot_general | solution.py:531
  301.1 8.6 %multiply_reduce_fusion = (f32[8,12,128]{2,1,0:T(8,128)S(1)}, f32[8,12,128,145]{2,3,1,0:T(8,128)}) fusion(f32[8,12,128,145]{2,3,1,0:T(8,128)} %copy-done.20, f32[8,12,128]{2,1,0:T(8,128)S(1)} %copy-done.86, bf16[8,145,12,64]{1,3,2,0:T(8,128)(2,1)S(1)} %bitcast.290, bf16[8,128,12,64]{1,0,3,2:T(8,128)(2,1)S(1)} %bitcast.298), kind=kOutput, calls=%fused_computation.24 | convolution fusion | flops 233398272 | bytes 17707008 | tf_op jit(solution)/shard_map/iqhd,ikhd->ihqk/dot_general | solution.py:414
  309.7 7.3 %multiply_convert_fusion.1 = bf16[8,12,128,145]{2,3,1,0:T(8,128)(2,1)S(1)} fusion(f32[8,12,128,145]{2,3,1,0:T(8,128)} %get-tuple-element.255, f32[8,12,128]{2,1,0:T(8,128)S(1)} %get-tuple-element.254, f32[8,12,128,145]{2,3,1,0:T(8,128)} %copy-done.20, f32[8,12,128]{2,1,0:T(8,128)S(1)} %copy-done.86), kind=kLoop, calls=%fused_computation.23 | loop fusion | flops 7127040 | bytes 17915904 | tf_op jit(solution)/shard_map/convert_element_type | solution.py:416
  331.0 6.3 convolution_bitcast_fusion
  337.3 7.0 %multiply_reduce_fusion.1 = (f32[8,12,128]{2,1,0:T(8,128)S(1)}, f32[8,12,128,128]{2,3,1,0:T(8,128)}) fusion(f32[8,12,128,128]{2,3,1,0:T(8,128)} %copy-done.21, f32[8,12,128]{2,1,0:T(8,128)S(1)} %copy-done.84, bf16[8,128,1,12,64]{1,0,4,3,2:T(8,128)(2,1)S(1)} %copy-done.29, bf16[8,128,12,64]{1,0,3,2:T(8,128)(2,1)S(1)} %bitcast.301), kind=kOutput, calls=%fused_computation.32 | convolution fusion | flops 206032896 | bytes 15826944 | tf_op jit(solution)/shard_map/iqhd,ikhd->ihqk/dot_general | solution.py:414
  344.4 6.9 %multiply_convert_fusion.3 = bf16[8,12,128,128]{2,3,1,0:T(8,128)(2,1)S(1)} fusion(f32[8,12,128,128]{2,3,1,0:T(8,128)} %get-tuple-element.258, f32[8,12,128]{2,1,0:T(8,128)S(1)} %get-tuple-element.257, f32[8,12,128,128]{2,3,1,0:T(8,128)} %copy-done.21, f32[8,12,128]{2,1,0:T(8,128)S(1)} %copy-done.84), kind=kLoop, calls=%fused_computation.31 | loop fusion | flops 6291456 | bytes 15826944 | tf_op jit(solution)/shard_map/convert_element_type | solution.py:416
  362.8 9.3 %copy.146 = bf16[8,128,3,12,64]{1,0,4,3,2:T(8,128)(2,1)S(1)} copy(bf16[8,128,3,12,64]{1,4,3,0,2:T(8,128)(2,1)S(1)} %maximum_convert_fusion) | data formatting | bytes 9437184 | tf_op jit(solution)/shard_map/convert_element_type | solution.py:595
  372.2 6.0 add_add_fusion.6
  378.2 5.4 fusion.10.refs_0_
  390.5 9.5 %fusion.18 = f32[8,145,1024]{2,1,0:T(8,128)} fusion(bf16[1024,1536]{1,0:T(8,128)(2,1)} %get-tuple-element.75, bf16[8,145,768]{2,1,0:T(8,128)(2,1)} %copy.150, bf16[8,145,768]{2,1,0:T(8,128)(2,1)} %copy.149), kind=kOutput, calls=%fused_computation.60 | convolution fusion | flops 3656171520 | bytes 11460608 | tf_op jit(solution)/shard_map/ipe,ve->ipv/dot_general | solution.py:573
  400.1 6.5 %bitcast_convert_fusion.refs_1_ = bf16[1024,1536]{1,0:T(8,128)(2,1)} fusion(bf16[8,145,768]{2,1,0:T(8,128)(2,1)S(1)} %copy-done.26, bf16[8,145,768]{2,1,0:T(8,128)(2,1)S(1)} %copy-done.27, bf16[8,144,1024]{2,1,0:T(8,128)(2,1)S(1)} %copy-done.25, bf16[8,1,1024]{2,1,0:T(2,128)(2,1)S(1)} %copy-done.94), kind=kOutput, calls=%fused_computation.28 | convolution fusion | flops 3662495744 | bytes 9084928 | tf_op jit(solution)/shard_map/ipv,ipe->ve/dot_general | solution.py:570
  406.6 10.1 %convolution_convert_fusion.1.refs_0_ = bf16[768,3072]{1,0:T(8,128)(2,1)} fusion(bf16[1024,3072]{1,0:T(8,128)(2,1)} %get-tuple-element.260, f32[1024,768]{1,0:T(8,128)S(1)} %copy-done.17, f32[768]{0:T(1024)S(1)} %copy-done.107, f32[768]{0:T(1024)S(1)} %mul.311, f32[1024]{0:T(1024)S(1)} %fusion.83, f32[1024]{0:T(1024)S(1)} %broadcast_multiply_fusion.1), kind=kOutput, calls=%fused_computation.37 | convolution fusion | flops 4838129664 | bytes 14170112 | tf_op jit(solution)/shard_map/rd,rf->df/dot_general | solution.py:527
  416.7 7.4 %convolution_convert_fusion.refs_0_ = bf16[3072,768]{1,0:T(8,128)(2,1)} fusion(bf16[1024,3072]{1,0:T(8,128)(2,1)S(1)} %bitcast.331, bf16[1024,768]{1,0:T(8,128)(2,1)S(1)} %copy-done.40), kind=kOutput, calls=%fused_computation.36 | convolution fusion | flops 4834197504 | bytes 12582912 | tf_op jit(solution)/shard_map/rf,rd->fd/dot_general | solution.py:520
  435.4 5.1 disassemble.4
  451.3 4.6 slice.276
  461.7 4.7 all-to-all-start.1
  467.0 5.1 disassemble.6
  472.1 4.9 disassemble.7
  477.1 5.7 disassemble.5
  494.7 6.5 %collective-permute-done.50 = bf16[4,192,384]{2,1,0:T(8,128)(2,1)S(1)} collective-permute-done((bf16[4,192,384]{2,1,0:T(8,128)(2,1)S(1)}, bf16[4,192,384]{2,1,0:T(8,128)(2,1)S(1)}, u32[]{:S(2)}, u32[]{:S(2)}) %collective-permute-start.50) | collective-permute-done | bytes 589856 | tf_op jit(solution)/shard_map/ppermute | solution.py:60
  501.8 5.7 collective-permute-done.72
  507.9 6.0 collective-permute-done.83
  516.2 12.0 %collective-permute-done.61 = bf16[4,224,384]{2,1,0:T(8,128)(2,1)S(1)} collective-permute-done((bf16[4,224,384]{2,1,0:T(8,128)(2,1)S(1)}, bf16[4,224,384]{2,1,0:T(8,128)(2,1)S(1)}, u32[]{:S(2)}, u32[]{:S(2)}) %collective-permute-start.61) | collective-permute-done | bytes 688160 | tf_op jit(solution)/shard_map/ppermute | solution.py:60
  529.7 10.4 %collective-permute-done.47 = bf16[4,192,384]{2,1,0:T(8,128)(2,1)S(1)} collective-permute-done((bf16[4,192,384]{2,1,0:T(8,128)(2,1)S(1)}, bf16[4,192,384]{2,1,0:T(8,128)(2,1)S(1)}, u32[]{:S(2)}, u32[]{:S(2)}) %collective-permute-start.47) | collective-permute-done | bytes 589856 | tf_op jit(solution)/shard_map/ppermute | solution.py:60
  541.1 5.4 collective-permute-done.69
  550.6 7.1 %collective-permute-done.80 = bf16[4,192,384]{2,1,0:T(8,128)(2,1)S(1)} collective-permute-done((bf16[4,192,384]{2,1,0:T(8,128)(2,1)S(1)}, bf16[4,192,384]{2,1,0:T(8,128)(2,1)S(1)}, u32[]{:S(2)}, u32[]{:S(2)}) %collective-permute-start.80) | collective-permute-done | bytes 589856 | tf_op jit(solution)/shard_map/ppermute | solution.py:60
  566.3 6.3 collective-permute-done.58
  581.1 6.5 %collective-permute-start.87 = (bf16[192,384]{1,0:T(8,128)(2,1)S(1)}, bf16[192,384]{1,0:T(8,128)(2,1)}, u32[]{:S(2)}, u32[]{:S(2)}) collective-permute-start(bf16[192,384]{1,0:T(8,128)(2,1)S(1)} %get-tuple-element.224), channel_id=1, source_target_pairs={{0,8},{1,9},{2,10},{3,11},{4,12},{5,13},{6,14},{7,15},{8,16},{9,17... | collective-permute-start | bytes 442376 | tf_op jit(solution)/shard_map/ppermute | solution.py:60
  587.7 8.9 %collective-permute-done.75.refs_2_ = bf16[192,384]{1,0:T(8,128)(2,1)S(1)} collective-permute-done((bf16[192,384]{1,0:T(8,128)(2,1)S(1)}, bf16[192,384]{1,0:T(8,128)(2,1)S(1)}, u32[]{:S(2)}, u32[]{:S(2)}) %collective-permute-start.75) | collective-permute-done | bytes 147488 | tf_op jit(solution)/shard_map/ppermute | solution.py:60
  597.5 10.1 %collective-permute-start.65 = (bf16[224,384]{1,0:T(8,128)(2,1)S(1)}, bf16[224,384]{1,0:T(8,128)(2,1)S(1)}, u32[]{:S(2)}, u32[]{:S(2)}) collective-permute-start(bf16[224,384]{1,0:T(8,128)(2,1)S(1)} %get-tuple-element.220), channel_id=1, source_target_pairs={{0,8},{1,9},{2,10},{3,11},{4,12},{5,13},{6,14},{7,15},{8,16},{9,17... | collective-permute-start | bytes 516104 | tf_op jit(solution)/shard_map/ppermute | solution.py:60
  625.8 4.9 copy.154
  (634 shorter events, 273.3 us)
Async XLA Ops:
  2.8 44.1 %collective-permute-start.11 = (bf16[16,128]{1,0:T(8,128)(2,1)}, bf16[16,128]{1,0:T(8,128)(2,1)}, u32[]{:S(2)}, u32[]{:S(2)}) collective-permute-start(bf16[16,128]{1,0:T(8,128)(2,1)} %get-tuple-element.239), channel_id=1, source_target_pairs={{0,4},{1,5},{2,6},{3,7},{4,0},{5,1},{6,2},{7,3},{8,12},{9,13},{10,... | collective-permute-start | bytes 12296 | tf_op jit(solution)/shard_map/ppermute | solution.py:60
  17.1 79.4 %all-to-all-start = ((bf16[4,2,4,36,1024]{4,2,1,3,0:T(4,128)(2,1)}), bf16[4,2,4,36,1024]{4,2,1,3,0:T(4,128)(2,1)}, u32[]{:S(2)}, u32[]{:S(2)}) async-start(bf16[4,2,4,36,1024]{4,2,1,3,0:T(4,128)(2,1)} %bitcast.279), calls=%async_computation | async-start | bytes 4718592 | tf_op jit(solution)/shard_map/all_to_all | solution.py:639
  44.7 19.8 %collective-permute-start.4 = (bf16[4,192,384]{2,1,0:T(8,128)(2,1)}, bf16[4,192,384]{2,1,0:T(8,128)(2,1)}, u32[]{:S(2)}, u32[]{:S(2)}) collective-permute-start(bf16[4,192,384]{2,1,0:T(8,128)(2,1)} %pad_maximum_fusion.7.refs_0_), channel_id=1, source_target_pairs={{0,4},{1,3},{2,6},{3,1},{4,0},{5,7},{6,2},{7,5},{8,12},{9,11},{10,... | collective-permute-start | bytes 1769480 | tf_op jit(solution)/shard_map/ppermute | solution.py:60
  59.0 21.6 %collective-permute-start.5 = (bf16[4,192,384]{2,1,0:T(8,128)(2,1)}, bf16[4,192,384]{2,1,0:T(8,128)(2,1)}, u32[]{:S(2)}, u32[]{:S(2)}) collective-permute-start(bf16[4,192,384]{2,1,0:T(8,128)(2,1)} %pad_maximum_fusion.7.refs_0_), channel_id=1, source_target_pairs={{0,2},{1,5},{2,0},{3,7},{4,6},{5,1},{6,4},{7,3},{8,10},{9,13},{10,... | collective-permute-start | bytes 1769480 | tf_op jit(solution)/shard_map/ppermute | solution.py:60
  78.9 24.5 %collective-permute-start.7 = (bf16[4,192,384]{2,1,0:T(8,128)(2,1)}, bf16[4,192,384]{2,1,0:T(8,128)(2,1)}, u32[]{:S(2)}, u32[]{:S(2)}) collective-permute-start(bf16[4,192,384]{2,1,0:T(8,128)(2,1)} %pad_maximum_fusion.7.refs_0_), channel_id=1, source_target_pairs={{0,1},{1,0},{2,3},{3,2},{4,5},{5,4},{6,7},{7,6},{8,9},{9,8},{10,11... | collective-permute-start | bytes 1769480 | tf_op jit(solution)/shard_map/ppermute | solution.py:60
  80.6 24.1 %collective-permute-start.8 = (bf16[4,192,384]{2,1,0:T(8,128)(2,1)}, bf16[4,192,384]{2,1,0:T(8,128)(2,1)}, u32[]{:S(2)}, u32[]{:S(2)}) collective-permute-start(bf16[4,192,384]{2,1,0:T(8,128)(2,1)} %collective-permute-done.4.refs_1_), channel_id=1, source_target_pairs={{0,1},{1,0},{2,3},{3,2},{4,5},{5,4},{6,7},{7,6},{8,9},{9,8},{10,11... | collective-permute-start | bytes 1769480 | tf_op jit(solution)/shard_map/ppermute | solution.py:60
  80.6 24.1 %collective-permute-start.9 = (bf16[4,192,384]{2,1,0:T(8,128)(2,1)}, bf16[4,192,384]{2,1,0:T(8,128)(2,1)}, u32[]{:S(2)}, u32[]{:S(2)}) collective-permute-start(bf16[4,192,384]{2,1,0:T(8,128)(2,1)} %collective-permute-done.5.refs_2_), channel_id=1, source_target_pairs={{0,1},{1,0},{2,3},{3,2},{4,5},{5,4},{6,7},{7,6},{8,9},{9,8},{10,11... | collective-permute-start | bytes 1769480 | tf_op jit(solution)/shard_map/ppermute | solution.py:60
  81.2 24.5 %collective-permute-start.10 = (bf16[4,192,384]{2,1,0:T(8,128)(2,1)}, bf16[4,192,384]{2,1,0:T(8,128)(2,1)}, u32[]{:S(2)}, u32[]{:S(2)}) collective-permute-start(bf16[4,192,384]{2,1,0:T(8,128)(2,1)} %collective-permute-done.6.refs_3_), channel_id=1, source_target_pairs={{0,1},{1,0},{2,3},{3,2},{4,5},{5,4},{6,7},{7,6},{8,9},{9,8},{10,11... | collective-permute-start | bytes 1769480 | tf_op jit(solution)/shard_map/ppermute | solution.py:60
  95.8 24.4 %collective-permute-start.28 = (bf16[4,192,384]{2,1,0:T(8,128)(2,1)}, bf16[4,192,384]{2,1,0:T(8,128)(2,1)}, u32[]{:S(2)}, u32[]{:S(2)}) collective-permute-start(bf16[4,192,384]{2,1,0:T(8,128)(2,1)} %pad_maximum_fusion.8.refs_0_), channel_id=1, source_target_pairs={{0,4},{1,3},{2,6},{3,1},{4,0},{5,7},{6,2},{7,5},{8,12},{9,11},{10,... | collective-permute-start | bytes 1769480 | tf_op jit(solution)/shard_map/ppermute | solution.py:60
  104.8 19.1 %collective-permute-start.38 = (bf16[4,192,384]{2,1,0:T(8,128)(2,1)}, bf16[4,192,384]{2,1,0:T(8,128)(2,1)}, u32[]{:S(2)}, u32[]{:S(2)}) collective-permute-start(bf16[4,192,384]{2,1,0:T(8,128)(2,1)} %pad_maximum_fusion.9.refs_0_), channel_id=1, source_target_pairs={{0,4},{1,3},{2,6},{3,1},{4,0},{5,7},{6,2},{7,5},{8,12},{9,11},{10,... | collective-permute-start | bytes 1769480 | tf_op jit(solution)/shard_map/ppermute | solution.py:60
  105.6 22.4 %collective-permute-start.39 = (bf16[4,192,384]{2,1,0:T(8,128)(2,1)}, bf16[4,192,384]{2,1,0:T(8,128)(2,1)}, u32[]{:S(2)}, u32[]{:S(2)}) collective-permute-start(bf16[4,192,384]{2,1,0:T(8,128)(2,1)} %pad_maximum_fusion.9.refs_0_), channel_id=1, source_target_pairs={{0,2},{1,5},{2,0},{3,7},{4,6},{5,1},{6,4},{7,3},{8,10},{9,13},{10,... | collective-permute-start | bytes 1769480 | tf_op jit(solution)/shard_map/ppermute | solution.py:60
  120.3 19.5 %collective-permute-start.30 = (bf16[4,192,384]{2,1,0:T(8,128)(2,1)}, bf16[4,192,384]{2,1,0:T(8,128)(2,1)S(1)}, u32[]{:S(2)}, u32[]{:S(2)}) collective-permute-start(bf16[4,192,384]{2,1,0:T(8,128)(2,1)} %collective-permute-done.28.refs_1_), channel_id=1, source_target_pairs={{0,2},{1,5},{2,0},{3,7},{4,6},{5,1},{6,4},{7,3},{8,10},{9,13},{10,... | collective-permute-start | bytes 1769480 | tf_op jit(solution)/shard_map/ppermute | solution.py:60
  121.5 21.3 %collective-permute-start.18 = (bf16[4,224,384]{2,1,0:T(8,128)(2,1)S(1)}, bf16[4,224,384]{2,1,0:T(8,128)(2,1)S(1)}, u32[]{:S(2)}, u32[]{:S(2)}) collective-permute-start(bf16[4,224,384]{2,1,0:T(8,128)(2,1)S(1)} %pad_maximum_fusion.6.refs_0_), channel_id=1, source_target_pairs={{0,4},{1,3},{2,6},{3,1},{4,0},{5,7},{6,2},{7,5},{8,12},{9,11},{10,... | collective-permute-start | bytes 2064392 | tf_op jit(solution)/shard_map/ppermute | solution.py:60
  123.9 20.3 %collective-permute-start.32 = (bf16[4,192,384]{2,1,0:T(8,128)(2,1)}, bf16[4,192,384]{2,1,0:T(8,128)(2,1)S(1)}, u32[]{:S(2)}, u32[]{:S(2)}) collective-permute-start(bf16[4,192,384]{2,1,0:T(8,128)(2,1)} %collective-permute-done.28.refs_1_), channel_id=1, source_target_pairs={{0,1},{1,0},{2,3},{3,2},{4,5},{5,4},{6,7},{7,6},{8,9},{9,8},{10,11... | collective-permute-start | bytes 1769480 | tf_op jit(solution)/shard_map/ppermute | solution.py:60
  128.1 18.2 %collective-permute-start.40 = (bf16[4,192,384]{2,1,0:T(8,128)(2,1)}, bf16[4,192,384]{2,1,0:T(8,128)(2,1)}, u32[]{:S(2)}, u32[]{:S(2)}) collective-permute-start(bf16[4,192,384]{2,1,0:T(8,128)(2,1)} %collective-permute-done.38.refs_1_), channel_id=1, source_target_pairs={{0,2},{1,5},{2,0},{3,7},{4,6},{5,1},{6,4},{7,3},{8,10},{9,13},{10,... | collective-permute-start | bytes 1769480 | tf_op jit(solution)/shard_map/ppermute | solution.py:60
  142.8 18.8 %collective-permute-start.19 = (bf16[4,224,384]{2,1,0:T(8,128)(2,1)S(1)}, bf16[4,224,384]{2,1,0:T(8,128)(2,1)}, u32[]{:S(2)}, u32[]{:S(2)}) collective-permute-start(bf16[4,224,384]{2,1,0:T(8,128)(2,1)S(1)} %pad_maximum_fusion.6.refs_0_), channel_id=1, source_target_pairs={{0,2},{1,5},{2,0},{3,7},{4,6},{5,1},{6,4},{7,3},{8,10},{9,13},{10,... | collective-permute-start | bytes 2064392 | tf_op jit(solution)/shard_map/ppermute | solution.py:60
  144.2 17.9 %collective-permute-start.42 = (bf16[4,192,384]{2,1,0:T(8,128)(2,1)}, bf16[4,192,384]{2,1,0:T(8,128)(2,1)}, u32[]{:S(2)}, u32[]{:S(2)}) collective-permute-start(bf16[4,192,384]{2,1,0:T(8,128)(2,1)} %collective-permute-done.38.refs_1_), channel_id=1, source_target_pairs={{0,1},{1,0},{2,3},{3,2},{4,5},{5,4},{6,7},{7,6},{8,9},{9,8},{10,11... | collective-permute-start | bytes 1769480 | tf_op jit(solution)/shard_map/ppermute | solution.py:60
  144.5 17.7 %collective-permute-start.43 = (bf16[4,192,384]{2,1,0:T(8,128)(2,1)}, bf16[4,192,384]{2,1,0:T(8,128)(2,1)}, u32[]{:S(2)}, u32[]{:S(2)}) collective-permute-start(bf16[4,192,384]{2,1,0:T(8,128)(2,1)} %collective-permute-done.39.refs_2_), channel_id=1, source_target_pairs={{0,1},{1,0},{2,3},{3,2},{4,5},{5,4},{6,7},{7,6},{8,9},{9,8},{10,11... | collective-permute-start | bytes 1769480 | tf_op jit(solution)/shard_map/ppermute | solution.py:60
  440.5 43.5 %collective-permute-start.49 = (bf16[4,192,384]{2,1,0:T(8,128)(2,1)}, bf16[4,192,384]{2,1,0:T(8,128)(2,1)}, u32[]{:S(2)}, u32[]{:S(2)}) collective-permute-start(bf16[4,192,384]{2,1,0:T(8,128)(2,1)} %get-tuple-element.87), channel_id=1, source_target_pairs={{0,1},{1,0},{2,3},{3,2},{4,5},{5,4},{6,7},{7,6},{8,9},{9,8},{10,11... | collective-permute-start | bytes 1769480 | tf_op jit(solution)/shard_map/ppermute | solution.py:60
  445.9 39.5 %collective-permute-start.46 = (bf16[4,192,384]{2,1,0:T(8,128)(2,1)}, bf16[4,192,384]{2,1,0:T(8,128)(2,1)S(1)}, u32[]{:S(2)}, u32[]{:S(2)}) collective-permute-start(bf16[4,192,384]{2,1,0:T(8,128)(2,1)} %get-tuple-element.83), channel_id=1, source_target_pairs={{0,1},{1,0},{2,3},{3,2},{4,5},{5,4},{6,7},{7,6},{8,9},{9,8},{10,11... | collective-permute-start | bytes 1769480 | tf_op jit(solution)/shard_map/ppermute | solution.py:60
  446.0 36.8 %collective-permute-start.94 = (f32[104,128]{1,0:T(8,128)S(1)}, f32[104,128]{1,0:T(8,128)S(1)}, u32[]{:S(2)}, u32[]{:S(2)}) collective-permute-start(f32[104,128]{1,0:T(8,128)S(1)} %add.425), channel_id=1, source_target_pairs={{0,24},{1,25},{2,26},{3,27},{4,28},{5,29},{6,30},{7,31},{8,0},{9,1... | collective-permute-start | bytes 159752 | tf_op jit(solution)/shard_map/ppermute | solution.py:60
  448.0 35.4 %collective-permute-start.92 = (f32[104,128]{1,0:T(8,128)S(1)}, f32[104,128]{1,0:T(8,128)S(1)}, u32[]{:S(2)}, u32[]{:S(2)}) collective-permute-start(f32[104,128]{1,0:T(8,128)S(1)} %add.425), channel_id=1, source_target_pairs={{0,8},{1,9},{2,10},{3,11},{4,12},{5,13},{6,14},{7,15},{8,16},{9,17... | collective-permute-start | bytes 159752 | tf_op jit(solution)/shard_map/ppermute | solution.py:60
  448.1 35.4 %collective-permute-start.93 = (f32[104,128]{1,0:T(8,128)S(1)}, f32[104,128]{1,0:T(8,128)S(1)}, u32[]{:S(2)}, u32[]{:S(2)}) collective-permute-start(f32[104,128]{1,0:T(8,128)S(1)} %add.425), channel_id=1, source_target_pairs={{0,16},{1,17},{2,18},{3,19},{4,20},{5,21},{6,22},{7,23},{8,24},{9,... | collective-permute-start | bytes 159752 | tf_op jit(solution)/shard_map/ppermute | solution.py:60
  461.7 157.6 %all-to-all-start.1 = ((bf16[4,2,4,36,1024]{4,2,1,3,0:T(4,128)(2,1)}), bf16[4,2,4,36,1024]{4,2,1,3,0:T(4,128)(2,1)}, u32[]{:S(2)}, u32[]{:S(2)}) async-start(bf16[4,2,4,36,1024]{4,2,1,3,0:T(4,128)(2,1)} %bitcast.278), calls=%async_computation.1 | async-start | bytes 4718592 | tf_op jit(solution)/shard_map/all_to_all | solution.py:646
  491.8 22.0 %collective-permute-start.83 = (bf16[4,192,384]{2,1,0:T(8,128)(2,1)S(1)}, bf16[4,192,384]{2,1,0:T(8,128)(2,1)S(1)}, u32[]{:S(2)}, u32[]{:S(2)}) collective-permute-start(bf16[4,192,384]{2,1,0:T(8,128)(2,1)S(1)} %add_convert_fusion.16), channel_id=1, source_target_pairs={{0,2},{1,5},{2,0},{3,7},{4,6},{5,1},{6,4},{7,3},{8,10},{9,13},{10,... | collective-permute-start | bytes 1769480 | tf_op jit(solution)/shard_map/ppermute | solution.py:60
  494.1 21.6 %collective-permute-start.45 = (bf16[4,192,384]{2,1,0:T(8,128)(2,1)S(1)}, bf16[4,192,384]{2,1,0:T(8,128)(2,1)S(1)}, u32[]{:S(2)}, u32[]{:S(2)}) collective-permute-start(bf16[4,192,384]{2,1,0:T(8,128)(2,1)S(1)} %copy-done.120), channel_id=1, source_target_pairs={{0,1},{1,0},{2,3},{3,2},{4,5},{5,4},{6,7},{7,6},{8,9},{9,8},{10,11... | collective-permute-start | bytes 1769480 | tf_op jit(solution)/shard_map/ppermute | solution.py:60
  494.2 21.6 %collective-permute-start.59 = (bf16[4,224,384]{2,1,0:T(8,128)(2,1)S(1)}, bf16[4,224,384]{2,1,0:T(8,128)(2,1)S(1)}, u32[]{:S(2)}, u32[]{:S(2)}) collective-permute-start(bf16[4,224,384]{2,1,0:T(8,128)(2,1)S(1)} %copy-done.117), channel_id=1, source_target_pairs={{0,1},{1,0},{2,3},{3,2},{4,5},{5,4},{6,7},{7,6},{8,9},{9,8},{10,11... | collective-permute-start | bytes 2064392 | tf_op jit(solution)/shard_map/ppermute | solution.py:60
  501.2 27.0 %collective-permute-start.61 = (bf16[4,224,384]{2,1,0:T(8,128)(2,1)S(1)}, bf16[4,224,384]{2,1,0:T(8,128)(2,1)S(1)}, u32[]{:S(2)}, u32[]{:S(2)}) collective-permute-start(bf16[4,224,384]{2,1,0:T(8,128)(2,1)S(1)} %add_convert_fusion.9), channel_id=1, source_target_pairs={{0,2},{1,5},{2,0},{3,7},{4,6},{5,1},{6,4},{7,3},{8,10},{9,13},{10,... | collective-permute-start | bytes 2064392 | tf_op jit(solution)/shard_map/ppermute | solution.py:60
  507.5 32.7 %collective-permute-start.47 = (bf16[4,192,384]{2,1,0:T(8,128)(2,1)S(1)}, bf16[4,192,384]{2,1,0:T(8,128)(2,1)S(1)}, u32[]{:S(2)}, u32[]{:S(2)}) collective-permute-start(bf16[4,192,384]{2,1,0:T(8,128)(2,1)S(1)} %add_convert_fusion.33), channel_id=1, source_target_pairs={{0,2},{1,5},{2,0},{3,7},{4,6},{5,1},{6,4},{7,3},{8,10},{9,13},{10,... | collective-permute-start | bytes 1769480 | tf_op jit(solution)/shard_map/ppermute | solution.py:60
  513.8 26.3 %collective-permute-start.51 = (bf16[4,192,384]{2,1,0:T(8,128)(2,1)S(1)}, bf16[4,192,384]{2,1,0:T(8,128)(2,1)S(1)}, u32[]{:S(2)}, u32[]{:S(2)}) collective-permute-start(bf16[4,192,384]{2,1,0:T(8,128)(2,1)S(1)} %add_convert_fusion.29), channel_id=1, source_target_pairs={{0,4},{1,3},{2,6},{3,1},{4,0},{5,7},{6,2},{7,5},{8,12},{9,11},{10,... | collective-permute-start | bytes 1769480 | tf_op jit(solution)/shard_map/ppermute | solution.py:60
  515.7 25.3 %collective-permute-start.67 = (bf16[4,192,384]{2,1,0:T(8,128)(2,1)S(1)}, bf16[4,192,384]{2,1,0:T(8,128)(2,1)S(1)}, u32[]{:S(2)}, u32[]{:S(2)}) collective-permute-start(bf16[4,192,384]{2,1,0:T(8,128)(2,1)S(1)} %copy-done.121), channel_id=1, source_target_pairs={{0,1},{1,0},{2,3},{3,2},{4,5},{5,4},{6,7},{7,6},{8,9},{9,8},{10,11... | collective-permute-start | bytes 1769480 | tf_op jit(solution)/shard_map/ppermute | solution.py:60
  515.7 30.7 %collective-permute-start.69 = (bf16[4,192,384]{2,1,0:T(8,128)(2,1)S(1)}, bf16[4,192,384]{2,1,0:T(8,128)(2,1)S(1)}, u32[]{:S(2)}, u32[]{:S(2)}) collective-permute-start(bf16[4,192,384]{2,1,0:T(8,128)(2,1)S(1)} %add_convert_fusion.26), channel_id=1, source_target_pairs={{0,2},{1,5},{2,0},{3,7},{4,6},{5,1},{6,4},{7,3},{8,10},{9,13},{10,... | collective-permute-start | bytes 1769480 | tf_op jit(solution)/shard_map/ppermute | solution.py:60
  528.2 18.7 %collective-permute-start.73 = (bf16[4,192,384]{2,1,0:T(8,128)(2,1)S(1)}, bf16[4,192,384]{2,1,0:T(8,128)(2,1)S(1)}, u32[]{:S(2)}, u32[]{:S(2)}) collective-permute-start(bf16[4,192,384]{2,1,0:T(8,128)(2,1)S(1)} %add_convert_fusion.22), channel_id=1, source_target_pairs={{0,4},{1,3},{2,6},{3,1},{4,0},{5,7},{6,2},{7,5},{8,12},{9,11},{10,... | collective-permute-start | bytes 1769480 | tf_op jit(solution)/shard_map/ppermute | solution.py:60
  540.2 24.8 %collective-permute-start.56 = (bf16[4,224,384]{2,1,0:T(8,128)(2,1)S(1)}, bf16[4,224,384]{2,1,0:T(8,128)(2,1)S(1)}, u32[]{:S(2)}, u32[]{:S(2)}) collective-permute-start(bf16[4,224,384]{2,1,0:T(8,128)(2,1)S(1)} %copy-done.116), channel_id=1, source_target_pairs={{0,1},{1,0},{2,3},{3,2},{4,5},{5,4},{6,7},{7,6},{8,9},{9,8},{10,11... | collective-permute-start | bytes 2064392 | tf_op jit(solution)/shard_map/ppermute | solution.py:60
  546.5 26.1 %collective-permute-start.58 = (bf16[4,224,384]{2,1,0:T(8,128)(2,1)S(1)}, bf16[4,224,384]{2,1,0:T(8,128)(2,1)S(1)}, u32[]{:S(2)}, u32[]{:S(2)}) collective-permute-start(bf16[4,224,384]{2,1,0:T(8,128)(2,1)S(1)} %add_convert_fusion.12), channel_id=1, source_target_pairs={{0,2},{1,5},{2,0},{3,7},{4,6},{5,1},{6,4},{7,3},{8,10},{9,13},{10,... | collective-permute-start | bytes 2064392 | tf_op jit(solution)/shard_map/ppermute | solution.py:60
  549.2 24.9 %collective-permute-start.62 = (bf16[4,224,384]{2,1,0:T(8,128)(2,1)S(1)}, bf16[4,224,384]{2,1,0:T(8,128)(2,1)S(1)}, u32[]{:S(2)}, u32[]{:S(2)}) collective-permute-start(bf16[4,224,384]{2,1,0:T(8,128)(2,1)S(1)} %add_convert_fusion.8), channel_id=1, source_target_pairs={{0,4},{1,3},{2,6},{3,1},{4,0},{5,7},{6,2},{7,5},{8,12},{9,11},{10,... | collective-permute-start | bytes 2064392 | tf_op jit(solution)/shard_map/ppermute | solution.py:60
  557.8 18.7 %collective-permute-start.52 = (bf16[192,384]{1,0:T(8,128)(2,1)S(1)}, bf16[192,384]{1,0:T(8,128)(2,1)S(1)}, u32[]{:S(2)}, u32[]{:S(2)}) collective-permute-start(bf16[192,384]{1,0:T(8,128)(2,1)S(1)} %get-tuple-element.234), channel_id=1, source_target_pairs={{0,24},{1,25},{2,26},{3,27},{4,28},{5,29},{6,30},{7,31},{8,0},{9,1... | collective-permute-start | bytes 442376 | tf_op jit(solution)/shard_map/ppermute | solution.py:60
  574.1 22.5 %collective-permute-start.75 = (bf16[192,384]{1,0:T(8,128)(2,1)S(1)}, bf16[192,384]{1,0:T(8,128)(2,1)S(1)}, u32[]{:S(2)}, u32[]{:S(2)}) collective-permute-start(bf16[192,384]{1,0:T(8,128)(2,1)S(1)} %get-tuple-element.229), channel_id=1, source_target_pairs={{0,16},{1,17},{2,18},{3,19},{4,20},{5,21},{6,22},{7,23},{8,24},{9,... | collective-permute-start | bytes 442376 | tf_op jit(solution)/shard_map/ppermute | solution.py:60
  576.5 20.1 %collective-permute-start.76 = (bf16[192,384]{1,0:T(8,128)(2,1)S(1)}, bf16[192,384]{1,0:T(8,128)(2,1)S(1)}, u32[]{:S(2)}, u32[]{:S(2)}) collective-permute-start(bf16[192,384]{1,0:T(8,128)(2,1)S(1)} %get-tuple-element.228), channel_id=1, source_target_pairs={{0,8},{1,9},{2,10},{3,11},{4,12},{5,13},{6,14},{7,15},{8,16},{9,17... | collective-permute-start | bytes 442376 | tf_op jit(solution)/shard_map/ppermute | solution.py:60
  576.6 21.0 %collective-permute-start.85 = (bf16[192,384]{1,0:T(8,128)(2,1)S(1)}, bf16[192,384]{1,0:T(8,128)(2,1)S(1)}, u32[]{:S(2)}, u32[]{:S(2)}) collective-permute-start(bf16[192,384]{1,0:T(8,128)(2,1)S(1)} %get-tuple-element.226), channel_id=1, source_target_pairs={{0,24},{1,25},{2,26},{3,27},{4,28},{5,29},{6,30},{7,31},{8,0},{9,1... | collective-permute-start | bytes 442376 | tf_op jit(solution)/shard_map/ppermute | solution.py:60
  581.1 32.0 %collective-permute-start.86 = (bf16[192,384]{1,0:T(8,128)(2,1)S(1)}, bf16[192,384]{1,0:T(8,128)(2,1)}, u32[]{:S(2)}, u32[]{:S(2)}) collective-permute-start(bf16[192,384]{1,0:T(8,128)(2,1)S(1)} %get-tuple-element.225), channel_id=1, source_target_pairs={{0,16},{1,17},{2,18},{3,19},{4,20},{5,21},{6,22},{7,23},{8,24},{9,... | collective-permute-start | bytes 442376 | tf_op jit(solution)/shard_map/ppermute | solution.py:60
  581.1 32.0 %collective-permute-start.87 = (bf16[192,384]{1,0:T(8,128)(2,1)S(1)}, bf16[192,384]{1,0:T(8,128)(2,1)}, u32[]{:S(2)}, u32[]{:S(2)}) collective-permute-start(bf16[192,384]{1,0:T(8,128)(2,1)S(1)} %get-tuple-element.224), channel_id=1, source_target_pairs={{0,8},{1,9},{2,10},{3,11},{4,12},{5,13},{6,14},{7,15},{8,16},{9,17... | collective-permute-start | bytes 442376 | tf_op jit(solution)/shard_map/ppermute | solution.py:60
  596.6 19.1 %collective-permute-start.63 = (bf16[224,384]{1,0:T(8,128)(2,1)S(1)}, bf16[224,384]{1,0:T(8,128)(2,1)S(1)}, u32[]{:S(2)}, u32[]{:S(2)}) collective-permute-start(bf16[224,384]{1,0:T(8,128)(2,1)S(1)} %get-tuple-element.222), channel_id=1, source_target_pairs={{0,24},{1,25},{2,26},{3,27},{4,28},{5,29},{6,30},{7,31},{8,0},{9,1... | collective-permute-start | bytes 516104 | tf_op jit(solution)/shard_map/ppermute | solution.py:60
  596.6 19.3 %collective-permute-start.64 = (bf16[224,384]{1,0:T(8,128)(2,1)S(1)}, bf16[224,384]{1,0:T(8,128)(2,1)S(1)}, u32[]{:S(2)}, u32[]{:S(2)}) collective-permute-start(bf16[224,384]{1,0:T(8,128)(2,1)S(1)} %get-tuple-element.221), channel_id=1, source_target_pairs={{0,16},{1,17},{2,18},{3,19},{4,20},{5,21},{6,22},{7,23},{8,24},{9,... | collective-permute-start | bytes 516104 | tf_op jit(solution)/shard_map/ppermute | solution.py:60
  597.5 18.4 %collective-permute-start.65 = (bf16[224,384]{1,0:T(8,128)(2,1)S(1)}, bf16[224,384]{1,0:T(8,128)(2,1)S(1)}, u32[]{:S(2)}, u32[]{:S(2)}) collective-permute-start(bf16[224,384]{1,0:T(8,128)(2,1)S(1)} %get-tuple-element.220), channel_id=1, source_target_pairs={{0,8},{1,9},{2,10},{3,11},{4,12},{5,13},{6,14},{7,15},{8,16},{9,17... | collective-permute-start | bytes 516104 | tf_op jit(solution)/shard_map/ppermute | solution.py:60
  613.2 21.9 %collective-permute-start.55 = (f32[192,192]{1,0:T(8,128)}, f32[192,192]{1,0:T(8,128)S(1)}, u32[]{:S(2)}, u32[]{:S(2)}) collective-permute-start(f32[192,192]{1,0:T(8,128)} %get-tuple-element.89), channel_id=1, source_target_pairs={{0,1},{1,0},{2,3},{3,2},{4,5},{5,4},{6,7},{7,6},{8,9},{9,8},{10,11... | collective-permute-start | bytes 442376 | tf_op jit(solution)/shard_map/ppermute | solution.py:60
  613.2 24.4 %collective-permute-start.77 = (f32[192,192]{1,0:T(8,128)}, f32[192,192]{1,0:T(8,128)S(1)}, u32[]{:S(2)}, u32[]{:S(2)}) collective-permute-start(f32[192,192]{1,0:T(8,128)} %get-tuple-element.114), channel_id=1, source_target_pairs={{0,1},{1,0},{2,3},{3,2},{4,5},{5,4},{6,7},{7,6},{8,9},{9,8},{10,11... | collective-permute-start | bytes 442376 | tf_op jit(solution)/shard_map/ppermute | solution.py:60
  619.0 21.1 %collective-permute-start.66 = (f32[224,192]{1,0:T(8,128)}, f32[224,192]{1,0:T(8,128)S(1)}, u32[]{:S(2)}, u32[]{:S(2)}) collective-permute-start(f32[224,192]{1,0:T(8,128)} %get-tuple-element.101), channel_id=1, source_target_pairs={{0,1},{1,0},{2,3},{3,2},{4,5},{5,4},{6,7},{7,6},{8,9},{9,8},{10,11... | collective-permute-start | bytes 516104 | tf_op jit(solution)/shard_map/ppermute | solution.py:60
  (187 other events, 2495.1 us)

commit v2 on v1

v2 whole, which is shorter than its diff:
```python
import functools

import jax
import jax.numpy as jnp
from jax import lax
from jax.experimental import pallas as pl
from jax.experimental.pallas import tpu as pltpu
from jax.sharding import PartitionSpec as P

HEAD = 64
EPS = 1e-06
NEG = -1e30
BF16 = jnp.bfloat16
F32 = jnp.float32
AXES = ("dp", "patch")
VMEM_SPEC = pl.BlockSpec(memory_space=pltpu.VMEM)
SMEM_SPEC = pl.BlockSpec(memory_space=pltpu.SMEM)
PARAMS = pltpu.CompilerParams(vmem_limit_bytes=62 * 2**20)

QKV, OUT, CQ, CKV, COUT, FIN, FOUT = range(7)
GATHER = ((QKV, OUT), (CQ, CKV, COUT), (FIN,), (FOUT,))
REDUCE = ((QKV,), (CQ, CKV, COUT, OUT), (FIN,), (FOUT,))


class Plan:
    def __init__(self, dp, patch, shards):
        self.dp, self.patch = dp, patch
        self.zs = dp // 2
        self.devices = dp * patch
        self.chunk = shards[OUT][1] * 2
        self.half = [s[0] // 2 for s in shards]
        self.cols = [s[1] for s in shards]
        self.chunks = [s[1] * 2 // self.chunk for s in shards]
        self.full = [(s[0] * dp, s[1] * patch) for s in shards]
        self.fast = (
            dp % 2 == 0
            and patch == 4
            and all(h % 16 == 0 for h in self.half)
            and all(s[1] * 2 % self.chunk == 0 for s in shards)
            and self.chunk % 128 == 0
        )

    def rows(self, group):
        return sum(self.half[w] * self.chunks[w] for w in group)

    def flip(self, pick):
        return [(i, i ^ pick(i)) for i in range(self.devices)]

    def core(self):
        return self.flip(lambda i: 1)

    def first(self):
        return self.flip(lambda i: 4 if i % 2 == 0 else 2)

    def second(self):
        return self.flip(lambda i: 2 if i % 2 == 0 else 4)

    def z_up(self, k):
        return [(i, (i + 8 * k) % self.devices) for i in range(self.devices)]


def send(value, perm):
    return lax.ppermute(value, AXES, perm)


def coords():
    dp, patch = lax.axis_index("dp"), lax.axis_index("patch")
    return jnp.stack([dp // 2, dp % 2, patch // 2, patch % 2]).astype(jnp.int32)


def piece_rows(group, plan):
    at, found = 0, []
    for w in group:
        for j in range(plan.chunks[w]):
            found.append((w, j, at))
            at += plan.half[w]
    return found


def group_starts(plan):
    starts, at = [], 0
    for group in GATHER:
        starts.append(at)
        at += plan.rows(group)
    return starts, at


def pack_split(plan, where, shards):
    _, total = group_starts(plan)
    wide = plan.chunk // 2

    def body(where_ref, *refs):
        shard_refs, (own_ref, send_ref) = refs[:7], refs[7:]
        core = where_ref[3]
        at = 0
        for group in GATHER:
            for w in group:
                high = plan.half[w]
                for b in range(plan.chunks[w]):
                    cut = slice(b * wide, (b + 1) * wide)
                    own_ref[at : at + high, :] = shard_refs[w][pl.ds(core * high, high), cut]
                    send_ref[at : at + high, :] = shard_refs[w][
                        pl.ds((1 - core) * high, high), cut
                    ]
                    at += high

    shape = jax.ShapeDtypeStruct((total, wide), BF16)
    return pl.pallas_call(
        body,
        out_shape=(shape, shape),
        in_specs=[SMEM_SPEC] + [VMEM_SPEC] * 7,
        out_specs=(VMEM_SPEC, VMEM_SPEC),
        compiler_params=PARAMS,
        name="pack_split",
    )(where, *shards)


def pack_join(plan, where, own, got):
    starts, total = group_starts(plan)
    wide = plan.chunk // 2

    def body(where_ref, own_ref, got_ref, *unit_refs):
        core = where_ref[3]

        def fill(low_ref, high_ref):
            for g, group in enumerate(GATHER):
                at = starts[g]
                for w in group:
                    high, count = plan.half[w], plan.chunks[w]
                    for j in range(count):
                        pair = []
                        for b in (2 * j, 2 * j + 1):
                            src = low_ref if b < count else high_ref
                            row = at + (b % count) * high
                            pair.append(src[row : row + high, :])
                        to = at - starts[g] + j * high
                        unit_refs[g][to : to + high, :] = jnp.concatenate(pair, axis=1)
                    at += count * high

        @pl.when(core == 0)
        def _():
            fill(own_ref, got_ref)

        @pl.when(core == 1)
        def _():
            fill(got_ref, own_ref)

    return pl.pallas_call(
        body,
        out_shape=tuple(jax.ShapeDtypeStruct((plan.rows(g), plan.chunk), BF16) for g in GATHER),
        in_specs=[SMEM_SPEC, VMEM_SPEC, VMEM_SPEC],
        out_specs=(VMEM_SPEC,) * len(GATHER),
        compiler_params=PARAMS,
        name="pack_join",
    )(where, own, got)


class Gathering:
    def __init__(self, plan, unit):
        self.plan, self.held, self.step = plan, [unit], 0

    def advance(self):
        plan, held = self.plan, self.held
        if self.step == 0:
            held = held + [send(held[0], plan.z_up(k)) for k in range(1, plan.zs)]
        elif self.step == 1:
            stack = jnp.stack(held)
            held = [stack, send(stack, plan.first()), send(stack, plan.second())]
            held.append(send(stack, plan.core()))
        elif self.step == 2:
            stack, near, side, stack_core = held
            far = send(near, plan.second())
            held = [stack, near, side, far, stack_core]
            held += [send(part, plan.core()) for part in (near, side, far)]
        self.held, self.step = held, self.step + 1


def each_place(plan, group, where_ref, visit):
    z, x, y, core = (where_ref[i] for i in range(4))
    for other in range(2):
        half = core ^ other
        for second in range(2):
            for first in range(2):
                x_at = x ^ jnp.where(half == 0, first, second)
                y_at = y ^ jnp.where(half == 0, second, first)
                for k in range(plan.zs):
                    z_at = lax.rem(z + plan.zs - k, plan.zs)
                    place = (z_at * 2 + x_at) * 2 + half
                    for w, j, row in piece_rows(group, plan):
                        high = plan.half[w]
                        to_row = pl.multiple_of(place * high, 16)
                        stack = other * 4 + second * 2 + first
                        visit(stack, k, row, w, j, to_row, y_at, high)


def assemble(plan, group, where, stacks):

    def body(where_ref, *refs):
        stack_refs, full_refs = refs[:8], dict(zip(group, refs[8:]))

        def visit(stack, k, row, w, j, to_row, to_y, high):
            to_col = pl.multiple_of(to_y * (plan.full[w][1] // 2) + j * plan.chunk, 128)
            full_refs[w][pl.ds(to_row, high), pl.ds(to_col, plan.chunk)] = stack_refs[stack][
                k, row : row + high, :
            ]

        each_place(plan, group, where_ref, visit)

    return pl.pallas_call(
        body,
        out_shape=tuple(jax.ShapeDtypeStruct(plan.full[w], BF16) for w in group),
        in_specs=[SMEM_SPEC] + [VMEM_SPEC] * 8,
        out_specs=(VMEM_SPEC,) * len(group),
        compiler_params=PARAMS,
        name="assemble",
    )(where, *stacks)


def add_low(one, two):
    return (one.astype(F32) + two.astype(F32)).astype(BF16)


class Reducing:
    def __init__(self, plan, group, where, stacks):
        self.plan, self.group, self.where = plan, group, where
        self.held, self.step = list(stacks), 0

    def advance(self):
        plan, held = self.plan, self.held
        if self.step == 0:
            held = held[:4] + [send(part, plan.core()) for part in held[4:]]
        elif self.step == 1:
            mine = [add_low(a, b) for a, b in zip(held[:4], held[4:])]
            held = mine[:2] + [send(part, plan.second()) for part in mine[2:]]
        elif self.step == 2:
            mine = [add_low(held[0], held[2]), add_low(held[1], held[3])]
            held = [mine[0], send(mine[1], plan.first())]
        elif self.step == 3:
            total = add_low(*held)
            parts = [send(total[k], plan.z_up(plan.zs - k)) for k in range(1, plan.zs)]
            held = [total[0]] + parts
        elif self.step == 4:
            own, give = unpack_split(plan, self.group, self.where, held)
            held = [own, send(give, plan.core())]
        elif self.step == 5:
            held = unpack_join(plan, self.group, self.where, *held)
        self.held, self.step = list(held), self.step + 1


def fence(chains, values):
    flat, tree = jax.tree.flatten([values, [chain.held for chain in chains]])
    values, held = jax.tree.unflatten(tree, lax.optimization_barrier(flat))
    for chain, arrays in zip(chains, held):
        chain.held = arrays
    return values


def unpack_split(plan, group, where, parts):
    rows, wide = plan.rows(group), plan.chunk // 2

    def body(where_ref, *refs):
        part_refs, (own_ref, give_ref) = refs[:-2], refs[-2:]
        core = where_ref[3]

        def fill(low_ref, high_ref):
            at = 0
            for w in group:
                high, count = plan.half[w], plan.chunks[w]
                for j in range(count):
                    row = at + j * high
                    value = sum(p[row : row + high, :].astype(F32) for p in part_refs)
                    for b in (2 * j, 2 * j + 1):
                        dst = low_ref if b < count else high_ref
                        to = at + (b % count) * high
                        cut = (b - 2 * j) * wide
                        dst[to : to + high, :] = value[:, cut : cut + wide]
                at += count * high

        @pl.when(core == 0)
        def _():
            fill(own_ref, give_ref)

        @pl.when(core == 1)
        def _():
            fill(give_ref, own_ref)

    shape = jax.ShapeDtypeStruct((rows, wide), F32)
    return pl.pallas_call(
        body,
        out_shape=(shape, shape),
        in_specs=[SMEM_SPEC] + [VMEM_SPEC] * len(parts),
        out_specs=(VMEM_SPEC, VMEM_SPEC),
        compiler_params=PARAMS,
        name="unpack_split",
    )(where, *parts)


def unpack_join(plan, group, where, own, got):
    wide = plan.chunk // 2

    def body(where_ref, own_ref, got_ref, *out_refs):
        core = where_ref[3]
        at = 0
        for w, out_ref in zip(group, out_refs):
            high, count = plan.half[w], plan.chunks[w]
            own_rows = pl.ds(pl.multiple_of(core * high, 16), high)
            got_rows = pl.ds(pl.multiple_of((1 - core) * high, 16), high)
            for b in range(count):
                row, cut = at + b * high, slice(b * wide, (b + 1) * wide)
                out_ref[own_rows, cut] = own_ref[row : row + high, :]
                out_ref[got_rows, cut] = got_ref[row : row + high, :]
            at += count * high

    return pl.pallas_call(
        body,
        out_shape=tuple(
            jax.ShapeDtypeStruct((2 * plan.half[w], plan.cols[w]), F32) for w in group
        ),
        in_specs=[SMEM_SPEC, VMEM_SPEC, VMEM_SPEC],
        out_specs=(VMEM_SPEC,) * len(group),
        compiler_params=PARAMS,
        name="unpack_join",
    )(where, own, got)


def gather_small(plan, where, vectors, bias):
    count, part = vectors.shape
    flat = jnp.concatenate([vectors.reshape(-1), bias])
    size = flat.shape[0]
    flat = jnp.pad(flat, (0, -size % 2048)).reshape(-1, 128)
    pair = jnp.stack([flat, send(flat, plan.flip(lambda i: 4))])
    every = jnp.stack([pair] + [send(pair, plan.z_up(k)) for k in range(1, plan.zs)])
    every = every.reshape((plan.dp,) + flat.shape)
    at = jnp.arange(plan.dp, dtype=jnp.int32)
    slot = lax.rem(where[0] - at // 2 + plan.zs, plan.zs) * 2 + ((at % 2) ^ where[1])
    every = jnp.take(every, slot, axis=0).reshape(plan.dp, -1)[:, :size].astype(F32)
    rows = every[:, : count * part].reshape(plan.dp, count, part)
    rows = rows.transpose(1, 0, 2).reshape(count, plan.dp * part)
    return rows, every[:, count * part :].reshape(-1)


def reduce_small(plan, where, rows, bias):
    count, width = rows.shape
    flat = jnp.concatenate([rows.reshape(-1), bias]).astype(F32)
    size = flat.shape[0]
    flat = jnp.pad(flat, (0, -size % 1024)).reshape(-1, 128)
    for bit in (1, 2, 4):
        flat = flat + send(flat, plan.flip(lambda i: bit))
    flat = flat + sum(send(flat, plan.z_up(k)) for k in range(1, plan.zs))
    flat = flat.reshape(-1)
    dp = where[0] * 2 + where[1]
    whole = flat[: count * width].reshape(count, width)
    own = lax.dynamic_slice_in_dim(whole, dp * (width // plan.dp), width // plan.dp, axis=1)
    tail = flat[count * width : size]
    step = bias.shape[0] // plan.dp
    return own, lax.dynamic_slice_in_dim(tail, dp * step, step, axis=0)


def fetch_plain(weights, vectors, bias):
    whole = [
        lax.all_gather(lax.all_gather(w, "dp", axis=0, tiled=True), "patch", axis=1, tiled=True)
        for w in weights
    ]
    rows = lax.all_gather(vectors, "dp", axis=1, tiled=True)
    return whole, rows.astype(F32), lax.all_gather(bias, "dp", axis=0, tiled=True).astype(F32)


def reduce_plain(grad):
    part = lax.psum_scatter(grad, "dp", scatter_dimension=0, tiled=True)
    return lax.psum_scatter(part, "patch", scatter_dimension=1, tiled=True).astype(F32)


def reduce_small_plain(rows, bias):
    rows = lax.psum_scatter(rows, "dp", scatter_dimension=1, tiled=True)
    bias = lax.psum_scatter(bias, "dp", scatter_dimension=0, tiled=True)
    return lax.psum(rows, "patch"), lax.psum(bias, "patch")


def dot(a, b):
    return lax.dot_general(a, b, (((1,), (0,)), ((), ())), preferred_element_type=F32)


def dot_t(a, b):
    return lax.dot_general(a, b, (((1,), (1,)), ((), ())), preferred_element_type=F32)


def dot_l(a, b):
    return lax.dot_general(a, b, (((0,), (0,)), ((), ())), preferred_element_type=F32)


def norm_parts(total):
    center = total - jnp.mean(total, -1, keepdims=True)
    spread = lax.rsqrt(jnp.mean(center * center, -1, keepdims=True) + EPS)
    return center * spread, spread


def norm_pull(grad, hat, spread, gain):
    scaled = grad * gain
    return spread * (
        scaled
        - jnp.mean(scaled, -1, keepdims=True)
        - hat * jnp.mean(scaled * hat, -1, keepdims=True)
    )


def error_function(x):
    x = jnp.clip(x, -4.0, 4.0)
    s = x * x
    top = jnp.full_like(s, -2.72614225801306e-10)
    for c in (
        2.77068142495902e-08,
        -2.10102402082508e-06,
        -5.69250639462346e-05,
        -7.34990630326855e-04,
        -2.95459980854025e-03,
        -1.60960333262415e-02,
    ):
        top = top * s + c
    low = jnp.full_like(s, -1.45660718464996e-05)
    for c in (
        -2.13374055278905e-04,
        -1.68282697438203e-03,
        -7.37332916720468e-03,
        -1.42647390514189e-02,
    ):
        low = low * s + c
    return x * top / low


def col_sum(value):
    return jnp.sum(value.astype(F32), 0, keepdims=True)


def soft(scores):
    grown = jnp.exp(scores - jnp.max(scores, -1, keepdims=True))
    return grown * (1.0 / jnp.sum(grown, -1, keepdims=True))


def soft_pull(probs, grad):
    return probs * (grad - jnp.sum(probs * grad, -1, keepdims=True))


def lane_masks():
    lane = lax.broadcasted_iota(jnp.int32, (1, 2 * HEAD), 1)
    low = (lane < HEAD).astype(F32)
    return low.astype(BF16), (1.0 - low).astype(BF16), lane < HEAD


def whole(shape):
    return pl.BlockSpec(
        shape, lambda i: (0,) * len(shape), pipeline_mode=pl.Buffered(1)
    )


def summed(shape):
    return pl.BlockSpec(shape, lambda i: (0,) * len(shape))


def tiled(shape):
    return pl.BlockSpec(shape, lambda i: (i,) + (0,) * (len(shape) - 1))


def spec_of(shape, dtype):
    return jax.ShapeDtypeStruct(shape, dtype)


def call(body, name, steps, ins, outs, flops, scratch=()):
    out_shape = tuple(shape for shape, _ in outs)
    moved = sum(a.size * a.dtype.itemsize for a, _ in ins)
    moved += sum(o.size * jnp.dtype(o.dtype).itemsize for o in out_shape)
    return pl.pallas_call(
        body,
        grid=(steps,),
        out_shape=out_shape,
        in_specs=[spec for _, spec in ins],
        out_specs=tuple(spec for _, spec in outs),
        scratch_shapes=list(scratch),
        compiler_params=PARAMS,
        cost_estimate=pl.CostEstimate(
            flops=int(flops), bytes_accessed=int(moved), transcendentals=0
        ),
        name=name,
    )(*[a for a, _ in ins])


def self_forward(dims, text, w_qkv, w_out, rows, lengths):
    d, items, length, group = dims.d, dims.items, dims.length, dims.group
    pairs, tokens, block = d // (2 * HEAD), items * length, group * length
    scale = HEAD ** (-0.5)

    def body(len_ref, x_ref, wqkv_ref, wout_ref, row_ref, qkv_ref, prob_ref, ctx_ref, tot_ref):
        step = pl.program_id(0)
        low, high, _ = lane_masks()
        x = x_ref[...]
        for part, bias in ((0, 0), (1, None), (2, 1)):
            cut = slice(part * d, (part + 1) * d)
            value = dot(x, wqkv_ref[:, cut])
            if bias is not None:
                value = value + row_ref[bias : bias + 1, :]
            qkv_ref[:, cut] = value.astype(BF16)
        place = lax.broadcasted_iota(jnp.int32, (1, length), 1)
        for i in range(group):
            ok = place < len_ref[step * group + i]
            r = slice(i * length, (i + 1) * length)
            for p in range(pairs):
                q, k, v = (
                    qkv_ref[r, part * d + p * 128 : part * d + (p + 1) * 128] for part in range(3)
                )
                scores = dot_t(q, jnp.concatenate([k * low, k * high], 0)) * scale
                probs = jnp.concatenate(
                    [
                        soft(jnp.where(ok, scores[:, h * length : (h + 1) * length], NEG))
                        for h in range(2)
                    ],
                    1,
                ).astype(BF16)
                prob_ref[i, p] = probs
                ctx = dot(probs, jnp.concatenate([v * low, v * high], 0))
                ctx_ref[r, p * 128 : (p + 1) * 128] = ctx.astype(BF16)
        tot_ref[...] = x.astype(F32) + dot(ctx_ref[...], wout_ref[...]) + row_ref[2:3, :]

    return call(
        body,
        "self_forward",
        items // group,
        [
            (lengths, SMEM_SPEC),
            (text, tiled((block, d))),
            (w_qkv, whole((d, 3 * d))),
            (w_out, whole((d, d))),
            (rows, whole(rows.shape)),
        ],
        [
            (spec_of((tokens, 3 * d), BF16), tiled((block, 3 * d))),
            (spec_of((items, pairs, length, 2 * length), BF16), tiled((group, pairs, length, 2 * length))),
            (spec_of((tokens, d), BF16), tiled((block, d))),
            (spec_of((tokens, d), F32), tiled((block, d))),
        ],
        2 * tokens * d * 6 * d,
    )


def cross_forward(dims, total_one, patches, mask, w_cq, w_ckv, w_cout, rows):
    d, items, length, group = dims.d, dims.items, dims.length, dims.group
    pairs, tokens, block = d // (2 * HEAD), items * length, group * length
    count, vis = patches.shape[1], patches.shape[2]
    scale = HEAD ** (-0.5)

    def body(tot_ref, patch_ref, mask_ref, wcq_ref, wckv_ref, wcout_ref, row_ref,
             h_ref, cq_ref, kv_ref, prob_ref, ctx_ref, two_ref):
        low, high, _ = lane_masks()
        hat, _ = norm_parts(tot_ref[...])
        hidden = hat * row_ref[3:4, :] + row_ref[4:5, :]
        h_ref[...] = hidden.astype(BF16)
        cq_ref[...] = (dot(h_ref[...], wcq_ref[...]) + row_ref[5:6, :]).astype(BF16)
        patch = patch_ref[...].reshape(group * count, vis)
        keys = dot(patch, wckv_ref[:, :d]).astype(BF16)
        kv_ref[:, :, :d] = keys.reshape(group, count, d)
        values = (dot(patch, wckv_ref[:, d:]) + row_ref[6:7, :]).astype(BF16)
        kv_ref[:, :, d:] = values.reshape(group, count, d)
        for i in range(group):
            ok = mask_ref[i].astype(F32) > 0.5
            r = slice(i * length, (i + 1) * length)
            for p in range(pairs):
                c = slice(p * 128, (p + 1) * 128)
                q, k, v = cq_ref[r, c], kv_ref[i, :, c], kv_ref[i, :, d + p * 128 : d + (p + 1) * 128]
                ctx = 0.0
                for h, side in enumerate((low, high)):
                    scores = dot_t(q, k * side) * scale
                    probs = soft(jnp.where(ok, scores, NEG)).astype(BF16)
                    prob_ref[i, 2 * p + h] = probs
                    ctx = ctx + dot(probs, v * side)
                ctx_ref[r, c] = ctx.astype(BF16)
        two_ref[...] = hidden + dot(ctx_ref[...], wcout_ref[...]) + row_ref[7:8, :]

    return call(
        body,
        "cross_forward",
        items // group,
        [
            (total_one, tiled((block, d))),
            (patches, tiled((group, count, vis))),
            (mask, tiled((group, length, count))),
            (w_cq, whole((d, d))),
            (w_ckv, whole((vis, 2 * d))),
            (w_cout, whole((d, d))),
            (rows, whole(rows.shape)),
        ],
        [
            (spec_of((tokens, d), BF16), tiled((block, d))),
            (spec_of((tokens, d), BF16), tiled((block, d))),
            (spec_of((items, count, 2 * d), BF16), tiled((group, count, 2 * d))),
            (spec_of((items, 2 * pairs, length, count), BF16), tiled((group, 2 * pairs, length, count))),
            (spec_of((tokens, d), BF16), tiled((block, d))),
            (spec_of((tokens, d), F32), tiled((block, d))),
        ],
        2 * tokens * d * 4 * d + 2 * items * count * vis * 2 * d,
    )


def ffn_forward(dims, total_two, cotangent, w_fin, w_fout, rows, bias):
    d, items, length, group = dims.d, dims.items, dims.length, dims.group
    tokens, block, ff = items * length, group * length, w_fin.shape[1]
    piece = d

    def body(tot_ref, cot_ref, win_ref, wout_ref, row_ref, bias_ref,
             out_ref, h_ref, act_ref, slope_ref, g_ref, glow_ref, sum_ref):
        @pl.when(pl.program_id(0) == 0)
        def _():
            sum_ref[...] = jnp.zeros_like(sum_ref)

        hat, _ = norm_parts(tot_ref[...])
        hidden = hat * row_ref[8:9, :] + row_ref[9:10, :]
        h_ref[...] = hidden.astype(BF16)
        total = hidden + row_ref[10:11, :]
        for at in range(0, ff, piece):
            cut = slice(at, at + piece)
            pre = dot(h_ref[...], win_ref[:, cut]) + bias_ref[:, cut]
            half = 0.5 + 0.5 * error_function(pre * 0.5**0.5)
            act = (pre * half).astype(BF16)
            act_ref[:, cut] = act
            bell = jnp.exp(-0.5 * pre * pre) * 0.3989422804014327
            slope_ref[:, cut] = (half + pre * bell).astype(BF16)
            total = total + dot(act, wout_ref[cut, :])
        hat, spread = norm_parts(total)
        gain = row_ref[11:12, :]
        out_ref[...] = hat * gain + row_ref[12:13, :]
        cot = cot_ref[...].astype(F32)
        grad = norm_pull(cot, hat, spread, gain)
        g_ref[...] = grad
        low = grad.astype(BF16)
        glow_ref[...] = low
        sum_ref[0:1, :] += col_sum(cot * hat)
        sum_ref[1:2, :] += col_sum(cot)
        sum_ref[2:3, :] += col_sum(low)

    return call(
        body,
        "ffn_forward",
        items // group,
        [
            (total_two, tiled((block, d))),
            (cotangent, tiled((block, d))),
            (w_fin, whole((d, ff))),
            (w_fout, whole((ff, d))),
            (rows, whole(rows.shape)),
            (bias, whole(bias.shape)),
        ],
        [
            (spec_of((tokens, d), F32), tiled((block, d))),
            (spec_of((tokens, d), BF16), tiled((block, d))),
            (spec_of((tokens, ff), BF16), tiled((block, ff))),
            (spec_of((tokens, ff), BF16), tiled((block, ff))),
            (spec_of((tokens, d), F32), tiled((block, d))),
            (spec_of((tokens, d), BF16), tiled((block, d))),
            (spec_of((8, d), F32), summed((8, d))),
        ],
        4 * tokens * d * ff,
    )


def ffn_backward(dims, grad_three, grad_low, slope, total_two, w_fin, w_fout, rows):
    d, items, length, group = dims.d, dims.items, dims.length, dims.group
    tokens, block, ff = items * length, group * length, w_fin.shape[1]
    piece = d

    def body(g_ref, glow_ref, slope_ref, tot_ref, win_ref, wout_ref, row_ref,
             pre_ref, two_ref, twolow_ref, sum_ref, bias_ref):
        @pl.when(pl.program_id(0) == 0)
        def _():
            sum_ref[...] = jnp.zeros_like(sum_ref)
            bias_ref[...] = jnp.zeros_like(bias_ref)

        grad = g_ref[...]
        for at in range(0, ff, piece):
            cut = slice(at, at + piece)
            pre = dot_t(glow_ref[...], wout_ref[cut, :]) * slope_ref[:, cut].astype(F32)
            pre = pre.astype(BF16)
            pre_ref[:, cut] = pre
            bias_ref[0:1, cut] += col_sum(pre)
            grad = grad + dot_t(pre, win_ref[:, cut])
        hat, spread = norm_parts(tot_ref[...])
        two = norm_pull(grad, hat, spread, row_ref[8:9, :])
        two_ref[...] = two
        low = two.astype(BF16)
        twolow_ref[...] = low
        sum_ref[0:1, :] += col_sum(grad * hat)
        sum_ref[1:2, :] += col_sum(grad)
        sum_ref[2:3, :] += col_sum(low)

    return call(
        body,
        "ffn_backward",
        items // group,
        [
            (grad_three, tiled((block, d))),
            (grad_low, tiled((block, d))),
            (slope, tiled((block, ff))),
            (total_two, tiled((block, d))),
            (w_fin, whole((d, ff))),
            (w_fout, whole((ff, d))),
            (rows, whole(rows.shape)),
        ],
        [
            (spec_of((tokens, ff), BF16), tiled((block, ff))),
            (spec_of((tokens, d), F32), tiled((block, d))),
            (spec_of((tokens, d), BF16), tiled((block, d))),
            (spec_of((8, d), F32), summed((8, d))),
            (spec_of((8, ff), F32), summed((8, ff))),
        ],
        4 * tokens * d * ff,
    )


def cross_backward(dims, grad_two, grad_low, query, kv, probs, total_one, w_cq, w_ckv, w_cout, rows):
    d, items, length, group = dims.d, dims.items, dims.length, dims.group
    pairs, tokens, block = d // (2 * HEAD), items * length, group * length
    count, vis = kv.shape[1], w_ckv.shape[0]
    scale = HEAD ** (-0.5)

    def body(g_ref, glow_ref, q_ref, kv_ref, prob_ref, tot_ref, wcq_ref, wckv_ref, wcout_ref, row_ref,
             gq_ref, gkv_ref, gp_ref, one_ref, onelow_ref, sum_ref, ctx_ref):
        @pl.when(pl.program_id(0) == 0)
        def _():
            sum_ref[...] = jnp.zeros_like(sum_ref)

        low, high, is_low = lane_masks()
        ctx_ref[...] = dot_t(glow_ref[...], wcout_ref[...]).astype(BF16)
        for i in range(group):
            r = slice(i * length, (i + 1) * length)
            for p in range(pairs):
                c = slice(p * 128, (p + 1) * 128)
                cv = slice(d + p * 128, d + (p + 1) * 128)
                q, k, v, out = q_ref[r, c], kv_ref[i, :, c], kv_ref[i, :, cv], ctx_ref[r, c]
                grad_q, grad_k, grad_v = 0.0, [], []
                for h, side in enumerate((low, high)):
                    soft_low = prob_ref[i, 2 * p + h]
                    score = soft_pull(soft_low.astype(F32), dot_t(out, v * side)).astype(BF16)
                    grad_q = grad_q + dot(score, k * side)
                    grad_k.append(dot_l(score, q))
                    grad_v.append(dot_l(soft_low, out))
                gq_ref[r, c] = (grad_q * scale).astype(BF16)
                gkv_ref[i, :, c] = (jnp.where(is_low, *grad_k) * scale).astype(BF16)
                gkv_ref[i, :, cv] = jnp.where(is_low, *grad_v).astype(BF16)
        grad_kv = gkv_ref[...].reshape(group * count, 2 * d)
        gp_ref[...] = dot_t(grad_kv, wckv_ref[...]).astype(BF16).reshape(group, count, vis)
        grad = g_ref[...] + dot_t(gq_ref[...], wcq_ref[...])
        hat, spread = norm_parts(tot_ref[...])
        one = norm_pull(grad, hat, spread, row_ref[3:4, :])
        one_ref[...] = one
        one_low = one.astype(BF16)
        onelow_ref[...] = one_low
        sum_ref[0:1, :] += col_sum(grad * hat)
        sum_ref[1:2, :] += col_sum(grad)
        sum_ref[2:3, :] += col_sum(one_low)
        sum_ref[3:4, :] += col_sum(gq_ref[...])
        sum_ref[4:5, :] += col_sum(grad_kv[:, d:])

    return call(
        body,
        "cross_backward",
        items // group,
        [
            (grad_two, tiled((block, d))),
            (grad_low, tiled((block, d))),
            (query, tiled((block, d))),
            (kv, tiled((group, count, 2 * d))),
            (probs, tiled((group, 2 * pairs, length, count))),
            (total_one, tiled((block, d))),
            (w_cq, whole((d, d))),
            (w_ckv, whole((vis, 2 * d))),
            (w_cout, whole((d, d))),
            (rows, whole(rows.shape)),
        ],
        [
            (spec_of((tokens, d), BF16), tiled((block, d))),
            (spec_of((items, count, 2 * d), BF16), tiled((group, count, 2 * d))),
            (spec_of((items, count, vis), BF16), tiled((group, count, vis))),
            (spec_of((tokens, d), F32), tiled((block, d))),
            (spec_of((tokens, d), BF16), tiled((block, d))),
            (spec_of((8, d), F32), summed((8, d))),
        ],
        2 * tokens * d * 6 * d + 2 * items * count * vis * 2 * d,
        [pltpu.VMEM((block, d), BF16)],
    )


def self_backward(dims, grad_one, grad_low, qkv, probs, w_qkv, w_out):
    d, items, length, group = dims.d, dims.items, dims.length, dims.group
    pairs, tokens, block = d // (2 * HEAD), items * length, group * length
    scale = HEAD ** (-0.5)

    def body(g_ref, glow_ref, qkv_ref, prob_ref, wqkv_ref, wout_ref, gqkv_ref, text_ref, sum_ref, ctx_ref):
        @pl.when(pl.program_id(0) == 0)
        def _():
            sum_ref[...] = jnp.zeros_like(sum_ref)

        low, high, is_low = lane_masks()
        ctx_ref[...] = dot_t(glow_ref[...], wout_ref[...]).astype(BF16)
        for i in range(group):
            r = slice(i * length, (i + 1) * length)
            for p in range(pairs):
                cuts = [slice(part * d + p * 128, part * d + (p + 1) * 128) for part in range(3)]
                q, k, v = (qkv_ref[r, cut] for cut in cuts)
                out = ctx_ref[r, cuts[0]]
                soft_low = prob_ref[i, p]
                grad = dot_t(out, jnp.concatenate([v * low, v * high], 0))
                score = jnp.concatenate(
                    [
                        soft_pull(
                            soft_low[:, h * length : (h + 1) * length].astype(F32),
                            grad[:, h * length : (h + 1) * length],
                        )
                        for h in range(2)
                    ],
                    1,
                ).astype(BF16)
                grad_q = dot(score, jnp.concatenate([k * low, k * high], 0))
                grad_k = dot_l(score, q)
                grad_v = dot_l(soft_low, out)
                gqkv_ref[r, cuts[0]] = (grad_q * scale).astype(BF16)
                gqkv_ref[r, cuts[1]] = (
                    jnp.where(is_low, grad_k[:length], grad_k[length:]) * scale
                ).astype(BF16)
                gqkv_ref[r, cuts[2]] = jnp.where(is_low, grad_v[:length], grad_v[length:]).astype(BF16)
        text_ref[...] = g_ref[...] + dot_t(gqkv_ref[...], wqkv_ref[...])
        sum_ref[0:1, :] += col_sum(gqkv_ref[:, :d])
        sum_ref[1:2, :] += col_sum(gqkv_ref[:, 2 * d :])

    return call(
        body,
        "self_backward",
        items // group,
        [
            (grad_one, tiled((block, d))),
            (grad_low, tiled((block, d))),
            (qkv, tiled((block, 3 * d))),
            (probs, tiled((group, pairs, length, 2 * length))),
            (w_qkv, whole((d, 3 * d))),
            (w_out, whole((d, d))),
        ],
        [
            (spec_of((tokens, 3 * d), BF16), tiled((block, 3 * d))),
            (spec_of((tokens, d), F32), tiled((block, d))),
            (spec_of((8, d), F32), summed((8, d))),
        ],
        2 * tokens * d * 8 * d,
        [pltpu.VMEM((block, d), BF16)],
    )


def weight_grads(plan, group, where, factors):
    high_rows = max(plan.full[w][0] for w in group)

    def body(where_ref, *refs):
        ins, stack_refs, made = refs[: 2 * len(group)], refs[2 * len(group) : -1], refs[-1]
        for n, w in enumerate(group):
            left, right = ins[2 * n], ins[2 * n + 1]
            rows, half = plan.full[w][0], plan.full[w][1] // 2
            for j in range(plan.chunks[w]):
                for y in range(2):
                    cut = slice(y * half + j * plan.chunk, y * half + (j + 1) * plan.chunk)
                    for at in range(0, rows, 256):
                        value = dot_l(left[:, at : at + 256], right[:, cut])
                        made[y, at : at + 256, :] = value.astype(BF16)

                def visit(stack, k, row, w_at, j_at, to_row, to_y, high):
                    if w_at == w and j_at == j:
                        stack_refs[stack][k, row : row + high, :] = made[
                            to_y, pl.ds(to_row, high), :
                        ]

                each_place(plan, group, where_ref, visit)

    shape = jax.ShapeDtypeStruct((plan.zs, plan.rows(group), plan.chunk), BF16)
    flat = [a for pair in factors for a in pair]
    flops = sum(2 * a.shape[0] * a.shape[1] * b.shape[1] for a, b in factors)
    moved = sum(a.size * 2 for a in flat) + 8 * shape.size * 2
    return pl.pallas_call(
        body,
        out_shape=(shape,) * 8,
        in_specs=[SMEM_SPEC] + [VMEM_SPEC] * len(flat),
        out_specs=(VMEM_SPEC,) * 8,
        scratch_shapes=[pltpu.VMEM((2, high_rows, plan.chunk), BF16)],
        compiler_params=PARAMS,
        cost_estimate=pl.CostEstimate(flops=flops, bytes_accessed=moved, transcendentals=0),
        name="weight_grads",
    )(where, *flat)


class Dims:
    def __init__(self, d, items, length):
        self.d, self.items, self.length = d, items, length
        self.group = 2 if items % 2 == 0 else 1


def cross_mask(lengths, counts, boxes, length, pad):
    place = jnp.arange(length, dtype=jnp.int32)[None, :]
    boxed = (counts[:, None] > 0) & (place < lengths[:, None])
    phrase = jnp.where(boxed, place * counts[:, None] // lengths[:, None], 0)
    chosen = phrase[:, :, None] == jnp.arange(boxes.shape[1], dtype=jnp.int32)
    inside = jnp.einsum(
        "itj,ijp->itp",
        chosen.astype(BF16),
        (boxes > 0).astype(BF16),
        preferred_element_type=F32,
    )
    grid_ok = jnp.where(boxed[:, :, None], inside, 1.0).astype(BF16)
    own = jnp.ones(grid_ok.shape[:2] + (1,), BF16)
    return jnp.concatenate([grid_ok, own, jnp.zeros(grid_ok.shape[:2] + (pad,), BF16)], -1)


def trade_in(image_grid, count):
    micro, items, own, width = image_grid.shape
    cut = image_grid.reshape(micro, count, items // count, own, width).transpose(1, 0, 2, 3, 4)
    got = lax.all_to_all(cut, "patch", split_axis=0, concat_axis=0, tiled=True)
    return got.transpose(1, 2, 0, 3, 4).reshape(micro * items // count, count * own, width)


def trade_back(grads, micro, count):
    items, patches, width = grads.shape
    cut = grads.reshape(micro, items // micro, count, patches // count, width)
    got = lax.all_to_all(
        cut.transpose(2, 0, 1, 3, 4), "patch", split_axis=0, concat_axis=0, tiled=True
    )
    got = got.transpose(1, 0, 2, 3, 4)
    return got.reshape(micro, items // micro * count, patches // count, width)


def on_device(
    plan,
    text_in,
    image_grid,
    image_cls,
    text_lengths,
    phrase_counts,
    phrase_boxes,
    cotangent,
    *params,
):
    micro, width = text_in.shape[0], text_in.shape[2]
    shards, vectors, ffn_bias = params[:7], params[7], params[8]
    where = coords()
    items = text_lengths.size
    text, cot = text_in.reshape(-1, width), cotangent.reshape(-1, width)
    lengths = text_lengths.reshape(-1)
    dims = Dims(width, items, text.shape[0] // items)
    rows, bias = gather_small(plan, where, vectors, ffn_bias)
    rows = jnp.pad(rows, ((0, -rows.shape[0] % 8), (0, 0)))
    own, give = pack_split(plan, where, shards)
    units = pack_join(plan, where, own, send(give, plan.core()))
    grid = trade_in(image_grid, plan.patch)
    real = grid.shape[1]
    pad = -(real + 1) % 16
    patches = jnp.concatenate(
        [
            grid,
            image_cls.reshape(items, 1, -1),
            jnp.zeros((items, pad, grid.shape[2]), BF16),
        ],
        axis=1,
    )
    boxes = phrase_boxes.reshape((items,) + phrase_boxes.shape[2:])
    mask = cross_mask(lengths, phrase_counts.reshape(-1), boxes, dims.length, pad)

    weights = {}

    def ready(g):
        full = assemble(plan, GATHER[g], where, gathers[g].held)
        for w, value in zip(GATHER[g], full):
            weights[w] = value

    gathers = [Gathering(plan, unit) for unit in units]
    gathers[0].advance()
    fence(gathers, [])
    gathers[0].advance()
    gathers[1].advance()
    rows, patches, mask, bias = fence(gathers, [rows, patches, mask, bias])
    gathers[0].advance()
    gathers[1].advance()
    gathers[2].advance()
    fence(gathers, [])
    gathers[1].advance()
    gathers[2].advance()
    gathers[3].advance()
    ready(0)
    qkv, probs, ctx, total_one = self_forward(dims, text, weights[QKV], weights[OUT], rows, lengths)
    total_one = fence(gathers[1:], total_one)
    gathers[2].advance()
    gathers[3].advance()
    ready(1)
    hidden_one, query, kv, cross_probs, cross_ctx, total_two = cross_forward(
        dims, total_one, patches, mask, weights[CQ], weights[CKV], weights[COUT], rows
    )
    total_two = fence(gathers[3:], total_two)
    gathers[3].advance()
    ready(2)
    ready(3)
    layer_out, hidden_two, act, slope, grad_three, low_three, sum_three = ffn_forward(
        dims, total_two, cot, weights[FIN], weights[FOUT], rows, bias[None]
    )
    reduces = {}

    def reduce(g, factors):
        stacks = weight_grads(plan, REDUCE[g], where, factors)
        reduces[g] = Reducing(plan, REDUCE[g], where, stacks)

    def hold(values):
        return fence(list(reduces.values()), values)

    def go(*groups):
        for g in groups:
            reduces[g].advance()

    reduce(3, [(act, low_three)])
    grad_three = hold(grad_three)
    go(3)
    grad_pre, grad_two, low_two, sum_two, sum_pre = ffn_backward(
        dims, grad_three, low_three, slope, total_two, weights[FIN], weights[FOUT], rows
    )
    grad_pre, grad_two = hold([grad_pre, grad_two])
    go(3)
    reduce(2, [(hidden_two, grad_pre)])
    grad_two = hold(grad_two)
    go(3, 2)
    grad_query, grad_kv, grad_patch, grad_one, low_one, sum_one = cross_backward(
        dims, grad_two, low_two, query, kv, cross_probs, total_one,
        weights[CQ], weights[CKV], weights[COUT], rows,
    )
    grad_query, grad_one, grad_patch, low_one = hold([grad_query, grad_one, grad_patch, low_one])
    go(3, 2)
    flat_patches = patches.reshape(-1, patches.shape[2])
    flat_kv = grad_kv.reshape(-1, grad_kv.shape[2])
    reduce(
        1,
        [(hidden_one, grad_query), (flat_patches, flat_kv), (cross_ctx, low_two), (ctx, low_one)],
    )
    grad_one = hold(grad_one)
    go(3, 2, 1)
    grad_qkv, text_grad, sum_self = self_backward(
        dims, grad_one, low_one, qkv, probs, weights[QKV], weights[OUT]
    )
    grad_qkv, sum_self = hold([grad_qkv, sum_self])
    rows_grad = jnp.concatenate(
        [
            sum_self[0:2],
            sum_one[2:3],
            sum_one[0:2],
            sum_one[3:5],
            sum_two[2:3],
            sum_two[0:2],
            sum_three[2:3],
            sum_three[0:2],
        ]
    )
    rows_grad, bias_grad = reduce_small(plan, where, rows_grad, sum_pre[0])
    go(3, 2, 1)
    reduce(0, [(text, grad_qkv)])
    hold([])
    go(2, 1, 0)
    go(2)
    grid_grad = trade_back(grad_patch[:, :real], micro, plan.patch).astype(F32)
    grid_grad = hold(grid_grad)
    go(1, 0)
    hold([])
    go(1, 0)
    go(1)
    hold([])
    go(0)
    hold([])
    go(0)
    go(0)
    grads = [None] * 7
    for g, group in enumerate(REDUCE):
        for w, value in zip(group, reduces[g].held):
            grads[w] = value
    cls_grad = grad_patch[:, real].astype(F32).reshape(image_cls.shape)
    return (
        layer_out.reshape(text_in.shape),
        text_grad.reshape(text_in.shape),
        grid_grad,
        cls_grad,
        *grads,
        rows_grad,
        bias_grad,
    )


def on_device_plain(
    plan,
    text_in,
    image_grid,
    image_cls,
    text_lengths,
    phrase_counts,
    phrase_boxes,
    cotangent,
    *params,
):
    micro, width = text_in.shape[0], text_in.shape[2]
    shards, vectors, ffn_bias = params[:7], params[7], params[8]
    items = text_lengths.size
    text, cot = text_in.reshape(-1, width), cotangent.reshape(-1, width)
    lengths = text_lengths.reshape(-1)
    dims = Dims(width, items, text.shape[0] // items)
    weights, rows, bias = fetch_plain(shards, vectors, ffn_bias)
    rows = jnp.pad(rows, ((0, -rows.shape[0] % 8), (0, 0)))
    grid = trade_in(image_grid, plan.patch)
    real = grid.shape[1]
    pad = -(real + 1) % 16
    patches = jnp.concatenate(
        [
            grid,
            image_cls.reshape(items, 1, -1),
            jnp.zeros((items, pad, grid.shape[2]), BF16),
        ],
        axis=1,
    )
    boxes = phrase_boxes.reshape((items,) + phrase_boxes.shape[2:])
    mask = cross_mask(lengths, phrase_counts.reshape(-1), boxes, dims.length, pad)

    qkv, probs, ctx, total_one = self_forward(dims, text, weights[QKV], weights[OUT], rows, lengths)
    hidden_one, query, kv, cross_probs, cross_ctx, total_two = cross_forward(
        dims, total_one, patches, mask, weights[CQ], weights[CKV], weights[COUT], rows
    )
    layer_out, hidden_two, act, slope, grad_three, low_three, sum_three = ffn_forward(
        dims, total_two, cot, weights[FIN], weights[FOUT], rows, bias[None]
    )
    grads = [None] * 7

    def reduce(g, factors):
        for w, (a, b) in zip(REDUCE[g], factors):
            grads[w] = reduce_plain(dot_l(a, b).astype(BF16))

    reduce(3, [(act, low_three)])
    grad_pre, grad_two, low_two, sum_two, sum_pre = ffn_backward(
        dims, grad_three, low_three, slope, total_two, weights[FIN], weights[FOUT], rows
    )
    reduce(2, [(hidden_two, grad_pre)])
    grad_query, grad_kv, grad_patch, grad_one, low_one, sum_one = cross_backward(
        dims, grad_two, low_two, query, kv, cross_probs, total_one,
        weights[CQ], weights[CKV], weights[COUT], rows,
    )
    flat_patches = patches.reshape(-1, patches.shape[2])
    flat_kv = grad_kv.reshape(-1, grad_kv.shape[2])
    reduce(
        1,
        [(hidden_one, grad_query), (flat_patches, flat_kv), (cross_ctx, low_two), (ctx, low_one)],
    )
    grad_qkv, text_grad, sum_self = self_backward(
        dims, grad_one, low_one, qkv, probs, weights[QKV], weights[OUT]
    )
    reduce(0, [(text, grad_qkv)])
    rows_grad = jnp.concatenate(
        [
            sum_self[0:2],
            sum_one[2:3],
            sum_one[0:2],
            sum_one[3:5],
            sum_two[2:3],
            sum_two[0:2],
            sum_three[2:3],
            sum_three[0:2],
        ]
    )
    rows_grad, bias_grad = reduce_small_plain(rows_grad, sum_pre[0])
    cls_grad = grad_patch[:, real].astype(F32).reshape(image_cls.shape)
    grid_grad = trade_back(grad_patch[:, :real], micro, plan.patch).astype(F32)
    return (
        layer_out.reshape(text_in.shape),
        text_grad.reshape(text_in.shape),
        grid_grad,
        cls_grad,
        *grads,
        rows_grad,
        bias_grad,
    )


def solution(mesh):
    dp, patch = mesh.shape["dp"], mesh.shape["patch"]
    both = P(None, ("dp", "patch"), None)
    weight = P("dp", "patch")

    def run(*args):
        shards = [(w.shape[0] // dp, w.shape[1] // patch) for w in args[7:14]]
        plan = Plan(dp, patch, shards)
        return jax.shard_map(
            functools.partial(on_device if plan.fast else on_device_plain, plan),
            mesh=mesh,
            in_specs=(
                both,
                P(None, "dp", "patch", None),
                both,
                P(None, ("dp", "patch")),
                P(None, ("dp", "patch")),
                P(None, ("dp", "patch"), None, None),
                both,
            )
            + (weight,) * 7
            + (P(None, "dp"), P("dp")),
            out_specs=(both, both, P(None, "dp", "patch", None), both)
            + (weight,) * 7
            + (P(None, "dp"), P("dp")),
            check_vma=False,
        )(*args)

    return run
```

time: 649 us -> 573 us (0.88)
  matrix products: 197 us -> 0.39 us
  Pallas kernels: 61.2 us -> 256 us
  local copies, waits for them, and re-layouts: 105 us -> 63.7 us
  waiting for transfers between devices: 119 us -> 98.9 us
  starting transfers between devices: 106 us -> 88.6 us
    dot_general x33 -> x1, matrix products: 197 us -> 0.39 us  [cross_mask(): jnp.einsum('itj,ijp->itp', chosen.astype(BF16), (boxes > 0).astype(BF16),...]
    pallas_call x5 -> x11, Pallas kernels: 23 us -> 218 us  [the longest x6 162 us: call(): pl.pallas_call(body, grid=(steps,), out_shape=out_shape, in_specs=[spec f...]
    convert_element_type x16 -> x27, other arithmetic: 4.69 us -> 38.1 us  [add_low(): return (one.astype(F32) + two.astype(F32)).astype(BF16)]
    ppermute x95, waiting for transfers between devices: 119 us -> 98.9 us  [send(): return lax.ppermute(value, AXES, perm)]
    convert_element_type x8 -> x2, local copies, waits for them, and re-layouts: 24.4 us -> 6.41 us  [the longest x1 5.78 us: on_device(): grid_grad = trade_back(grad_patch[:, :real], micro, plan.patch).astype(F32)]
    ppermute x95, starting transfers between devices: 96.5 us -> 79.5 us  [send(): return lax.ppermute(value, AXES, perm)]
    reduce_sum x13 -> x0, other arithmetic: 15 us -> none  [the longest x3 5.67 us: norm_forward(): center = total_in - jnp.mean(total_in, -1, keepdims=True)]
    convert_element_type x4 -> x2, other arithmetic: 18 us -> 3.79 us  [the longest x1 2.8 us: on_device(): grid_grad = trade_back(grad_patch[:, :real], micro, plan.patch).astype(F32)]
  transfers between devices with their start and end apart: 97 -> 97, of which waited for: 25 -> 21; matrix products, arithmetic and copies ran while one was open for 15% -> 16% of each run, Pallas kernels for 8% -> 36%
where the time goes in v2:
time: 573 us; the launch traced here: 563 us
  Pallas kernels  256 us (45%)
  waiting for transfers between devices  98.9 us (17%)
  starting transfers between devices  88.6 us (15%)
  local copies, waits for them, and re-layouts  63.7 us (11%)
  other arithmetic  53.4 us (9%)
    pallas_call x6, Pallas kernels, call(): pl.pallas_call(body, grid=(steps,), out_shape=out_shape, in_specs=[spec f...  162 us
    ppermute x95, waiting for transfers between devices, send(): return lax.ppermute(value, AXES, perm)  98.9 us
    ppermute x95, starting transfers between devices, send(): return lax.ppermute(value, AXES, perm)  79.5 us
    pallas_call x4, Pallas kernels, weight_grads(): pl.pallas_call(body, out_shape=(shape,) * 8, in_specs=[SMEM_SPEC] + [VMEM...  53.8 us
    convert_element_type x27, other arithmetic, add_low(): return (one.astype(F32) + two.astype(F32)).astype(BF16)  38.1 us
    pallas_call x4, Pallas kernels, assemble(): pl.pallas_call(body, out_shape=tuple((jax.ShapeDtypeStruct(plan.full[w],...  20.5 us
    unnamed x136, local copies, waits for them, and re-layouts  18.5 us
  transfers between devices with their start and end apart: 97, of which 21 were waited for; matrix products, arithmetic and copies ran while one was open for 16% of the time, Pallas kernels for 36%

profile of v2, /device:TPU:0, one launch (start us, length us, event | category | flops | bytes accessed | tf_op | source)
XLA Modules:
  0.0 563.1 jit_solution(8202769163754530570)
XLA Ops:
  2.2 2.9 collective-permute-start
  9.7 4.1 reshape.374
  13.7 2.7 copy.66
  16.5 4.6 all-to-all-start
  23.2 2.7 collective-permute-start.2
  35.9 2.9 collective-permute-done.7
  38.8 8.1 %collective-permute-done.6 = bf16[192,384]{1,0:T(8,128)(2,1)S(1)} collective-permute-done((bf16[192,384]{1,0:T(8,128)(2,1)}, bf16[192,384]{1,0:T(8,128)(2,1)S(1)}, u32[]{:S(2)}, u32[]{:S(2)}) %collective-permute-start.6) | collective-permute-done | bytes 147488 | tf_op jit(solution)/shard_map/ppermute | solution.py:63
  53.8 3.9 reshape.375
  61.1 2.3 maximum_maximum_fusion.patch_ref
  63.4 4.5 collective-permute-done.12
  72.7 3.1 collective-permute-done.23
  76.4 7.8 %collective-permute-done.22 = bf16[192,384]{1,0:T(8,128)(2,1)S(1)} collective-permute-done((bf16[192,384]{1,0:T(8,128)(2,1)S(1)}, bf16[192,384]{1,0:T(8,128)(2,1)S(1)}, u32[]{:S(2)}, u32[]{:S(2)}) %collective-permute-start.22) | collective-permute-done | bytes 147488 | tf_op jit(solution)/shard_map/ppermute | solution.py:63
  87.5 14.3 %collective-permute-done.19.refs_2_ = bf16[4,224,384]{2,1,0:T(8,128)(2,1)} collective-permute-done((bf16[4,224,384]{2,1,0:T(8,128)(2,1)S(1)}, bf16[4,224,384]{2,1,0:T(8,128)(2,1)}, u32[]{:S(2)}, u32[]{:S(2)}) %collective-permute-start.19) | collective-permute-done | bytes 688160 | tf_op jit(solution)/shard_map/ppermute | solution.py:63
  105.3 5.2 collective-permute-done.33
  110.5 6.4 %collective-permute-done.32 = bf16[192,384]{1,0:T(8,128)(2,1)} collective-permute-done((bf16[192,384]{1,0:T(8,128)(2,1)}, bf16[192,384]{1,0:T(8,128)(2,1)}, u32[]{:S(2)}, u32[]{:S(2)}) %collective-permute-start.32) | collective-permute-done | bytes 147488 | tf_op jit(solution)/shard_map/ppermute | solution.py:63
  117.5 5.0 assemble.4
  125.5 15.0 %self_forward.1 = (bf16[1024,2304]{1,0:T(8,128)(2,1)}, bf16[8,6,128,256]{3,2,1,0:T(8,128)(2,1)}, bf16[1024,768]{1,0:T(8,128)(2,1)}, f32[1024,768]{1,0:T(8,128)}) custom-call(s32[8]{0:T(128)} %copy-done.63, bf16[1024,768]{1,0:T(8,128)(2,1)} %bitcast.131, bf16[768,2304]{1,0:T(8,128)(2,1)} %get-tuple-element.325.wqkv_ref, ...), custom_call_target="tpu_custom_call" | custom-call | flops 7247757312 | bytes 18923552 | tf_op jit(solution)/shard_map/self_forward/pallas_call | solution.py:471
  145.1 5.6 assemble.5
  150.7 32.4 %cross_forward.1 = (bf16[1024,768]{1,0:T(8,128)(2,1)}, bf16[1024,768]{1,0:T(8,128)(2,1)}, bf16[8,160,1536]{2,1,0:T(8,128)(2,1)}, bf16[8,12,128,160]{3,2,1,0:T(8,...) custom-call(f32[1024,768]{1,0:T(8,128)} %get-tuple-element.338.tot_ref, ...), custom_call_target="tpu_custom_call" | custom-call | flops 8858370048 | bytes 27377664 | tf_op jit(solution)/shard_map/cross_forward/pallas_call | solution.py:471
  184.9 8.3 %collective-permute-done.41.refs_3_ = bf16[4,192,384]{2,1,0:T(8,128)(2,1)S(1)} collective-permute-done((bf16[4,192,384]{2,1,0:T(8,128)(2,1)}, bf16[4,192,384]{2,1,0:T(8,128)(2,1)S(1)}, u32[]{:S(2)}, u32[]{:S(2)}) %collective-permute-start.41) | collective-permute-done | bytes 589856 | tf_op jit(solution)/shard_map/ppermute | solution.py:63
  194.1 5.0 assemble.6.win_ref
  199.9 5.0 assemble.7.wout_ref
  204.9 32.6 %ffn_forward.1 = (f32[1024,768]{1,0:T(8,128)}, bf16[1024,768]{1,0:T(8,128)(2,1)}, bf16[1024,3072]{1,0:T(8,128)(2,1)}, bf16[1024,3072]{1,0:T(8,128)(2,1)}, f32[10...) custom-call(f32[1024,768]{1,0:T(8,128)} %get-tuple-element.357.tot_ref, bf16[1024,768]{1,0:T(8,128)(2,1)} %bitcast.130, ...), custom_call_target="tpu_custom_call" | custom-call | flops 9663676416 | bytes 36261888 | tf_op jit(solution)/shard_map/ffn_forward/pallas_call | solution.py:471
  239.5 12.2 %weight_grads.4 = (bf16[4,192,384]{2,1,0:T(8,128)(2,1)}, bf16[4,192,384]{2,1,0:T(8,128)(2,1)}, bf16[4,192,384]{2,1,0:T(8,128)(2,1)}, bf16[4,192,384]{2,1,0:T(8,1...) custom-call(s32[4]{0:T(128)} %pad_add_fusion.where_ref, ...), custom_call_target="tpu_custom_call" | custom-call | flops 4831838208 | bytes 12582912 | tf_op jit(solution)/shard_map/weight_grads/pallas_call | solution.py:879
  252.8 18.5 %ffn_backward.1 = (bf16[1024,3072]{1,0:T(8,128)(2,1)}, f32[1024,768]{1,0:T(8,128)}, bf16[1024,768]{1,0:T(8,128)(2,1)}, f32[8,768]{1,0:T(8,128)}, f32[8,3072]{1,0:T(8,128)}) custom-call(f32[1024,768]{1,0:T(8,128)} %get-tuple-element.379.g_ref, bf16[1024,768]{1,0:T(8,128)(2,1)} %get-tuple-element.370.refs_1_.glow_ref, ...), custom_call_target="tpu_custom_call" | custom-call | flops 9663676416 | bytes 34775040 | tf_op jit(solution)/shard_map/ffn_backward/pallas_call | solution.py:471
  275.0 2.4 add_convert_fusion.17
  283.1 12.4 %weight_grads.5 = (bf16[4,192,384]{2,1,0:T(8,128)(2,1)}, bf16[4,192,384]{2,1,0:T(8,128)(2,1)}, bf16[4,192,384]{2,1,0:T(8,128)(2,1)}, bf16[4,192,384]{2,1,0:T(8,1...) custom-call(s32[4]{0:T(128)} %pad_add_fusion.where_ref, ...), custom_call_target="tpu_custom_call" | custom-call | flops 4831838208 | bytes 12582912 | tf_op jit(solution)/shard_map/weight_grads/pallas_call | solution.py:879
  300.5 35.8 %cross_backward.1 = (bf16[1024,768]{1,0:T(8,128)(2,1)}, bf16[8,160,1536]{2,1,0:T(8,128)(2,1)}, bf16[8,160,1024]{2,1,0:T(8,128)(2,1)}, f32[1024,768]{1,0:T(8,128)...) custom-call(f32[1024,768]{1,0:T(8,128)} %get-tuple-element.410.g_ref, ...), custom_call_target="tpu_custom_call" | custom-call | flops 11274289152 | bytes 35725312 | tf_op jit(solution)/shard_map/cross_backward/pallas_call | solution.py:471
  341.4 3.3 slice.107
  344.6 2.6 reshape.398
  347.2 3.3 copy.65
  350.5 4.5 all-to-all-start.1
  358.8 2.3 collective-permute-start.56
  367.1 19.3 %weight_grads.6 = (bf16[4,272,384]{2,1,0:T(8,128)(2,1)}, bf16[4,272,384]{2,1,0:T(8,128)(2,1)}, bf16[4,272,384]{2,1,0:T(8,128)(2,1)}, bf16[4,272,384]{2,1,0:T(8,1...) custom-call(s32[4]{0:T(128)} %pad_add_fusion.where_ref, ...), custom_call_target="tpu_custom_call" | custom-call | flops 7650410496 | bytes 22675456 | tf_op jit(solution)/shard_map/weight_grads/pallas_call | solution.py:879
  389.9 6.3 %collective-permute-done.59 = bf16[4,192,384]{2,1,0:T(8,128)(2,1)} collective-permute-done((bf16[4,192,384]{2,1,0:T(8,128)(2,1)}, bf16[4,192,384]{2,1,0:T(8,128)(2,1)}, u32[]{:S(2)}, u32[]{:S(2)}) %collective-permute-start.59) | collective-permute-done | bytes 589856 | tf_op jit(solution)/shard_map/ppermute | solution.py:63
  403.1 27.4 %self_backward.1 = (bf16[1024,2304]{1,0:T(8,128)(2,1)}, f32[1024,768]{1,0:T(8,128)}, f32[8,768]{1,0:T(8,128)}) custom-call(f32[1024,768]{1,0:T(8,128)} %get-tuple-element.456.g_ref, bf16[1024,768]{1,0:T(8,128)(2,1)} %get-tuple-element.447.refs_7_.glow_ref, bf16[1024,2304]{1,0:T(8,128)(2,1)} %get-tuple-element.457.qkv_ref, ...), custom_call_target="tpu_custom_call" | custom-call | flops 9663676416 | bytes 25190400 | tf_op jit(solution)/shard_map/self_backward/pallas_call | solution.py:471
  440.3 2.4 add_convert_fusion.4
  444.4 9.8 %weight_grads.7 = (bf16[4,144,384]{2,1,0:T(8,128)(2,1)}, bf16[4,144,384]{2,1,0:T(8,128)(2,1)}, bf16[4,144,384]{2,1,0:T(8,128)(2,1)}, bf16[4,144,384]{2,1,0:T(8,1...) custom-call(s32[4]{0:T(128)} %pad_add_fusion.where_ref, ...), custom_call_target="tpu_custom_call" | custom-call | flops 3623878656 | bytes 9830400 | tf_op jit(solution)/shard_map/weight_grads/pallas_call | solution.py:879
  457.7 2.6 collective-permute-start.67
  473.5 9.3 %collective-permute-done.91 = f32[104,128]{1,0:T(8,128)S(1)} collective-permute-done((f32[104,128]{1,0:T(8,128)S(1)}, f32[104,128]{1,0:T(8,128)S(1)}, u32[]{:S(2)}, u32[]{:S(2)}) %collective-permute-start.91) | collective-permute-done | bytes 53280 | tf_op jit(solution)/shard_map/ppermute | solution.py:63
  483.9 2.8 convert_bitcast_fusion
  486.7 5.8 %copy.53 = f32[2,4,4,36,1024]{4,0,3,2,1:T(2,128)} copy(f32[2,4,4,36,1024]{4,2,0,3,1:T(4,128)S(1)} %convert_bitcast_fusion) | data formatting | bytes 9437184 | tf_op jit(solution)/shard_map/convert_element_type | solution.py:1062
  509.1 3.4 collective-permute-done.80.refs_3_
  513.3 6.7 %collective-permute-done.79.refs_2_ = bf16[272,384]{1,0:T(8,128)(2,1)S(1)} collective-permute-done((bf16[272,384]{1,0:T(8,128)(2,1)S(1)}, bf16[272,384]{1,0:T(8,128)(2,1)S(1)}, u32[]{:S(2)}, u32[]{:S(2)}) %collective-permute-start.79) | collective-permute-done | bytes 208928 | tf_op jit(solution)/shard_map/ppermute | solution.py:63
  520.1 7.9 %collective-permute-start.92 = (f32[104,128]{1,0:T(8,128)S(1)}, f32[104,128]{1,0:T(8,128)S(1)}, u32[]{:S(2)}, u32[]{:S(2)}) collective-permute-start(f32[104,128]{1,0:T(8,128)S(1)} %add.241), channel_id=1, source_target_pairs={{0,8},{1,9},{2,10},{3,11},{4,12},{5,13},{6,14},{7,15},{8,16},{9,17... | collective-permute-start | bytes 159752 | tf_op jit(solution)/shard_map/ppermute | solution.py:63
  542.6 3.2 collective-permute-done.87.refs_3_
  545.8 3.0 collective-permute-done.86.refs_2_
  552.3 7.3 %copy.54 = f32[2,16,36,1024]{3,1,2,0:T(8,128)} copy(f32[2,16,36,1024]{3,0,2,1:T(2,128)} %bitcast.105) | data formatting | bytes 9437184
  (404 shorter events, 162.2 us)
Async XLA Ops:
  2.2 21.0 %collective-permute-start = (bf16[16,128]{1,0:T(8,128)(2,1)S(1)}, bf16[16,128]{1,0:T(8,128)(2,1)S(1)}, u32[]{:S(2)}, u32[]{:S(2)}) collective-permute-start(bf16[16,128]{1,0:T(8,128)(2,1)S(1)} %get-tuple-element.635), channel_id=1, source_target_pairs={{0,4},{1,5},{2,6},{3,7},{4,0},{5,1},{6,2},{7,3},{8,12},{9,13},{10,... | collective-permute-start | bytes 12296 | tf_op jit(solution)/shard_map/ppermute | solution.py:63
  9.7 20.0 %collective-permute-start.4 = (bf16[800,192]{1,0:T(8,128)(2,1)}, bf16[800,192]{1,0:T(8,128)(2,1)S(1)}, u32[]{:S(2)}, u32[]{:S(2)}) collective-permute-start(bf16[800,192]{1,0:T(8,128)(2,1)} %get-tuple-element.295), channel_id=1, source_target_pairs={{0,1},{1,0},{2,3},{3,2},{4,5},{5,4},{6,7},{7,6},{8,9},{9,8},{10,11... | collective-permute-start | bytes 921608 | tf_op jit(solution)/shard_map/ppermute | solution.py:63
  16.5 37.3 %all-to-all-start = ((bf16[4,2,4,36,1024]{4,2,1,3,0:T(4,128)(2,1)}), bf16[4,2,4,36,1024]{4,2,1,3,0:T(4,128)(2,1)}, u32[]{:S(2)}, u32[]{:S(2)}) async-start(bf16[4,2,4,36,1024]{4,2,1,3,0:T(4,128)(2,1)} %bitcast.103), calls=%async_computation | async-start | bytes 4718592 | tf_op jit(solution)/shard_map/all_to_all | solution.py:916
  47.9 20.0 %collective-permute-start.10 = (bf16[4,192,384]{2,1,0:T(8,128)(2,1)S(1)}, bf16[4,192,384]{2,1,0:T(8,128)(2,1)S(1)}, u32[]{:S(2)}, u32[]{:S(2)}) collective-permute-start(bf16[4,192,384]{2,1,0:T(8,128)(2,1)S(1)} %pad_maximum_fusion.1.refs_0_), channel_id=1, source_target_pairs={{0,1},{1,0},{2,3},{3,2},{4,5},{5,4},{6,7},{7,6},{8,9},{9,8},{10,11... | collective-permute-start | bytes 1769480 | tf_op jit(solution)/shard_map/ppermute | solution.py:63
  48.0 20.0 %collective-permute-start.9 = (bf16[4,192,384]{2,1,0:T(8,128)(2,1)S(1)}, bf16[4,192,384]{2,1,0:T(8,128)(2,1)}, u32[]{:S(2)}, u32[]{:S(2)}) collective-permute-start(bf16[4,192,384]{2,1,0:T(8,128)(2,1)S(1)} %pad_maximum_fusion.1.refs_0_), channel_id=1, source_target_pairs={{0,2},{1,5},{2,0},{3,7},{4,6},{5,1},{6,4},{7,3},{8,10},{9,13},{10,... | collective-permute-start | bytes 1769480 | tf_op jit(solution)/shard_map/ppermute | solution.py:63
  49.8 18.2 %collective-permute-start.8 = (bf16[4,192,384]{2,1,0:T(8,128)(2,1)S(1)}, bf16[4,192,384]{2,1,0:T(8,128)(2,1)}, u32[]{:S(2)}, u32[]{:S(2)}) collective-permute-start(bf16[4,192,384]{2,1,0:T(8,128)(2,1)S(1)} %pad_maximum_fusion.1.refs_0_), channel_id=1, source_target_pairs={{0,4},{1,3},{2,6},{3,1},{4,0},{5,7},{6,2},{7,5},{8,12},{9,11},{10,... | collective-permute-start | bytes 1769480 | tf_op jit(solution)/shard_map/ppermute | solution.py:63
  84.2 17.6 %collective-permute-start.19 = (bf16[4,224,384]{2,1,0:T(8,128)(2,1)S(1)}, bf16[4,224,384]{2,1,0:T(8,128)(2,1)}, u32[]{:S(2)}, u32[]{:S(2)}) collective-permute-start(bf16[4,224,384]{2,1,0:T(8,128)(2,1)S(1)} %pad_maximum_fusion.refs_0_), channel_id=1, source_target_pairs={{0,2},{1,5},{2,0},{3,7},{4,6},{5,1},{6,4},{7,3},{8,10},{9,13},{10,... | collective-permute-start | bytes 2064392 | tf_op jit(solution)/shard_map/ppermute | solution.py:63
  102.7 21.1 %collective-permute-start.30 = (bf16[4,192,384]{2,1,0:T(8,128)(2,1)S(1)}, bf16[4,192,384]{2,1,0:T(8,128)(2,1)}, u32[]{:S(2)}, u32[]{:S(2)}) collective-permute-start(bf16[4,192,384]{2,1,0:T(8,128)(2,1)S(1)} %pad_maximum_fusion.2.refs_0_), channel_id=1, source_target_pairs={{0,1},{1,0},{2,3},{3,2},{4,5},{5,4},{6,7},{7,6},{8,9},{9,8},{10,11... | collective-permute-start | bytes 1769480 | tf_op jit(solution)/shard_map/ppermute | solution.py:63
  103.9 18.6 %collective-permute-start.31 = (bf16[192,384]{1,0:T(8,128)(2,1)}, bf16[192,384]{1,0:T(8,128)(2,1)}, u32[]{:S(2)}, u32[]{:S(2)}) collective-permute-start(bf16[192,384]{1,0:T(8,128)(2,1)} %get-tuple-element.353), channel_id=1, source_target_pairs={{0,8},{1,9},{2,10},{3,11},{4,12},{5,13},{6,14},{7,15},{8,16},{9,17... | collective-permute-start | bytes 442376 | tf_op jit(solution)/shard_map/ppermute | solution.py:63
  110.5 30.0 %collective-permute-start.25 = (bf16[4,224,384]{2,1,0:T(8,128)(2,1)}, bf16[4,224,384]{2,1,0:T(8,128)(2,1)}, u32[]{:S(2)}, u32[]{:S(2)}) collective-permute-start(bf16[4,224,384]{2,1,0:T(8,128)(2,1)} %collective-permute-done.18.refs_1_), channel_id=1, source_target_pairs={{0,1},{1,0},{2,3},{3,2},{4,5},{5,4},{6,7},{7,6},{8,9},{9,8},{10,11... | collective-permute-start | bytes 2064392 | tf_op jit(solution)/shard_map/ppermute | solution.py:63
  117.0 23.6 %collective-permute-start.26 = (bf16[4,224,384]{2,1,0:T(8,128)(2,1)}, bf16[4,224,384]{2,1,0:T(8,128)(2,1)}, u32[]{:S(2)}, u32[]{:S(2)}) collective-permute-start(bf16[4,224,384]{2,1,0:T(8,128)(2,1)} %collective-permute-done.19.refs_2_), channel_id=1, source_target_pairs={{0,1},{1,0},{2,3},{3,2},{4,5},{5,4},{6,7},{7,6},{8,9},{9,8},{10,11... | collective-permute-start | bytes 2064392 | tf_op jit(solution)/shard_map/ppermute | solution.py:63
  117.0 23.6 %collective-permute-start.27 = (bf16[4,224,384]{2,1,0:T(8,128)(2,1)}, bf16[4,224,384]{2,1,0:T(8,128)(2,1)}, u32[]{:S(2)}, u32[]{:S(2)}) collective-permute-start(bf16[4,224,384]{2,1,0:T(8,128)(2,1)} %collective-permute-done.24.refs_3_), channel_id=1, source_target_pairs={{0,1},{1,0},{2,3},{3,2},{4,5},{5,4},{6,7},{7,6},{8,9},{9,8},{10,11... | collective-permute-start | bytes 2064392 | tf_op jit(solution)/shard_map/ppermute | solution.py:63
  122.5 18.1 %collective-permute-start.29 = (bf16[4,192,384]{2,1,0:T(8,128)(2,1)S(1)}, bf16[4,192,384]{2,1,0:T(8,128)(2,1)S(1)}, u32[]{:S(2)}, u32[]{:S(2)}) collective-permute-start(bf16[4,192,384]{2,1,0:T(8,128)(2,1)S(1)} %pad_maximum_fusion.2.refs_0_), channel_id=1, source_target_pairs={{0,2},{1,5},{2,0},{3,7},{4,6},{5,1},{6,4},{7,3},{8,10},{9,13},{10,... | collective-permute-start | bytes 1769480 | tf_op jit(solution)/shard_map/ppermute | solution.py:63
  142.7 40.4 %collective-permute-start.36 = (bf16[4,192,384]{2,1,0:T(8,128)(2,1)S(1)}, bf16[4,192,384]{2,1,0:T(8,128)(2,1)}, u32[]{:S(2)}, u32[]{:S(2)}) collective-permute-start(bf16[4,192,384]{2,1,0:T(8,128)(2,1)S(1)} %pad_maximum_fusion.3.refs_0_), channel_id=1, source_target_pairs={{0,1},{1,0},{2,3},{3,2},{4,5},{5,4},{6,7},{7,6},{8,9},{9,8},{10,11... | collective-permute-start | bytes 1769480 | tf_op jit(solution)/shard_map/ppermute | solution.py:63
  142.7 40.3 %collective-permute-start.35 = (bf16[4,192,384]{2,1,0:T(8,128)(2,1)S(1)}, bf16[4,192,384]{2,1,0:T(8,128)(2,1)}, u32[]{:S(2)}, u32[]{:S(2)}) collective-permute-start(bf16[4,192,384]{2,1,0:T(8,128)(2,1)S(1)} %pad_maximum_fusion.3.refs_0_), channel_id=1, source_target_pairs={{0,2},{1,5},{2,0},{3,7},{4,6},{5,1},{6,4},{7,3},{8,10},{9,13},{10,... | collective-permute-start | bytes 1769480 | tf_op jit(solution)/shard_map/ppermute | solution.py:63
  143.5 39.5 %collective-permute-start.34 = (bf16[4,192,384]{2,1,0:T(8,128)(2,1)S(1)}, bf16[4,192,384]{2,1,0:T(8,128)(2,1)}, u32[]{:S(2)}, u32[]{:S(2)}) collective-permute-start(bf16[4,192,384]{2,1,0:T(8,128)(2,1)S(1)} %pad_maximum_fusion.3.refs_0_), channel_id=1, source_target_pairs={{0,4},{1,3},{2,6},{3,1},{4,0},{5,7},{6,2},{7,5},{8,12},{9,11},{10,... | collective-permute-start | bytes 1769480 | tf_op jit(solution)/shard_map/ppermute | solution.py:63
  143.8 40.6 %collective-permute-start.39 = (bf16[4,192,384]{2,1,0:T(8,128)(2,1)S(1)}, bf16[4,192,384]{2,1,0:T(8,128)(2,1)}, u32[]{:S(2)}, u32[]{:S(2)}) collective-permute-start(bf16[4,192,384]{2,1,0:T(8,128)(2,1)S(1)} %collective-permute-done.29.refs_2_), channel_id=1, source_target_pairs={{0,1},{1,0},{2,3},{3,2},{4,5},{5,4},{6,7},{7,6},{8,9},{9,8},{10,11... | collective-permute-start | bytes 1769480 | tf_op jit(solution)/shard_map/ppermute | solution.py:63
  143.8 40.1 %collective-permute-start.37 = (bf16[4,192,384]{2,1,0:T(8,128)(2,1)}, bf16[4,192,384]{2,1,0:T(8,128)(2,1)}, u32[]{:S(2)}, u32[]{:S(2)}) collective-permute-start(bf16[4,192,384]{2,1,0:T(8,128)(2,1)} %copy-done.14), channel_id=1, source_target_pairs={{0,2},{1,5},{2,0},{3,7},{4,6},{5,1},{6,4},{7,3},{8,10},{9,13},{10,... | collective-permute-start | bytes 1769480 | tf_op jit(solution)/shard_map/ppermute | solution.py:63
  251.8 23.2 %collective-permute-start.45 = (bf16[4,192,384]{2,1,0:T(8,128)(2,1)}, bf16[4,192,384]{2,1,0:T(8,128)(2,1)S(1)}, u32[]{:S(2)}, u32[]{:S(2)}) collective-permute-start(bf16[4,192,384]{2,1,0:T(8,128)(2,1)} %get-tuple-element.387), channel_id=1, source_target_pairs={{0,1},{1,0},{2,3},{3,2},{4,5},{5,4},{6,7},{7,6},{8,9},{9,8},{10,11... | collective-permute-start | bytes 1769480 | tf_op jit(solution)/shard_map/ppermute | solution.py:63
  252.2 22.7 %collective-permute-start.46 = (bf16[4,192,384]{2,1,0:T(8,128)(2,1)}, bf16[4,192,384]{2,1,0:T(8,128)(2,1)S(1)}, u32[]{:S(2)}, u32[]{:S(2)}) collective-permute-start(bf16[4,192,384]{2,1,0:T(8,128)(2,1)} %get-tuple-element.388), channel_id=1, source_target_pairs={{0,1},{1,0},{2,3},{3,2},{4,5},{5,4},{6,7},{7,6},{8,9},{9,8},{10,11... | collective-permute-start | bytes 1769480 | tf_op jit(solution)/shard_map/ppermute | solution.py:63
  252.3 22.7 %collective-permute-start.47 = (bf16[4,192,384]{2,1,0:T(8,128)(2,1)}, bf16[4,192,384]{2,1,0:T(8,128)(2,1)}, u32[]{:S(2)}, u32[]{:S(2)}) collective-permute-start(bf16[4,192,384]{2,1,0:T(8,128)(2,1)} %get-tuple-element.389), channel_id=1, source_target_pairs={{0,1},{1,0},{2,3},{3,2},{4,5},{5,4},{6,7},{7,6},{8,9},{9,8},{10,11... | collective-permute-start | bytes 1769480 | tf_op jit(solution)/shard_map/ppermute | solution.py:63
  252.8 22.3 %collective-permute-start.48 = (bf16[4,192,384]{2,1,0:T(8,128)(2,1)}, bf16[4,192,384]{2,1,0:T(8,128)(2,1)}, u32[]{:S(2)}, u32[]{:S(2)}) collective-permute-start(bf16[4,192,384]{2,1,0:T(8,128)(2,1)} %get-tuple-element.390), channel_id=1, source_target_pairs={{0,1},{1,0},{2,3},{3,2},{4,5},{5,4},{6,7},{7,6},{8,9},{9,8},{10,11... | collective-permute-start | bytes 1769480 | tf_op jit(solution)/shard_map/ppermute | solution.py:63
  277.5 18.0 %collective-permute-start.50 = (bf16[4,192,384]{2,1,0:T(8,128)(2,1)}, bf16[4,192,384]{2,1,0:T(8,128)(2,1)}, u32[]{:S(2)}, u32[]{:S(2)}) collective-permute-start(bf16[4,192,384]{2,1,0:T(8,128)(2,1)} %add_convert_fusion.17), channel_id=1, source_target_pairs={{0,2},{1,5},{2,0},{3,7},{4,6},{5,1},{6,4},{7,3},{8,10},{9,13},{10,... | collective-permute-start | bytes 1769480 | tf_op jit(solution)/shard_map/ppermute | solution.py:63
  297.8 42.5 %collective-permute-start.51 = (bf16[4,192,384]{2,1,0:T(8,128)(2,1)}, bf16[4,192,384]{2,1,0:T(8,128)(2,1)}, u32[]{:S(2)}, u32[]{:S(2)}) collective-permute-start(bf16[4,192,384]{2,1,0:T(8,128)(2,1)} %add_convert_fusion.15), channel_id=1, source_target_pairs={{0,4},{1,3},{2,6},{3,1},{4,0},{5,7},{6,2},{7,5},{8,12},{9,11},{10,... | collective-permute-start | bytes 1769480 | tf_op jit(solution)/shard_map/ppermute | solution.py:63
  299.5 40.8 %collective-permute-start.52 = (bf16[4,192,384]{2,1,0:T(8,128)(2,1)}, bf16[4,192,384]{2,1,0:T(8,128)(2,1)S(1)}, u32[]{:S(2)}, u32[]{:S(2)}) collective-permute-start(bf16[4,192,384]{2,1,0:T(8,128)(2,1)} %get-tuple-element.427), channel_id=1, source_target_pairs={{0,1},{1,0},{2,3},{3,2},{4,5},{5,4},{6,7},{7,6},{8,9},{9,8},{10,11... | collective-permute-start | bytes 1769480 | tf_op jit(solution)/shard_map/ppermute | solution.py:63
  299.5 40.8 %collective-permute-start.53 = (bf16[4,192,384]{2,1,0:T(8,128)(2,1)}, bf16[4,192,384]{2,1,0:T(8,128)(2,1)S(1)}, u32[]{:S(2)}, u32[]{:S(2)}) collective-permute-start(bf16[4,192,384]{2,1,0:T(8,128)(2,1)} %get-tuple-element.428), channel_id=1, source_target_pairs={{0,1},{1,0},{2,3},{3,2},{4,5},{5,4},{6,7},{7,6},{8,9},{9,8},{10,11... | collective-permute-start | bytes 1769480 | tf_op jit(solution)/shard_map/ppermute | solution.py:63
  300.0 40.3 %collective-permute-start.54 = (bf16[4,192,384]{2,1,0:T(8,128)(2,1)}, bf16[4,192,384]{2,1,0:T(8,128)(2,1)}, u32[]{:S(2)}, u32[]{:S(2)}) collective-permute-start(bf16[4,192,384]{2,1,0:T(8,128)(2,1)} %get-tuple-element.429), channel_id=1, source_target_pairs={{0,1},{1,0},{2,3},{3,2},{4,5},{5,4},{6,7},{7,6},{8,9},{9,8},{10,11... | collective-permute-start | bytes 1769480 | tf_op jit(solution)/shard_map/ppermute | solution.py:63
  300.0 40.3 %collective-permute-start.55 = (bf16[4,192,384]{2,1,0:T(8,128)(2,1)}, bf16[4,192,384]{2,1,0:T(8,128)(2,1)}, u32[]{:S(2)}, u32[]{:S(2)}) collective-permute-start(bf16[4,192,384]{2,1,0:T(8,128)(2,1)} %get-tuple-element.430), channel_id=1, source_target_pairs={{0,1},{1,0},{2,3},{3,2},{4,5},{5,4},{6,7},{7,6},{8,9},{9,8},{10,11... | collective-permute-start | bytes 1769480 | tf_op jit(solution)/shard_map/ppermute | solution.py:63
  350.5 133.4 %all-to-all-start.1 = ((bf16[4,2,4,36,1024]{4,2,1,3,0:T(4,128)(2,1)}), bf16[4,2,4,36,1024]{4,2,1,3,0:T(4,128)(2,1)}, u32[]{:S(2)}, u32[]{:S(2)}) async-start(bf16[4,2,4,36,1024]{4,2,1,3,0:T(4,128)(2,1)} %bitcast.106), calls=%async_computation.1 | async-start | bytes 4718592 | tf_op jit(solution)/shard_map/all_to_all | solution.py:923
  357.1 30.8 %collective-permute-start.58 = (bf16[192,384]{1,0:T(8,128)(2,1)}, bf16[192,384]{1,0:T(8,128)(2,1)}, u32[]{:S(2)}, u32[]{:S(2)}) collective-permute-start(bf16[192,384]{1,0:T(8,128)(2,1)} %get-tuple-element.622), channel_id=1, source_target_pairs={{0,8},{1,9},{2,10},{3,11},{4,12},{5,13},{6,14},{7,15},{8,16},{9,17... | collective-permute-start | bytes 442376 | tf_op jit(solution)/shard_map/ppermute | solution.py:63
  357.1 30.8 %collective-permute-start.57 = (bf16[192,384]{1,0:T(8,128)(2,1)}, bf16[192,384]{1,0:T(8,128)(2,1)}, u32[]{:S(2)}, u32[]{:S(2)}) collective-permute-start(bf16[192,384]{1,0:T(8,128)(2,1)} %get-tuple-element.623), channel_id=1, source_target_pairs={{0,16},{1,17},{2,18},{3,19},{4,20},{5,21},{6,22},{7,23},{8,24},{9,... | collective-permute-start | bytes 442376 | tf_op jit(solution)/shard_map/ppermute | solution.py:63
  358.8 29.1 %collective-permute-start.56 = (bf16[192,384]{1,0:T(8,128)(2,1)S(1)}, bf16[192,384]{1,0:T(8,128)(2,1)}, u32[]{:S(2)}, u32[]{:S(2)}) collective-permute-start(bf16[192,384]{1,0:T(8,128)(2,1)S(1)} %get-tuple-element.624), channel_id=1, source_target_pairs={{0,24},{1,25},{2,26},{3,27},{4,28},{5,29},{6,30},{7,31},{8,0},{9,1... | collective-permute-start | bytes 442376 | tf_op jit(solution)/shard_map/ppermute | solution.py:63
  363.1 26.8 %collective-permute-start.60 = (bf16[4,192,384]{2,1,0:T(8,128)(2,1)}, bf16[4,192,384]{2,1,0:T(8,128)(2,1)}, u32[]{:S(2)}, u32[]{:S(2)}) collective-permute-start(bf16[4,192,384]{2,1,0:T(8,128)(2,1)} %add_convert_fusion.10), channel_id=1, source_target_pairs={{0,2},{1,5},{2,0},{3,7},{4,6},{5,1},{6,4},{7,3},{8,10},{9,13},{10,... | collective-permute-start | bytes 1769480 | tf_op jit(solution)/shard_map/ppermute | solution.py:63
  367.1 29.1 %collective-permute-start.59 = (bf16[4,192,384]{2,1,0:T(8,128)(2,1)}, bf16[4,192,384]{2,1,0:T(8,128)(2,1)}, u32[]{:S(2)}, u32[]{:S(2)}) collective-permute-start(bf16[4,192,384]{2,1,0:T(8,128)(2,1)} %add_convert_fusion.11), channel_id=1, source_target_pairs={{0,2},{1,5},{2,0},{3,7},{4,6},{5,1},{6,4},{7,3},{8,10},{9,13},{10,... | collective-permute-start | bytes 1769480 | tf_op jit(solution)/shard_map/ppermute | solution.py:63
  400.5 30.0 %collective-permute-start.62 = (bf16[4,192,384]{2,1,0:T(8,128)(2,1)}, bf16[4,192,384]{2,1,0:T(8,128)(2,1)}, u32[]{:S(2)}, u32[]{:S(2)}) collective-permute-start(bf16[4,192,384]{2,1,0:T(8,128)(2,1)} %add_convert_fusion.8), channel_id=1, source_target_pairs={{0,4},{1,3},{2,6},{3,1},{4,0},{5,7},{6,2},{7,5},{8,12},{9,11},{10,... | collective-permute-start | bytes 1769480 | tf_op jit(solution)/shard_map/ppermute | solution.py:63
  400.8 29.7 %collective-permute-start.63 = (bf16[4,272,384]{2,1,0:T(8,128)(2,1)}, bf16[4,272,384]{2,1,0:T(8,128)(2,1)}, u32[]{:S(2)}, u32[]{:S(2)}) collective-permute-start(bf16[4,272,384]{2,1,0:T(8,128)(2,1)} %get-tuple-element.477), channel_id=1, source_target_pairs={{0,1},{1,0},{2,3},{3,2},{4,5},{5,4},{6,7},{7,6},{8,9},{9,8},{10,11... | collective-permute-start | bytes 2506760 | tf_op jit(solution)/shard_map/ppermute | solution.py:63
  401.1 29.4 %collective-permute-start.64 = (bf16[4,272,384]{2,1,0:T(8,128)(2,1)}, bf16[4,272,384]{2,1,0:T(8,128)(2,1)S(1)}, u32[]{:S(2)}, u32[]{:S(2)}) collective-permute-start(bf16[4,272,384]{2,1,0:T(8,128)(2,1)} %get-tuple-element.478), channel_id=1, source_target_pairs={{0,1},{1,0},{2,3},{3,2},{4,5},{5,4},{6,7},{7,6},{8,9},{9,8},{10,11... | collective-permute-start | bytes 2506760 | tf_op jit(solution)/shard_map/ppermute | solution.py:63
  401.3 29.2 %collective-permute-start.65 = (bf16[4,272,384]{2,1,0:T(8,128)(2,1)}, bf16[4,272,384]{2,1,0:T(8,128)(2,1)}, u32[]{:S(2)}, u32[]{:S(2)}) collective-permute-start(bf16[4,272,384]{2,1,0:T(8,128)(2,1)} %get-tuple-element.479), channel_id=1, source_target_pairs={{0,1},{1,0},{2,3},{3,2},{4,5},{5,4},{6,7},{7,6},{8,9},{9,8},{10,11... | collective-permute-start | bytes 2506760 | tf_op jit(solution)/shard_map/ppermute | solution.py:63
  402.8 27.7 %collective-permute-start.66 = (bf16[4,272,384]{2,1,0:T(8,128)(2,1)}, bf16[4,272,384]{2,1,0:T(8,128)(2,1)}, u32[]{:S(2)}, u32[]{:S(2)}) collective-permute-start(bf16[4,272,384]{2,1,0:T(8,128)(2,1)} %get-tuple-element.480), channel_id=1, source_target_pairs={{0,1},{1,0},{2,3},{3,2},{4,5},{5,4},{6,7},{7,6},{8,9},{9,8},{10,11... | collective-permute-start | bytes 2506760 | tf_op jit(solution)/shard_map/ppermute | solution.py:63
  432.3 25.4 %collective-permute-start.89 = (f32[104,128]{1,0:T(8,128)}, f32[104,128]{1,0:T(8,128)}, u32[]{:S(2)}, u32[]{:S(2)}) collective-permute-start(f32[104,128]{1,0:T(8,128)} %fusion.1), channel_id=1, source_target_pairs={{0,1},{1,0},{2,3},{3,2},{4,5},{5,4},{6,7},{7,6},{8,9},{9,8},{10,11... | collective-permute-start | bytes 159752 | tf_op jit(solution)/shard_map/ppermute | solution.py:63
  434.6 27.1 %collective-permute-start.69 = (bf16[192,384]{1,0:T(8,128)(2,1)}, bf16[192,384]{1,0:T(8,128)(2,1)}, u32[]{:S(2)}, u32[]{:S(2)}) collective-permute-start(bf16[192,384]{1,0:T(8,128)(2,1)} %get-tuple-element.618), channel_id=1, source_target_pairs={{0,8},{1,9},{2,10},{3,11},{4,12},{5,13},{6,14},{7,15},{8,16},{9,17... | collective-permute-start | bytes 442376 | tf_op jit(solution)/shard_map/ppermute | solution.py:63
  434.6 28.8 %collective-permute-start.68 = (bf16[192,384]{1,0:T(8,128)(2,1)}, bf16[192,384]{1,0:T(8,128)(2,1)}, u32[]{:S(2)}, u32[]{:S(2)}) collective-permute-start(bf16[192,384]{1,0:T(8,128)(2,1)} %get-tuple-element.619), channel_id=1, source_target_pairs={{0,16},{1,17},{2,18},{3,19},{4,20},{5,21},{6,22},{7,23},{8,24},{9,... | collective-permute-start | bytes 442376 | tf_op jit(solution)/shard_map/ppermute | solution.py:63
  438.5 25.5 %collective-permute-start.71 = (bf16[4,272,384]{2,1,0:T(8,128)(2,1)}, bf16[4,272,384]{2,1,0:T(8,128)(2,1)}, u32[]{:S(2)}, u32[]{:S(2)}) collective-permute-start(bf16[4,272,384]{2,1,0:T(8,128)(2,1)} %add_convert_fusion.3), channel_id=1, source_target_pairs={{0,2},{1,5},{2,0},{3,7},{4,6},{5,1},{6,4},{7,3},{8,10},{9,13},{10,... | collective-permute-start | bytes 2506760 | tf_op jit(solution)/shard_map/ppermute | solution.py:63
  442.6 21.4 %collective-permute-start.70 = (bf16[4,272,384]{2,1,0:T(8,128)(2,1)}, bf16[4,272,384]{2,1,0:T(8,128)(2,1)}, u32[]{:S(2)}, u32[]{:S(2)}) collective-permute-start(bf16[4,272,384]{2,1,0:T(8,128)(2,1)} %add_convert_fusion.4), channel_id=1, source_target_pairs={{0,2},{1,5},{2,0},{3,7},{4,6},{5,1},{6,4},{7,3},{8,10},{9,13},{10,... | collective-permute-start | bytes 2506760 | tf_op jit(solution)/shard_map/ppermute | solution.py:63
  468.9 26.9 %collective-permute-start.73 = (bf16[4,272,384]{2,1,0:T(8,128)(2,1)}, bf16[4,272,384]{2,1,0:T(8,128)(2,1)}, u32[]{:S(2)}, u32[]{:S(2)}) collective-permute-start(bf16[4,272,384]{2,1,0:T(8,128)(2,1)} %add_convert_fusion.1), channel_id=1, source_target_pairs={{0,4},{1,3},{2,6},{3,1},{4,0},{5,7},{6,2},{7,5},{8,12},{9,11},{10,... | collective-permute-start | bytes 2506760 | tf_op jit(solution)/shard_map/ppermute | solution.py:63
  497.1 30.9 %collective-permute-start.82 = (bf16[4,144,384]{2,1,0:T(8,128)(2,1)S(1)}, bf16[4,144,384]{2,1,0:T(8,128)(2,1)S(1)}, u32[]{:S(2)}, u32[]{:S(2)}) collective-permute-start(bf16[4,144,384]{2,1,0:T(8,128)(2,1)S(1)} %add_convert_fusion.24), channel_id=1, source_target_pairs={{0,2},{1,5},{2,0},{3,7},{4,6},{5,1},{6,4},{7,3},{8,10},{9,13},{10,... | collective-permute-start | bytes 1327112 | tf_op jit(solution)/shard_map/ppermute | solution.py:63
  499.9 28.1 %collective-permute-start.81 = (bf16[4,144,384]{2,1,0:T(8,128)(2,1)S(1)}, bf16[4,144,384]{2,1,0:T(8,128)(2,1)S(1)}, u32[]{:S(2)}, u32[]{:S(2)}) collective-permute-start(bf16[4,144,384]{2,1,0:T(8,128)(2,1)S(1)} %add_convert_fusion.25), channel_id=1, source_target_pairs={{0,2},{1,5},{2,0},{3,7},{4,6},{5,1},{6,4},{7,3},{8,10},{9,13},{10,... | collective-permute-start | bytes 1327112 | tf_op jit(solution)/shard_map/ppermute | solution.py:63
  512.6 17.7 %collective-permute-start.94 = (f32[104,128]{1,0:T(8,128)S(1)}, f32[104,128]{1,0:T(8,128)S(1)}, u32[]{:S(2)}, u32[]{:S(2)}) collective-permute-start(f32[104,128]{1,0:T(8,128)S(1)} %add.241), channel_id=1, source_target_pairs={{0,24},{1,25},{2,26},{3,27},{4,28},{5,29},{6,30},{7,31},{8,0},{9,1... | collective-permute-start | bytes 159752 | tf_op jit(solution)/shard_map/ppermute | solution.py:63
  (115 other events, 1239.9 us)

commit v3 on v2

--- a/solution.py
+++ b/solution.py
@@ -19,7 +19,7 @@
 
 QKV, OUT, CQ, CKV, COUT, FIN, FOUT = range(7)
 GATHER = ((QKV, OUT), (CQ, CKV, COUT), (FIN,), (FOUT,))
-REDUCE = ((QKV,), (CQ, CKV, COUT, OUT), (FIN,), (FOUT,))
+REDUCE = ((QKV, OUT), (CQ, CKV, COUT), (FIN,), (FOUT,))
 
 
 class Plan:
@@ -216,8 +216,28 @@
     )(where, *stacks)
 
 
-def add_low(one, two):
-    return (one.astype(F32) + two.astype(F32)).astype(BF16)
+def add_low(ones, twos):
+    n = len(ones)
+    shape = ones[0].shape
+
+    def body(*refs):
+        for a, b, out in zip(refs[:n], refs[n : 2 * n], refs[2 * n :]):
+            out[...] = (a[...].astype(F32) + b[...].astype(F32)).astype(BF16)
+
+    spec = pl.BlockSpec((1,) + shape[1:], lambda i: (i, 0, 0))
+    size = shape[0] * shape[1] * shape[2]
+    return pl.pallas_call(
+        body,
+        grid=(shape[0],),
+        out_shape=(jax.ShapeDtypeStruct(shape, BF16),) * n,
+        in_specs=[spec] * (2 * n),
+        out_specs=(spec,) * n,
+        compiler_params=PARAMS,
+        cost_estimate=pl.CostEstimate(
+            flops=n * size, bytes_accessed=6 * n * size, transcendentals=0
+        ),
+        name="add_low",
+    )(*ones, *twos)
 
 
 class Reducing:
@@ -230,13 +250,13 @@
         if self.step == 0:
             held = held[:4] + [send(part, plan.core()) for part in held[4:]]
         elif self.step == 1:
-            mine = [add_low(a, b) for a, b in zip(held[:4], held[4:])]
-            held = mine[:2] + [send(part, plan.second()) for part in mine[2:]]
+            mine = add_low(held[:4], held[4:])
+            held = list(mine[:2]) + [send(part, plan.second()) for part in mine[2:]]
         elif self.step == 2:
-            mine = [add_low(held[0], held[2]), add_low(held[1], held[3])]
+            mine = add_low(held[:2], held[2:])
             held = [mine[0], send(mine[1], plan.first())]
         elif self.step == 3:
-            total = add_low(*held)
+            (total,) = add_low(held[:1], held[1:])
             parts = [send(total[k], plan.z_up(plan.zs - k)) for k in range(1, plan.zs)]
             held = [total[0]] + parts
         elif self.step == 4:
@@ -339,21 +359,31 @@
     return rows, every[:, count * part :].reshape(-1)
 
 
-def reduce_small(plan, where, rows, bias):
-    count, width = rows.shape
-    flat = jnp.concatenate([rows.reshape(-1), bias]).astype(F32)
-    size = flat.shape[0]
-    flat = jnp.pad(flat, (0, -size % 1024)).reshape(-1, 128)
-    for bit in (1, 2, 4):
-        flat = flat + send(flat, plan.flip(lambda i: bit))
-    flat = flat + sum(send(flat, plan.z_up(k)) for k in range(1, plan.zs))
-    flat = flat.reshape(-1)
-    dp = where[0] * 2 + where[1]
-    whole = flat[: count * width].reshape(count, width)
-    own = lax.dynamic_slice_in_dim(whole, dp * (width // plan.dp), width // plan.dp, axis=1)
-    tail = flat[count * width : size]
-    step = bias.shape[0] // plan.dp
-    return own, lax.dynamic_slice_in_dim(tail, dp * step, step, axis=0)
+class ReducingSmall:
+    def __init__(self, plan, where, rows, bias):
+        self.plan, self.where, self.shape, self.tail = plan, where, rows.shape, bias.shape[0]
+        flat = jnp.concatenate([rows.reshape(-1), bias])
+        flat = jnp.pad(flat, (0, -flat.shape[0] % 1024)).reshape(-1, 128)
+        self.held, self.step = [flat], 0
+
+    def advance(self):
+        plan = self.plan
+        flat = sum(self.held)
+        if self.step < 3:
+            bit = 1 << self.step
+            self.held = [flat, send(flat, plan.flip(lambda i: bit))]
+        else:
+            self.held = [flat] + [send(flat, plan.z_up(k)) for k in range(1, plan.zs)]
+        self.step += 1
+
+    def result(self):
+        plan, (count, width) = self.plan, self.shape
+        flat = sum(self.held).reshape(-1)
+        dp = self.where[0] * 2 + self.where[1]
+        main = flat[: count * width].reshape(count, width)
+        own = lax.dynamic_slice_in_dim(main, dp * (width // plan.dp), width // plan.dp, axis=1)
+        tail, step = flat[count * width : count * width + self.tail], self.tail // plan.dp
+        return own, lax.dynamic_slice_in_dim(tail, dp * step, step, axis=0)
 
 
 def fetch_plain(weights, vectors, bias):
@@ -376,6 +406,9 @@
     return lax.psum(rows, "patch"), lax.psum(bias, "patch")
 
 
+TAIL = (0.112528827, 0.117839666, 0.0706314405, 0.2046457425, -0.190499398, 0.3478185715, -0.201092832, 0.03812798145)
+
+
 def dot(a, b):
     return lax.dot_general(a, b, (((1,), (0,)), ((), ())), preferred_element_type=F32)
 
@@ -403,28 +436,14 @@
     )
 
 
-def error_function(x):
-    x = jnp.clip(x, -4.0, 4.0)
-    s = x * x
-    top = jnp.full_like(s, -2.72614225801306e-10)
-    for c in (
-        2.77068142495902e-08,
-        -2.10102402082508e-06,
-        -5.69250639462346e-05,
-        -7.34990630326855e-04,
-        -2.95459980854025e-03,
-        -1.60960333262415e-02,
-    ):
-        top = top * s + c
-    low = jnp.full_like(s, -1.45660718464996e-05)
-    for c in (
-        -2.13374055278905e-04,
-        -1.68282697438203e-03,
-        -7.37332916720468e-03,
-        -1.42647390514189e-02,
-    ):
-        low = low * s + c
-    return x * top / low
+def gelu_parts(x):
+    bell = jnp.exp(-0.5 * (x * x))
+    t = 1.0 / (1.0 + (0.4 * 0.5**0.5) * jnp.abs(x))
+    tail = jnp.full_like(t, TAIL[-1])
+    for c in TAIL[-2::-1]:
+        tail = tail * t + c
+    tail = tail * (t * bell)
+    return jnp.where(x < 0.0, tail, 1.0 - tail), bell
 
 
 def col_sum(value):
@@ -432,18 +451,28 @@
 
 
 def soft(scores):
-    grown = jnp.exp(scores - jnp.max(scores, -1, keepdims=True))
-    return grown * (1.0 / jnp.sum(grown, -1, keepdims=True))
+    grown = jnp.exp(scores - jnp.max(scores, 0, keepdims=True))
+    return grown * (1.0 / jnp.sum(grown, 0, keepdims=True))
 
 
 def soft_pull(probs, grad):
-    return probs * (grad - jnp.sum(probs * grad, -1, keepdims=True))
+    return probs * (grad - jnp.sum(probs * grad, 0, keepdims=True))
+
+
+def spread_heads(value, low, high):
+    return jnp.concatenate([value * low, value * high], 0)
+
+
+def join_heads(value):
+    count = value.shape[1] // 2
+    value = jnp.concatenate([value[:HEAD, :count], value[HEAD:, count:]], 0)
+    return value.astype(BF16).T
 
 
 def lane_masks():
     lane = lax.broadcasted_iota(jnp.int32, (1, 2 * HEAD), 1)
     low = (lane < HEAD).astype(F32)
-    return low.astype(BF16), (1.0 - low).astype(BF16), lane < HEAD
+    return low.astype(BF16), (1.0 - low).astype(BF16)
 
 
 def whole(shape):
@@ -490,7 +519,7 @@
 
     def body(len_ref, x_ref, wqkv_ref, wout_ref, row_ref, qkv_ref, prob_ref, ctx_ref, tot_ref):
         step = pl.program_id(0)
-        low, high, _ = lane_masks()
+        low, high = lane_masks()
         x = x_ref[...]
         for part, bias in ((0, 0), (1, None), (2, 1)):
             cut = slice(part * d, (part + 1) * d)
@@ -498,7 +527,7 @@
             if bias is not None:
                 value = value + row_ref[bias : bias + 1, :]
             qkv_ref[:, cut] = value.astype(BF16)
-        place = lax.broadcasted_iota(jnp.int32, (1, length), 1)
+        place = lax.broadcasted_iota(jnp.int32, (length, 1), 0)
         for i in range(group):
             ok = place < len_ref[step * group + i]
             r = slice(i * length, (i + 1) * length)
@@ -506,17 +535,10 @@
                 q, k, v = (
                     qkv_ref[r, part * d + p * 128 : part * d + (p + 1) * 128] for part in range(3)
                 )
-                scores = dot_t(q, jnp.concatenate([k * low, k * high], 0)) * scale
-                probs = jnp.concatenate(
-                    [
-                        soft(jnp.where(ok, scores[:, h * length : (h + 1) * length], NEG))
-                        for h in range(2)
-                    ],
-                    1,
-                ).astype(BF16)
+                scores = dot_t(k, spread_heads(q, low, high)) * scale
+                probs = soft(jnp.where(ok, scores, NEG)).astype(BF16)
                 prob_ref[i, p] = probs
-                ctx = dot(probs, jnp.concatenate([v * low, v * high], 0))
-                ctx_ref[r, p * 128 : (p + 1) * 128] = ctx.astype(BF16)
+                ctx_ref[r, p * 128 : (p + 1) * 128] = join_heads(dot(v.T, probs))
         tot_ref[...] = x.astype(F32) + dot(ctx_ref[...], wout_ref[...]) + row_ref[2:3, :]
 
     return call(
@@ -540,19 +562,27 @@
     )
 
 
-def cross_forward(dims, total_one, patches, mask, w_cq, w_ckv, w_cout, rows):
+def cross_forward(dims, total_one, grids, cls, mask, w_cq, w_ckv, w_cout, rows):
     d, items, length, group = dims.d, dims.items, dims.length, dims.group
     pairs, tokens, block = d // (2 * HEAD), items * length, group * length
-    count, vis = patches.shape[1], patches.shape[2]
+    count, part, vis = mask.shape[1], grids[0].shape[1], cls.shape[2]
     scale = HEAD ** (-0.5)
-
-    def body(tot_ref, patch_ref, mask_ref, wcq_ref, wckv_ref, wcout_ref, row_ref,
-             h_ref, cq_ref, kv_ref, prob_ref, ctx_ref, two_ref):
-        low, high, _ = lane_masks()
+    parts = len(grids)
+
+    def body(tot_ref, *refs):
+        grid_refs = refs[:parts]
+        cls_ref, mask_ref, wcq_ref, wckv_ref, wcout_ref, row_ref = refs[parts : parts + 6]
+        h_ref, cq_ref, kv_ref, prob_ref, ctx_ref, two_ref, patch_ref = refs[parts + 6 :]
+        low, high = lane_masks()
         hat, _ = norm_parts(tot_ref[...])
         hidden = hat * row_ref[3:4, :] + row_ref[4:5, :]
         h_ref[...] = hidden.astype(BF16)
         cq_ref[...] = (dot(h_ref[...], wcq_ref[...]) + row_ref[5:6, :]).astype(BF16)
+        for i in range(group):
+            for k in range(parts):
+                patch_ref[i, k * part : (k + 1) * part, :] = grid_refs[k][i]
+            rest = jnp.zeros((count - parts * part - 1, vis), BF16)
+            patch_ref[i, parts * part :, :] = jnp.concatenate([cls_ref[i], rest], 0)
         patch = patch_ref[...].reshape(group * count, vis)
         keys = dot(patch, wckv_ref[:, :d]).astype(BF16)
         kv_ref[:, :, :d] = keys.reshape(group, count, d)
@@ -560,27 +590,26 @@
         kv_ref[:, :, d:] = values.reshape(group, count, d)
         for i in range(group):
             ok = mask_ref[i].astype(F32) > 0.5
+            ok = jnp.concatenate([ok, ok], 1)
             r = slice(i * length, (i + 1) * length)
             for p in range(pairs):
                 c = slice(p * 128, (p + 1) * 128)
                 q, k, v = cq_ref[r, c], kv_ref[i, :, c], kv_ref[i, :, d + p * 128 : d + (p + 1) * 128]
-                ctx = 0.0
-                for h, side in enumerate((low, high)):
-                    scores = dot_t(q, k * side) * scale
-                    probs = soft(jnp.where(ok, scores, NEG)).astype(BF16)
-                    prob_ref[i, 2 * p + h] = probs
-                    ctx = ctx + dot(probs, v * side)
-                ctx_ref[r, c] = ctx.astype(BF16)
+                scores = dot_t(k, spread_heads(q, low, high)) * scale
+                probs = soft(jnp.where(ok, scores, NEG)).astype(BF16)
+                prob_ref[i, p] = probs
+                ctx_ref[r, c] = join_heads(dot(v.T, probs))
         two_ref[...] = hidden + dot(ctx_ref[...], wcout_ref[...]) + row_ref[7:8, :]
 
     return call(
         body,
         "cross_forward",
         items // group,
-        [
-            (total_one, tiled((block, d))),
-            (patches, tiled((group, count, vis))),
-            (mask, tiled((group, length, count))),
+        [(total_one, tiled((block, d)))]
+        + [(grid, tiled((group, part, vis))) for grid in grids]
+        + [
+            (cls, tiled((group, 1, vis))),
+            (mask, tiled((group, count, length))),
             (w_cq, whole((d, d))),
             (w_ckv, whole((vis, 2 * d))),
             (w_cout, whole((d, d))),
@@ -590,9 +619,10 @@
             (spec_of((tokens, d), BF16), tiled((block, d))),
             (spec_of((tokens, d), BF16), tiled((block, d))),
             (spec_of((items, count, 2 * d), BF16), tiled((group, count, 2 * d))),
-            (spec_of((items, 2 * pairs, length, count), BF16), tiled((group, 2 * pairs, length, count))),
+            (spec_of((items, pairs, count, 2 * length), BF16), tiled((group, pairs, count, 2 * length))),
             (spec_of((tokens, d), BF16), tiled((block, d))),
             (spec_of((tokens, d), F32), tiled((block, d))),
+            (spec_of((items, count, vis), BF16), tiled((group, count, vis))),
         ],
         2 * tokens * d * 4 * d + 2 * items * count * vis * 2 * d,
     )
@@ -616,11 +646,10 @@
         for at in range(0, ff, piece):
             cut = slice(at, at + piece)
             pre = dot(h_ref[...], win_ref[:, cut]) + bias_ref[:, cut]
-            half = 0.5 + 0.5 * error_function(pre * 0.5**0.5)
-            act = (pre * half).astype(BF16)
+            under, bell = gelu_parts(pre)
+            act = (pre * under).astype(BF16)
             act_ref[:, cut] = act
-            bell = jnp.exp(-0.5 * pre * pre) * 0.3989422804014327
-            slope_ref[:, cut] = (half + pre * bell).astype(BF16)
+            slope_ref[:, cut] = (under + (pre * 0.3989422804014327) * bell).astype(BF16)
             total = total + dot(act, wout_ref[cut, :])
         hat, spread = norm_parts(total)
         gain = row_ref[11:12, :]
@@ -712,38 +741,78 @@
     )
 
 
-def cross_backward(dims, grad_two, grad_low, query, kv, probs, total_one, w_cq, w_ckv, w_cout, rows):
+def pair_pull(q, k, v, out, probs, low, high):
+    outs = spread_heads(out, low, high)
+    score = soft_pull(probs.astype(F32), dot_t(v, outs)).astype(BF16)
+    grad_k = dot(score, spread_heads(q, low, high))
+    return dot(k.T, score), grad_k, dot(probs, outs)
+
+
+def cross_attend_back(dims, grad_low, query, kv, probs, w_cout):
     d, items, length, group = dims.d, dims.items, dims.length, dims.group
     pairs, tokens, block = d // (2 * HEAD), items * length, group * length
-    count, vis = kv.shape[1], w_ckv.shape[0]
+    count = kv.shape[1]
     scale = HEAD ** (-0.5)
 
-    def body(g_ref, glow_ref, q_ref, kv_ref, prob_ref, tot_ref, wcq_ref, wckv_ref, wcout_ref, row_ref,
-             gq_ref, gkv_ref, gp_ref, one_ref, onelow_ref, sum_ref, ctx_ref):
+    def body(glow_ref, q_ref, kv_ref, prob_ref, wcout_ref, gq_ref, gkv_ref, sum_ref, ctx_ref):
         @pl.when(pl.program_id(0) == 0)
         def _():
             sum_ref[...] = jnp.zeros_like(sum_ref)
 
-        low, high, is_low = lane_masks()
+        low, high = lane_masks()
         ctx_ref[...] = dot_t(glow_ref[...], wcout_ref[...]).astype(BF16)
         for i in range(group):
             r = slice(i * length, (i + 1) * length)
             for p in range(pairs):
                 c = slice(p * 128, (p + 1) * 128)
                 cv = slice(d + p * 128, d + (p + 1) * 128)
-                q, k, v, out = q_ref[r, c], kv_ref[i, :, c], kv_ref[i, :, cv], ctx_ref[r, c]
-                grad_q, grad_k, grad_v = 0.0, [], []
-                for h, side in enumerate((low, high)):
-                    soft_low = prob_ref[i, 2 * p + h]
-                    score = soft_pull(soft_low.astype(F32), dot_t(out, v * side)).astype(BF16)
-                    grad_q = grad_q + dot(score, k * side)
-                    grad_k.append(dot_l(score, q))
-                    grad_v.append(dot_l(soft_low, out))
-                gq_ref[r, c] = (grad_q * scale).astype(BF16)
-                gkv_ref[i, :, c] = (jnp.where(is_low, *grad_k) * scale).astype(BF16)
-                gkv_ref[i, :, cv] = jnp.where(is_low, *grad_v).astype(BF16)
-        grad_kv = gkv_ref[...].reshape(group * count, 2 * d)
-        gp_ref[...] = dot_t(grad_kv, wckv_ref[...]).astype(BF16).reshape(group, count, vis)
+                grad_q, grad_k, grad_v = pair_pull(
+                    q_ref[r, c], kv_ref[i, :, c], kv_ref[i, :, cv], ctx_ref[r, c], prob_ref[i, p], low, high
+                )
+                gq_ref[r, c] = join_heads(grad_q * scale)
+                gkv_ref[i, :, c] = (grad_k * scale).astype(BF16)
+                gkv_ref[i, :, cv] = grad_v.astype(BF16)
+        sum_ref[0:1, :] += col_sum(gq_ref[...])
+        sum_ref[1:2, :] += col_sum(gkv_ref[:, :, d:].reshape(group * count, d))
+
+    return call(
+        body,
+        "cross_attend_back",
+        items // group,
+        [
+            (grad_low, tiled((block, d))),
+            (query, tiled((block, d))),
+            (kv, tiled((group, count, 2 * d))),
+            (probs, tiled((group, pairs, count, 2 * length))),
+            (w_cout, whole((d, d))),
+        ],
+        [
+            (spec_of((tokens, d), BF16), tiled((block, d))),
+            (spec_of((items, count, 2 * d), BF16), tiled((group, count, 2 * d))),
+            (spec_of((8, d), F32), summed((8, d))),
+        ],
+        2 * tokens * d * 4 * d,
+        [pltpu.VMEM((block, d), BF16)],
+    )
+
+
+def cross_project_back(dims, grad_two, grad_query, grad_kv, total_one, w_cq, w_ckv, rows, parts, part):
+    d, items, length, group = dims.d, dims.items, dims.length, dims.group
+    tokens, block = items * length, group * length
+    count, vis = grad_kv.shape[1], w_ckv.shape[0]
+
+    def body(g_ref, gq_ref, gkv_ref, tot_ref, wcq_ref, wckv_ref, row_ref, *refs):
+        grid_refs, (cls_ref, one_ref, onelow_ref, sum_ref) = refs[:parts], refs[parts:]
+
+        @pl.when(pl.program_id(0) == 0)
+        def _():
+            sum_ref[...] = jnp.zeros_like(sum_ref)
+
+        for i in range(group):
+            value = dot_t(gkv_ref[i], wckv_ref[...])
+            for k in range(parts):
+                grid_refs[k][i] = value[k * part : (k + 1) * part, :].astype(BF16)
+            cls_ref[i] = value[parts * part : parts * part + 1, :]
         grad = g_ref[...] + dot_t(gq_ref[...], wcq_ref[...])
         hat, spread = norm_parts(tot_ref[...])
         one = norm_pull(grad, hat, spread, row_ref[3:4, :])
@@ -753,100 +822,117 @@
         sum_ref[0:1, :] += col_sum(grad * hat)
         sum_ref[1:2, :] += col_sum(grad)
         sum_ref[2:3, :] += col_sum(one_low)
-        sum_ref[3:4, :] += col_sum(gq_ref[...])
-        sum_ref[4:5, :] += col_sum(grad_kv[:, d:])
 
     return call(
         body,
-        "cross_backward",
+        "cross_project_back",
         items // group,
         [
             (grad_two, tiled((block, d))),
-            (grad_low, tiled((block, d))),
-            (query, tiled((block, d))),
-            (kv, tiled((group, count, 2 * d))),
-            (probs, tiled((group, 2 * pairs, length, count))),
+            (grad_query, tiled((block, d))),
+            (grad_kv, tiled((group, count, 2 * d))),
             (total_one, tiled((block, d))),
             (w_cq, whole((d, d))),
             (w_ckv, whole((vis, 2 * d))),
-            (w_cout, whole((d, d))),
             (rows, whole(rows.shape)),
         ],
-        [
-            (spec_of((tokens, d), BF16), tiled((block, d))),
-            (spec_of((items, count, 2 * d), BF16), tiled((group, count, 2 * d))),
-            (spec_of((items, count, vis), BF16), tiled((group, count, vis))),
+        [(spec_of((items, part, vis), BF16), tiled((group, part, vis)))] * parts
+        + [
+            (spec_of((items, 1, vis), F32), tiled((group, 1, vis))),
             (spec_of((tokens, d), F32), tiled((block, d))),
             (spec_of((tokens, d), BF16), tiled((block, d))),
             (spec_of((8, d), F32), summed((8, d))),
         ],
-        2 * tokens * d * 6 * d + 2 * items * count * vis * 2 * d,
-        [pltpu.VMEM((block, d), BF16)],
-    )
-
-
-def self_backward(dims, grad_one, grad_low, qkv, probs, w_qkv, w_out):
+        2 * tokens * d * d + 2 * items * count * vis * 2 * d,
+    )
+
+
+def self_attend_back(dims, grad_low, qkv, probs, w_out):
     d, items, length, group = dims.d, dims.items, dims.length, dims.group
     pairs, tokens, block = d // (2 * HEAD), items * length, group * length
     scale = HEAD ** (-0.5)
 
-    def body(g_ref, glow_ref, qkv_ref, prob_ref, wqkv_ref, wout_ref, gqkv_ref, text_ref, sum_ref, ctx_ref):
+    def body(glow_ref, qkv_ref, prob_ref, wout_ref, gqkv_ref, sum_ref, ctx_ref):
         @pl.when(pl.program_id(0) == 0)
         def _():
             sum_ref[...] = jnp.zeros_like(sum_ref)
 
-        low, high, is_low = lane_masks()
+        low, high = lane_masks()
         ctx_ref[...] = dot_t(glow_ref[...], wout_ref[...]).astype(BF16)
         for i in range(group):
             r = slice(i * length, (i + 1) * length)
             for p in range(pairs):
                 cuts = [slice(part * d + p * 128, part * d + (p + 1) * 128) for part in range(3)]
                 q, k, v = (qkv_ref[r, cut] for cut in cuts)
-                out = ctx_ref[r, cuts[0]]
-                soft_low = prob_ref[i, p]
-                grad = dot_t(out, jnp.concatenate([v * low, v * high], 0))
-                score = jnp.concatenate(
-                    [
-                        soft_pull(
-                            soft_low[:, h * length : (h + 1) * length].astype(F32),
-                            grad[:, h * length : (h + 1) * length],
-                        )
-                        for h in range(2)
-                    ],
-                    1,
-                ).astype(BF16)
-                grad_q = dot(score, jnp.concatenate([k * low, k * high], 0))
-                grad_k = dot_l(score, q)
-                grad_v = dot_l(soft_low, out)
-                gqkv_ref[r, cuts[0]] = (grad_q * scale).astype(BF16)
-                gqkv_ref[r, cuts[1]] = (
-                    jnp.where(is_low, grad_k[:length], grad_k[length:]) * scale
-                ).astype(BF16)
-                gqkv_ref[r, cuts[2]] = jnp.where(is_low, grad_v[:length], grad_v[length:]).astype(BF16)
-        text_ref[...] = g_ref[...] + dot_t(gqkv_ref[...], wqkv_ref[...])
+                grad_q, grad_k, grad_v = pair_pull(q, k, v, ctx_ref[r, cuts[0]], prob_ref[i, p], low, high)
+                gqkv_ref[r, cuts[0]] = join_heads(grad_q * scale)
+                gqkv_ref[r, cuts[1]] = (grad_k * scale).astype(BF16)
+                gqkv_ref[r, cuts[2]] = grad_v.astype(BF16)
         sum_ref[0:1, :] += col_sum(gqkv_ref[:, :d])
         sum_ref[1:2, :] += col_sum(gqkv_ref[:, 2 * d :])
 
     return call(
         body,
-        "self_backward",
+        "self_attend_back",
         items // group,
         [
-            (grad_one, tiled((block, d))),
             (grad_low, tiled((block, d))),
             (qkv, tiled((block, 3 * d))),
             (probs, tiled((group, pairs, length, 2 * length))),
+            (w_out, whole((d, d))),
+        ],
+        [
+            (spec_of((tokens, 3 * d), BF16), tiled((block, 3 * d))),
+            (spec_of((8, d), F32), summed((8, d))),
+        ],
+        2 * tokens * d * 4 * d,
+        [pltpu.VMEM((block, d), BF16)],
+    )
+
+
+def self_project_back(dims, grad_one, grad_qkv, w_qkv):
+    d, items, length, group = dims.d, dims.items, dims.length, dims.group
+    tokens, block = items * length, group * length
+
+    def body(g_ref, gqkv_ref, wqkv_ref, text_ref):
+        text_ref[...] = g_ref[...] + dot_t(gqkv_ref[...], wqkv_ref[...])
+
+    return call(
+        body,
+        "self_project_back",
+        items // group,
+        [
+            (grad_one, tiled((block, d))),
+            (grad_qkv, tiled((block, 3 * d))),
             (w_qkv, whole((d, 3 * d))),
-            (w_out, whole((d, d))),
-        ],
-        [
-            (spec_of((tokens, 3 * d), BF16), tiled((block, 3 * d))),
-            (spec_of((tokens, d), F32), tiled((block, d))),
-            (spec_of((8, d), F32), summed((8, d))),
-        ],
-        2 * tokens * d * 8 * d,
-        [pltpu.VMEM((block, d), BF16)],
-    )
+        ],
+        [(spec_of((tokens, d), F32), tiled((block, d)))],
+        2 * tokens * d * 3 * d,
+    )[0]
+
+
+def place_grids(turn, micro, pieces):
+    items, part, vis = pieces[0].shape
+    each, parts = items // micro, len(pieces)
+
+    def body(turn_ref, *refs):
+        for k in range(parts):
+            at = (turn_ref[0] ^ k) * each
+            refs[-1][0, pl.ds(at, each)] = refs[k][...].astype(F32)
+
+    return call(
+        body,
+        "place_grids",
+        micro,
+        [(turn, SMEM_SPEC)] + [(p, tiled((each, part, vis))) for p in pieces],
+        [
+            (
+                spec_of((micro, each * parts, part, vis), F32),
+                tiled((1, each * parts, part, vis)),
+            )
+        ],
+        0,
+    )[0]
 
 
 def weight_grads(plan, group, where, factors):
@@ -894,287 +980,252 @@
         self.group = 2 if items % 2 == 0 else 1
 
 
-def cross_mask(lengths, counts, boxes, length, pad):
+def cross_mask(lengths, counts, boxes, length, count):
     place = jnp.arange(length, dtype=jnp.int32)[None, :]
     boxed = (counts[:, None] > 0) & (place < lengths[:, None])
     phrase = jnp.where(boxed, place * counts[:, None] // lengths[:, None], 0)
-    chosen = phrase[:, :, None] == jnp.arange(boxes.shape[1], dtype=jnp.int32)
+    chosen = phrase[:, None, :] == jnp.arange(boxes.shape[1], dtype=jnp.int32)[None, :, None]
     inside = jnp.einsum(
-        "itj,ijp->itp",
+        "ijp,ijt->ipt",
+        (boxes > 0).astype(BF16),
         chosen.astype(BF16),
-        (boxes > 0).astype(BF16),
         preferred_element_type=F32,
     )
-    grid_ok = jnp.where(boxed[:, :, None], inside, 1.0).astype(BF16)
-    own = jnp.ones(grid_ok.shape[:2] + (1,), BF16)
-    return jnp.concatenate([grid_ok, own, jnp.zeros(grid_ok.shape[:2] + (pad,), BF16)], -1)
-
-
-def trade_in(image_grid, count):
-    micro, items, own, width = image_grid.shape
-    cut = image_grid.reshape(micro, count, items // count, own, width).transpose(1, 0, 2, 3, 4)
-    got = lax.all_to_all(cut, "patch", split_axis=0, concat_axis=0, tiled=True)
-    return got.transpose(1, 2, 0, 3, 4).reshape(micro * items // count, count * own, width)
-
-
-def trade_back(grads, micro, count):
-    items, patches, width = grads.shape
-    cut = grads.reshape(micro, items // micro, count, patches // count, width)
-    got = lax.all_to_all(
-        cut.transpose(2, 0, 1, 3, 4), "patch", split_axis=0, concat_axis=0, tiled=True
-    )
-    got = got.transpose(1, 0, 2, 3, 4)
-    return got.reshape(micro, items // micro * count, patches // count, width)
-
-
-def on_device(
-    plan,
-    text_in,
-    image_grid,
-    image_cls,
-    text_lengths,
-    phrase_counts,
-    phrase_boxes,
-    cotangent,
-    *params,
-):
-    micro, width = text_in.shape[0], text_in.shape[2]
-    shards, vectors, ffn_bias = params[:7], params[7], params[8]
-    where = coords()
-    items = text_lengths.size
-    text, cot = text_in.reshape(-1, width), cotangent.reshape(-1, width)
-    lengths = text_lengths.reshape(-1)
-    dims = Dims(width, items, text.shape[0] // items)
-    rows, bias = gather_small(plan, where, vectors, ffn_bias)
-    rows = jnp.pad(rows, ((0, -rows.shape[0] % 8), (0, 0)))
-    own, give = pack_split(plan, where, shards)
-    units = pack_join(plan, where, own, send(give, plan.core()))
-    grid = trade_in(image_grid, plan.patch)
-    real = grid.shape[1]
-    pad = -(real + 1) % 16
-    patches = jnp.concatenate(
-        [
-            grid,
-            image_cls.reshape(items, 1, -1),
-            jnp.zeros((items, pad, grid.shape[2]), BF16),
-        ],
-        axis=1,
-    )
-    boxes = phrase_boxes.reshape((items,) + phrase_boxes.shape[2:])
-    mask = cross_mask(lengths, phrase_counts.reshape(-1), boxes, dims.length, pad)
-
-    weights = {}
-
-    def ready(g):
-        full = assemble(plan, GATHER[g], where, gathers[g].held)
-        for w, value in zip(GATHER[g], full):
-            weights[w] = value
-
-    gathers = [Gathering(plan, unit) for unit in units]
-    gathers[0].advance()
-    fence(gathers, [])
-    gathers[0].advance()
-    gathers[1].advance()
-    rows, patches, mask, bias = fence(gathers, [rows, patches, mask, bias])
-    gathers[0].advance()
-    gathers[1].advance()
-    gathers[2].advance()
-    fence(gathers, [])
-    gathers[1].advance()
-    gathers[2].advance()
-    gathers[3].advance()
-    ready(0)
-    qkv, probs, ctx, total_one = self_forward(dims, text, weights[QKV], weights[OUT], rows, lengths)
-    total_one = fence(gathers[1:], total_one)
-    gathers[2].advance()
-    gathers[3].advance()
-    ready(1)
-    hidden_one, query, kv, cross_probs, cross_ctx, total_two = cross_forward(
-        dims, total_one, patches, mask, weights[CQ], weights[CKV], weights[COUT], rows
-    )
-    total_two = fence(gathers[3:], total_two)
-    gathers[3].advance()
-    ready(2)
-    ready(3)
-    layer_out, hidden_two, act, slope, grad_three, low_three, sum_three = ffn_forward(
-        dims, total_two, cot, weights[FIN], weights[FOUT], rows, bias[None]
-    )
-    reduces = {}
-
-    def reduce(g, factors):
-        stacks = weight_grads(plan, REDUCE[g], where, factors)
-        reduces[g] = Reducing(plan, REDUCE[g], where, stacks)
-
-    def hold(values):
-        return fence(list(reduces.values()), values)
-
-    def go(*groups):
-        for g in groups:
-            reduces[g].advance()
-
-    reduce(3, [(act, low_three)])
-    grad_three = hold(grad_three)
-    go(3)
-    grad_pre, grad_two, low_two, sum_two, sum_pre = ffn_backward(
-        dims, grad_three, low_three, slope, total_two, weights[FIN], weights[FOUT], rows
-    )
-    grad_pre, grad_two = hold([grad_pre, grad_two])
-    go(3)
-    reduce(2, [(hidden_two, grad_pre)])
-    grad_two = hold(grad_two)
-    go(3, 2)
-    grad_query, grad_kv, grad_patch, grad_one, low_one, sum_one = cross_backward(
-        dims, grad_two, low_two, query, kv, cross_probs, total_one,
-        weights[CQ], weights[CKV], weights[COUT], rows,
-    )
-    grad_query, grad_one, grad_patch, low_one = hold([grad_query, grad_one, grad_patch, low_one])
-    go(3, 2)
-    flat_patches = patches.reshape(-1, patches.shape[2])
-    flat_kv = grad_kv.reshape(-1, grad_kv.shape[2])
-    reduce(
-        1,
-        [(hidden_one, grad_query), (flat_patches, flat_kv), (cross_ctx, low_two), (ctx, low_one)],
-    )
-    grad_one = hold(grad_one)
-    go(3, 2, 1)
-    grad_qkv, text_grad, sum_self = self_backward(
-        dims, grad_one, low_one, qkv, probs, weights[QKV], weights[OUT]
-    )
-    grad_qkv, sum_self = hold([grad_qkv, sum_self])
-    rows_grad = jnp.concatenate(
+    grid_ok = jnp.where(boxed[:, None, :], inside, 1.0).astype(BF16)
+    items, real = grid_ok.shape[:2]
+    own = jnp.ones((items, 1, length), BF16)
+    return jnp.concatenate([grid_ok, own, jnp.zeros((items, count - real - 1, length), BF16)], 1)
+
+
+def trade(pieces, parts):
+    return [pieces[0]] + [
+        lax.ppermute(pieces[k], "patch", [(i, i ^ k) for i in range(parts)])
+        for k in range(1, parts)
+    ]
+
+
+class Work:
+    def __init__(self, args, parts):
+        (self.text_in, self.image_grid, self.image_cls, lengths, counts, boxes, cot) = args
+        self.parts = parts
+        self.micro, d = self.text_in.shape[0], self.text_in.shape[2]
+        self.items = lengths.size
+        self.text, self.cot = self.text_in.reshape(-1, d), cot.reshape(-1, d)
+        self.lengths, self.counts = lengths.reshape(-1), counts.reshape(-1)
+        self.boxes = boxes.reshape((self.items,) + boxes.shape[2:])
+        self.dims = Dims(d, self.items, self.text.shape[0] // self.items)
+        self.turn = lax.axis_index("patch").astype(jnp.int32)
+        self.part, self.vis = self.image_grid.shape[2:]
+        self.each = self.items // self.micro
+        self.count = -(-(parts * self.part + 1) // 16) * 16
+        self.cls = self.image_cls.reshape(self.items, 1, self.vis)
+
+    def cut_grids(self):
+        return [
+            lax.dynamic_slice_in_dim(
+                self.image_grid, (self.turn ^ k) * self.each, self.each, axis=1
+            ).reshape(self.items, self.part, self.vis)
+            for k in range(self.parts)
+        ]
+
+    def mask(self):
+        boxes = self.boxes.reshape(self.items, -1, self.parts, self.part)
+        order = jnp.arange(self.parts, dtype=jnp.int32) ^ self.turn
+        boxes = jnp.take(boxes, order, axis=2).reshape(self.boxes.shape)
+        return cross_mask(self.lengths, self.counts, boxes, self.dims.length, self.count)
+
+    def finish(self, layer_out, text_grad, grids, cls, grads, rows_grad, bias_grad):
+        grid_grad = place_grids(self.turn.reshape(1), self.micro, grids)
+        return (
+            layer_out.reshape(self.text_in.shape),
+            text_grad.reshape(self.text_in.shape),
+            grid_grad,
+            cls.reshape(self.image_cls.shape),
+            *grads,
+            rows_grad,
+            bias_grad,
+        )
+
+
+def rows_of(sum_self, sum_attend, sum_one, sum_two, sum_three):
+    return jnp.concatenate(
         [
             sum_self[0:2],
             sum_one[2:3],
             sum_one[0:2],
-            sum_one[3:5],
+            sum_attend[0:2],
             sum_two[2:3],
             sum_two[0:2],
             sum_three[2:3],
             sum_three[0:2],
         ]
     )
-    rows_grad, bias_grad = reduce_small(plan, where, rows_grad, sum_pre[0])
+
+
+def on_device(plan, *args):
+    work, shards, vectors, ffn_bias = Work(args[:7], plan.patch), args[7:14], args[14], args[15]
+    dims, where, parts = work.dims, coords(), plan.patch
+    weights = {}
+
+    own, give = pack_split(plan, where, shards)
+    units = pack_join(plan, where, own, send(give, plan.core()))
+    gathers = [Gathering(plan, unit) for unit in units]
+    grids = work.cut_grids()
+
+    def ready(g):
+        full = assemble(plan, GATHER[g], where, gathers[g].held)
+        for w, value in zip(GATHER[g], full):
+            weights[w] = value
+
+    def step(*groups):
+        for g in groups:
+            gathers[g].advance()
+
+    step(0)
+    grids = fence(gathers, grids)
+    grids = trade(grids, parts)
+    rows, bias = gather_small(plan, where, vectors, ffn_bias)
+    rows = jnp.pad(rows, ((0, -rows.shape[0] % 8), (0, 0)))
+    step(0, 1)
+    rows, bias = fence(gathers, [rows, bias])
+    step(0, 2)
+    fence(gathers, [])
+    step(1, 3)
+    ready(0)
+    qkv, probs, ctx, total_one = self_forward(
+        dims, work.text, weights[QKV], weights[OUT], rows, work.lengths
+    )
+    mask = work.mask()
+    total_one, grids, mask = fence(gathers[1:], [total_one, grids, mask])
+    step(1)
+    fence(gathers[1:], [])
+    step(2, 3)
+    ready(1)
+    hidden_one, query, kv, cross_probs, cross_ctx, total_two, patches = cross_forward(
+        dims, total_one, grids, work.cls, mask, weights[CQ], weights[CKV], weights[COUT], rows
+    )
+    total_two = fence(gathers[2:], total_two)
+    step(2, 3)
+    total_two = fence(gathers[2:], total_two)
+    ready(2)
+    ready(3)
+    layer_out, hidden_two, act, slope, grad_three, low_three, sum_three = ffn_forward(
+        dims, total_two, work.cot, weights[FIN], weights[FOUT], rows, bias[None]
+    )
+
+    reduces = {}
+
+    def reduce(g, factors):
+        stacks = weight_grads(plan, REDUCE[g], where, factors)
+        reduces[g] = Reducing(plan, REDUCE[g], where, stacks)
+
+    def hold(*values):
+        return fence(list(reduces.values()), list(values))
+
+    def go(*groups):
+        for g in groups:
+            reduces[g].advance()
+
+    reduce(3, [(act, low_three)])
+    (grad_three,) = hold(grad_three)
+    go(3)
+    grad_pre, grad_two, low_two, sum_two, sum_pre = ffn_backward(
+        dims, grad_three, low_three, slope, total_two, weights[FIN], weights[FOUT], rows
+    )
+    grad_pre, grad_two, low_two = hold(grad_pre, grad_two, low_two)
+    go(3)
+    reduce(2, [(hidden_two, grad_pre)])
+    (low_two,) = hold(low_two)
+    go(3, 2)
+    grad_query, grad_kv, sum_attend = cross_attend_back(
+        dims, low_two, query, kv, cross_probs, weights[COUT]
+    )
+    grad_query, grad_kv = hold(grad_query, grad_kv)
+    go(3, 2)
+    flat_kv = grad_kv.reshape(-1, grad_kv.shape[2])
+    reduce(
+        1,
+        [
+            (hidden_one, grad_query),
+            (patches.reshape(-1, work.vis), flat_kv),
+            (cross_ctx, low_two),
+        ],
+    )
+    grad_query, grad_kv = hold(grad_query, grad_kv)
     go(3, 2, 1)
-    reduce(0, [(text, grad_qkv)])
-    hold([])
-    go(2, 1, 0)
-    go(2)
-    grid_grad = trade_back(grad_patch[:, :real], micro, plan.patch).astype(F32)
-    grid_grad = hold(grid_grad)
-    go(1, 0)
-    hold([])
-    go(1, 0)
-    go(1)
-    hold([])
-    go(0)
-    hold([])
+    *grids, cls, grad_one, low_one, sum_one = cross_project_back(
+        dims, grad_two, grad_query, grad_kv, total_one, weights[CQ], weights[CKV], rows, parts, work.part
+    )
+    low_one, *grids = hold(low_one, *grids)
+    go(3, 2, 1)
+    grids = trade(grids, parts)
+    grad_qkv, sum_self = self_attend_back(dims, low_one, qkv, probs, weights[OUT])
+    grad_qkv, sum_self = hold(grad_qkv, sum_self)
+    go(2, 1)
+    reduce(0, [(work.text, grad_qkv), (ctx, low_one)])
+    reduces["small"] = ReducingSmall(
+        plan, where, rows_of(sum_self, sum_attend, sum_one, sum_two, sum_three), sum_pre[0]
+    )
+    grad_qkv, *grids = hold(grad_qkv, *grids)
+    go(2, 1, 0, "small")
+    text_grad = self_project_back(dims, grad_one, grad_qkv, weights[QKV])
+    hold()
+    go(1, 0, "small")
+    hold()
+    go(1, 0, "small")
+    hold()
+    go(0, "small")
+    hold()
     go(0)
     go(0)
     grads = [None] * 7
     for g, group in enumerate(REDUCE):
         for w, value in zip(group, reduces[g].held):
             grads[w] = value
-    cls_grad = grad_patch[:, real].astype(F32).reshape(image_cls.shape)
-    return (
-        layer_out.reshape(text_in.shape),
-        text_grad.reshape(text_in.shape),
-        grid_grad,
-        cls_grad,
-        *grads,
-        rows_grad,
-        bias_grad,
-    )
-
-
-def on_device_plain(
-    plan,
-    text_in,
-    image_grid,
-    image_cls,
-    text_lengths,
-    phrase_counts,
-    phrase_boxes,
-    cotangent,
-    *params,
-):
-    micro, width = text_in.shape[0], text_in.shape[2]
-    shards, vectors, ffn_bias = params[:7], params[7], params[8]
-    items = text_lengths.size
-    text, cot = text_in.reshape(-1, width), cotangent.reshape(-1, width)
-    lengths = text_lengths.reshape(-1)
-    dims = Dims(width, items, text.shape[0] // items)
-    weights, rows, bias = fetch_plain(shards, vectors, ffn_bias)
+    return work.finish(layer_out, text_grad, grids, cls, grads, *reduces["small"].result())
+
+
+def on_device_plain(plan, *args):
+    work, parts = Work(args[:7], plan.patch), plan.patch
+    dims = work.dims
+    weights, rows, bias = fetch_plain(args[7:14], args[14], args[15])
     rows = jnp.pad(rows, ((0, -rows.shape[0] % 8), (0, 0)))
-    grid = trade_in(image_grid, plan.patch)
-    real = grid.shape[1]
-    pad = -(real + 1) % 16
-    patches = jnp.concatenate(
-        [
-            grid,
-            image_cls.reshape(items, 1, -1),
-            jnp.zeros((items, pad, grid.shape[2]), BF16),
-        ],
-        axis=1,
-    )
-    boxes = phrase_boxes.reshape((items,) + phrase_boxes.shape[2:])
-    mask = cross_mask(lengths, phrase_counts.reshape(-1), boxes, dims.length, pad)
-
-    qkv, probs, ctx, total_one = self_forward(dims, text, weights[QKV], weights[OUT], rows, lengths)
-    hidden_one, query, kv, cross_probs, cross_ctx, total_two = cross_forward(
-        dims, total_one, patches, mask, weights[CQ], weights[CKV], weights[COUT], rows
+    grids = trade(work.cut_grids(), parts)
+    qkv, probs, ctx, total_one = self_forward(
+        dims, work.text, weights[QKV], weights[OUT], rows, work.lengths
+    )
+    hidden_one, query, kv, cross_probs, cross_ctx, total_two, patches = cross_forward(
+        dims, total_one, grids, work.cls, work.mask(), weights[CQ], weights[CKV], weights[COUT], rows
     )
     layer_out, hidden_two, act, slope, grad_three, low_three, sum_three = ffn_forward(
-        dims, total_two, cot, weights[FIN], weights[FOUT], rows, bias[None]
-    )
-    grads = [None] * 7
-
-    def reduce(g, factors):
-        for w, (a, b) in zip(REDUCE[g], factors):
-            grads[w] = reduce_plain(dot_l(a, b).astype(BF16))
-
-    reduce(3, [(act, low_three)])
+        dims, total_two, work.cot, weights[FIN], weights[FOUT], rows, bias[None]
+    )
     grad_pre, grad_two, low_two, sum_two, sum_pre = ffn_backward(
         dims, grad_three, low_three, slope, total_two, weights[FIN], weights[FOUT], rows
     )
-    reduce(2, [(hidden_two, grad_pre)])
-    grad_query, grad_kv, grad_patch, grad_one, low_one, sum_one = cross_backward(
-        dims, grad_two, low_two, query, kv, cross_probs, total_one,
-        weights[CQ], weights[CKV], weights[COUT], rows,
-    )
-    flat_patches = patches.reshape(-1, patches.shape[2])
+    grad_query, grad_kv, sum_attend = cross_attend_back(
+        dims, low_two, query, kv, cross_probs, weights[COUT]
+    )
+    *grids, cls, grad_one, low_one, sum_one = cross_project_back(
+        dims, grad_two, grad_query, grad_kv, total_one, weights[CQ], weights[CKV], rows, parts, work.part
+    )
+    grad_qkv, sum_self = self_attend_back(dims, low_one, qkv, probs, weights[OUT])
+    text_grad = self_project_back(dims, grad_one, grad_qkv, weights[QKV])
     flat_kv = grad_kv.reshape(-1, grad_kv.shape[2])
-    reduce(
-        1,
-        [(hidden_one, grad_query), (flat_patches, flat_kv), (cross_ctx, low_two), (ctx, low_one)],
-    )
-    grad_qkv, text_grad, sum_self = self_backward(
-        dims, grad_one, low_one, qkv, probs, weights[QKV], weights[OUT]
-    )
-    reduce(0, [(text, grad_qkv)])
-    rows_grad = jnp.concatenate(
-        [
-            sum_self[0:2],
-            sum_one[2:3],
-            sum_one[0:2],
-            sum_one[3:5],
-            sum_two[2:3],
-            sum_two[0:2],
-            sum_three[2:3],
-            sum_three[0:2],
-        ]
-    )
-    rows_grad, bias_grad = reduce_small_plain(rows_grad, sum_pre[0])
-    cls_grad = grad_patch[:, real].astype(F32).reshape(image_cls.shape)
-    grid_grad = trade_back(grad_patch[:, :real], micro, plan.patch).astype(F32)
-    return (
-        layer_out.reshape(text_in.shape),
-        text_grad.reshape(text_in.shape),
-        grid_grad,
-        cls_grad,
-        *grads,
-        rows_grad,
-        bias_grad,
-    )
+    factors = [
+        (work.text, grad_qkv),
+        (ctx, low_one),
+        (hidden_one, grad_query),
+        (patches.reshape(-1, work.vis), flat_kv),
+        (cross_ctx, low_two),
+        (hidden_two, grad_pre),
+        (act, low_three),
+    ]
+    grads = [reduce_plain(dot_l(a, b).astype(BF16)) for a, b in factors]
+    small = reduce_small_plain(
+        rows_of(sum_self, sum_attend, sum_one, sum_two, sum_three), sum_pre[0]
+    )
+    return work.finish(layer_out, text_grad, trade(grids, parts), cls, grads, *small)
 
 
 def solution(mesh):

time: 573 us -> 568 us (level)
  other arithmetic: 53.4 us -> 7.37 us
  Pallas kernels: 256 us -> 291 us
  waiting for transfers between devices: 98.9 us -> 107 us
  starting transfers between devices: 88.6 us -> 80.6 us
  local copies, waits for them, and re-layouts: 63.7 us -> 70.2 us
    pallas_call x0 -> x12, Pallas kernels: none -> 47.8 us  [add_low(): pl.pallas_call(body, grid=(shape[0],), out_shape=(jax.ShapeDtypeStruct(sh...]
    convert_element_type x29 -> x0, other arithmetic: 41.9 us -> none  [the longest x27 38.1 us: add_low(): return (one.astype(F32) + two.astype(F32)).astype(BF16)]
    ppermute x0 -> x6, waiting for transfers between devices: none -> 18.6 us  [trade(): lax.ppermute(pieces[k], 'patch', [(i, i ^ k) for i in range(parts)])]
    optimization_barrier x0 -> x9, local copies, waits for them, and re-layouts: none -> 17 us  [fence(): values, held = jax.tree.unflatten(tree, lax.optimization_barrier(flat))]
    reshape x10 -> x8, local copies, waits for them, and re-layouts: 18.6 us -> 4.31 us  [the longest x3 2.95 us: cut_grids(): return [lax.dynamic_slice_in_dim(self.image_grid, (self.turn ^ k) * self....]
    pallas_call x6 -> x9, Pallas kernels: 162 us -> 149 us  [call(): pl.pallas_call(body, grid=(steps,), out_shape=out_shape, in_specs=[spec f...]
    ppermute x95, waiting for transfers between devices: 98.9 us -> 88.9 us  [send(): return lax.ppermute(value, AXES, perm)]
    all_to_all x2 -> x0, starting transfers between devices: 9.14 us -> none  [the longest x1 4.62 us: trade_in(): got = lax.all_to_all(cut, 'patch', split_axis=0, concat_axis=0, tiled=True)]
  transfers between devices with their start and end apart: 97 -> 101, of which waited for: 21 -> 19; matrix products, arithmetic and copies ran while one was open for 16% -> 11% of each run, Pallas kernels for 36% -> 36%
where the time goes in v3:
time: 568 us; the launch traced here: 559 us
  Pallas kernels  291 us (51%)
  waiting for transfers between devices  107 us (19%)
  starting transfers between devices  80.6 us (14%)
  local copies, waits for them, and re-layouts  70.2 us (12%)
  other arithmetic  7.37 us (1%)
    pallas_call x9, Pallas kernels, call(): pl.pallas_call(body, grid=(steps,), out_shape=out_shape, in_specs=[spec f...  149 us
    ppermute x95, waiting for transfers between devices, send(): return lax.ppermute(value, AXES, perm)  88.9 us
    ppermute x95, starting transfers between devices, send(): return lax.ppermute(value, AXES, perm)  76.8 us
    pallas_call x4, Pallas kernels, weight_grads(): pl.pallas_call(body, out_shape=(shape,) * 8, in_specs=[SMEM_SPEC] + [VMEM...  53.7 us
    pallas_call x12, Pallas kernels, add_low(): pl.pallas_call(body, grid=(shape[0],), out_shape=(jax.ShapeDtypeStruct(sh...  47.8 us
    unnamed x143, local copies, waits for them, and re-layouts  21.4 us
    pallas_call x4, Pallas kernels, assemble(): pl.pallas_call(body, out_shape=tuple((jax.ShapeDtypeStruct(plan.full[w],...  20.2 us
    ppermute x6, waiting for transfers between devices, trade(): lax.ppermute(pieces[k], 'patch', [(i, i ^ k) for i in range(parts)])  18.6 us
  transfers between devices with their start and end apart: 101, of which 19 were waited for; matrix products, arithmetic and copies ran while one was open for 11% of the time, Pallas kernels for 36%

profile of v3, /device:TPU:0, one launch (start us, length us, event | category | flops | bytes accessed | tf_op | source)
XLA Modules:
  0.0 558.8 jit_solution(4185915293333730877)
XLA Ops:
  2.2 2.9 collective-permute-start
  9.7 4.4 constant_dynamic-slice_fusion.1
  16.4 3.6 collective-permute-start.7
  39.7 3.4 collective-permute-done.13
  47.0 7.4 %collective-permute-done.12 = bf16[224,384]{1,0:T(8,128)(2,1)S(1)} collective-permute-done((bf16[224,384]{1,0:T(8,128)(2,1)S(1)}, bf16[224,384]{1,0:T(8,128)(2,1)S(1)}, u32[]{:S(2)}, u32[]{:S(2)}) %collective-permute-start.12) | collective-permute-done | bytes 172064 | tf_op jit(solution)/shard_map/ppermute | solution.py:63
  65.0 6.6 %collective-permute-done.19 = bf16[192,384]{1,0:T(8,128)(2,1)} collective-permute-done((bf16[192,384]{1,0:T(8,128)(2,1)}, bf16[192,384]{1,0:T(8,128)(2,1)}, u32[]{:S(2)}, u32[]{:S(2)}) %collective-permute-start.19) | collective-permute-done | bytes 147488 | tf_op jit(solution)/shard_map/ppermute | solution.py:63
  78.5 9.6 %collective-permute-done.22 = bf16[8,36,1024]{2,0,1:T(8,128)(2,1)} collective-permute-done((bf16[8,36,1024]{2,0,1:T(8,128)(2,1)}, bf16[8,36,1024]{2,0,1:T(8,128)(2,1)}, u32[]{:S(2)}, u32[]{:S(2)}) %collective-permute-start.22) | collective-permute-done | bytes 589856 | tf_op jit(solution)/shard_map/ppermute | solution.py:1002
  89.1 4.9 assemble.4
  94.0 6.0 %collective-permute-done.23 = bf16[8,36,1024]{2,0,1:T(8,128)(2,1)} collective-permute-done((bf16[8,36,1024]{2,0,1:T(8,128)(2,1)}, bf16[8,36,1024]{2,0,1:T(8,128)(2,1)}, u32[]{:S(2)}, u32[]{:S(2)}) %collective-permute-start.23) | collective-permute-done | bytes 589856 | tf_op jit(solution)/shard_map/ppermute | solution.py:1002
  100.9 14.3 %self_forward.1 = (bf16[1024,2304]{1,0:T(8,128)(2,1)}, bf16[8,6,128,256]{3,2,1,0:T(8,128)(2,1)}, bf16[1024,768]{1,0:T(8,128)(2,1)}, f32[1024,768]{1,0:T(8,128)}) custom-call(s32[8]{0:T(128)} %copy-done.66, bf16[1024,768]{1,0:T(8,128)(2,1)} %bitcast.125, bf16[768,2304]{1,0:T(8,128)(2,1)} %get-tuple-element.418.wqkv_ref, ...), custom_call_target="tpu_custom_call" | custom-call | flops 7247757312 | bytes 18923552 | tf_op jit(solution)/shard_map/self_forward/pallas_call | solution.py:500
  117.0 9.6 %collective-permute-done.30.refs_3_ = bf16[4,224,384]{2,1,0:T(8,128)(2,1)S(1)} collective-permute-done((bf16[4,224,384]{2,1,0:T(8,128)(2,1)}, bf16[4,224,384]{2,1,0:T(8,128)(2,1)S(1)}, u32[]{:S(2)}, u32[]{:S(2)}) %collective-permute-start.30) | collective-permute-done | bytes 688160 | tf_op jit(solution)/shard_map/ppermute | solution.py:63
  142.6 5.5 assemble.5
  149.2 23.0 %cross_forward.1 = (bf16[1024,768]{1,0:T(8,128)(2,1)}, bf16[1024,768]{1,0:T(8,128)(2,1)}, bf16[8,160,1536]{2,1,0:T(8,128)(2,1)}, bf16[8,6,160,256]{3,2,1,0:T(8,1...) custom-call(f32[1024,768]{1,0:T(8,128)} %get-tuple-element.435.tot_ref, ...), custom_call_target="tpu_custom_call" | custom-call | flops 8858370048 | bytes 29753344 | tf_op jit(solution)/shard_map/cross_forward/pallas_call | solution.py:500
  175.1 7.3 %collective-permute-done.40.refs_3_ = bf16[4,192,384]{2,1,0:T(8,128)(2,1)S(1)} collective-permute-done((bf16[4,192,384]{2,1,0:T(8,128)(2,1)S(1)}, bf16[4,192,384]{2,1,0:T(8,128)(2,1)S(1)}, u32[]{:S(2)}, u32[]{:S(2)}) %collective-permute-start.40) | collective-permute-done | bytes 589856 | tf_op jit(solution)/shard_map/ppermute | solution.py:63
  182.4 6.3 %collective-permute-done.44.refs_3_ = bf16[4,192,384]{2,1,0:T(8,128)(2,1)S(1)} collective-permute-done((bf16[4,192,384]{2,1,0:T(8,128)(2,1)}, bf16[4,192,384]{2,1,0:T(8,128)(2,1)S(1)}, u32[]{:S(2)}, u32[]{:S(2)}) %collective-permute-start.44) | collective-permute-done | bytes 589856 | tf_op jit(solution)/shard_map/ppermute | solution.py:63
  190.8 4.9 assemble.6.win_ref
  195.8 4.9 assemble.7.wout_ref
  200.6 30.3 %ffn_forward.1 = (f32[1024,768]{1,0:T(8,128)}, bf16[1024,768]{1,0:T(8,128)(2,1)}, bf16[1024,3072]{1,0:T(8,128)(2,1)}, bf16[1024,3072]{1,0:T(8,128)(2,1)}, f32[10...) custom-call(f32[1024,768]{1,0:T(8,128)} %get-tuple-element.482.tot_ref, bf16[1024,768]{1,0:T(8,128)(2,1)} %bitcast.124, ...), custom_call_target="tpu_custom_call" | custom-call | flops 9663676416 | bytes 36261888 | tf_op jit(solution)/shard_map/ffn_forward/pallas_call | solution.py:500
  230.9 12.2 %weight_grads.4 = (bf16[4,192,384]{2,1,0:T(8,128)(2,1)}, bf16[4,192,384]{2,1,0:T(8,128)(2,1)}, bf16[4,192,384]{2,1,0:T(8,128)(2,1)}, bf16[4,192,384]{2,1,0:T(8,1...) custom-call(s32[4]{0:T(128)} %pad_add_fusion.where_ref, ...), custom_call_target="tpu_custom_call" | custom-call | flops 4831838208 | bytes 12582912 | tf_op jit(solution)/shard_map/weight_grads/pallas_call | solution.py:965
  244.1 18.3 %ffn_backward.1 = (bf16[1024,3072]{1,0:T(8,128)(2,1)}, f32[1024,768]{1,0:T(8,128)}, bf16[1024,768]{1,0:T(8,128)(2,1)}, f32[8,768]{1,0:T(8,128)}, f32[8,3072]{1,0:T(8,128)}) custom-call(f32[1024,768]{1,0:T(8,128)} %get-tuple-element.512.g_ref, bf16[1024,768]{1,0:T(8,128)(2,1)} %get-tuple-element.503.refs_1_.glow_ref, ...), custom_call_target="tpu_custom_call" | custom-call | flops 9663676416 | bytes 34775040 | tf_op jit(solution)/shard_map/ffn_backward/pallas_call | solution.py:500
  263.6 4.6 add_low.12
  270.3 12.4 %weight_grads.5 = (bf16[4,192,384]{2,1,0:T(8,128)(2,1)}, bf16[4,192,384]{2,1,0:T(8,128)(2,1)}, bf16[4,192,384]{2,1,0:T(8,128)(2,1)}, bf16[4,192,384]{2,1,0:T(8,1...) custom-call(s32[4]{0:T(128)} %pad_add_fusion.where_ref, ...), custom_call_target="tpu_custom_call" | custom-call | flops 4831838208 | bytes 12582912 | tf_op jit(solution)/shard_map/weight_grads/pallas_call | solution.py:965
  285.5 3.7 add_low.13
  291.2 17.3 %cross_attend_back.1 = (bf16[1024,768]{1,0:T(8,128)(2,1)}, bf16[8,160,1536]{2,1,0:T(8,128)(2,1)}, f32[8,768]{1,0:T(8,128)}) custom-call(bf16[1024,768]{1,0:T(8,128)(2,1)} %get-tuple-element.549.glow_ref.refs_5_, bf16[1024,768]{1,0:T(8,128)(2,1)} %get-tuple-element.550.q_ref, bf16[8,160,1536]{2,1,0:T(8,128)(2,1)} %get-tuple-element.551.kv_ref, ...), custom_call_target="tpu_custom_call" | custom-call | flops 4831838208 | bytes 17719296 | tf_op jit(solution)/shard_map/cross_attend_back/pallas_call | solution.py:500
  308.6 3.8 add_low.14
  314.3 2.8 collective-permute-start.61
  319.5 4.7 add_low.15
  326.3 16.3 %weight_grads.6 = (bf16[4,224,384]{2,1,0:T(8,128)(2,1)}, bf16[4,224,384]{2,1,0:T(8,128)(2,1)}, bf16[4,224,384]{2,1,0:T(8,128)(2,1)}, bf16[4,224,384]{2,1,0:T(8,1...) custom-call(s32[4]{0:T(128)} %pad_add_fusion.where_ref, ...), custom_call_target="tpu_custom_call" | custom-call | flops 6442450944 | bytes 18350080 | tf_op jit(solution)/shard_map/weight_grads/pallas_call | solution.py:965
  346.2 4.1 add_low.16
  351.3 15.8 %cross_project_back.1 = (bf16[8,36,1024]{2,1,0:T(8,128)(2,1)}, bf16[8,36,1024]{2,1,0:T(8,128)(2,1)}, bf16[8,36,1024]{2,1,0:T(8,128)(2,1)}, bf16[8,36,1024]{2,1,0...) custom-call(f32[1024,768]{1,0:T(8,128)} %get-tuple-element.525.g_ref, ...), custom_call_target="tpu_custom_call" | custom-call | flops 5234491392 | bytes 23306240 | tf_op jit(solution)/shard_map/cross_project_back/pallas_call | solution.py:500
  368.3 4.7 add_low.18
  375.1 3.4 add_low.17
  384.2 16.7 %self_attend_back.1 = (bf16[1024,2304]{1,0:T(8,128)(2,1)}, f32[8,768]{1,0:T(8,128)}) custom-call(bf16[1024,768]{1,0:T(8,128)(2,1)} %get-tuple-element.624.glow_ref.refs_3_, bf16[1024,2304]{1,0:T(8,128)(2,1)} %get-tuple-element.625.qkv_ref, bf16[8,6,128,256]{3,2,1,0:T(8,128)(2,1)} %get-tuple-element.626.prob_ref, bf16[768,768]{1,0:T(8,128)(2,1)} %get-tuple-element.419.wout_ref), custom_call_target="tpu_custom_call" | custom-call | flops 4831838208 | bytes 15360000 | tf_op jit(solution)/shard_map/self_attend_back/pallas_call | solution.py:500
  403.9 3.9 add_low.19
  424.7 12.8 %weight_grads.7 = (bf16[4,192,384]{2,1,0:T(8,128)(2,1)}, bf16[4,192,384]{2,1,0:T(8,128)(2,1)}, bf16[4,192,384]{2,1,0:T(8,128)(2,1)}, bf16[4,192,384]{2,1,0:T(8,1...) custom-call(s32[4]{0:T(128)} %pad_add_fusion.where_ref, ...), custom_call_target="tpu_custom_call" | custom-call | flops 4831838208 | bytes 14155776 | tf_op jit(solution)/shard_map/weight_grads/pallas_call | solution.py:965
  438.4 3.0 collective-permute-done.76
  443.3 3.5 add_low.20
  449.4 8.0 %collective-permute-done.82.refs_3_ = bf16[224,384]{1,0:T(8,128)(2,1)} collective-permute-done((bf16[224,384]{1,0:T(8,128)(2,1)S(1)}, bf16[224,384]{1,0:T(8,128)(2,1)}, u32[]{:S(2)}, u32[]{:S(2)}) %collective-permute-start.82) | collective-permute-done | bytes 172064 | tf_op jit(solution)/shard_map/ppermute | solution.py:63
  457.6 8.9 %collective-permute-done.81.refs_2_ = bf16[224,384]{1,0:T(8,128)(2,1)} collective-permute-done((bf16[224,384]{1,0:T(8,128)(2,1)S(1)}, bf16[224,384]{1,0:T(8,128)(2,1)}, u32[]{:S(2)}, u32[]{:S(2)}) %collective-permute-start.81) | collective-permute-done | bytes 172064 | tf_op jit(solution)/shard_map/ppermute | solution.py:63
  473.8 4.4 add_low.21
  483.7 12.2 %collective-permute-done.91 = f32[104,128]{1,0:T(8,128)S(1)} collective-permute-done((f32[104,128]{1,0:T(8,128)S(1)}, f32[104,128]{1,0:T(8,128)S(1)}, u32[]{:S(2)}, u32[]{:S(2)}) %collective-permute-start.91) | collective-permute-done | bytes 53280 | tf_op jit(solution)/shard_map/ppermute | solution.py:63
  496.9 3.7 add_low.22
  505.3 6.0 %collective-permute-done.93 = f32[104,128]{1,0:T(8,128)S(1)} collective-permute-done((f32[104,128]{1,0:T(8,128)S(1)}, f32[104,128]{1,0:T(8,128)S(1)}, u32[]{:S(2)}, u32[]{:S(2)}) %collective-permute-start.93) | collective-permute-done | bytes 53280 | tf_op jit(solution)/shard_map/ppermute | solution.py:63
  514.7 3.4 add_low.23
  519.9 2.8 collective-permute-start.96
  525.3 9.1 %self_project_back.1 = f32[1024,768]{1,0:T(8,128)} custom-call(f32[1024,768]{1,0:T(8,128)} %get-tuple-element.598.g_ref, bf16[1024,2304]{1,0:T(8,128)(2,1)} %get-tuple-element.678.refs_1_.gqkv_ref, bf16[768,2304]{1,0:T(8,128)(2,1)} %get-tuple-element.418.wqkv_ref), custom_call_target="tpu_custom_call" | custom-call | flops 3623878656 | bytes 14548992 | tf_op jit(solution)/shard_map/self_project_back/pallas_call | solution.py:500
  539.1 3.7 place_grids.1
  542.8 7.5 %copy.69 = f32[2,16,36,1024]{3,1,2,0:T(8,128)} copy(f32[2,16,36,1024]{3,2,1,0:T(8,128)} %place_grids.1) | data formatting | bytes 9437184
  (423 shorter events, 168.3 us)
Async XLA Ops:
  2.2 25.0 %collective-permute-start = (bf16[16,128]{1,0:T(8,128)(2,1)S(1)}, bf16[16,128]{1,0:T(8,128)(2,1)S(1)}, u32[]{:S(2)}, u32[]{:S(2)}) collective-permute-start(bf16[16,128]{1,0:T(8,128)(2,1)S(1)} %get-tuple-element.823), channel_id=1, source_target_pairs={{0,4},{1,5},{2,6},{3,7},{4,0},{5,1},{6,2},{7,3},{8,12},{9,13},{10,... | collective-permute-start | bytes 12296 | tf_op jit(solution)/shard_map/ppermute | solution.py:63
  34.0 20.4 %collective-permute-start.10 = (bf16[4,192,384]{2,1,0:T(8,128)(2,1)S(1)}, bf16[4,192,384]{2,1,0:T(8,128)(2,1)S(1)}, u32[]{:S(2)}, u32[]{:S(2)}) collective-permute-start(bf16[4,192,384]{2,1,0:T(8,128)(2,1)S(1)} %pad_maximum_fusion.1.refs_0_), channel_id=1, source_target_pairs={{0,1},{1,0},{2,3},{3,2},{4,5},{5,4},{6,7},{7,6},{8,9},{9,8},{10,11... | collective-permute-start | bytes 1769480 | tf_op jit(solution)/shard_map/ppermute | solution.py:63
  34.1 20.4 %collective-permute-start.9 = (bf16[4,192,384]{2,1,0:T(8,128)(2,1)S(1)}, bf16[4,192,384]{2,1,0:T(8,128)(2,1)S(1)}, u32[]{:S(2)}, u32[]{:S(2)}) collective-permute-start(bf16[4,192,384]{2,1,0:T(8,128)(2,1)S(1)} %pad_maximum_fusion.1.refs_0_), channel_id=1, source_target_pairs={{0,2},{1,5},{2,0},{3,7},{4,6},{5,1},{6,4},{7,3},{8,10},{9,13},{10,... | collective-permute-start | bytes 1769480 | tf_op jit(solution)/shard_map/ppermute | solution.py:63
  35.7 19.5 %collective-permute-start.8 = (bf16[4,192,384]{2,1,0:T(8,128)(2,1)S(1)}, bf16[4,192,384]{2,1,0:T(8,128)(2,1)S(1)}, u32[]{:S(2)}, u32[]{:S(2)}) collective-permute-start(bf16[4,192,384]{2,1,0:T(8,128)(2,1)S(1)} %pad_maximum_fusion.1.refs_0_), channel_id=1, source_target_pairs={{0,4},{1,3},{2,6},{3,1},{4,0},{5,7},{6,2},{7,5},{8,12},{9,11},{10,... | collective-permute-start | bytes 1769480 | tf_op jit(solution)/shard_map/ppermute | solution.py:63
  73.8 26.2 %collective-permute-start.23 = (bf16[8,36,1024]{2,0,1:T(8,128)(2,1)}, bf16[8,36,1024]{2,0,1:T(8,128)(2,1)}, u32[]{:S(2)}, u32[]{:S(2)}) collective-permute-start(bf16[8,36,1024]{2,0,1:T(8,128)(2,1)} %reshape.372), channel_id=1, source_target_pairs={{0,3},{1,2},{2,1},{3,0},{4,7},{5,6},{6,5},{7,4},{8,11},{9,10},{10,... | collective-permute-start | bytes 1769480 | tf_op jit(solution)/shard_map/ppermute | solution.py:1002
  76.4 38.9 %collective-permute-start.26 = (bf16[4,224,384]{2,1,0:T(8,128)(2,1)S(1)}, bf16[4,224,384]{2,1,0:T(8,128)(2,1)S(1)}, u32[]{:S(2)}, u32[]{:S(2)}) collective-permute-start(bf16[4,224,384]{2,1,0:T(8,128)(2,1)S(1)} %pad_maximum_fusion.refs_0_), channel_id=1, source_target_pairs={{0,1},{1,0},{2,3},{3,2},{4,5},{5,4},{6,7},{7,6},{8,9},{9,8},{10,11... | collective-permute-start | bytes 2064392 | tf_op jit(solution)/shard_map/ppermute | solution.py:63
  76.8 38.6 %collective-permute-start.25 = (bf16[4,224,384]{2,1,0:T(8,128)(2,1)S(1)}, bf16[4,224,384]{2,1,0:T(8,128)(2,1)}, u32[]{:S(2)}, u32[]{:S(2)}) collective-permute-start(bf16[4,224,384]{2,1,0:T(8,128)(2,1)S(1)} %pad_maximum_fusion.refs_0_), channel_id=1, source_target_pairs={{0,2},{1,5},{2,0},{3,7},{4,6},{5,1},{6,4},{7,3},{8,10},{9,13},{10,... | collective-permute-start | bytes 2064392 | tf_op jit(solution)/shard_map/ppermute | solution.py:63
  77.7 37.7 %collective-permute-start.24 = (bf16[4,224,384]{2,1,0:T(8,128)(2,1)S(1)}, bf16[4,224,384]{2,1,0:T(8,128)(2,1)}, u32[]{:S(2)}, u32[]{:S(2)}) collective-permute-start(bf16[4,224,384]{2,1,0:T(8,128)(2,1)S(1)} %pad_maximum_fusion.refs_0_), channel_id=1, source_target_pairs={{0,4},{1,3},{2,6},{3,1},{4,0},{5,7},{6,2},{7,5},{8,12},{9,11},{10,... | collective-permute-start | bytes 2064392 | tf_op jit(solution)/shard_map/ppermute | solution.py:63
  138.4 33.9 %collective-permute-start.38 = (bf16[4,192,384]{2,1,0:T(8,128)(2,1)S(1)}, bf16[4,192,384]{2,1,0:T(8,128)(2,1)}, u32[]{:S(2)}, u32[]{:S(2)}) collective-permute-start(bf16[4,192,384]{2,1,0:T(8,128)(2,1)S(1)} %pad_maximum_fusion.3.refs_0_), channel_id=1, source_target_pairs={{0,2},{1,5},{2,0},{3,7},{4,6},{5,1},{6,4},{7,3},{8,10},{9,13},{10,... | collective-permute-start | bytes 1769480 | tf_op jit(solution)/shard_map/ppermute | solution.py:63
  139.2 33.1 %collective-permute-start.37 = (bf16[4,192,384]{2,1,0:T(8,128)(2,1)S(1)}, bf16[4,192,384]{2,1,0:T(8,128)(2,1)}, u32[]{:S(2)}, u32[]{:S(2)}) collective-permute-start(bf16[4,192,384]{2,1,0:T(8,128)(2,1)S(1)} %pad_maximum_fusion.3.refs_0_), channel_id=1, source_target_pairs={{0,4},{1,3},{2,6},{3,1},{4,0},{5,7},{6,2},{7,5},{8,12},{9,11},{10,... | collective-permute-start | bytes 1769480 | tf_op jit(solution)/shard_map/ppermute | solution.py:63
  141.4 30.9 %collective-permute-start.36 = (bf16[4,192,384]{2,1,0:T(8,128)(2,1)S(1)}, bf16[4,192,384]{2,1,0:T(8,128)(2,1)}, u32[]{:S(2)}, u32[]{:S(2)}) collective-permute-start(bf16[4,192,384]{2,1,0:T(8,128)(2,1)S(1)} %pad_maximum_fusion.2.refs_0_), channel_id=1, source_target_pairs={{0,1},{1,0},{2,3},{3,2},{4,5},{5,4},{6,7},{7,6},{8,9},{9,8},{10,11... | collective-permute-start | bytes 1769480 | tf_op jit(solution)/shard_map/ppermute | solution.py:63
  141.4 30.9 %collective-permute-start.35 = (bf16[4,192,384]{2,1,0:T(8,128)(2,1)S(1)}, bf16[4,192,384]{2,1,0:T(8,128)(2,1)}, u32[]{:S(2)}, u32[]{:S(2)}) collective-permute-start(bf16[4,192,384]{2,1,0:T(8,128)(2,1)S(1)} %pad_maximum_fusion.2.refs_0_), channel_id=1, source_target_pairs={{0,2},{1,5},{2,0},{3,7},{4,6},{5,1},{6,4},{7,3},{8,10},{9,13},{10,... | collective-permute-start | bytes 1769480 | tf_op jit(solution)/shard_map/ppermute | solution.py:63
  148.1 24.2 %collective-permute-start.34 = (bf16[4,192,384]{2,1,0:T(8,128)(2,1)S(1)}, bf16[4,192,384]{2,1,0:T(8,128)(2,1)S(1)}, u32[]{:S(2)}, u32[]{:S(2)}) collective-permute-start(bf16[4,192,384]{2,1,0:T(8,128)(2,1)S(1)} %pad_maximum_fusion.2.refs_0_), channel_id=1, source_target_pairs={{0,4},{1,3},{2,6},{3,1},{4,0},{5,7},{6,2},{7,5},{8,12},{9,11},{10,... | collective-permute-start | bytes 1769480 | tf_op jit(solution)/shard_map/ppermute | solution.py:63
  243.1 19.3 %collective-permute-start.48 = (bf16[4,192,384]{2,1,0:T(8,128)(2,1)}, bf16[4,192,384]{2,1,0:T(8,128)(2,1)S(1)}, u32[]{:S(2)}, u32[]{:S(2)}) collective-permute-start(bf16[4,192,384]{2,1,0:T(8,128)(2,1)} %get-tuple-element.521), channel_id=1, source_target_pairs={{0,1},{1,0},{2,3},{3,2},{4,5},{5,4},{6,7},{7,6},{8,9},{9,8},{10,11... | collective-permute-start | bytes 1769480 | tf_op jit(solution)/shard_map/ppermute | solution.py:63
  243.6 18.8 %collective-permute-start.49 = (bf16[4,192,384]{2,1,0:T(8,128)(2,1)}, bf16[4,192,384]{2,1,0:T(8,128)(2,1)S(1)}, u32[]{:S(2)}, u32[]{:S(2)}) collective-permute-start(bf16[4,192,384]{2,1,0:T(8,128)(2,1)} %get-tuple-element.522), channel_id=1, source_target_pairs={{0,1},{1,0},{2,3},{3,2},{4,5},{5,4},{6,7},{7,6},{8,9},{9,8},{10,11... | collective-permute-start | bytes 1769480 | tf_op jit(solution)/shard_map/ppermute | solution.py:63
  243.6 18.8 %collective-permute-start.50 = (bf16[4,192,384]{2,1,0:T(8,128)(2,1)}, bf16[4,192,384]{2,1,0:T(8,128)(2,1)S(1)}, u32[]{:S(2)}, u32[]{:S(2)}) collective-permute-start(bf16[4,192,384]{2,1,0:T(8,128)(2,1)} %get-tuple-element.523), channel_id=1, source_target_pairs={{0,1},{1,0},{2,3},{3,2},{4,5},{5,4},{6,7},{7,6},{8,9},{9,8},{10,11... | collective-permute-start | bytes 1769480 | tf_op jit(solution)/shard_map/ppermute | solution.py:63
  244.1 18.4 %collective-permute-start.51 = (bf16[4,192,384]{2,1,0:T(8,128)(2,1)}, bf16[4,192,384]{2,1,0:T(8,128)(2,1)}, u32[]{:S(2)}, u32[]{:S(2)}) collective-permute-start(bf16[4,192,384]{2,1,0:T(8,128)(2,1)} %get-tuple-element.524), channel_id=1, source_target_pairs={{0,1},{1,0},{2,3},{3,2},{4,5},{5,4},{6,7},{7,6},{8,9},{9,8},{10,11... | collective-permute-start | bytes 1769480 | tf_op jit(solution)/shard_map/ppermute | solution.py:63
  289.2 19.3 %collective-permute-start.54 = (bf16[4,192,384]{2,1,0:T(8,128)(2,1)}, bf16[4,192,384]{2,1,0:T(8,128)(2,1)}, u32[]{:S(2)}, u32[]{:S(2)}) collective-permute-start(bf16[4,192,384]{2,1,0:T(8,128)(2,1)} %get-tuple-element.560), channel_id=1, source_target_pairs={{0,4},{1,3},{2,6},{3,1},{4,0},{5,7},{6,2},{7,5},{8,12},{9,11},{10,... | collective-permute-start | bytes 1769480 | tf_op jit(solution)/shard_map/ppermute | solution.py:63
  290.2 18.3 %collective-permute-start.55 = (bf16[4,192,384]{2,1,0:T(8,128)(2,1)}, bf16[4,192,384]{2,1,0:T(8,128)(2,1)S(1)}, u32[]{:S(2)}, u32[]{:S(2)}) collective-permute-start(bf16[4,192,384]{2,1,0:T(8,128)(2,1)} %get-tuple-element.565), channel_id=1, source_target_pairs={{0,1},{1,0},{2,3},{3,2},{4,5},{5,4},{6,7},{7,6},{8,9},{9,8},{10,11... | collective-permute-start | bytes 1769480 | tf_op jit(solution)/shard_map/ppermute | solution.py:63
  290.2 18.3 %collective-permute-start.56 = (bf16[4,192,384]{2,1,0:T(8,128)(2,1)}, bf16[4,192,384]{2,1,0:T(8,128)(2,1)S(1)}, u32[]{:S(2)}, u32[]{:S(2)}) collective-permute-start(bf16[4,192,384]{2,1,0:T(8,128)(2,1)} %get-tuple-element.566), channel_id=1, source_target_pairs={{0,1},{1,0},{2,3},{3,2},{4,5},{5,4},{6,7},{7,6},{8,9},{9,8},{10,11... | collective-permute-start | bytes 1769480 | tf_op jit(solution)/shard_map/ppermute | solution.py:63
  290.7 17.9 %collective-permute-start.58 = (bf16[4,192,384]{2,1,0:T(8,128)(2,1)}, bf16[4,192,384]{2,1,0:T(8,128)(2,1)}, u32[]{:S(2)}, u32[]{:S(2)}) collective-permute-start(bf16[4,192,384]{2,1,0:T(8,128)(2,1)} %get-tuple-element.568), channel_id=1, source_target_pairs={{0,1},{1,0},{2,3},{3,2},{4,5},{5,4},{6,7},{7,6},{8,9},{9,8},{10,11... | collective-permute-start | bytes 1769480 | tf_op jit(solution)/shard_map/ppermute | solution.py:63
  314.3 28.3 %collective-permute-start.61 = (bf16[192,384]{1,0:T(8,128)(2,1)}, bf16[192,384]{1,0:T(8,128)(2,1)}, u32[]{:S(2)}, u32[]{:S(2)}) collective-permute-start(bf16[192,384]{1,0:T(8,128)(2,1)} %get-tuple-element.816), channel_id=1, source_target_pairs={{0,8},{1,9},{2,10},{3,11},{4,12},{5,13},{6,14},{7,15},{8,16},{9,17... | collective-permute-start | bytes 442376 | tf_op jit(solution)/shard_map/ppermute | solution.py:63
  317.1 25.5 %collective-permute-start.60 = (bf16[192,384]{1,0:T(8,128)(2,1)}, bf16[192,384]{1,0:T(8,128)(2,1)}, u32[]{:S(2)}, u32[]{:S(2)}) collective-permute-start(bf16[192,384]{1,0:T(8,128)(2,1)} %get-tuple-element.817), channel_id=1, source_target_pairs={{0,16},{1,17},{2,18},{3,19},{4,20},{5,21},{6,22},{7,23},{8,24},{9,... | collective-permute-start | bytes 442376 | tf_op jit(solution)/shard_map/ppermute | solution.py:63
  318.6 23.9 %collective-permute-start.59 = (bf16[192,384]{1,0:T(8,128)(2,1)}, bf16[192,384]{1,0:T(8,128)(2,1)}, u32[]{:S(2)}, u32[]{:S(2)}) collective-permute-start(bf16[192,384]{1,0:T(8,128)(2,1)} %get-tuple-element.818), channel_id=1, source_target_pairs={{0,24},{1,25},{2,26},{3,27},{4,28},{5,29},{6,30},{7,31},{8,0},{9,1... | collective-permute-start | bytes 442376 | tf_op jit(solution)/shard_map/ppermute | solution.py:63
  324.2 18.4 %collective-permute-start.62 = (bf16[4,192,384]{2,1,0:T(8,128)(2,1)}, bf16[4,192,384]{2,1,0:T(8,128)(2,1)S(1)}, u32[]{:S(2)}, u32[]{:S(2)}) collective-permute-start(bf16[4,192,384]{2,1,0:T(8,128)(2,1)} %get-tuple-element.583), channel_id=1, source_target_pairs={{0,2},{1,5},{2,0},{3,7},{4,6},{5,1},{6,4},{7,3},{8,10},{9,13},{10,... | collective-permute-start | bytes 1769480 | tf_op jit(solution)/shard_map/ppermute | solution.py:63
  324.7 17.9 %collective-permute-start.63 = (bf16[4,192,384]{2,1,0:T(8,128)(2,1)}, bf16[4,192,384]{2,1,0:T(8,128)(2,1)S(1)}, u32[]{:S(2)}, u32[]{:S(2)}) collective-permute-start(bf16[4,192,384]{2,1,0:T(8,128)(2,1)} %get-tuple-element.584), channel_id=1, source_target_pairs={{0,2},{1,5},{2,0},{3,7},{4,6},{5,1},{6,4},{7,3},{8,10},{9,13},{10,... | collective-permute-start | bytes 1769480 | tf_op jit(solution)/shard_map/ppermute | solution.py:63
  345.1 22.1 %collective-permute-start.66 = (bf16[4,224,384]{2,1,0:T(8,128)(2,1)}, bf16[4,224,384]{2,1,0:T(8,128)(2,1)S(1)}, u32[]{:S(2)}, u32[]{:S(2)}) collective-permute-start(bf16[4,224,384]{2,1,0:T(8,128)(2,1)} %get-tuple-element.620), channel_id=1, source_target_pairs={{0,1},{1,0},{2,3},{3,2},{4,5},{5,4},{6,7},{7,6},{8,9},{9,8},{10,11... | collective-permute-start | bytes 2064392 | tf_op jit(solution)/shard_map/ppermute | solution.py:63
  345.6 21.6 %collective-permute-start.67 = (bf16[4,224,384]{2,1,0:T(8,128)(2,1)}, bf16[4,224,384]{2,1,0:T(8,128)(2,1)S(1)}, u32[]{:S(2)}, u32[]{:S(2)}) collective-permute-start(bf16[4,224,384]{2,1,0:T(8,128)(2,1)} %get-tuple-element.621), channel_id=1, source_target_pairs={{0,1},{1,0},{2,3},{3,2},{4,5},{5,4},{6,7},{7,6},{8,9},{9,8},{10,11... | collective-permute-start | bytes 2064392 | tf_op jit(solution)/shard_map/ppermute | solution.py:63
  345.6 21.6 %collective-permute-start.68 = (bf16[4,224,384]{2,1,0:T(8,128)(2,1)}, bf16[4,224,384]{2,1,0:T(8,128)(2,1)}, u32[]{:S(2)}, u32[]{:S(2)}) collective-permute-start(bf16[4,224,384]{2,1,0:T(8,128)(2,1)} %get-tuple-element.622), channel_id=1, source_target_pairs={{0,1},{1,0},{2,3},{3,2},{4,5},{5,4},{6,7},{7,6},{8,9},{9,8},{10,11... | collective-permute-start | bytes 2064392 | tf_op jit(solution)/shard_map/ppermute | solution.py:63
  346.1 21.1 %collective-permute-start.69 = (bf16[4,224,384]{2,1,0:T(8,128)(2,1)}, bf16[4,224,384]{2,1,0:T(8,128)(2,1)}, u32[]{:S(2)}, u32[]{:S(2)}) collective-permute-start(bf16[4,224,384]{2,1,0:T(8,128)(2,1)} %get-tuple-element.623), channel_id=1, source_target_pairs={{0,1},{1,0},{2,3},{3,2},{4,5},{5,4},{6,7},{7,6},{8,9},{9,8},{10,11... | collective-permute-start | bytes 2064392 | tf_op jit(solution)/shard_map/ppermute | solution.py:63
  373.0 29.9 %collective-permute-start.73 = (bf16[4,224,384]{2,1,0:T(8,128)(2,1)}, bf16[4,224,384]{2,1,0:T(8,128)(2,1)S(1)}, u32[]{:S(2)}, u32[]{:S(2)}) collective-permute-start(bf16[4,224,384]{2,1,0:T(8,128)(2,1)} %get-tuple-element.643), channel_id=1, source_target_pairs={{0,2},{1,5},{2,0},{3,7},{4,6},{5,1},{6,4},{7,3},{8,10},{9,13},{10,... | collective-permute-start | bytes 2064392 | tf_op jit(solution)/shard_map/ppermute | solution.py:63
  373.9 29.0 %collective-permute-start.74 = (bf16[4,224,384]{2,1,0:T(8,128)(2,1)}, bf16[4,224,384]{2,1,0:T(8,128)(2,1)S(1)}, u32[]{:S(2)}, u32[]{:S(2)}) collective-permute-start(bf16[4,224,384]{2,1,0:T(8,128)(2,1)} %get-tuple-element.644), channel_id=1, source_target_pairs={{0,2},{1,5},{2,0},{3,7},{4,6},{5,1},{6,4},{7,3},{8,10},{9,13},{10,... | collective-permute-start | bytes 2064392 | tf_op jit(solution)/shard_map/ppermute | solution.py:63
  380.4 22.4 %collective-permute-start.72 = (bf16[192,384]{1,0:T(8,128)(2,1)}, bf16[192,384]{1,0:T(8,128)(2,1)}, u32[]{:S(2)}, u32[]{:S(2)}) collective-permute-start(bf16[192,384]{1,0:T(8,128)(2,1)} %get-tuple-element.812), channel_id=1, source_target_pairs={{0,8},{1,9},{2,10},{3,11},{4,12},{5,13},{6,14},{7,15},{8,16},{9,17... | collective-permute-start | bytes 442376 | tf_op jit(solution)/shard_map/ppermute | solution.py:63
  381.7 21.2 %collective-permute-start.71 = (bf16[192,384]{1,0:T(8,128)(2,1)}, bf16[192,384]{1,0:T(8,128)(2,1)}, u32[]{:S(2)}, u32[]{:S(2)}) collective-permute-start(bf16[192,384]{1,0:T(8,128)(2,1)} %get-tuple-element.813), channel_id=1, source_target_pairs={{0,16},{1,17},{2,18},{3,19},{4,20},{5,21},{6,22},{7,23},{8,24},{9,... | collective-permute-start | bytes 442376 | tf_op jit(solution)/shard_map/ppermute | solution.py:63
  383.0 19.9 %collective-permute-start.70 = (bf16[192,384]{1,0:T(8,128)(2,1)}, bf16[192,384]{1,0:T(8,128)(2,1)}, u32[]{:S(2)}, u32[]{:S(2)}) collective-permute-start(bf16[192,384]{1,0:T(8,128)(2,1)} %get-tuple-element.814), channel_id=1, source_target_pairs={{0,24},{1,25},{2,26},{3,27},{4,28},{5,29},{6,30},{7,31},{8,0},{9,1... | collective-permute-start | bytes 442376 | tf_op jit(solution)/shard_map/ppermute | solution.py:63
  407.8 33.6 %collective-permute-start.79 = (bf16[4,224,384]{2,1,0:T(8,128)(2,1)}, bf16[4,224,384]{2,1,0:T(8,128)(2,1)S(1)}, u32[]{:S(2)}, u32[]{:S(2)}) collective-permute-start(bf16[4,224,384]{2,1,0:T(8,128)(2,1)} %get-tuple-element.662), channel_id=1, source_target_pairs={{0,4},{1,3},{2,6},{3,1},{4,0},{5,7},{6,2},{7,5},{8,12},{9,11},{10,... | collective-permute-start | bytes 2064392 | tf_op jit(solution)/shard_map/ppermute | solution.py:63
  414.6 23.8 %collective-permute-start.77 = (bf16[8,36,1024]{2,0,1:T(8,128)(2,1)}, bf16[8,36,1024]{2,0,1:T(8,128)(2,1)S(1)}, u32[]{:S(2)}, u32[]{:S(2)}) collective-permute-start(bf16[8,36,1024]{2,0,1:T(8,128)(2,1)} %copy.65), channel_id=1, source_target_pairs={{0,3},{1,2},{2,1},{3,0},{4,7},{5,6},{6,5},{7,4},{8,11},{9,10},{10,... | collective-permute-start | bytes 1769480 | tf_op jit(solution)/shard_map/ppermute | solution.py:1002
  414.6 26.8 %collective-permute-start.76 = (bf16[8,36,1024]{2,0,1:T(8,128)(2,1)}, bf16[8,36,1024]{2,0,1:T(8,128)(2,1)S(1)}, u32[]{:S(2)}, u32[]{:S(2)}) collective-permute-start(bf16[8,36,1024]{2,0,1:T(8,128)(2,1)} %copy.64), channel_id=1, source_target_pairs={{0,2},{1,3},{2,0},{3,1},{4,6},{5,7},{6,4},{7,5},{8,10},{9,11},{10,... | collective-permute-start | bytes 1769480 | tf_op jit(solution)/shard_map/ppermute | solution.py:1002
  415.2 26.2 %collective-permute-start.75 = (bf16[8,36,1024]{2,0,1:T(8,128)(2,1)}, bf16[8,36,1024]{2,0,1:T(8,128)(2,1)}, u32[]{:S(2)}, u32[]{:S(2)}) collective-permute-start(bf16[8,36,1024]{2,0,1:T(8,128)(2,1)} %copy.63), channel_id=1, source_target_pairs={{0,1},{1,0},{2,3},{3,2},{4,5},{5,4},{6,7},{7,6},{8,9},{9,8},{10,11... | collective-permute-start | bytes 1769480 | tf_op jit(solution)/shard_map/ppermute | solution.py:1002
  442.2 30.5 %collective-permute-start.83 = (bf16[4,192,384]{2,1,0:T(8,128)(2,1)}, bf16[4,192,384]{2,1,0:T(8,128)(2,1)S(1)}, u32[]{:S(2)}, u32[]{:S(2)}) collective-permute-start(bf16[4,192,384]{2,1,0:T(8,128)(2,1)} %get-tuple-element.693), channel_id=1, source_target_pairs={{0,1},{1,0},{2,3},{3,2},{4,5},{5,4},{6,7},{7,6},{8,9},{9,8},{10,11... | collective-permute-start | bytes 1769480 | tf_op jit(solution)/shard_map/ppermute | solution.py:63
  442.8 29.9 %collective-permute-start.84 = (bf16[4,192,384]{2,1,0:T(8,128)(2,1)}, bf16[4,192,384]{2,1,0:T(8,128)(2,1)S(1)}, u32[]{:S(2)}, u32[]{:S(2)}) collective-permute-start(bf16[4,192,384]{2,1,0:T(8,128)(2,1)} %get-tuple-element.694), channel_id=1, source_target_pairs={{0,1},{1,0},{2,3},{3,2},{4,5},{5,4},{6,7},{7,6},{8,9},{9,8},{10,11... | collective-permute-start | bytes 1769480 | tf_op jit(solution)/shard_map/ppermute | solution.py:63
  442.8 29.9 %collective-permute-start.85 = (bf16[4,192,384]{2,1,0:T(8,128)(2,1)}, bf16[4,192,384]{2,1,0:T(8,128)(2,1)}, u32[]{:S(2)}, u32[]{:S(2)}) collective-permute-start(bf16[4,192,384]{2,1,0:T(8,128)(2,1)} %get-tuple-element.695), channel_id=1, source_target_pairs={{0,1},{1,0},{2,3},{3,2},{4,5},{5,4},{6,7},{7,6},{8,9},{9,8},{10,11... | collective-permute-start | bytes 1769480 | tf_op jit(solution)/shard_map/ppermute | solution.py:63
  443.3 29.4 %collective-permute-start.86 = (bf16[4,192,384]{2,1,0:T(8,128)(2,1)}, bf16[4,192,384]{2,1,0:T(8,128)(2,1)}, u32[]{:S(2)}, u32[]{:S(2)}) collective-permute-start(bf16[4,192,384]{2,1,0:T(8,128)(2,1)} %get-tuple-element.696), channel_id=1, source_target_pairs={{0,1},{1,0},{2,3},{3,2},{4,5},{5,4},{6,7},{7,6},{8,9},{9,8},{10,11... | collective-permute-start | bytes 1769480 | tf_op jit(solution)/shard_map/ppermute | solution.py:63
  514.0 36.3 %collective-permute-start.98 = (f32[104,128]{1,0:T(8,128)S(1)}, f32[104,128]{1,0:T(8,128)}, u32[]{:S(2)}, u32[]{:S(2)}) collective-permute-start(f32[104,128]{1,0:T(8,128)S(1)} %add.162), channel_id=1, source_target_pairs={{0,16},{1,17},{2,18},{3,19},{4,20},{5,21},{6,22},{7,23},{8,24},{9,... | collective-permute-start | bytes 159752 | tf_op jit(solution)/shard_map/ppermute | solution.py:63
  514.0 36.3 %collective-permute-start.97 = (f32[104,128]{1,0:T(8,128)S(1)}, f32[104,128]{1,0:T(8,128)}, u32[]{:S(2)}, u32[]{:S(2)}) collective-permute-start(f32[104,128]{1,0:T(8,128)S(1)} %add.162), channel_id=1, source_target_pairs={{0,8},{1,9},{2,10},{3,11},{4,12},{5,13},{6,14},{7,15},{8,16},{9,17... | collective-permute-start | bytes 159752 | tf_op jit(solution)/shard_map/ppermute | solution.py:63
  519.9 30.4 %collective-permute-start.96 = (bf16[192,384]{1,0:T(8,128)(2,1)S(1)}, bf16[192,384]{1,0:T(8,128)(2,1)S(1)}, u32[]{:S(2)}, u32[]{:S(2)}) collective-permute-start(bf16[192,384]{1,0:T(8,128)(2,1)S(1)} %get-tuple-element.808), channel_id=1, source_target_pairs={{0,8},{1,9},{2,10},{3,11},{4,12},{5,13},{6,14},{7,15},{8,16},{9,17... | collective-permute-start | bytes 442376 | tf_op jit(solution)/shard_map/ppermute | solution.py:63
  522.7 27.6 %collective-permute-start.95 = (bf16[192,384]{1,0:T(8,128)(2,1)S(1)}, bf16[192,384]{1,0:T(8,128)(2,1)S(1)}, u32[]{:S(2)}, u32[]{:S(2)}) collective-permute-start(bf16[192,384]{1,0:T(8,128)(2,1)S(1)} %get-tuple-element.809), channel_id=1, source_target_pairs={{0,16},{1,17},{2,18},{3,19},{4,20},{5,21},{6,22},{7,23},{8,24},{9,... | collective-permute-start | bytes 442376 | tf_op jit(solution)/shard_map/ppermute | solution.py:63
  523.6 26.7 %collective-permute-start.94 = (bf16[192,384]{1,0:T(8,128)(2,1)S(1)}, bf16[192,384]{1,0:T(8,128)(2,1)}, u32[]{:S(2)}, u32[]{:S(2)}) collective-permute-start(bf16[192,384]{1,0:T(8,128)(2,1)S(1)} %get-tuple-element.810), channel_id=1, source_target_pairs={{0,24},{1,25},{2,26},{3,27},{4,28},{5,29},{6,30},{7,31},{8,0},{9,1... | collective-permute-start | bytes 442376 | tf_op jit(solution)/shard_map/ppermute | solution.py:63
  (122 other events, 1363.4 us)

commit v4 on v3

--- a/solution.py
+++ b/solution.py
@@ -18,8 +18,7 @@
 PARAMS = pltpu.CompilerParams(vmem_limit_bytes=62 * 2**20)
 
 QKV, OUT, CQ, CKV, COUT, FIN, FOUT = range(7)
-GATHER = ((QKV, OUT), (CQ, CKV, COUT), (FIN,), (FOUT,))
-REDUCE = ((QKV, OUT), (CQ, CKV, COUT), (FIN,), (FOUT,))
+GROUPS = ((QKV, OUT), (CQ, CKV, COUT), (FIN, FOUT))
 
 
 class Plan:
@@ -79,7 +78,7 @@
 
 def group_starts(plan):
     starts, at = [], 0
-    for group in GATHER:
+    for group in GROUPS:
         starts.append(at)
         at += plan.rows(group)
     return starts, at
@@ -90,10 +89,12 @@
     wide = plan.chunk // 2
 
     def body(where_ref, *refs):
-        shard_refs, (own_ref, send_ref) = refs[:7], refs[7:]
+        shard_refs, (own_ref, send_ref, turned) = list(refs[:7]), refs[7:]
         core = where_ref[3]
+        turned[...] = shard_refs[FOUT][...].T
+        shard_refs[FOUT] = turned
         at = 0
-        for group in GATHER:
+        for group in GROUPS:
             for w in group:
                 high = plan.half[w]
                 for b in range(plan.chunks[w]):
@@ -110,9 +111,10 @@
         out_shape=(shape, shape),
         in_specs=[SMEM_SPEC] + [VMEM_SPEC] * 7,
         out_specs=(VMEM_SPEC, VMEM_SPEC),
+        scratch_shapes=[pltpu.VMEM(shards[FOUT].shape, BF16)],
         compiler_params=PARAMS,
         name="pack_split",
-    )(where, *shards)
+    )(where, *shards[:FOUT], shards[FOUT].T)
 
 
 def pack_join(plan, where, own, got):
@@ -123,7 +125,7 @@
         core = where_ref[3]
 
         def fill(low_ref, high_ref):
-            for g, group in enumerate(GATHER):
+            for g, group in enumerate(GROUPS):
                 at = starts[g]
                 for w in group:
                     high, count = plan.half[w], plan.chunks[w]
@@ -147,9 +149,9 @@
 
     return pl.pallas_call(
         body,
-        out_shape=tuple(jax.ShapeDtypeStruct((plan.rows(g), plan.chunk), BF16) for g in GATHER),
+        out_shape=tuple(jax.ShapeDtypeStruct((plan.rows(g), plan.chunk), BF16) for g in GROUPS),
         in_specs=[SMEM_SPEC, VMEM_SPEC, VMEM_SPEC],
-        out_specs=(VMEM_SPEC,) * len(GATHER),
+        out_specs=(VMEM_SPEC,) * len(GROUPS),
         compiler_params=PARAMS,
         name="pack_join",
     )(where, own, got)
@@ -165,13 +167,12 @@
             held = held + [send(held[0], plan.z_up(k)) for k in range(1, plan.zs)]
         elif self.step == 1:
             stack = jnp.stack(held)
-            held = [stack, send(stack, plan.first()), send(stack, plan.second())]
-            held.append(send(stack, plan.core()))
+            held = [stack, send(stack, plan.first())]
         elif self.step == 2:
-            stack, near, side, stack_core = held
-            far = send(near, plan.second())
-            held = [stack, near, side, far, stack_core]
-            held += [send(part, plan.core()) for part in (near, side, far)]
+            held = held + [send(part, plan.second()) for part in held]
+            held = held + [send(part, plan.core()) for part in held[:2]]
+        elif self.step == 3:
+            held = held + [send(part, plan.core()) for part in held[2:4]]
         self.held, self.step = held, self.step + 1
 
 
@@ -189,55 +190,54 @@
                     for w, j, row in piece_rows(group, plan):
                         high = plan.half[w]
                         to_row = pl.multiple_of(place * high, 16)
-                        stack = other * 4 + second * 2 + first
-                        visit(stack, k, row, w, j, to_row, y_at, high)
-
-
-def assemble(plan, group, where, stacks):
-
-    def body(where_ref, *refs):
-        stack_refs, full_refs = refs[:8], dict(zip(group, refs[8:]))
-
-        def visit(stack, k, row, w, j, to_row, to_y, high):
-            to_col = pl.multiple_of(to_y * (plan.full[w][1] // 2) + j * plan.chunk, 128)
-            full_refs[w][pl.ds(to_row, high), pl.ds(to_col, plan.chunk)] = stack_refs[stack][
-                k, row : row + high, :
-            ]
-
-        each_place(plan, group, where_ref, visit)
+                        visit(other, second * 2 + first, k, row, w, j, to_row, y_at, high)
+
+
+def add_low(ones, twos, widths):
+    count, slots, rows, chunk = ones.shape
+
+    def body(one_ref, two_ref, *out_refs):
+        at = 0
+        for width, out in zip(widths, out_refs):
+            for n in range(width):
+                out[n] = (one_ref[at].astype(F32) + two_ref[at].astype(F32)).astype(BF16)
+                at += 1
+
+    def spec(n):
+        return pl.BlockSpec((n, 1, rows, chunk), lambda i: (0, i, 0, 0))
 
     return pl.pallas_call(
         body,
-        out_shape=tuple(jax.ShapeDtypeStruct(plan.full[w], BF16) for w in group),
-        in_specs=[SMEM_SPEC] + [VMEM_SPEC] * 8,
-        out_specs=(VMEM_SPEC,) * len(group),
-        compiler_params=PARAMS,
-        name="assemble",
-    )(where, *stacks)
-
-
-def add_low(ones, twos):
-    n = len(ones)
-    shape = ones[0].shape
-
-    def body(*refs):
-        for a, b, out in zip(refs[:n], refs[n : 2 * n], refs[2 * n :]):
-            out[...] = (a[...].astype(F32) + b[...].astype(F32)).astype(BF16)
-
-    spec = pl.BlockSpec((1,) + shape[1:], lambda i: (i, 0, 0))
-    size = shape[0] * shape[1] * shape[2]
-    return pl.pallas_call(
-        body,
-        grid=(shape[0],),
-        out_shape=(jax.ShapeDtypeStruct(shape, BF16),) * n,
-        in_specs=[spec] * (2 * n),
-        out_specs=(spec,) * n,
+        grid=(slots,),
+        out_shape=tuple(jax.ShapeDtypeStruct((n, slots, rows, chunk), BF16) for n in widths),
+        in_specs=[spec(count), spec(count)],
+        out_specs=tuple(spec(n) for n in widths),
         compiler_params=PARAMS,
         cost_estimate=pl.CostEstimate(
-            flops=n * size, bytes_accessed=6 * n * size, transcendentals=0
+            flops=ones.size, bytes_accessed=6 * ones.size, transcendentals=0
         ),
         name="add_low",
-    )(*ones, *twos)
+    )(ones, twos)
+
+
+def add_slots(ones, twos):
+    _, slots, rows, chunk = ones.shape
+
+    def body(one_ref, two_ref, *out_refs):
+        for n in range(slots):
+            out_refs[n][...] = (one_ref[0, n].astype(F32) + two_ref[0, n].astype(F32)).astype(BF16)
+
+    return pl.pallas_call(
+        body,
+        out_shape=(jax.ShapeDtypeStruct((rows, chunk), BF16),) * slots,
+        in_specs=[VMEM_SPEC, VMEM_SPEC],
+        out_specs=(VMEM_SPEC,) * slots,
+        compiler_params=PARAMS,
+        cost_estimate=pl.CostEstimate(
+            flops=ones.size, bytes_accessed=6 * ones.size, transcendentals=0
+        ),
+        name="add_slots",
+    )(ones, twos)
 
 
 class Reducing:
@@ -248,17 +248,17 @@
     def advance(self):
         plan, held = self.plan, self.held
         if self.step == 0:
-            held = held[:4] + [send(part, plan.core()) for part in held[4:]]
+            held = [held[0], send(held[1], plan.core())]
         elif self.step == 1:
-            mine = add_low(held[:4], held[4:])
-            held = list(mine[:2]) + [send(part, plan.second()) for part in mine[2:]]
+            keep, give = add_low(*held, (2, 2))
+            held = [keep, send(give, plan.second())]
         elif self.step == 2:
-            mine = add_low(held[:2], held[2:])
-            held = [mine[0], send(mine[1], plan.first())]
+            keep, give = add_low(*held, (1, 1))
+            held = [keep, send(give, plan.first())]
         elif self.step == 3:
-            (total,) = add_low(held[:1], held[1:])
-            parts = [send(total[k], plan.z_up(plan.zs - k)) for k in range(1, plan.zs)]
-            held = [total[0]] + parts
+            slots = add_slots(*held)
+            parts = [send(slots[k], plan.z_up(plan.zs - k)) for k in range(1, plan.zs)]
+            held = [slots[0]] + parts
         elif self.step == 4:
             own, give = unpack_split(plan, self.group, self.where, held)
             held = [own, send(give, plan.core())]
@@ -317,11 +317,13 @@
 
 def unpack_join(plan, group, where, own, got):
     wide = plan.chunk // 2
-
-    def body(where_ref, own_ref, got_ref, *out_refs):
+    turned = [w == FOUT for w in group]
+
+    def body(where_ref, own_ref, got_ref, *refs):
         core = where_ref[3]
         at = 0
-        for w, out_ref in zip(group, out_refs):
+        for n, w in enumerate(group):
+            out_ref = refs[-1] if turned[n] else refs[n]
             high, count = plan.half[w], plan.chunks[w]
             own_rows = pl.ds(pl.multiple_of(core * high, 16), high)
             got_rows = pl.ds(pl.multiple_of((1 - core) * high, 16), high)
@@ -330,17 +332,23 @@
                 out_ref[own_rows, cut] = own_ref[row : row + high, :]
                 out_ref[got_rows, cut] = got_ref[row : row + high, :]
             at += count * high
-
-    return pl.pallas_call(
+            if turned[n]:
+                refs[n][...] = out_ref[...].T
+
+    shapes = [(2 * plan.half[w], plan.cols[w]) for w in group]
+    done = pl.pallas_call(
         body,
         out_shape=tuple(
-            jax.ShapeDtypeStruct((2 * plan.half[w], plan.cols[w]), F32) for w in group
+            jax.ShapeDtypeStruct(shape[::-1] if turn else shape, F32)
+            for shape, turn in zip(shapes, turned)
         ),
         in_specs=[SMEM_SPEC, VMEM_SPEC, VMEM_SPEC],
         out_specs=(VMEM_SPEC,) * len(group),
+        scratch_shapes=[pltpu.VMEM(shapes[-1], F32)],
         compiler_params=PARAMS,
         name="unpack_join",
     )(where, own, got)
+    return [value.T if turn else value for value, turn in zip(done, turned)]
 
 
 def gather_small(plan, where, vectors, bias):
@@ -512,12 +520,51 @@
     )(*[a for a, _ in ins])
 
 
-def self_forward(dims, text, w_qkv, w_out, rows, lengths):
+class Source:
+    def __init__(self, plan, group, where, given):
+        self.plan, self.group, self.pieces = plan, group, plan.fast
+        if self.pieces:
+            self.ins = [(where, SMEM_SPEC)] + [(part, whole(part.shape)) for part in given]
+            self.outs = [(spec_of(plan.full[w], BF16), summed(plan.full[w])) for w in group]
+        else:
+            self.ins = [(w, whole(w.shape)) for w in given]
+            self.outs = []
+        self.given = given
+
+    def open(self, in_refs, out_refs):
+        if not self.pieces:
+            return list(in_refs)
+        where_ref, parts = in_refs[0], in_refs[1:]
+        full = dict(zip(self.group, out_refs))
+        plan = self.plan
+
+        def visit(other, stack, k, row, w, j, to_row, to_y, high):
+            to_col = pl.multiple_of(to_y * (plan.full[w][1] // 2) + j * plan.chunk, 128)
+            part = parts[other * 4 + stack]
+            full[w][pl.ds(to_row, high), pl.ds(to_col, plan.chunk)] = part[k, row : row + high, :]
+
+        @pl.when(pl.program_id(0) == 0)
+        def _():
+            each_place(plan, self.group, where_ref, visit)
+
+        return list(out_refs)
+
+    def split(self, done):
+        if not self.pieces:
+            return done, self.given
+        return done[: -len(self.group)], done[-len(self.group) :]
+
+
+def self_forward(dims, source, text, rows, lengths):
     d, items, length, group = dims.d, dims.items, dims.length, dims.group
     pairs, tokens, block = d // (2 * HEAD), items * length, group * length
     scale = HEAD ** (-0.5)
 
-    def body(len_ref, x_ref, wqkv_ref, wout_ref, row_ref, qkv_ref, prob_ref, ctx_ref, tot_ref):
+    n_in = len(source.ins)
+
+    def body(len_ref, x_ref, row_ref, *refs):
+        qkv_ref, prob_ref, ctx_ref, tot_ref = refs[n_in : n_in + 4]
+        wqkv_ref, wout_ref = source.open(refs[:n_in], refs[n_in + 4 :])
         step = pl.program_id(0)
         low, high = lane_masks()
         x = x_ref[...]
@@ -541,43 +588,33 @@
                 ctx_ref[r, p * 128 : (p + 1) * 128] = join_heads(dot(v.T, probs))
         tot_ref[...] = x.astype(F32) + dot(ctx_ref[...], wout_ref[...]) + row_ref[2:3, :]
 
-    return call(
+    done = call(
         body,
         "self_forward",
         items // group,
-        [
-            (lengths, SMEM_SPEC),
-            (text, tiled((block, d))),
-            (w_qkv, whole((d, 3 * d))),
-            (w_out, whole((d, d))),
-            (rows, whole(rows.shape)),
-        ],
+        [(lengths, SMEM_SPEC), (text, tiled((block, d))), (rows, whole(rows.shape))] + source.ins,
         [
             (spec_of((tokens, 3 * d), BF16), tiled((block, 3 * d))),
             (spec_of((items, pairs, length, 2 * length), BF16), tiled((group, pairs, length, 2 * length))),
             (spec_of((tokens, d), BF16), tiled((block, d))),
             (spec_of((tokens, d), F32), tiled((block, d))),
-        ],
+        ]
+        + source.outs,
         2 * tokens * d * 6 * d,
     )
-
-
-def cross_forward(dims, total_one, grids, cls, mask, w_cq, w_ckv, w_cout, rows):
-    d, items, length, group = dims.d, dims.items, dims.length, dims.group
-    pairs, tokens, block = d // (2 * HEAD), items * length, group * length
-    count, part, vis = mask.shape[1], grids[0].shape[1], cls.shape[2]
-    scale = HEAD ** (-0.5)
-    parts = len(grids)
-
-    def body(tot_ref, *refs):
-        grid_refs = refs[:parts]
-        cls_ref, mask_ref, wcq_ref, wckv_ref, wcout_ref, row_ref = refs[parts : parts + 6]
-        h_ref, cq_ref, kv_ref, prob_ref, ctx_ref, two_ref, patch_ref = refs[parts + 6 :]
-        low, high = lane_masks()
-        hat, _ = norm_parts(tot_ref[...])
-        hidden = hat * row_ref[3:4, :] + row_ref[4:5, :]
-        h_ref[...] = hidden.astype(BF16)
-        cq_ref[...] = (dot(h_ref[...], wcq_ref[...]) + row_ref[5:6, :]).astype(BF16)
+    return source.split(done)
+
+
+def cross_keys(dims, source, grids, cls, rows, count):
+    d, items, group = dims.d, dims.items, dims.group
+    part, vis, parts = grids[0].shape[1], cls.shape[2], len(grids)
+    n_in = len(source.ins)
+
+    def body(*refs):
+        grid_refs, cls_ref, row_ref = refs[:parts], refs[parts], refs[parts + 1]
+        refs = refs[parts + 2 :]
+        kv_ref, patch_ref = refs[n_in : n_in + 2]
+        _, wckv_ref, _ = source.open(refs[:n_in], refs[n_in + 2 :])
         for i in range(group):
             for k in range(parts):
                 patch_ref[i, k * part : (k + 1) * part, :] = grid_refs[k][i]
@@ -588,6 +625,36 @@
         kv_ref[:, :, :d] = keys.reshape(group, count, d)
         values = (dot(patch, wckv_ref[:, d:]) + row_ref[6:7, :]).astype(BF16)
         kv_ref[:, :, d:] = values.reshape(group, count, d)
+
+    done = call(
+        body,
+        "cross_keys",
+        items // group,
+        [(grid, tiled((group, part, vis))) for grid in grids]
+        + [(cls, tiled((group, 1, vis))), (rows, whole(rows.shape))]
+        + source.ins,
+        [
+            (spec_of((items, count, 2 * d), BF16), tiled((group, count, 2 * d))),
+            (spec_of((items, count, vis), BF16), tiled((group, count, vis))),
+        ]
+        + source.outs,
+        2 * items * count * vis * 2 * d,
+    )
+    return source.split(done)
+
+
+def cross_forward(dims, total_one, kv, mask, w_cq, w_cout, rows):
+    d, items, length, group = dims.d, dims.items, dims.length, dims.group
+    pairs, tokens, block = d // (2 * HEAD), items * length, group * length
+    count = kv.shape[1]
+    scale = HEAD ** (-0.5)
+
+    def body(tot_ref, kv_ref, mask_ref, wcq_ref, wcout_ref, row_ref, h_ref, cq_ref, prob_ref, ctx_ref, two_ref):
+        low, high = lane_masks()
+        hat, _ = norm_parts(tot_ref[...])
+        hidden = hat * row_ref[3:4, :] + row_ref[4:5, :]
+        h_ref[...] = hidden.astype(BF16)
+        cq_ref[...] = (dot(h_ref[...], wcq_ref[...]) + row_ref[5:6, :]).astype(BF16)
         for i in range(group):
             ok = mask_ref[i].astype(F32) > 0.5
             ok = jnp.concatenate([ok, ok], 1)
@@ -605,36 +672,35 @@
         body,
         "cross_forward",
         items // group,
-        [(total_one, tiled((block, d)))]
-        + [(grid, tiled((group, part, vis))) for grid in grids]
-        + [
-            (cls, tiled((group, 1, vis))),
+        [
+            (total_one, tiled((block, d))),
+            (kv, tiled((group, count, 2 * d))),
             (mask, tiled((group, count, length))),
             (w_cq, whole((d, d))),
-            (w_ckv, whole((vis, 2 * d))),
             (w_cout, whole((d, d))),
             (rows, whole(rows.shape)),
         ],
         [
             (spec_of((tokens, d), BF16), tiled((block, d))),
             (spec_of((tokens, d), BF16), tiled((block, d))),
-            (spec_of((items, count, 2 * d), BF16), tiled((group, count, 2 * d))),
             (spec_of((items, pairs, count, 2 * length), BF16), tiled((group, pairs, count, 2 * length))),
             (spec_of((tokens, d), BF16), tiled((block, d))),
             (spec_of((tokens, d), F32), tiled((block, d))),
-            (spec_of((items, count, vis), BF16), tiled((group, count, vis))),
         ],
-        2 * tokens * d * 4 * d + 2 * items * count * vis * 2 * d,
-    )
-
-
-def ffn_forward(dims, total_two, cotangent, w_fin, w_fout, rows, bias):
+        2 * tokens * d * 6 * d,
+    )
+
+
+def ffn_forward(dims, source, total_two, cotangent, rows, bias):
     d, items, length, group = dims.d, dims.items, dims.length, dims.group
-    tokens, block, ff = items * length, group * length, w_fin.shape[1]
+    tokens, block, ff = items * length, group * length, bias.shape[1]
     piece = d
-
-    def body(tot_ref, cot_ref, win_ref, wout_ref, row_ref, bias_ref,
-             out_ref, h_ref, act_ref, slope_ref, g_ref, glow_ref, sum_ref):
+    n_in = len(source.ins)
+
+    def body(tot_ref, cot_ref, row_ref, bias_ref, *refs):
+        out_ref, h_ref, act_ref, slope_ref, g_ref, glow_ref, sum_ref = refs[n_in : n_in + 7]
+        win_ref, wout_ref = source.open(refs[:n_in], refs[n_in + 7 :])
+
         @pl.when(pl.program_id(0) == 0)
         def _():
             sum_ref[...] = jnp.zeros_like(sum_ref)
@@ -663,18 +729,17 @@
         sum_ref[1:2, :] += col_sum(cot)
         sum_ref[2:3, :] += col_sum(low)
 
-    return call(
+    done = call(
         body,
         "ffn_forward",
         items // group,
         [
             (total_two, tiled((block, d))),
             (cotangent, tiled((block, d))),
-            (w_fin, whole((d, ff))),
-            (w_fout, whole((ff, d))),
             (rows, whole(rows.shape)),
             (bias, whole(bias.shape)),
-        ],
+        ]
+        + source.ins,
         [
             (spec_of((tokens, d), F32), tiled((block, d))),
             (spec_of((tokens, d), BF16), tiled((block, d))),
@@ -683,9 +748,11 @@
             (spec_of((tokens, d), F32), tiled((block, d))),
             (spec_of((tokens, d), BF16), tiled((block, d))),
             (spec_of((8, d), F32), summed((8, d))),
-        ],
+        ]
+        + source.outs,
         4 * tokens * d * ff,
     )
+    return source.split(done)
 
 
 def ffn_backward(dims, grad_three, grad_low, slope, total_two, w_fin, w_fout, rows):
@@ -911,63 +978,96 @@
     )[0]
 
 
+def cut_grids(turn, image_grid, parts):
+    micro, items, part, vis = image_grid.shape
+    each = items // parts
+
+    def body(turn_ref, grid_ref, *out_refs):
+        def fill(own):
+            value = jnp.swapaxes(grid_ref[0], 0, 1)
+            for s in range(parts):
+                out_refs[s ^ own][...] = value[s * each : (s + 1) * each]
+
+        for own in range(parts):
+            pl.when(turn_ref[0] == own)(functools.partial(fill, own))
+
+    return call(
+        body,
+        "cut_grids",
+        micro,
+        [
+            (turn, SMEM_SPEC),
+            (image_grid.transpose(0, 2, 1, 3), tiled((1, part, items, vis))),
+        ],
+        [(spec_of((micro * each, part, vis), BF16), tiled((each, part, vis)))] * parts,
+        0,
+    )
+
+
 def place_grids(turn, micro, pieces):
     items, part, vis = pieces[0].shape
     each, parts = items // micro, len(pieces)
 
     def body(turn_ref, *refs):
-        for k in range(parts):
-            at = (turn_ref[0] ^ k) * each
-            refs[-1][0, pl.ds(at, each)] = refs[k][...].astype(F32)
-
-    return call(
+        def fill(own):
+            value = jnp.concatenate([refs[s ^ own][...].astype(F32) for s in range(parts)], 0)
+            refs[-1][0] = jnp.swapaxes(value, 0, 1)
+
+        for own in range(parts):
+            pl.when(turn_ref[0] == own)(functools.partial(fill, own))
+
+    shape = (micro, part, each * parts, vis)
+    done = call(
         body,
         "place_grids",
         micro,
         [(turn, SMEM_SPEC)] + [(p, tiled((each, part, vis))) for p in pieces],
-        [
-            (
-                spec_of((micro, each * parts, part, vis), F32),
-                tiled((1, each * parts, part, vis)),
-            )
-        ],
+        [(spec_of(shape, F32), tiled((1,) + shape[1:]))],
         0,
     )[0]
+    return done.transpose(0, 2, 1, 3)
 
 
 def weight_grads(plan, group, where, factors):
     high_rows = max(plan.full[w][0] for w in group)
+    wide = max(plan.full[w][1] for w in group)
+    flat = [a for pair in factors for a in pair]
+    count = len(flat)
 
     def body(where_ref, *refs):
-        ins, stack_refs, made = refs[: 2 * len(group)], refs[2 * len(group) : -1], refs[-1]
+        far, stack_refs = refs[:count], refs[count : count + 2]
+        near, made, sems = refs[count + 2 : 2 * count + 2], refs[-2], refs[-1]
+        copies = [pltpu.make_async_copy(far[n], near[n], sems.at[n]) for n in range(count)]
+        for copy in copies:
+            copy.start()
         for n, w in enumerate(group):
-            left, right = ins[2 * n], ins[2 * n + 1]
-            rows, half = plan.full[w][0], plan.full[w][1] // 2
-            for j in range(plan.chunks[w]):
-                for y in range(2):
-                    cut = slice(y * half + j * plan.chunk, y * half + (j + 1) * plan.chunk)
-                    for at in range(0, rows, 256):
-                        value = dot_l(left[:, at : at + 256], right[:, cut])
-                        made[y, at : at + 256, :] = value.astype(BF16)
-
-                def visit(stack, k, row, w_at, j_at, to_row, to_y, high):
-                    if w_at == w and j_at == j:
-                        stack_refs[stack][k, row : row + high, :] = made[
-                            to_y, pl.ds(to_row, high), :
-                        ]
-
-                each_place(plan, group, where_ref, visit)
-
-    shape = jax.ShapeDtypeStruct((plan.zs, plan.rows(group), plan.chunk), BF16)
-    flat = [a for pair in factors for a in pair]
+            left, right = near[2 * n], near[2 * n + 1]
+            rows, cols = plan.full[w]
+            copies[2 * n].wait()
+            copies[2 * n + 1].wait()
+            for at in range(0, rows, 256):
+                value = dot_l(left[:, at : at + 256], right[...])
+                made[at : at + 256, :cols] = value.astype(BF16)
+
+            def visit(other, stack, k, row, w_at, j, to_row, to_y, high):
+                if w_at == w:
+                    col = pl.multiple_of(to_y * (cols // 2) + j * plan.chunk, 128)
+                    stack_refs[other][stack, k, row : row + high, :] = made[
+                        pl.ds(to_row, high), pl.ds(col, plan.chunk)
+                    ]
+
+            each_place(plan, group, where_ref, visit)
+
+    shape = jax.ShapeDtypeStruct((4, plan.zs, plan.rows(group), plan.chunk), BF16)
     flops = sum(2 * a.shape[0] * a.shape[1] * b.shape[1] for a, b in factors)
-    moved = sum(a.size * 2 for a in flat) + 8 * shape.size * 2
+    moved = sum(a.size * 2 for a in flat) + 2 * shape.size * 2
     return pl.pallas_call(
         body,
-        out_shape=(shape,) * 8,
-        in_specs=[SMEM_SPEC] + [VMEM_SPEC] * len(flat),
-        out_specs=(VMEM_SPEC,) * 8,
-        scratch_shapes=[pltpu.VMEM((2, high_rows, plan.chunk), BF16)],
+        out_shape=(shape,) * 2,
+        in_specs=[SMEM_SPEC] + [pl.BlockSpec(memory_space=pl.ANY)] * count,
+        out_specs=(VMEM_SPEC,) * 2,
+        scratch_shapes=[pltpu.VMEM(a.shape, BF16) for a in flat]
+        + [pltpu.VMEM((high_rows, wide), BF16), pltpu.SemaphoreType.DMA((count,))],
         compiler_params=PARAMS,
         cost_estimate=pl.CostEstimate(flops=flops, bytes_accessed=moved, transcendentals=0),
         name="weight_grads",
@@ -1000,7 +1100,7 @@
 def trade(pieces, parts):
     return [pieces[0]] + [
         lax.ppermute(pieces[k], "patch", [(i, i ^ k) for i in range(parts)])
-        for k in range(1, parts)
+        for k in range(1, len(pieces))
     ]
 
 
@@ -1014,28 +1114,19 @@
         self.lengths, self.counts = lengths.reshape(-1), counts.reshape(-1)
         self.boxes = boxes.reshape((self.items,) + boxes.shape[2:])
         self.dims = Dims(d, self.items, self.text.shape[0] // self.items)
-        self.turn = lax.axis_index("patch").astype(jnp.int32)
+        self.turn = lax.axis_index("patch").astype(jnp.int32).reshape(1)
         self.part, self.vis = self.image_grid.shape[2:]
         self.each = self.items // self.micro
         self.count = -(-(parts * self.part + 1) // 16) * 16
         self.cls = self.image_cls.reshape(self.items, 1, self.vis)
 
-    def cut_grids(self):
-        return [
-            lax.dynamic_slice_in_dim(
-                self.image_grid, (self.turn ^ k) * self.each, self.each, axis=1
-            ).reshape(self.items, self.part, self.vis)
-            for k in range(self.parts)
-        ]
-
     def mask(self):
         boxes = self.boxes.reshape(self.items, -1, self.parts, self.part)
-        order = jnp.arange(self.parts, dtype=jnp.int32) ^ self.turn
+        order = jnp.arange(self.parts, dtype=jnp.int32) ^ self.turn[0]
         boxes = jnp.take(boxes, order, axis=2).reshape(self.boxes.shape)
         return cross_mask(self.lengths, self.counts, boxes, self.dims.length, self.count)
 
-    def finish(self, layer_out, text_grad, grids, cls, grads, rows_grad, bias_grad):
-        grid_grad = place_grids(self.turn.reshape(1), self.micro, grids)
+    def finish(self, layer_out, text_grad, grid_grad, cls, grads, rows_grad, bias_grad):
         return (
             layer_out.reshape(self.text_in.shape),
             text_grad.reshape(self.text_in.shape),
@@ -1065,59 +1156,54 @@
 def on_device(plan, *args):
     work, shards, vectors, ffn_bias = Work(args[:7], plan.patch), args[7:14], args[14], args[15]
     dims, where, parts = work.dims, coords(), plan.patch
-    weights = {}
 
     own, give = pack_split(plan, where, shards)
     units = pack_join(plan, where, own, send(give, plan.core()))
     gathers = [Gathering(plan, unit) for unit in units]
-    grids = work.cut_grids()
-
-    def ready(g):
-        full = assemble(plan, GATHER[g], where, gathers[g].held)
-        for w, value in zip(GATHER[g], full):
-            weights[w] = value
 
     def step(*groups):
         for g in groups:
             gathers[g].advance()
 
+    def source(g):
+        return Source(plan, GROUPS[g], where, gathers[g].held)
+
+    image_grid, vectors, ffn_bias = fence(gathers, [work.image_grid, vectors, ffn_bias])
     step(0)
-    grids = fence(gathers, grids)
-    grids = trade(grids, parts)
+    grids = trade(cut_grids(work.turn, image_grid, parts), parts)
+    (vectors, ffn_bias) = fence(gathers, [vectors, ffn_bias])
+    step(0, 1)
     rows, bias = gather_small(plan, where, vectors, ffn_bias)
     rows = jnp.pad(rows, ((0, -rows.shape[0] % 8), (0, 0)))
+    rows, bias, grids = fence(gathers, [rows, bias, grids])
+    step(0, 1, 2)
+    fence(gathers[:2], [])
     step(0, 1)
-    rows, bias = fence(gathers, [rows, bias])
-    step(0, 2)
-    fence(gathers, [])
-    step(1, 3)
-    ready(0)
-    qkv, probs, ctx, total_one = self_forward(
-        dims, work.text, weights[QKV], weights[OUT], rows, work.lengths
+    (qkv, probs, ctx, total_one), (w_qkv, w_out) = self_forward(
+        dims, source(0), work.text, rows, work.lengths
     )
     mask = work.mask()
     total_one, grids, mask = fence(gathers[1:], [total_one, grids, mask])
-    step(1)
-    fence(gathers[1:], [])
-    step(2, 3)
-    ready(1)
-    hidden_one, query, kv, cross_probs, cross_ctx, total_two, patches = cross_forward(
-        dims, total_one, grids, work.cls, mask, weights[CQ], weights[CKV], weights[COUT], rows
+    step(1, 2)
+    (kv, patches), (w_cq, w_ckv, w_cout) = cross_keys(
+        dims, source(1), grids, work.cls, rows, work.count
+    )
+    kv, total_one = fence(gathers[2:], [kv, total_one])
+    step(2)
+    hidden_one, query, cross_probs, cross_ctx, total_two = cross_forward(
+        dims, total_one, kv, mask, w_cq, w_cout, rows
     )
     total_two = fence(gathers[2:], total_two)
-    step(2, 3)
-    total_two = fence(gathers[2:], total_two)
-    ready(2)
-    ready(3)
-    layer_out, hidden_two, act, slope, grad_three, low_three, sum_three = ffn_forward(
-        dims, total_two, work.cot, weights[FIN], weights[FOUT], rows, bias[None]
+    step(2)
+    (layer_out, hidden_two, act, slope, grad_three, low_three, sum_three), (w_fin, w_fout) = ffn_forward(
+        dims, source(2), total_two, work.cot, rows, bias[None]
     )
 
     reduces = {}
 
     def reduce(g, factors):
-        stacks = weight_grads(plan, REDUCE[g], where, factors)
-        reduces[g] = Reducing(plan, REDUCE[g], where, stacks)
+        stacks = weight_grads(plan, GROUPS[g], where, factors)
+        reduces[g] = Reducing(plan, GROUPS[g], where, stacks)
 
     def hold(*values):
         return fence(list(reduces.values()), list(values))
@@ -1126,22 +1212,15 @@
         for g in groups:
             reduces[g].advance()
 
-    reduce(3, [(act, low_three)])
-    (grad_three,) = hold(grad_three)
-    go(3)
     grad_pre, grad_two, low_two, sum_two, sum_pre = ffn_backward(
-        dims, grad_three, low_three, slope, total_two, weights[FIN], weights[FOUT], rows
-    )
-    grad_pre, grad_two, low_two = hold(grad_pre, grad_two, low_two)
-    go(3)
-    reduce(2, [(hidden_two, grad_pre)])
+        dims, grad_three, low_three, slope, total_two, w_fin, w_fout, rows
+    )
+    reduce(2, [(hidden_two, grad_pre), (act, low_three)])
     (low_two,) = hold(low_two)
-    go(3, 2)
-    grad_query, grad_kv, sum_attend = cross_attend_back(
-        dims, low_two, query, kv, cross_probs, weights[COUT]
-    )
+    go(2)
+    grad_query, grad_kv, sum_attend = cross_attend_back(dims, low_two, query, kv, cross_probs, w_cout)
     grad_query, grad_kv = hold(grad_query, grad_kv)
-    go(3, 2)
+    go(2)
     flat_kv = grad_kv.reshape(-1, grad_kv.shape[2])
     reduce(
         1,
@@ -1151,38 +1230,38 @@
             (cross_ctx, low_two),
         ],
     )
-    grad_query, grad_kv = hold(grad_query, grad_kv)
-    go(3, 2, 1)
     *grids, cls, grad_one, low_one, sum_one = cross_project_back(
-        dims, grad_two, grad_query, grad_kv, total_one, weights[CQ], weights[CKV], rows, parts, work.part
+        dims, grad_two, grad_query, grad_kv, total_one, w_cq, w_ckv, rows, parts, work.part
     )
     low_one, *grids = hold(low_one, *grids)
-    go(3, 2, 1)
-    grids = trade(grids, parts)
-    grad_qkv, sum_self = self_attend_back(dims, low_one, qkv, probs, weights[OUT])
-    grad_qkv, sum_self = hold(grad_qkv, sum_self)
     go(2, 1)
+    grids[1:3] = trade(grids[:3], parts)[1:]
+    grad_qkv, sum_self = self_attend_back(dims, low_one, qkv, probs, w_out)
+    grad_qkv, sum_self, *grids = hold(grad_qkv, sum_self, *grids)
+    go(2, 1)
+    grids[3] = trade(grids, parts)[3]
     reduce(0, [(work.text, grad_qkv), (ctx, low_one)])
     reduces["small"] = ReducingSmall(
         plan, where, rows_of(sum_self, sum_attend, sum_one, sum_two, sum_three), sum_pre[0]
     )
     grad_qkv, *grids = hold(grad_qkv, *grids)
     go(2, 1, 0, "small")
-    text_grad = self_project_back(dims, grad_one, grad_qkv, weights[QKV])
-    hold()
+    (grad_qkv,) = hold(grad_qkv)
+    go(2, 1, 0, "small")
+    text_grad = self_project_back(dims, grad_one, grad_qkv, w_qkv)
+    text_grad, *grids = hold(text_grad, *grids)
     go(1, 0, "small")
-    hold()
+    grid_grad = place_grids(work.turn, work.micro, grids)
+    (grid_grad,) = hold(grid_grad)
     go(1, 0, "small")
-    hold()
-    go(0, "small")
     hold()
     go(0)
     go(0)
     grads = [None] * 7
-    for g, group in enumerate(REDUCE):
+    for g, group in enumerate(GROUPS):
         for w, value in zip(group, reduces[g].held):
             grads[w] = value
-    return work.finish(layer_out, text_grad, grids, cls, grads, *reduces["small"].result())
+    return work.finish(layer_out, text_grad, grid_grad, cls, grads, *reduces["small"].result())
 
 
 def on_device_plain(plan, *args):
@@ -1190,15 +1269,18 @@
     dims = work.dims
     weights, rows, bias = fetch_plain(args[7:14], args[14], args[15])
     rows = jnp.pad(rows, ((0, -rows.shape[0] % 8), (0, 0)))
-    grids = trade(work.cut_grids(), parts)
-    qkv, probs, ctx, total_one = self_forward(
-        dims, work.text, weights[QKV], weights[OUT], rows, work.lengths
-    )
-    hidden_one, query, kv, cross_probs, cross_ctx, total_two, patches = cross_forward(
-        dims, total_one, grids, work.cls, work.mask(), weights[CQ], weights[CKV], weights[COUT], rows
-    )
-    layer_out, hidden_two, act, slope, grad_three, low_three, sum_three = ffn_forward(
-        dims, total_two, work.cot, weights[FIN], weights[FOUT], rows, bias[None]
+    grids = trade(cut_grids(work.turn, work.image_grid, parts), parts)
+
+    def source(g):
+        return Source(plan, GROUPS[g], None, [weights[w] for w in GROUPS[g]])
+
+    (qkv, probs, ctx, total_one), _ = self_forward(dims, source(0), work.text, rows, work.lengths)
+    (kv, patches), _ = cross_keys(dims, source(1), grids, work.cls, rows, work.count)
+    hidden_one, query, cross_probs, cross_ctx, total_two = cross_forward(
+        dims, total_one, kv, work.mask(), weights[CQ], weights[COUT], rows
+    )
+    (layer_out, hidden_two, act, slope, grad_three, low_three, sum_three), _ = ffn_forward(
+        dims, source(2), total_two, work.cot, rows, bias[None]
     )
     grad_pre, grad_two, low_two, sum_two, sum_pre = ffn_backward(
         dims, grad_three, low_three, slope, total_two, weights[FIN], weights[FOUT], rows
@@ -1225,7 +1307,8 @@
     small = reduce_small_plain(
         rows_of(sum_self, sum_attend, sum_one, sum_two, sum_three), sum_pre[0]
     )
-    return work.finish(layer_out, text_grad, trade(grids, parts), cls, grads, *small)
+    grid_grad = place_grids(work.turn, work.micro, trade(grids, parts))
+    return work.finish(layer_out, text_grad, grid_grad, cls, grads, *small)
 
 
 def solution(mesh):

time: 568 us -> 495 us (0.87)
  Pallas kernels: 291 us -> 259 us
  local copies, waits for them, and re-layouts: 70.2 us -> 38.3 us
    pallas_call x24 -> x15, Pallas kernels: 129 us -> 84.5 us  [the longest x3 43.2 us: weight_grads(): pl.pallas_call(body, out_shape=(shape,) * 2, in_specs=[SMEM_SPEC] + [pl.B...]
    ppermute x6, waiting for transfers between devices: 18.6 us -> 0.02 us  [trade(): lax.ppermute(pieces[k], 'patch', [(i, i ^ k) for i in range(parts)])]
    ppermute x95 -> x62, waiting for transfers between devices: 88.9 us -> 106 us  [send(): return lax.ppermute(value, AXES, perm)]
    pallas_call x9 -> x11, Pallas kernels: 149 us -> 164 us  [call(): pl.pallas_call(body, grid=(steps,), out_shape=out_shape, in_specs=[spec f...]
    unnamed x143 -> x80, local copies, waits for them, and re-layouts: 21.4 us -> 8.17 us
    ppermute x95 -> x62, starting transfers between devices: 76.8 us -> 65.3 us  [send(): return lax.ppermute(value, AXES, perm)]
    squeeze x4 -> x0, local copies, waits for them, and re-layouts: 7.63 us -> none  [advance(): parts = [send(total[k], plan.z_up(plan.zs - k)) for k in range(1, plan.zs)]]
    dynamic_slice x5 -> x0, local copies, waits for them, and re-layouts: 7.52 us -> none  [cut_grids(): lax.dynamic_slice_in_dim(self.image_grid, (self.turn ^ k) * self.each, se...]
  transfers between devices with their start and end apart: 101 -> 68, of which waited for: 19 -> 21; matrix products, arithmetic and copies ran while one was open for 11% -> 7% of each run, Pallas kernels for 36% -> 32%
where the time goes in v4:
time: 495 us; the launch traced here: 488 us
  Pallas kernels  259 us (52%)
  waiting for transfers between devices  106 us (21%)
  starting transfers between devices  76 us (15%)
  local copies, waits for them, and re-layouts  38.3 us (8%)
  other arithmetic  6.15 us (1%)
    pallas_call x11, Pallas kernels, call(): pl.pallas_call(body, grid=(steps,), out_shape=out_shape, in_specs=[spec f...  164 us
    ppermute x62, waiting for transfers between devices, send(): return lax.ppermute(value, AXES, perm)  106 us
    ppermute x62, starting transfers between devices, send(): return lax.ppermute(value, AXES, perm)  65.3 us
    pallas_call x3, Pallas kernels, weight_grads(): pl.pallas_call(body, out_shape=(shape,) * 2, in_specs=[SMEM_SPEC] + [pl.B...  43.2 us
    pallas_call x6, Pallas kernels, add_low(): pl.pallas_call(body, grid=(slots,), out_shape=tuple((jax.ShapeDtypeStruct...  28.5 us
    optimization_barrier x9, local copies, waits for them, and re-layouts, fence(): values, held = jax.tree.unflatten(tree, lax.optimization_barrier(flat))  11.7 us
    ppermute x6, starting transfers between devices, trade(): lax.ppermute(pieces[k], 'patch', [(i, i ^ k) for i in range(parts)])  10.7 us
  transfers between devices with their start and end apart: 68, of which 21 were waited for; matrix products, arithmetic and copies ran while one was open for 7% of the time, Pallas kernels for 32%

profile of v4, /device:TPU:0, one launch (start us, length us, event | category | flops | bytes accessed | tf_op | source)
XLA Modules:
  0.0 487.8 jit_solution(15620178129748219742)
XLA Ops:
  1.3 2.2 pack_split.1
  6.3 2.1 pack_join.1
  8.5 5.0 %collective-permute-start.3 = (bf16[192,384]{1,0:T(8,128)(2,1)}, bf16[192,384]{1,0:T(8,128)(2,1)S(1)}, u32[]{:S(2)}, u32[]{:S(2)}) collective-permute-start(bf16[192,384]{1,0:T(8,128)(2,1)} %get-tuple-element.273), channel_id=1, source_target_pairs={{0,24},{1,25},{2,26},{3,27},{4,28},{5,29},{6,30},{7,31},{8,0},{9,1... | collective-permute-start | bytes 442376 | tf_op jit(solution)/shard_map/ppermute | solution.py:62
  14.5 3.6 collective-permute-done.3
  18.0 8.4 %collective-permute-done.2 = bf16[192,384]{1,0:T(8,128)(2,1)S(1)} collective-permute-done((bf16[192,384]{1,0:T(8,128)(2,1)}, bf16[192,384]{1,0:T(8,128)(2,1)S(1)}, u32[]{:S(2)}, u32[]{:S(2)}) %collective-permute-start.2) | collective-permute-done | bytes 147488 | tf_op jit(solution)/shard_map/ppermute | solution.py:62
  28.1 3.1 cut_grids.1
  32.8 2.3 copy.37
  43.6 2.2 collective-permute-start.9
  49.1 8.3 %collective-permute-done.13 = bf16[224,384]{1,0:T(8,128)(2,1)} collective-permute-done((bf16[224,384]{1,0:T(8,128)(2,1)S(1)}, bf16[224,384]{1,0:T(8,128)(2,1)}, u32[]{:S(2)}, u32[]{:S(2)}) %collective-permute-start.13) | collective-permute-done | bytes 172064 | tf_op jit(solution)/shard_map/ppermute | solution.py:62
  58.9 6.1 %collective-permute-done.12 = bf16[224,384]{1,0:T(8,128)(2,1)} collective-permute-done((bf16[224,384]{1,0:T(8,128)(2,1)S(1)}, bf16[224,384]{1,0:T(8,128)(2,1)}, u32[]{:S(2)}, u32[]{:S(2)}) %collective-permute-start.12) | collective-permute-done | bytes 172064 | tf_op jit(solution)/shard_map/ppermute | solution.py:62
  67.3 5.4 %collective-permute-start.17 = (bf16[4,192,384]{2,1,0:T(8,128)(2,1)S(1)}, bf16[4,192,384]{2,1,0:T(8,128)(2,1)}, u32[]{:S(2)}, u32[]{:S(2)}) collective-permute-start(bf16[4,192,384]{2,1,0:T(8,128)(2,1)S(1)} %pad_maximum_fusion.2.refs_1_), channel_id=1, source_target_pairs={{0,1},{1,0},{2,3},{3,2},{4,5},{5,4},{6,7},{7,6},{8,9},{9,8},{10,11... | collective-permute-start | bytes 1769480 | tf_op jit(solution)/shard_map/ppermute | solution.py:62
  76.1 12.8 %collective-permute-done.15.refs_3_ = bf16[4,192,384]{2,1,0:T(8,128)(2,1)} collective-permute-done((bf16[4,192,384]{2,1,0:T(8,128)(2,1)S(1)}, bf16[4,192,384]{2,1,0:T(8,128)(2,1)}, u32[]{:S(2)}, u32[]{:S(2)}) %collective-permute-start.15) | collective-permute-done | bytes 589856 | tf_op jit(solution)/shard_map/ppermute | solution.py:62
  88.9 6.3 %collective-permute-done.16.refs_4_ = bf16[4,192,384]{2,1,0:T(8,128)(2,1)} collective-permute-done((bf16[4,192,384]{2,1,0:T(8,128)(2,1)}, bf16[4,192,384]{2,1,0:T(8,128)(2,1)}, u32[]{:S(2)}, u32[]{:S(2)}) %collective-permute-start.16) | collective-permute-done | bytes 589856 | tf_op jit(solution)/shard_map/ppermute | solution.py:62
  99.5 5.6 %collective-permute-done.28 = bf16[384,384]{1,0:T(8,128)(2,1)S(1)} collective-permute-done((bf16[384,384]{1,0:T(8,128)(2,1)}, bf16[384,384]{1,0:T(8,128)(2,1)S(1)}, u32[]{:S(2)}, u32[]{:S(2)}) %collective-permute-start.28) | collective-permute-done | bytes 294944 | tf_op jit(solution)/shard_map/ppermute | solution.py:62
  105.7 13.1 %collective-permute-done.27 = bf16[384,384]{1,0:T(8,128)(2,1)S(1)} collective-permute-done((bf16[384,384]{1,0:T(8,128)(2,1)}, bf16[384,384]{1,0:T(8,128)(2,1)S(1)}, u32[]{:S(2)}, u32[]{:S(2)}) %collective-permute-start.27) | collective-permute-done | bytes 294944 | tf_op jit(solution)/shard_map/ppermute | solution.py:62
  121.6 16.2 %self_forward.1 = (bf16[1024,2304]{1,0:T(8,128)(2,1)}, bf16[8,6,128,256]{3,2,1,0:T(8,128)(2,1)}, bf16[1024,768]{1,0:T(8,128)(2,1)}, f32[1024,768]{1,0:T(8,128)},...) custom-call(s32[8]{0:T(128)} %copy-done.33, bf16[1024,768]{1,0:T(8,128)(2,1)} %bitcast.84, ...), custom_call_target="tpu_custom_call" | custom-call | flops 7247757312 | bytes 23642160 | tf_op jit(solution)/shard_map/self_forward/pallas_call | solution.py:508
  144.7 11.0 %cross_keys.1 = (bf16[8,160,1536]{2,1,0:T(8,128)(2,1)}, bf16[8,160,1024]{2,1,0:T(8,128)(2,1)}, bf16[768,768]{1,0:T(8,128)(2,1)}, bf16[1024,1536]{1,0:T(8,128)(2,1)}, bf16[768,768]{1,0:T(8,128)(2,1)}) custom-call(bf16[8,36,1024]{2,1,0:T(8,128)(2,1)} %get-tuple-element.300.refs_0_, bf16[8,36,1024]{2,1,0:T(8,128)(2,1)} %copy.43.refs_1_, ...), custom_call_target="tpu_custom_call" | custom-call | flops 4026531840 | bytes 19988496 | tf_op jit(solution)/shard_map/cross_keys/pallas_call | solution.py:508
  158.8 17.6 %cross_forward.1 = (bf16[1024,768]{1,0:T(8,128)(2,1)}, bf16[1024,768]{1,0:T(8,128)(2,1)}, bf16[8,6,160,256]{3,2,1,0:T(8,128)(2,1)}, bf16[1024,768]{1,0:T(8,128)(2,1)}, f32[1024,768]{1,0:T(8,128)}) custom-call(f32[1024,768]{1,0:T(8,128)} %get-tuple-element.316.tot_ref, bf16[8,160,1536]{2,1,0:T(8,128)(2,1)} %get-tuple-element.317.kv_ref, ...), custom_call_target="tpu_custom_call" | custom-call | flops 7247757312 | bytes 21610496 | tf_op jit(solution)/shard_map/cross_forward/pallas_call | solution.py:508
  176.5 8.3 %collective-permute-done.33.refs_4_ = bf16[4,384,384]{2,1,0:T(8,128)(2,1)} collective-permute-done((bf16[4,384,384]{2,1,0:T(8,128)(2,1)}, bf16[4,384,384]{2,1,0:T(8,128)(2,1)}, u32[]{:S(2)}, u32[]{:S(2)}) %collective-permute-start.33) | collective-permute-done | bytes 1179680 | tf_op jit(solution)/shard_map/ppermute | solution.py:62
  185.3 4.2 collective-permute-done.36.refs_7_
  190.5 34.3 %ffn_forward.1 = (f32[1024,768]{1,0:T(8,128)}, bf16[1024,768]{1,0:T(8,128)(2,1)}, bf16[1024,3072]{1,0:T(8,128)(2,1)}, bf16[1024,3072]{1,0:T(8,128)(2,1)}, f32[10...) custom-call(f32[1024,768]{1,0:T(8,128)} %get-tuple-element.324.tot_r, ...), custom_call_target="tpu_custom_call" | custom-call | flops 9663676416 | bytes 45699088 | tf_op jit(solution)/shard_map/ffn_forward/pallas_call | solution.py:508
  224.9 18.5 %ffn_backward.1 = (bf16[1024,3072]{1,0:T(8,128)(2,1)}, f32[1024,768]{1,0:T(8,128)}, bf16[1024,768]{1,0:T(8,128)(2,1)}, f32[8,768]{1,0:T(8,128)}, f32[8,3072]{1,0:T(8,128)}) custom-call(f32[1024,768]{1,0:T(8,128)} %get-tuple-element.333.g_ref, bf16[1024,768]{1,0:T(8,128)(2,1)} %get-tuple-element.334.glow_ref.refs_3_, ...), custom_call_target="tpu_custom_call" | custom-call | flops 9663676416 | bytes 34775040 | tf_op jit(solution)/shard_map/ffn_backward/pallas_call | solution.py:508
  243.3 18.4 %weight_grads.3 = (bf16[4,4,384,384]{3,2,1,0:T(8,128)(2,1)}, bf16[4,4,384,384]{3,2,1,0:T(8,128)(2,1)}) custom-call(s32[4]{0:T(128)} %pad_add_fusion.where_ref.refs_0_.refs_6_, bf16[1024,768]{1,0:T(8,128)(2,1)} %get-tuple-element.340.refs_0_, bf16[1024,3072]{1,0:T(8,128)(2,1)} %get-tuple-element.341.refs_1_, bf16[1024,3072]{1,0:T(8,128)(2,1)} %get-tuple-element.342.refs_2_, ...), custom_call_target="tpu_custom_call" | custom-call | flops 9663676416 | bytes 25165824 | tf_op jit(solution)/shard_map/weight_grads/pallas_call | solution.py:1064
  261.9 17.3 %cross_attend_back.1 = (bf16[1024,768]{1,0:T(8,128)(2,1)}, bf16[8,160,1536]{2,1,0:T(8,128)(2,1)}, f32[8,768]{1,0:T(8,128)}) custom-call(bf16[1024,768]{1,0:T(8,128)(2,1)} %get-tuple-element.345.glow_ref.refs_5_, bf16[1024,768]{1,0:T(8,128)(2,1)} %get-tuple-element.346.q_ref, bf16[8,160,1536]{2,1,0:T(8,128)(2,1)} %get-tuple-element.317.kv_ref, ...), custom_call_target="tpu_custom_call" | custom-call | flops 4831838208 | bytes 17719296 | tf_op jit(solution)/shard_map/cross_attend_back/pallas_call | solution.py:508
  279.2 6.7 %add_low.6 = (bf16[2,4,384,384]{3,2,1,0:T(8,128)(2,1)}, bf16[2,4,384,384]{3,2,1,0:T(8,128)(2,1)}) custom-call(bf16[4,4,384,384]{3,2,1,0:T(8,128)(2,1)} %get-tuple-element.361.one_ref, bf16[4,4,384,384]{3,2,1,0:T(8,128)(2,1)} %collective-permute-done.38.two_ref), custom_call_target="tpu_custom_call" | custom-call | flops 2359296 | bytes 14155776 | tf_op jit(solution)/shard_map/add_low/pallas_call | solution.py:209
  287.3 15.8 %cross_project_back.1 = (bf16[8,36,1024]{2,1,0:T(8,128)(2,1)}, bf16[8,36,1024]{2,1,0:T(8,128)(2,1)}, bf16[8,36,1024]{2,1,0:T(8,128)(2,1)}, bf16[8,36,1024]{2,1,0...) custom-call(f32[1024,768]{1,0:T(8,128)} %get-tuple-element.338.g_ref, ...), custom_call_target="tpu_custom_call" | custom-call | flops 5234491392 | bytes 23306240 | tf_op jit(solution)/shard_map/cross_project_back/pallas_call | solution.py:508
  303.1 13.2 %weight_grads.4 = (bf16[4,4,224,384]{3,2,1,0:T(8,128)(2,1)}, bf16[4,4,224,384]{3,2,1,0:T(8,128)(2,1)}) custom-call(s32[4]{0:T(128)} %pad_add_fusion.where_ref.refs_0_.refs_6_, bf16[1024,768]{1,0:T(8,128)(2,1)} %get-tuple-element.365.refs_0_, bf16[1024,768]{1,0:T(8,128)(2,1)} %get-tuple-element.352.gq_ref.refs_1_, bf16[1280,1024]{1,0:T(8,128)(2,1)} %bitcast.89, ...), custom_call_target="tpu_custom_call" | custom-call | flops 6442450944 | bytes 18350080 | tf_op jit(solution)/shard_map/weight_grads/pallas_call | solution.py:1064
  316.6 4.4 add_low.7
  325.4 16.7 %self_attend_back.1 = (bf16[1024,2304]{1,0:T(8,128)(2,1)}, f32[8,768]{1,0:T(8,128)}) custom-call(bf16[1024,768]{1,0:T(8,128)(2,1)} %get-tuple-element.370.glow_ref.refs_3_, bf16[1024,2304]{1,0:T(8,128)(2,1)} %get-tuple-element.371.qkv_ref, bf16[8,6,128,256]{3,2,1,0:T(8,128)(2,1)} %get-tuple-element.372.prob_ref, bf16[768,768]{1,0:T(8,128)(2,1)} %get-tuple-element.373.wout_ref), custom_call_target="tpu_custom_call" | custom-call | flops 4831838208 | bytes 15360000 | tf_op jit(solution)/shard_map/self_attend_back/pallas_call | solution.py:508
  343.0 5.3 %add_low.8 = (bf16[2,4,224,384]{3,2,1,0:T(8,128)(2,1)}, bf16[2,4,224,384]{3,2,1,0:T(8,128)(2,1)}) custom-call(bf16[4,4,224,384]{3,2,1,0:T(8,128)(2,1)} %get-tuple-element.397.one_ref, bf16[4,4,224,384]{3,2,1,0:T(8,128)(2,1)} %collective-permute-done.43.two_ref), custom_call_target="tpu_custom_call" | custom-call | flops 1376256 | bytes 8257536 | tf_op jit(solution)/shard_map/add_low/pallas_call | solution.py:209
  350.8 7.3 %collective-permute-start.44 = (bf16[8,36,1024]{2,0,1:T(8,128)(2,1)}, bf16[8,36,1024]{2,0,1:T(8,128)(2,1)S(1)}, u32[]{:S(2)}, u32[]{:S(2)}) collective-permute-start(bf16[8,36,1024]{2,0,1:T(8,128)(2,1)} %copy.49), channel_id=1, source_target_pairs={{0,3},{1,2},{2,1},{3,0},{4,7},{5,6},{6,5},{7,4},{8,11},{9,10},{10,... | collective-permute-start | bytes 1769480 | tf_op jit(solution)/shard_map/ppermute | solution.py:1102
  365.6 2.7 add_slots.3
  368.3 3.8 collective-permute-start.45
  373.7 11.6 %weight_grads.5 = (bf16[4,4,192,384]{3,2,1,0:T(8,128)(2,1)}, bf16[4,4,192,384]{3,2,1,0:T(8,128)(2,1)}) custom-call(s32[4]{0:T(128)} %pad_add_fusion.where_ref.refs_0_.refs_6_, bf16[1024,768]{1,0:T(8,128)(2,1)} %bitcast.85, bf16[1024,2304]{1,0:T(8,128)(2,1)} %get-tuple-element.424.refs_1_.gqkv_ref, bf16[1024,768]{1,0:T(8,128)(2,1)} %get-tuple-element.401.refs_2_, ...), custom_call_target="tpu_custom_call" | custom-call | flops 4831838208 | bytes 14155776 | tf_op jit(solution)/shard_map/weight_grads/pallas_call | solution.py:1064
  385.4 11.7 %collective-permute-done.46.refs_2_ = bf16[384,384]{1,0:T(8,128)(2,1)} collective-permute-done((bf16[384,384]{1,0:T(8,128)(2,1)}, bf16[384,384]{1,0:T(8,128)(2,1)}, u32[]{:S(2)}, u32[]{:S(2)}) %collective-permute-start.46) | collective-permute-done | bytes 294944 | tf_op jit(solution)/shard_map/ppermute | solution.py:62
  398.1 3.8 add_low.9
  402.5 2.3 unpack_split.3
  406.8 6.3 %collective-permute-done.50.two_ref = bf16[1,4,224,384]{3,2,1,0:T(8,128)(2,1)S(1)} collective-permute-done((bf16[1,4,224,384]{3,2,1,0:T(8,128)(2,1)}, bf16[1,4,224,384]{3,2,1,0:T(8,128)(2,1)S(1)}, u32[]{:S(2)}, u32[]{:S(2)}) %collective-permute-start.50) | collective-permute-done | bytes 688160 | tf_op jit(solution)/shard_map/ppermute | solution.py:62
  413.1 4.7 add_low.10
  420.0 2.2 add_slots.4
  422.2 3.0 collective-permute-start.54
  427.1 9.0 %self_project_back.1 = f32[1024,768]{1,0:T(8,128)} custom-call(f32[1024,768]{1,0:T(8,128)} %get-tuple-element.355.g_ref, bf16[1024,2304]{1,0:T(8,128)(2,1)} %get-tuple-element.424.refs_1_.gqkv_ref, bf16[768,2304]{1,0:T(8,128)(2,1)} %get-tuple-element.425.wqkv_ref), custom_call_target="tpu_custom_call" | custom-call | flops 3623878656 | bytes 14548992 | tf_op jit(solution)/shard_map/self_project_back/pallas_call | solution.py:508
  439.8 3.6 add_low.11
  447.7 2.2 copy.50.refs_1_
  452.3 4.2 place_grids.1
  462.2 2.4 collective-permute-start.66
  465.7 6.8 %collective-permute-done.66 = f32[104,128]{1,0:T(8,128)S(1)} collective-permute-done((f32[104,128]{1,0:T(8,128)S(1)}, f32[104,128]{1,0:T(8,128)S(1)}, u32[]{:S(2)}, u32[]{:S(2)}) %collective-permute-start.66) | collective-permute-done | bytes 53280 | tf_op jit(solution)/shard_map/ppermute | solution.py:62
  472.5 5.6 %collective-permute-start.64 = (f32[104,128]{1,0:T(8,128)S(1)}, f32[104,128]{1,0:T(8,128)S(1)}, u32[]{:S(2)}, u32[]{:S(2)}) collective-permute-start(f32[104,128]{1,0:T(8,128)S(1)} %add.146), channel_id=1, source_target_pairs={{0,8},{1,9},{2,10},{3,11},{4,12},{5,13},{6,14},{7,15},{8,16},{9,17... | collective-permute-start | bytes 159752 | tf_op jit(solution)/shard_map/ppermute | solution.py:62
  (277 shorter events, 98.5 us)
Async XLA Ops:
  13.4 13.0 %collective-permute-start.2 = (bf16[192,384]{1,0:T(8,128)(2,1)}, bf16[192,384]{1,0:T(8,128)(2,1)S(1)}, u32[]{:S(2)}, u32[]{:S(2)}) collective-permute-start(bf16[192,384]{1,0:T(8,128)(2,1)} %get-tuple-element.273), channel_id=1, source_target_pairs={{0,16},{1,17},{2,18},{3,19},{4,20},{5,21},{6,22},{7,23},{8,24},{9,... | collective-permute-start | bytes 442376 | tf_op jit(solution)/shard_map/ppermute | solution.py:62
  13.4 13.0 %collective-permute-start.1 = (bf16[192,384]{1,0:T(8,128)(2,1)}, bf16[192,384]{1,0:T(8,128)(2,1)S(1)}, u32[]{:S(2)}, u32[]{:S(2)}) collective-permute-start(bf16[192,384]{1,0:T(8,128)(2,1)} %get-tuple-element.273), channel_id=1, source_target_pairs={{0,8},{1,9},{2,10},{3,11},{4,12},{5,13},{6,14},{7,15},{8,16},{9,17... | collective-permute-start | bytes 442376 | tf_op jit(solution)/shard_map/ppermute | solution.py:62
  26.6 10.9 %collective-permute-start.4 = (bf16[16,128]{1,0:T(8,128)(2,1)S(1)}, bf16[16,128]{1,0:T(8,128)(2,1)S(1)}, u32[]{:S(2)}, u32[]{:S(2)}) collective-permute-start(bf16[16,128]{1,0:T(8,128)(2,1)S(1)} %get-tuple-element.502), channel_id=1, source_target_pairs={{0,4},{1,5},{2,6},{3,7},{4,0},{5,1},{6,2},{7,3},{8,12},{9,13},{10,... | collective-permute-start | bytes 12296 | tf_op jit(solution)/shard_map/ppermute | solution.py:62
  36.2 28.9 %collective-permute-start.10 = (bf16[8,36,1024]{2,0,1:T(8,128)(2,1)}, bf16[8,36,1024]{2,0,1:T(8,128)(2,1)S(1)}, u32[]{:S(2)}, u32[]{:S(2)}) collective-permute-start(bf16[8,36,1024]{2,0,1:T(8,128)(2,1)} %copy.38), channel_id=1, source_target_pairs={{0,3},{1,2},{2,1},{3,0},{4,7},{5,6},{6,5},{7,4},{8,11},{9,10},{10,... | collective-permute-start | bytes 1769480 | tf_op jit(solution)/shard_map/ppermute | solution.py:1102
  43.6 21.5 %collective-permute-start.9 = (bf16[8,36,1024]{2,0,1:T(8,128)(2,1)}, bf16[8,36,1024]{2,0,1:T(8,128)(2,1)S(1)}, u32[]{:S(2)}, u32[]{:S(2)}) collective-permute-start(bf16[8,36,1024]{2,0,1:T(8,128)(2,1)} %copy.37), channel_id=1, source_target_pairs={{0,2},{1,3},{2,0},{3,1},{4,6},{5,7},{6,4},{7,5},{8,10},{9,11},{10,... | collective-permute-start | bytes 1769480 | tf_op jit(solution)/shard_map/ppermute | solution.py:1102
  45.9 19.3 %collective-permute-start.8 = (bf16[8,36,1024]{2,0,1:T(8,128)(2,1)S(1)}, bf16[8,36,1024]{2,0,1:T(8,128)(2,1)S(1)}, u32[]{:S(2)}, u32[]{:S(2)}) collective-permute-start(bf16[8,36,1024]{2,0,1:T(8,128)(2,1)S(1)} %copy.36), channel_id=1, source_target_pairs={{0,1},{1,0},{2,3},{3,2},{4,5},{5,4},{6,7},{7,6},{8,9},{9,8},{10,11... | collective-permute-start | bytes 1769480 | tf_op jit(solution)/shard_map/ppermute | solution.py:1102
  46.0 11.4 %collective-permute-start.13 = (bf16[224,384]{1,0:T(8,128)(2,1)S(1)}, bf16[224,384]{1,0:T(8,128)(2,1)}, u32[]{:S(2)}, u32[]{:S(2)}) collective-permute-start(bf16[224,384]{1,0:T(8,128)(2,1)S(1)} %copy-done.23), channel_id=1, source_target_pairs={{0,16},{1,17},{2,18},{3,19},{4,20},{5,21},{6,22},{7,23},{8,24},{9,... | collective-permute-start | bytes 516104 | tf_op jit(solution)/shard_map/ppermute | solution.py:62
  47.9 17.2 %collective-permute-start.11 = (bf16[4,192,384]{2,1,0:T(8,128)(2,1)S(1)}, bf16[4,192,384]{2,1,0:T(8,128)(2,1)}, u32[]{:S(2)}, u32[]{:S(2)}) collective-permute-start(bf16[4,192,384]{2,1,0:T(8,128)(2,1)S(1)} %pad_maximum_fusion.2.refs_1_), channel_id=1, source_target_pairs={{0,4},{1,3},{2,6},{3,1},{4,0},{5,7},{6,2},{7,5},{8,12},{9,11},{10,... | collective-permute-start | bytes 1769480 | tf_op jit(solution)/shard_map/ppermute | solution.py:62
  66.7 28.5 %collective-permute-start.19 = (bf16[4,224,384]{2,1,0:T(8,128)(2,1)S(1)}, bf16[4,224,384]{2,1,0:T(8,128)(2,1)}, u32[]{:S(2)}, u32[]{:S(2)}) collective-permute-start(bf16[4,224,384]{2,1,0:T(8,128)(2,1)S(1)} %pad_maximum_fusion.1.refs_7_), channel_id=1, source_target_pairs={{0,4},{1,3},{2,6},{3,1},{4,0},{5,7},{6,2},{7,5},{8,12},{9,11},{10,... | collective-permute-start | bytes 2064392 | tf_op jit(solution)/shard_map/ppermute | solution.py:62
  72.8 16.1 %collective-permute-start.15 = (bf16[4,192,384]{2,1,0:T(8,128)(2,1)S(1)}, bf16[4,192,384]{2,1,0:T(8,128)(2,1)}, u32[]{:S(2)}, u32[]{:S(2)}) collective-permute-start(bf16[4,192,384]{2,1,0:T(8,128)(2,1)S(1)} %pad_maximum_fusion.2.refs_1_), channel_id=1, source_target_pairs={{0,2},{1,5},{2,0},{3,7},{4,6},{5,1},{6,4},{7,3},{8,10},{9,13},{10,... | collective-permute-start | bytes 1769480 | tf_op jit(solution)/shard_map/ppermute | solution.py:62
  74.2 14.6 %collective-permute-start.18 = (bf16[4,192,384]{2,1,0:T(8,128)(2,1)}, bf16[4,192,384]{2,1,0:T(8,128)(2,1)}, u32[]{:S(2)}, u32[]{:S(2)}) collective-permute-start(bf16[4,192,384]{2,1,0:T(8,128)(2,1)} %collective-permute-done.11.refs_2_), channel_id=1, source_target_pairs={{0,1},{1,0},{2,3},{3,2},{4,5},{5,4},{6,7},{7,6},{8,9},{9,8},{10,11... | collective-permute-start | bytes 1769480 | tf_op jit(solution)/shard_map/ppermute | solution.py:62
  74.2 21.0 %collective-permute-start.16 = (bf16[4,192,384]{2,1,0:T(8,128)(2,1)}, bf16[4,192,384]{2,1,0:T(8,128)(2,1)}, u32[]{:S(2)}, u32[]{:S(2)}) collective-permute-start(bf16[4,192,384]{2,1,0:T(8,128)(2,1)} %collective-permute-done.11.refs_2_), channel_id=1, source_target_pairs={{0,2},{1,5},{2,0},{3,7},{4,6},{5,1},{6,4},{7,3},{8,10},{9,13},{10,... | collective-permute-start | bytes 1769480 | tf_op jit(solution)/shard_map/ppermute | solution.py:62
  95.2 23.5 %collective-permute-start.20 = (bf16[4,192,384]{2,1,0:T(8,128)(2,1)}, bf16[4,192,384]{2,1,0:T(8,128)(2,1)}, u32[]{:S(2)}, u32[]{:S(2)}) collective-permute-start(bf16[4,192,384]{2,1,0:T(8,128)(2,1)} %collective-permute-done.15.refs_3_), channel_id=1, source_target_pairs={{0,1},{1,0},{2,3},{3,2},{4,5},{5,4},{6,7},{7,6},{8,9},{9,8},{10,11... | collective-permute-start | bytes 1769480 | tf_op jit(solution)/shard_map/ppermute | solution.py:62
  96.8 22.0 %collective-permute-start.27 = (bf16[384,384]{1,0:T(8,128)(2,1)}, bf16[384,384]{1,0:T(8,128)(2,1)S(1)}, u32[]{:S(2)}, u32[]{:S(2)}) collective-permute-start(bf16[384,384]{1,0:T(8,128)(2,1)} %get-tuple-element.312), channel_id=1, source_target_pairs={{0,16},{1,17},{2,18},{3,19},{4,20},{5,21},{6,22},{7,23},{8,24},{9,... | collective-permute-start | bytes 884744 | tf_op jit(solution)/shard_map/ppermute | solution.py:62
  98.3 22.2 %collective-permute-start.21 = (bf16[4,192,384]{2,1,0:T(8,128)(2,1)}, bf16[4,192,384]{2,1,0:T(8,128)(2,1)S(1)}, u32[]{:S(2)}, u32[]{:S(2)}) collective-permute-start(bf16[4,192,384]{2,1,0:T(8,128)(2,1)} %collective-permute-done.16.refs_4_), channel_id=1, source_target_pairs={{0,1},{1,0},{2,3},{3,2},{4,5},{5,4},{6,7},{7,6},{8,9},{9,8},{10,11... | collective-permute-start | bytes 1769480 | tf_op jit(solution)/shard_map/ppermute | solution.py:62
  99.1 38.7 %collective-permute-start.24 = (bf16[4,224,384]{2,1,0:T(8,128)(2,1)S(1)}, bf16[4,224,384]{2,1,0:T(8,128)(2,1)}, u32[]{:S(2)}, u32[]{:S(2)}) collective-permute-start(bf16[4,224,384]{2,1,0:T(8,128)(2,1)S(1)} %pad_maximum_fusion.1.refs_7_), channel_id=1, source_target_pairs={{0,1},{1,0},{2,3},{3,2},{4,5},{5,4},{6,7},{7,6},{8,9},{9,8},{10,11... | collective-permute-start | bytes 2064392 | tf_op jit(solution)/shard_map/ppermute | solution.py:62
  105.1 32.8 %collective-permute-start.22 = (bf16[4,224,384]{2,1,0:T(8,128)(2,1)S(1)}, bf16[4,224,384]{2,1,0:T(8,128)(2,1)}, u32[]{:S(2)}, u32[]{:S(2)}) collective-permute-start(bf16[4,224,384]{2,1,0:T(8,128)(2,1)S(1)} %pad_maximum_fusion.1.refs_7_), channel_id=1, source_target_pairs={{0,2},{1,5},{2,0},{3,7},{4,6},{5,1},{6,4},{7,3},{8,10},{9,13},{10,... | collective-permute-start | bytes 2064392 | tf_op jit(solution)/shard_map/ppermute | solution.py:62
  118.7 19.1 %collective-permute-start.25 = (bf16[4,224,384]{2,1,0:T(8,128)(2,1)}, bf16[4,224,384]{2,1,0:T(8,128)(2,1)}, u32[]{:S(2)}, u32[]{:S(2)}) collective-permute-start(bf16[4,224,384]{2,1,0:T(8,128)(2,1)} %collective-permute-done.19.refs_8_), channel_id=1, source_target_pairs={{0,1},{1,0},{2,3},{3,2},{4,5},{5,4},{6,7},{7,6},{8,9},{9,8},{10,11... | collective-permute-start | bytes 2064392 | tf_op jit(solution)/shard_map/ppermute | solution.py:62
  118.7 19.1 %collective-permute-start.23 = (bf16[4,224,384]{2,1,0:T(8,128)(2,1)}, bf16[4,224,384]{2,1,0:T(8,128)(2,1)}, u32[]{:S(2)}, u32[]{:S(2)}) collective-permute-start(bf16[4,224,384]{2,1,0:T(8,128)(2,1)} %collective-permute-done.19.refs_8_), channel_id=1, source_target_pairs={{0,2},{1,5},{2,0},{3,7},{4,6},{5,1},{6,4},{7,3},{8,10},{9,13},{10,... | collective-permute-start | bytes 2064392 | tf_op jit(solution)/shard_map/ppermute | solution.py:62
  121.3 16.5 %collective-permute-start.26 = (bf16[384,384]{1,0:T(8,128)(2,1)}, bf16[384,384]{1,0:T(8,128)(2,1)}, u32[]{:S(2)}, u32[]{:S(2)}) collective-permute-start(bf16[384,384]{1,0:T(8,128)(2,1)} %get-tuple-element.312), channel_id=1, source_target_pairs={{0,8},{1,9},{2,10},{3,11},{4,12},{5,13},{6,14},{7,15},{8,16},{9,17... | collective-permute-start | bytes 884744 | tf_op jit(solution)/shard_map/ppermute | solution.py:62
  139.4 16.4 %collective-permute-start.31 = (bf16[4,384,384]{2,1,0:T(8,128)(2,1)S(1)}, bf16[4,384,384]{2,1,0:T(8,128)(2,1)}, u32[]{:S(2)}, u32[]{:S(2)}) collective-permute-start(bf16[4,384,384]{2,1,0:T(8,128)(2,1)S(1)} %pad_maximum_fusion.refs_1_), channel_id=1, source_target_pairs={{0,4},{1,3},{2,6},{3,1},{4,0},{5,7},{6,2},{7,5},{8,12},{9,11},{10,... | collective-permute-start | bytes 3538952 | tf_op jit(solution)/shard_map/ppermute | solution.py:62
  155.7 20.7 %collective-permute-start.34 = (bf16[4,384,384]{2,1,0:T(8,128)(2,1)S(1)}, bf16[4,384,384]{2,1,0:T(8,128)(2,1)}, u32[]{:S(2)}, u32[]{:S(2)}) collective-permute-start(bf16[4,384,384]{2,1,0:T(8,128)(2,1)S(1)} %pad_maximum_fusion.refs_1_), channel_id=1, source_target_pairs={{0,1},{1,0},{2,3},{3,2},{4,5},{5,4},{6,7},{7,6},{8,9},{9,8},{10,11... | collective-permute-start | bytes 3538952 | tf_op jit(solution)/shard_map/ppermute | solution.py:62
  155.8 20.7 %collective-permute-start.32 = (bf16[4,384,384]{2,1,0:T(8,128)(2,1)S(1)}, bf16[4,384,384]{2,1,0:T(8,128)(2,1)}, u32[]{:S(2)}, u32[]{:S(2)}) collective-permute-start(bf16[4,384,384]{2,1,0:T(8,128)(2,1)S(1)} %pad_maximum_fusion.refs_1_), channel_id=1, source_target_pairs={{0,2},{1,5},{2,0},{3,7},{4,6},{5,1},{6,4},{7,3},{8,10},{9,13},{10,... | collective-permute-start | bytes 3538952 | tf_op jit(solution)/shard_map/ppermute | solution.py:62
  157.2 19.2 %collective-permute-start.35 = (bf16[4,384,384]{2,1,0:T(8,128)(2,1)}, bf16[4,384,384]{2,1,0:T(8,128)(2,1)}, u32[]{:S(2)}, u32[]{:S(2)}) collective-permute-start(bf16[4,384,384]{2,1,0:T(8,128)(2,1)} %collective-permute-done.31.refs_2_), channel_id=1, source_target_pairs={{0,1},{1,0},{2,3},{3,2},{4,5},{5,4},{6,7},{7,6},{8,9},{9,8},{10,11... | collective-permute-start | bytes 3538952 | tf_op jit(solution)/shard_map/ppermute | solution.py:62
  157.5 27.3 %collective-permute-start.33 = (bf16[4,384,384]{2,1,0:T(8,128)(2,1)}, bf16[4,384,384]{2,1,0:T(8,128)(2,1)}, u32[]{:S(2)}, u32[]{:S(2)}) collective-permute-start(bf16[4,384,384]{2,1,0:T(8,128)(2,1)} %collective-permute-done.31.refs_2_), channel_id=1, source_target_pairs={{0,2},{1,5},{2,0},{3,7},{4,6},{5,1},{6,4},{7,3},{8,10},{9,13},{10,... | collective-permute-start | bytes 3538952 | tf_op jit(solution)/shard_map/ppermute | solution.py:62
  261.7 17.5 %collective-permute-start.38 = (bf16[4,4,384,384]{3,2,1,0:T(8,128)(2,1)}, bf16[4,4,384,384]{3,2,1,0:T(8,128)(2,1)}, u32[]{:S(2)}, u32[]{:S(2)}) collective-permute-start(bf16[4,4,384,384]{3,2,1,0:T(8,128)(2,1)} %get-tuple-element.351), channel_id=1, source_target_pairs={{0,1},{1,0},{2,3},{3,2},{4,5},{5,4},{6,7},{7,6},{8,9},{9,8},{10,11... | collective-permute-start | bytes 14155784 | tf_op jit(solution)/shard_map/ppermute | solution.py:62
  286.0 30.3 %collective-permute-start.39 = (bf16[2,4,384,384]{3,2,1,0:T(8,128)(2,1)}, bf16[2,4,384,384]{3,2,1,0:T(8,128)(2,1)}, u32[]{:S(2)}, u32[]{:S(2)}) collective-permute-start(bf16[2,4,384,384]{3,2,1,0:T(8,128)(2,1)} %get-tuple-element.364), channel_id=1, source_target_pairs={{0,2},{1,5},{2,0},{3,7},{4,6},{5,1},{6,4},{7,3},{8,10},{9,13},{10,... | collective-permute-start | bytes 7077896 | tf_op jit(solution)/shard_map/ppermute | solution.py:62
  316.3 25.9 %collective-permute-start.43 = (bf16[4,4,224,384]{3,2,1,0:T(8,128)(2,1)}, bf16[4,4,224,384]{3,2,1,0:T(8,128)(2,1)}, u32[]{:S(2)}, u32[]{:S(2)}) collective-permute-start(bf16[4,4,224,384]{3,2,1,0:T(8,128)(2,1)} %get-tuple-element.385), channel_id=1, source_target_pairs={{0,1},{1,0},{2,3},{3,2},{4,5},{5,4},{6,7},{7,6},{8,9},{9,8},{10,11... | collective-permute-start | bytes 8257544 | tf_op jit(solution)/shard_map/ppermute | solution.py:62
  321.0 21.2 %collective-permute-start.42 = (bf16[1,4,384,384]{3,2,1,0:T(8,128)(2,1)}, bf16[1,4,384,384]{3,2,1,0:T(8,128)(2,1)S(1)}, u32[]{:S(2)}, u32[]{:S(2)}) collective-permute-start(bf16[1,4,384,384]{3,2,1,0:T(8,128)(2,1)} %get-tuple-element.383), channel_id=1, source_target_pairs={{0,4},{1,3},{2,6},{3,1},{4,0},{5,7},{6,2},{7,5},{8,12},{9,11},{10,... | collective-permute-start | bytes 3538952 | tf_op jit(solution)/shard_map/ppermute | solution.py:62
  324.7 17.5 %collective-permute-start.41 = (bf16[8,36,1024]{2,0,1:T(8,128)(2,1)}, bf16[8,36,1024]{2,0,1:T(8,128)(2,1)S(1)}, u32[]{:S(2)}, u32[]{:S(2)}) collective-permute-start(bf16[8,36,1024]{2,0,1:T(8,128)(2,1)} %copy.48), channel_id=1, source_target_pairs={{0,2},{1,3},{2,0},{3,1},{4,6},{5,7},{6,4},{7,5},{8,10},{9,11},{10,... | collective-permute-start | bytes 1769480 | tf_op jit(solution)/shard_map/ppermute | solution.py:1102
  325.4 16.8 %collective-permute-start.40 = (bf16[8,36,1024]{2,0,1:T(8,128)(2,1)}, bf16[8,36,1024]{2,0,1:T(8,128)(2,1)}, u32[]{:S(2)}, u32[]{:S(2)}) collective-permute-start(bf16[8,36,1024]{2,0,1:T(8,128)(2,1)} %copy.47), channel_id=1, source_target_pairs={{0,1},{1,0},{2,3},{3,2},{4,5},{5,4},{6,7},{7,6},{8,9},{9,8},{10,11... | collective-permute-start | bytes 1769480 | tf_op jit(solution)/shard_map/ppermute | solution.py:1102
  348.3 48.8 %collective-permute-start.48 = (bf16[2,4,224,384]{3,2,1,0:T(8,128)(2,1)}, bf16[2,4,224,384]{3,2,1,0:T(8,128)(2,1)S(1)}, u32[]{:S(2)}, u32[]{:S(2)}) collective-permute-start(bf16[2,4,224,384]{3,2,1,0:T(8,128)(2,1)} %get-tuple-element.400), channel_id=1, source_target_pairs={{0,2},{1,5},{2,0},{3,7},{4,6},{5,1},{6,4},{7,3},{8,10},{9,13},{10,... | collective-permute-start | bytes 4128776 | tf_op jit(solution)/shard_map/ppermute | solution.py:62
  350.8 46.2 %collective-permute-start.44 = (bf16[8,36,1024]{2,0,1:T(8,128)(2,1)}, bf16[8,36,1024]{2,0,1:T(8,128)(2,1)S(1)}, u32[]{:S(2)}, u32[]{:S(2)}) collective-permute-start(bf16[8,36,1024]{2,0,1:T(8,128)(2,1)} %copy.49), channel_id=1, source_target_pairs={{0,3},{1,2},{2,1},{3,0},{4,7},{5,6},{6,5},{7,4},{8,11},{9,10},{10,... | collective-permute-start | bytes 1769480 | tf_op jit(solution)/shard_map/ppermute | solution.py:1102
  368.3 17.0 %collective-permute-start.45 = (bf16[384,384]{1,0:T(8,128)(2,1)}, bf16[384,384]{1,0:T(8,128)(2,1)}, u32[]{:S(2)}, u32[]{:S(2)}) collective-permute-start(bf16[384,384]{1,0:T(8,128)(2,1)} %get-tuple-element.394), channel_id=1, source_target_pairs={{0,24},{1,25},{2,26},{3,27},{4,28},{5,29},{6,30},{7,31},{8,0},{9,1... | collective-permute-start | bytes 884744 | tf_op jit(solution)/shard_map/ppermute | solution.py:62
  372.1 24.9 %collective-permute-start.46 = (bf16[384,384]{1,0:T(8,128)(2,1)}, bf16[384,384]{1,0:T(8,128)(2,1)}, u32[]{:S(2)}, u32[]{:S(2)}) collective-permute-start(bf16[384,384]{1,0:T(8,128)(2,1)} %get-tuple-element.395), channel_id=1, source_target_pairs={{0,16},{1,17},{2,18},{3,19},{4,20},{5,21},{6,22},{7,23},{8,24},{9,... | collective-permute-start | bytes 884744 | tf_op jit(solution)/shard_map/ppermute | solution.py:62
  372.1 24.9 %collective-permute-start.47 = (bf16[384,384]{1,0:T(8,128)(2,1)}, bf16[384,384]{1,0:T(8,128)(2,1)}, u32[]{:S(2)}, u32[]{:S(2)}) collective-permute-start(bf16[384,384]{1,0:T(8,128)(2,1)} %get-tuple-element.396), channel_id=1, source_target_pairs={{0,8},{1,9},{2,10},{3,11},{4,12},{5,13},{6,14},{7,15},{8,16},{9,17... | collective-permute-start | bytes 884744 | tf_op jit(solution)/shard_map/ppermute | solution.py:62
  397.1 16.0 %collective-permute-start.51 = (bf16[4,4,192,384]{3,2,1,0:T(8,128)(2,1)}, bf16[4,4,192,384]{3,2,1,0:T(8,128)(2,1)}, u32[]{:S(2)}, u32[]{:S(2)}) collective-permute-start(bf16[4,4,192,384]{3,2,1,0:T(8,128)(2,1)} %get-tuple-element.422), channel_id=1, source_target_pairs={{0,1},{1,0},{2,3},{3,2},{4,5},{5,4},{6,7},{7,6},{8,9},{9,8},{10,11... | collective-permute-start | bytes 7077896 | tf_op jit(solution)/shard_map/ppermute | solution.py:62
  401.9 11.1 %collective-permute-start.50 = (bf16[1,4,224,384]{3,2,1,0:T(8,128)(2,1)}, bf16[1,4,224,384]{3,2,1,0:T(8,128)(2,1)S(1)}, u32[]{:S(2)}, u32[]{:S(2)}) collective-permute-start(bf16[1,4,224,384]{3,2,1,0:T(8,128)(2,1)} %get-tuple-element.420), channel_id=1, source_target_pairs={{0,4},{1,3},{2,6},{3,1},{4,0},{5,7},{6,2},{7,5},{8,12},{9,11},{10,... | collective-permute-start | bytes 2064392 | tf_op jit(solution)/shard_map/ppermute | solution.py:62
  417.8 21.0 %collective-permute-start.56 = (bf16[2,4,192,384]{3,2,1,0:T(8,128)(2,1)}, bf16[2,4,192,384]{3,2,1,0:T(8,128)(2,1)S(1)}, u32[]{:S(2)}, u32[]{:S(2)}) collective-permute-start(bf16[2,4,192,384]{3,2,1,0:T(8,128)(2,1)} %get-tuple-element.443), channel_id=1, source_target_pairs={{0,2},{1,5},{2,0},{3,7},{4,6},{5,1},{6,4},{7,3},{8,10},{9,13},{10,... | collective-permute-start | bytes 3538952 | tf_op jit(solution)/shard_map/ppermute | solution.py:62
  418.6 19.7 %collective-permute-start.57 = (f32[104,128]{1,0:T(8,128)S(1)}, f32[104,128]{1,0:T(8,128)S(1)}, u32[]{:S(2)}, u32[]{:S(2)}) collective-permute-start(f32[104,128]{1,0:T(8,128)S(1)} %add.144), channel_id=1, source_target_pairs={{0,2},{1,3},{2,0},{3,1},{4,6},{5,7},{6,4},{7,5},{8,10},{9,11},{10,... | collective-permute-start | bytes 159752 | tf_op jit(solution)/shard_map/ppermute | solution.py:62
  422.2 16.1 %collective-permute-start.53 = (bf16[224,384]{1,0:T(8,128)(2,1)}, bf16[224,384]{1,0:T(8,128)(2,1)}, u32[]{:S(2)}, u32[]{:S(2)}) collective-permute-start(bf16[224,384]{1,0:T(8,128)(2,1)} %get-tuple-element.437), channel_id=1, source_target_pairs={{0,24},{1,25},{2,26},{3,27},{4,28},{5,29},{6,30},{7,31},{8,0},{9,1... | collective-permute-start | bytes 516104 | tf_op jit(solution)/shard_map/ppermute | solution.py:62
  422.2 16.6 %collective-permute-start.54 = (bf16[224,384]{1,0:T(8,128)(2,1)}, bf16[224,384]{1,0:T(8,128)(2,1)}, u32[]{:S(2)}, u32[]{:S(2)}) collective-permute-start(bf16[224,384]{1,0:T(8,128)(2,1)} %get-tuple-element.438), channel_id=1, source_target_pairs={{0,16},{1,17},{2,18},{3,19},{4,20},{5,21},{6,22},{7,23},{8,24},{9,... | collective-permute-start | bytes 516104 | tf_op jit(solution)/shard_map/ppermute | solution.py:62
  425.1 13.7 %collective-permute-start.55 = (bf16[224,384]{1,0:T(8,128)(2,1)}, bf16[224,384]{1,0:T(8,128)(2,1)}, u32[]{:S(2)}, u32[]{:S(2)}) collective-permute-start(bf16[224,384]{1,0:T(8,128)(2,1)} %get-tuple-element.439), channel_id=1, source_target_pairs={{0,8},{1,9},{2,10},{3,11},{4,12},{5,13},{6,14},{7,15},{8,16},{9,17... | collective-permute-start | bytes 516104 | tf_op jit(solution)/shard_map/ppermute | solution.py:62
  443.5 13.0 %collective-permute-start.59 = (bf16[1,4,192,384]{3,2,1,0:T(8,128)(2,1)}, bf16[1,4,192,384]{3,2,1,0:T(8,128)(2,1)S(1)}, u32[]{:S(2)}, u32[]{:S(2)}) collective-permute-start(bf16[1,4,192,384]{3,2,1,0:T(8,128)(2,1)} %get-tuple-element.462), channel_id=1, source_target_pairs={{0,4},{1,3},{2,6},{3,1},{4,0},{5,7},{6,2},{7,5},{8,12},{9,11},{10,... | collective-permute-start | bytes 1769480 | tf_op jit(solution)/shard_map/ppermute | solution.py:62
  459.4 21.3 %collective-permute-start.61 = (bf16[192,384]{1,0:T(8,128)(2,1)}, bf16[192,384]{1,0:T(8,128)(2,1)S(1)}, u32[]{:S(2)}, u32[]{:S(2)}) collective-permute-start(bf16[192,384]{1,0:T(8,128)(2,1)} %get-tuple-element.477), channel_id=1, source_target_pairs={{0,24},{1,25},{2,26},{3,27},{4,28},{5,29},{6,30},{7,31},{8,0},{9,1... | collective-permute-start | bytes 442376 | tf_op jit(solution)/shard_map/ppermute | solution.py:62
  460.7 20.0 %collective-permute-start.62 = (bf16[192,384]{1,0:T(8,128)(2,1)}, bf16[192,384]{1,0:T(8,128)(2,1)S(1)}, u32[]{:S(2)}, u32[]{:S(2)}) collective-permute-start(bf16[192,384]{1,0:T(8,128)(2,1)} %get-tuple-element.478), channel_id=1, source_target_pairs={{0,16},{1,17},{2,18},{3,19},{4,20},{5,21},{6,22},{7,23},{8,24},{9,... | collective-permute-start | bytes 442376 | tf_op jit(solution)/shard_map/ppermute | solution.py:62
  460.7 20.0 %collective-permute-start.63 = (bf16[192,384]{1,0:T(8,128)(2,1)}, bf16[192,384]{1,0:T(8,128)(2,1)S(1)}, u32[]{:S(2)}, u32[]{:S(2)}) collective-permute-start(bf16[192,384]{1,0:T(8,128)(2,1)} %get-tuple-element.479), channel_id=1, source_target_pairs={{0,8},{1,9},{2,10},{3,11},{4,12},{5,13},{6,14},{7,15},{8,16},{9,17... | collective-permute-start | bytes 442376 | tf_op jit(solution)/shard_map/ppermute | solution.py:62
  464.6 16.1 %collective-permute-start.65 = (f32[104,128]{1,0:T(8,128)S(1)}, f32[104,128]{1,0:T(8,128)S(1)}, u32[]{:S(2)}, u32[]{:S(2)}) collective-permute-start(f32[104,128]{1,0:T(8,128)S(1)} %add.146), channel_id=1, source_target_pairs={{0,16},{1,17},{2,18},{3,19},{4,20},{5,21},{6,22},{7,23},{8,24},{9,... | collective-permute-start | bytes 159752 | tf_op jit(solution)/shard_map/ppermute | solution.py:62
  (59 other events, 715.4 us)
